TPU v7x, 256 devices: a whole 4x4x8 slice. The times are simulated.
256 devices in a mesh: prow: 4 (over z_hi, core), pcol: 4 (over y), pl: 16 (over z_lo, x).
Axes of the slice: x: 4, y: 4, z: 8 (z_hi: 2, z_lo: 4; z = z_hi * 4 + z_lo), core: 2. Of those that a mesh axis runs over, the one named last changes fastest.
Arguments:
- factor_cols: bfloat16 [32768, 4096], P(('prow', 'pcol'), 'pl'), may hold values from -0.09375 to 0.09375
- modal_at_loads: bfloat16 [2048, 32768], P(None, ('prow', 'pcol')), may hold values from -0.03125 to 0.03125
- mode_shapes: bfloat16 [8192, 2048], P(('prow', 'pl')), may hold values from -0.125 to 0.125
- natural_freq: float32 [2048], replicated, may hold values from 0.5 to 2
- damping: float32 [2048], replicated, may hold values from 0.05 to 0.2
Outputs:
- cospectrum: float32 [8192, 8192], P(('prow', 'pl'), 'pcol')
All inputs are finite; a program needn't handle non-finite values.
Results may differ from a plain program's by a relative error of at most 0.022.
Values may be sent and summed in bfloat16 or wider, within the bound.
A program may use at most 128 MiB of HBM per device.

v0:
```python
import jax
import jax.numpy as jnp
from jax import lax
from jax.sharding import PartitionSpec as P


def from_root(array, axis, root):
    mine = lax.axis_index(axis) == root
    return lax.psum(jnp.where(mine, array, jnp.zeros_like(array)), axis)


def transfer_pair(natural_freq, damping):
    detuning = natural_freq * natural_freq - 1.0
    damper = 2.0 * damping * natural_freq
    modulus = detuning * detuning + damper * damper
    return (detuning / modulus, -damper / modulus)


def outer_rows(left_rows, right_rows):
    return lax.dot_general(
        left_rows, right_rows, (((1,), (1,)), ((), ())), preferred_element_type=jnp.float32
    )


def body(factor_cols, modal_at_loads, mode_shapes, natural_freq, damping):
    in_phase, quadrature = transfer_pair(natural_freq, damping)
    own_rows = lax.psum_scatter(
        jnp.dot(modal_at_loads, factor_cols, preferred_element_type=jnp.float32),
        ("prow", "pcol"),
        scatter_dimension=0,
        tiled=True,
    )
    modal_load = lax.all_gather(own_rows.astype(jnp.bfloat16), ("prow", "pcol"), axis=0, tiled=True)
    modal_wide = modal_load.astype(jnp.float32)
    pseudo = jnp.concatenate(
        [
            (in_phase[:, None] * modal_wide).astype(jnp.bfloat16),
            (quadrature[:, None] * modal_wide).astype(jnp.bfloat16),
        ],
        axis=1,
    )
    block = pseudo.shape[0] // lax.axis_size(("prow", "pcol"))
    first_row = lax.axis_index(("prow", "pcol")) * block
    own_pseudo = lax.dynamic_slice_in_dim(pseudo, first_row, block, 0)
    partial_gram = outer_rows(own_pseudo, pseudo)
    gram_block = lax.psum(partial_gram.astype(jnp.bfloat16), "pl")
    modal_gram = lax.all_gather(gram_block, ("prow", "pcol"), axis=0, tiled=True)
    weighted = jnp.dot(mode_shapes, modal_gram, preferred_element_type=jnp.float32).astype(
        jnp.bfloat16
    )
    panel_piece = from_root(mode_shapes, "prow", lax.axis_index("pcol"))
    return outer_rows(weighted, lax.all_gather(panel_piece, "pl", axis=0, tiled=True))


def solution(mesh):
    in_specs = (
        P(("prow", "pcol"), "pl"),
        P(None, ("prow", "pcol")),
        P(("prow", "pl"), None),
        P(),
        P(),
    )
    out_specs = P(("prow", "pl"), "pcol")
    return jax.shard_map(body, mesh=mesh, in_specs=in_specs, out_specs=out_specs, check_vma=False)
```

profile of v0, /device:TPU:39, one launch (start us, length us, event | category | flops | bytes accessed | tf_op | source)
XLA Modules:
  0.0 561.5 jit_solution(14018947487908811836)
XLA Ops:
  7.4 0.0 copy-start
  7.4 0.0 copy-start.1
  7.4 0.0 copy-start.3
  7.4 0.0 copy-start.2
  7.4 0.0 reduce-scatter.2.cloned.1.call-start
  7.4 1.2 copy-done
  8.6 7.1 %fusion.8 = f32[2048,256]{1,0:T(8,128)} fusion(bf16[2048,2048]{1,0:T(8,128)(2,1)} %param.6, bf16[2048,256]{1,0:T(8,128)(2,1)S(1)} %copy-done), kind=kOutput, calls=%fused_computation.19 | convolution fusion | flops 2147483648 | bytes 11534336 | tf_op jit(solution)/shard_map/dot_general | solution.py:28
  15.7 0.0 reduce-scatter.2.cloned.1.call-update
  15.7 0.0 all-gather.4.cloned.1.call-start
  15.7 87.0 %reduce-scatter.2.cloned.1.call-done = f32[128,256]{1,0:T(8,128)} async-done(((f32[2048,256]{1,0:T(8,128)}), f32[128,256]{1,0:T(8,128)}) %reduce-scatter.2.cloned.1.call-update) | async-done | bytes 131088 | tf_op jit(solution)/shard_map/reduce_scatter | solution.py:27
  102.7 1.5 convert_element_type.19
  104.2 0.0 all-gather.4.cloned.1.call-update
  104.3 0.0 all-reduce.5.cloned.1.call-start
  104.3 0.0 copy-done.1
  104.3 0.8 broadcast_select_fusion
  105.2 0.0 all-reduce.5.cloned.1.call-update
  105.2 0.0 all-reduce.3.cloned.1.call-start
  105.3 0.0 copy-done.3
  105.3 0.0 copy-done.2
  105.3 57.7 %all-gather.4.cloned.1.call-done = bf16[2048,256]{1,0:T(8,128)(2,1)} async-done(((bf16[128,256]{1,0:T(8,128)(2,1)}), bf16[2048,256]{1,0:T(8,128)(2,1)}) %all-gather.4.cloned.1.call-update) | async-done | bytes 1048592 | tf_op jit(solution)/shard_map/all_gather | solution.py:33
  163.0 1.8 fusion
  164.8 1.7 convolution_convert_fusion.1
  166.4 0.0 all-reduce.3.cloned.1.call-update
  166.4 0.0 all-gather.8.cloned.1.call-start
  166.5 0.0 all-reduce.5.cloned.1.call-done
  166.5 0.5 all-gather.8.cloned.1.call-update
  167.0 0.0 all-gather.6.cloned.1.call-start
  167.1 140.2 %all-reduce.3.cloned.1.call-done = bf16[128,2048]{1,0:T(8,128)(2,1)} async-done(((bf16[128,2048]{1,0:T(8,128)(2,1)}), bf16[128,2048]{1,0:T(8,128)(2,1)}) %all-reduce.3.cloned.1.call-update) | async-done | bytes 524304 | tf_op jit(solution)/shard_map/psum | solution.py:46
  307.2 0.0 all-gather.6.cloned.1.call-update
  307.3 118.7 %all-gather.8.cloned.1.call-done = bf16[2048,2048]{1,0:T(8,128)(2,1)} async-done(((bf16[128,2048]{1,0:T(8,128)(2,1)}), bf16[2048,2048]{1,0:T(8,128)(2,1)}) %all-gather.8.cloned.1.call-update) | async-done | bytes 8388624 | tf_op jit(solution)/shard_map/all_gather | solution.py:52
  426.0 112.4 %all-gather.6.cloned.1.call-done = bf16[2048,2048]{1,0:T(8,128)(2,1)} async-done(((bf16[128,2048]{1,0:T(8,128)(2,1)}), bf16[2048,2048]{1,0:T(8,128)(2,1)}) %all-gather.6.cloned.1.call-update) | async-done | bytes 8388624 | tf_op jit(solution)/shard_map/all_gather | solution.py:47
  538.4 15.5 %fusion.2 = f32[128,2048]{1,0:T(8,128)} fusion(bf16[2048,2048]{1,0:T(8,128)(2,1)} %all-gather.8.cloned.1.call-done, bf16[2048,2048]{1,0:T(8,128)(2,1)} %all-gather.6.cloned.1.call-done, bf16[128,2048]{1,0:T(8,128)(2,1)S(1)} %copy-done.1), kind=kOutput, calls=%fused_computation.9 | convolution fusion | flops 2147745792 | bytes 18350080 | tf_op jit(solution)/shard_map/dot_general | solution.py:20
  (1 shorter events, 0.0 us)
Async XLA Ops:
  7.4 1.2 copy-start
  7.4 97.0 %copy-start.1 = (bf16[128,2048]{1,0:T(8,128)(2,1)S(1)}, bf16[128,2048]{1,0:T(8,128)(2,1)}, u32[]{:S(2)}) copy-start(bf16[128,2048]{1,0:T(8,128)(2,1)} %param.7) | copy-start | bytes 1572868
  7.4 97.9 %copy-start.3 = (f32[2048]{0:T(1024)S(1)}, f32[2048]{0:T(1024)}, u32[]{:S(2)}) copy-start(f32[2048]{0:T(1024)} %param.9) | copy-start | bytes 24580
  7.4 97.9 %copy-start.2 = (f32[2048]{0:T(1024)S(1)}, f32[2048]{0:T(1024)}, u32[]{:S(2)}) copy-start(f32[2048]{0:T(1024)} %param.8) | copy-start | bytes 24580
  7.4 95.3 %reduce-scatter.2.cloned.1.call-start = ((), (), s32[]{:S(2)}) async-start(), calls=%async_computation.1 | async-start | bytes 2228224 | tf_op jit(solution)/shard_map/reduce_scatter | solution.py:27
  15.7 147.3 %all-gather.4.cloned.1.call-start = ((), (), s32[]{:S(2)}) async-start(), calls=%async_computation.2 | async-start | bytes 1114112 | tf_op jit(solution)/shard_map/all_gather | solution.py:33
  104.3 62.2 %all-reduce.5.cloned.1.call-start = ((), (), s32[]{:S(2)}) async-start(), calls=%async_computation.5 | async-start | bytes 1048576 | tf_op jit(solution)/shard_map/psum | solution.py:9
  105.2 202.0 %all-reduce.3.cloned.1.call-start = ((), (), s32[]{:S(2)}) async-start(), calls=%async_computation.3 | async-start | bytes 1048576 | tf_op jit(solution)/shard_map/psum | solution.py:46
  166.4 259.5 %all-gather.8.cloned.1.call-start = ((), (), s32[]{:S(2)}) async-start(), calls=%async_computation.6 | async-start | bytes 8912896 | tf_op jit(solution)/shard_map/all_gather | solution.py:52
  167.0 371.4 %all-gather.6.cloned.1.call-start = ((), (), s32[]{:S(2)}) async-start(), calls=%async_computation.4 | async-start | bytes 8912896 | tf_op jit(solution)/shard_map/all_gather | solution.py:47
Sparse Core Ops, SparseCore 0:
  15.8 86.8 reduce-scatter.1
  105.5 57.4 all-gather.3
Sparse Core Ops, SparseCore 1:
  107.4 57.2 all-reduce.4
  167.1 140.1 all-reduce.2
  309.0 116.9 all-gather.7
  429.1 109.2 all-gather.5
where the time goes:
time: 564 us; the launch traced here: 562 us
  waiting for transfers between devices  517 us (92%)
  matrix products  24.2 us (4%)
  between operations  15.1 us (3%)
    psum x1, waiting for transfers between devices, body(): gram_block = lax.psum(partial_gram.astype(jnp.bfloat16), 'pl')  140 us
    all_gather x1, waiting for transfers between devices, body(): lax.all_gather(panel_piece, 'pl', axis=0, tiled=True)  119 us
    all_gather x1, waiting for transfers between devices, body(): lax.all_gather(gram_block, ('prow', 'pcol'), axis=0, tiled=True)  112 us
    reduce_scatter x1, waiting for transfers between devices, body(): lax.psum_scatter(jnp.dot(modal_at_loads, factor_cols, preferred_element_t...  87 us
    all_gather x1, waiting for transfers between devices, body(): lax.all_gather(own_rows.astype(jnp.bfloat16), ('prow', 'pcol'), axis=0, t...  57.7 us
    dot_general x2, matrix products, outer_rows(): lax.dot_general(left_rows, right_rows, (((1,), (1,)), ((), ())), preferre...  17.1 us
  transfers between devices with their start and end apart: 6, of which 5 were waited for; matrix products, arithmetic and copies ran while one was open for 1% of the time, Pallas kernels for 0%

commit v1 on v0

v1 whole, which is shorter than its diff:
```python
import jax
import jax.numpy as jnp
from jax import lax
from jax.sharding import PartitionSpec as P


def transfer_pair(natural_freq, damping):
    detuning = natural_freq * natural_freq - 1.0
    damper = 2.0 * damping * natural_freq
    modulus = detuning * detuning + damper * damper
    return (detuning / modulus, -damper / modulus)


def outer_rows(left_rows, right_rows):
    return lax.dot_general(
        left_rows, right_rows, (((1,), (1,)), ((), ())), preferred_element_type=jnp.float32
    )


def make_body(n_row, n_col):
    swap = [(c * n_col + r, r * n_col + c) for r in range(n_row) for c in range(n_col)]

    def body(factor_cols, modal_at_loads, mode_shapes, natural_freq, damping):
        in_phase, quadrature = transfer_pair(natural_freq, damping)
        own_rows = lax.psum_scatter(
            jnp.dot(modal_at_loads, factor_cols, preferred_element_type=jnp.float32),
            ("prow", "pcol"),
            scatter_dimension=0,
            tiled=True,
        )
        modal_load = lax.all_gather(own_rows.astype(jnp.bfloat16), ("prow", "pcol"), axis=0, tiled=True)
        modal_wide = modal_load.astype(jnp.float32)
        pseudo = jnp.concatenate(
            [
                (in_phase[:, None] * modal_wide).astype(jnp.bfloat16),
                (quadrature[:, None] * modal_wide).astype(jnp.bfloat16),
            ],
            axis=1,
        )
        block = pseudo.shape[0] // (n_row * n_col)
        row, col = lax.axis_index("prow"), lax.axis_index("pcol")
        first_row = (col * n_row + row) * block
        own_pseudo = lax.dynamic_slice_in_dim(pseudo, first_row, block, 0)
        partial_gram = outer_rows(own_pseudo, pseudo)
        gram_block = lax.psum(partial_gram.astype(jnp.bfloat16), "pl")
        gram_panel = lax.all_gather(gram_block, "prow", axis=0, tiled=True)
        weighted_part = outer_rows(mode_shapes, gram_panel).astype(jnp.bfloat16)
        weighted = lax.all_gather(weighted_part, "pcol", axis=1, tiled=True)
        panel_piece = lax.ppermute(mode_shapes, ("prow", "pcol"), swap)
        return outer_rows(weighted, lax.all_gather(panel_piece, "pl", axis=0, tiled=True))

    return body


def solution(mesh):
    in_specs = (
        P(("prow", "pcol"), "pl"),
        P(None, ("prow", "pcol")),
        P(("prow", "pl"), None),
        P(),
        P(),
    )
    out_specs = P(("prow", "pl"), "pcol")
    body = make_body(mesh.shape["prow"], mesh.shape["pcol"])
    return jax.shard_map(body, mesh=mesh, in_specs=in_specs, out_specs=out_specs, check_vma=False)
```

time: 564 us -> 489 us (0.87)
  waiting for transfers between devices: 517 us -> 421 us
  starting transfers between devices: 0.25 us -> 14.3 us
  blocking collectives: 0 us -> 10 us
  matrix products: 24.2 us -> 18.3 us
    all_gather x1, waiting for transfers between devices: 112 us -> 42.4 us  [body(): gram_panel = lax.all_gather(gram_block, 'prow', axis=0, tiled=True)]
    all_gather x1, waiting for transfers between devices: 119 us -> 91.5 us  [body(): lax.all_gather(panel_piece, 'pl', axis=0, tiled=True)]
    ppermute x0 -> x1, starting transfers between devices: none -> 14.1 us  [body(): panel_piece = lax.ppermute(mode_shapes, ('prow', 'pcol'), swap)]
    all_gather x0 -> x1, blocking collectives: none -> 10 us  [body(): weighted = lax.all_gather(weighted_part, 'pcol', axis=1, tiled=True)]
    ppermute x0 -> x1, waiting for transfers between devices: none -> 8.1 us  [body(): panel_piece = lax.ppermute(mode_shapes, ('prow', 'pcol'), swap)]
    dot_general x2 -> x3, matrix products: 17.1 us -> 11.2 us  [outer_rows(): lax.dot_general(left_rows, right_rows, (((1,), (1,)), ((), ())), preferre...]
  transfers between devices with their start and end apart: 6 -> 6, of which waited for: 5 -> 6; matrix products, arithmetic and copies ran while one was open for 1% -> 0% of each run, Pallas kernels for 0% -> 0%
where the time goes in v1:
time: 489 us; the launch traced here: 482 us
  waiting for transfers between devices  421 us (86%)
  matrix products  18.3 us (4%)
  starting transfers between devices  14.3 us (3%)
  between operations  13.2 us (3%)
  blocking collectives  10 us (2%)
    psum x1, waiting for transfers between devices, body(): gram_block = lax.psum(partial_gram.astype(jnp.bfloat16), 'pl')  137 us
    all_gather x1, waiting for transfers between devices, body(): lax.all_gather(panel_piece, 'pl', axis=0, tiled=True)  91.5 us
    reduce_scatter x1, waiting for transfers between devices, body(): lax.psum_scatter(jnp.dot(modal_at_loads, factor_cols, preferred_element_t...  87 us
    all_gather x1, waiting for transfers between devices, body(): lax.all_gather(own_rows.astype(jnp.bfloat16), ('prow', 'pcol'), axis=0, t...  55.6 us
    all_gather x1, waiting for transfers between devices, body(): gram_panel = lax.all_gather(gram_block, 'prow', axis=0, tiled=True)  42.4 us
    ppermute x1, starting transfers between devices, body(): panel_piece = lax.ppermute(mode_shapes, ('prow', 'pcol'), swap)  14.1 us
    dot_general x3, matrix products, outer_rows(): lax.dot_general(left_rows, right_rows, (((1,), (1,)), ((), ())), preferre...  11.2 us
    all_gather x1, blocking collectives, body(): weighted = lax.all_gather(weighted_part, 'pcol', axis=1, tiled=True)  10 us
  transfers between devices with their start and end apart: 6, of which 6 were waited for; matrix products, arithmetic and copies ran while one was open for 0% of the time, Pallas kernels for 0%

profile of v1, /device:TPU:39, one launch (start us, length us, event | category | flops | bytes accessed | tf_op | source)
XLA Modules:
  0.0 482.4 jit_solution(12734103664353830712)
XLA Ops:
  6.5 0.0 copy-start
  6.5 0.0 reduce-scatter.2.cloned.1.call-start
  6.5 1.2 copy-done
  7.8 7.1 %fusion.8 = f32[2048,256]{1,0:T(8,128)} fusion(bf16[2048,2048]{1,0:T(8,128)(2,1)} %param.6, bf16[2048,256]{1,0:T(8,128)(2,1)S(1)} %copy-done), kind=kOutput, calls=%fused_computation.18 | convolution fusion | flops 2147483648 | bytes 11534336 | tf_op jit(solution)/shard_map/dot_general | solution.py:26
  14.8 0.0 copy-start.3
  14.8 0.0 copy-start.4
  14.8 0.0 reduce-scatter.2.cloned.1.call-update
  14.9 0.0 all-gather.4.cloned.1.call-start
  14.9 87.0 %reduce-scatter.2.cloned.1.call-done = f32[128,256]{1,0:T(8,128)} async-done(((f32[2048,256]{1,0:T(8,128)}), f32[128,256]{1,0:T(8,128)}) %reduce-scatter.2.cloned.1.call-update) | async-done | bytes 131088 | tf_op jit(solution)/shard_map/reduce_scatter | solution.py:25
  101.9 1.5 convert_element_type.21
  103.4 0.0 all-gather.4.cloned.1.call-update
  103.5 0.0 all-reduce.2.cloned.1.call-start
  103.5 0.0 copy-done.3
  103.5 0.0 copy-done.4
  103.6 55.6 %all-gather.4.cloned.1.call-done = bf16[2048,256]{1,0:T(8,128)(2,1)} async-done(((bf16[128,256]{1,0:T(8,128)(2,1)}), bf16[2048,256]{1,0:T(8,128)(2,1)}) %all-gather.4.cloned.1.call-update) | async-done | bytes 1048592 | tf_op jit(solution)/shard_map/all_gather | solution.py:31
  159.1 1.8 fusion
  160.9 0.0 copy-start.2
  160.9 1.6 convolution_convert_fusion
  162.5 0.0 all-reduce.2.cloned.1.call-update
  162.5 0.0 all-gather.6.cloned.1.call-start
  162.6 136.7 %all-reduce.2.cloned.1.call-done = bf16[128,2048]{1,0:T(8,128)(2,1)} async-done(((bf16[128,2048]{1,0:T(8,128)(2,1)}), bf16[128,2048]{1,0:T(8,128)(2,1)}) %all-reduce.2.cloned.1.call-update) | async-done | bytes 524304 | tf_op jit(solution)/shard_map/psum | solution.py:45
  299.3 0.0 all-gather.6.cloned.1.call-update
  299.3 0.0 all-gather.8.cloned.1.call-start
  299.4 0.0 copy-done.2
  299.4 14.1 %collective-permute-start = (bf16[128,2048]{1,0:T(8,128)(2,1)S(1)}, bf16[128,2048]{1,0:T(8,128)(2,1)S(1)}, u32[]{:S(2)}, u32[]{:S(2)}) collective-permute-start(bf16[128,2048]{1,0:T(8,128)(2,1)S(1)} %copy-done.2), channel_id=1, source_target_pairs={{0,0},{64,16},{128,32},{192,48},{16,64},{80,80},{144,96},{208,112}... | collective-permute-start | bytes 1572872 | tf_op jit(solution)/shard_map/ppermute | solution.py:49
  313.5 8.1 %collective-permute-done = bf16[128,2048]{1,0:T(8,128)(2,1)S(1)} collective-permute-done((bf16[128,2048]{1,0:T(8,128)(2,1)S(1)}, bf16[128,2048]{1,0:T(8,128)(2,1)S(1)}, u32[]{:S(2)}, u32[]{:S(2)}) %collective-permute-start) | collective-permute-done | bytes 524320 | tf_op jit(solution)/shard_map/ppermute | solution.py:49
  321.6 0.0 copy-start.1
  321.6 0.8 copy-done.1
  322.4 0.0 all-gather.8.cloned.1.call-update
  322.4 42.4 %all-gather.6.cloned.1.call-done = bf16[512,2048]{1,0:T(8,128)(2,1)} async-done(((bf16[128,2048]{1,0:T(8,128)(2,1)}), bf16[512,2048]{1,0:T(8,128)(2,1)}) %all-gather.6.cloned.1.call-update) | async-done | bytes 2097168 | tf_op jit(solution)/shard_map/all_gather | solution.py:46
  364.8 2.3 fusion.2
  367.1 10.0 %all_gather.14 = bf16[128,2048]{0,1:T(8,128)(2,1)S(1)} all-gather(bf16[128,512]{0,1:T(8,128)(2,1)S(1)} %fusion.2), channel_id=1, replica_groups=mesh['prow'=4,'pcol'=4,'pl'=16] {'pcol'}, dimensions={1}, use_global_device_ids=true | all-gather | bytes 655360 | tf_op jit(solution)/shard_map/all_gather | solution.py:48
  377.1 91.5 %all-gather.8.cloned.1.call-done = bf16[2048,2048]{1,0:T(8,128)(2,1)} async-done(((bf16[128,2048]{1,0:T(8,128)(2,1)}), bf16[2048,2048]{1,0:T(8,128)(2,1)}) %all-gather.8.cloned.1.call-update) | async-done | bytes 8388624 | tf_op jit(solution)/shard_map/all_gather | solution.py:50
  468.6 7.3 %fusion.9 = f32[128,2048]{1,0:T(8,128)} fusion(bf16[128,2048]{0,1:T(8,128)(2,1)S(1)} %all_gather.14, bf16[2048,2048]{1,0:T(8,128)(2,1)} %all-gather.8.cloned.1.call-done), kind=kOutput, calls=%fused_computation.19 | convolution fusion | flops 1073741824 | bytes 9961472 | tf_op jit(solution)/shard_map/dot_general | solution.py:15
  (1 shorter events, 0.0 us)
Async XLA Ops:
  6.5 1.2 copy-start
  6.5 95.4 %reduce-scatter.2.cloned.1.call-start = ((), (), s32[]{:S(2)}) async-start(), calls=%async_computation.1 | async-start | bytes 2228224 | tf_op jit(solution)/shard_map/reduce_scatter | solution.py:25
  14.8 88.7 %copy-start.3 = (f32[2048]{0:T(1024)S(1)}, f32[2048]{0:T(1024)}, u32[]{:S(2)}) copy-start(f32[2048]{0:T(1024)} %param.8) | copy-start | bytes 24580
  14.8 88.7 %copy-start.4 = (f32[2048]{0:T(1024)S(1)}, f32[2048]{0:T(1024)}, u32[]{:S(2)}) copy-start(f32[2048]{0:T(1024)} %param.9) | copy-start | bytes 24580
  14.9 144.3 %all-gather.4.cloned.1.call-start = ((), (), s32[]{:S(2)}) async-start(), calls=%async_computation.2 | async-start | bytes 1114112 | tf_op jit(solution)/shard_map/all_gather | solution.py:31
  103.5 195.8 %all-reduce.2.cloned.1.call-start = ((), (), s32[]{:S(2)}) async-start(), calls=%async_computation.3 | async-start | bytes 1048576 | tf_op jit(solution)/shard_map/psum | solution.py:45
  160.9 138.5 %copy-start.2 = (bf16[128,2048]{1,0:T(8,128)(2,1)S(1)}, bf16[128,2048]{1,0:T(8,128)(2,1)}, u32[]{:S(2)}) copy-start(bf16[128,2048]{1,0:T(8,128)(2,1)} %param.7) | copy-start | bytes 1572868
  162.5 202.2 %all-gather.6.cloned.1.call-start = ((), (), s32[]{:S(2)}) async-start(), calls=%async_computation.4 | async-start | bytes 2621440 | tf_op jit(solution)/shard_map/all_gather | solution.py:46
  299.3 169.3 %all-gather.8.cloned.1.call-start = ((), (), s32[]{:S(2)}) async-start(), calls=%async_computation.5 | async-start | bytes 8912896 | tf_op jit(solution)/shard_map/all_gather | solution.py:50
  299.4 22.2 %collective-permute-start = (bf16[128,2048]{1,0:T(8,128)(2,1)S(1)}, bf16[128,2048]{1,0:T(8,128)(2,1)S(1)}, u32[]{:S(2)}, u32[]{:S(2)}) collective-permute-start(bf16[128,2048]{1,0:T(8,128)(2,1)S(1)} %copy-done.2), channel_id=1, source_target_pairs={{0,0},{64,16},{128,32},{192,48},{16,64},{80,80},{144,96},{208,112}... | collective-permute-start | bytes 1572872 | tf_op jit(solution)/shard_map/ppermute | solution.py:49
  321.6 0.8 copy-start.1
Sparse Core Ops, SparseCore 0:
  15.0 86.8 reduce-scatter.1
  104.6 54.4 all-gather.3
  162.7 136.5 all-reduce.1
  301.1 63.5 all-gather.5
  366.5 102.0 all-gather.7

commit v2 on v1

v2 whole, which is shorter than its diff:
```python
import functools
import math

import jax
import jax.numpy as jnp
from jax import lax
from jax.experimental import pallas as pl
from jax.experimental.pallas import tpu as pltpu
from jax.sharding import PartitionSpec as P

MESH = pl.DeviceIdType.MESH


def transfer_pair(natural_freq, damping):
    detuning = natural_freq * natural_freq - 1.0
    damper = 2.0 * damping * natural_freq
    modulus = detuning * detuning + damper * damper
    return (detuning / modulus, -damper / modulus)


def outer_rows(left_rows, right_rows):
    return lax.dot_general(
        left_rows, right_rows, (((1,), (1,)), ((), ())), preferred_element_type=jnp.float32
    )


def exchange_kernel(x_ref, out_ref, send_sem, recv_sem, local_sem, *, axes, sizes, group, same):
    coords = {a: lax.axis_index(a) for a in axes}
    count = math.prod(sizes[a] for a in group)
    me = 0
    for a in group:
        me = me * sizes[a] + coords[a]

    def device(member):
        place = dict(coords)
        for a in reversed(group):
            place[a] = lax.rem(member, sizes[a])
            member = member // sizes[a]
        return tuple(place[a] for a in axes)

    def source(member):
        return x_ref if same else x_ref.at[member]

    def copy(offset):
        peer = lax.rem(me + offset, count)
        return pltpu.make_async_remote_copy(
            src_ref=source(peer),
            dst_ref=out_ref.at[me],
            send_sem=send_sem.at[offset],
            recv_sem=recv_sem.at[offset],
            device_id=device(peer),
            device_id_type=MESH,
        )

    def landing(offset):
        sender = lax.rem(me + count - offset, count)
        return pltpu.make_async_remote_copy(
            src_ref=source(me),
            dst_ref=out_ref.at[sender],
            send_sem=send_sem.at[offset],
            recv_sem=recv_sem.at[offset],
            device_id=device(sender),
            device_id_type=MESH,
        )

    local = pltpu.make_async_copy(source(me), out_ref.at[me], local_sem)
    local.start()
    for offset in range(1, count):
        copy(offset).start()
    local.wait()
    for offset in range(1, count):
        copy(offset).wait_send()
    for offset in range(1, count):
        landing(offset).wait_recv()


def exchange(x, group, axes, sizes, same):
    count = math.prod(sizes[a] for a in group)
    block = x.shape if same else x.shape[1:]
    kernel = functools.partial(exchange_kernel, axes=axes, sizes=sizes, group=group, same=same)
    return pl.pallas_call(
        kernel,
        out_shape=jax.ShapeDtypeStruct((count,) + tuple(block), x.dtype),
        in_specs=[pl.BlockSpec(memory_space=pl.ANY)],
        out_specs=pl.BlockSpec(memory_space=pl.ANY),
        scratch_shapes=[
            pltpu.SemaphoreType.DMA((count,)),
            pltpu.SemaphoreType.DMA((count,)),
            pltpu.SemaphoreType.DMA(()),
        ],
        compiler_params=pltpu.CompilerParams(has_side_effects=True),
    )(x)


def make_body(axes, sizes):
    n_row, n_col, n_pl = sizes["prow"], sizes["pcol"], sizes["pl"]
    swap = [(c * n_col + r, r * n_col + c) for r in range(n_row) for c in range(n_col)]
    ex = functools.partial(exchange, axes=axes, sizes=sizes)

    def body(factor_cols, modal_at_loads, mode_shapes, natural_freq, damping):
        in_phase, quadrature = transfer_pair(natural_freq, damping)
        modes = modal_at_loads.shape[0]
        block = modes // (n_row * n_col)
        partial_load = jnp.dot(modal_at_loads, factor_cols, preferred_element_type=jnp.float32)
        pieces = ex(partial_load.reshape(n_row * n_col, block, -1), ("prow", "pcol"), same=False)
        own_rows = jnp.sum(pieces, axis=0).astype(jnp.bfloat16)
        modal_load = ex(own_rows, ("prow", "pcol"), same=True).reshape(modes, -1)
        modal_wide = modal_load.astype(jnp.float32)
        pseudo = jnp.concatenate(
            [
                (in_phase[:, None] * modal_wide).astype(jnp.bfloat16),
                (quadrature[:, None] * modal_wide).astype(jnp.bfloat16),
            ],
            axis=1,
        )
        row, col = lax.axis_index("prow"), lax.axis_index("pcol")
        first_row = (col * n_row + row) * block
        own_pseudo = lax.dynamic_slice_in_dim(pseudo, first_row, block, 0)
        partial_gram = outer_rows(own_pseudo, pseudo)
        chunk = modes // n_pl
        by_chunk = partial_gram.reshape(block, n_pl, chunk).transpose(1, 0, 2)
        gram_sums = ex(by_chunk, ("pl",), same=False)
        gram_piece = jnp.sum(gram_sums, axis=0).astype(jnp.bfloat16)
        gram_all = ex(gram_piece, ("prow", "pl"), same=True)
        gram_panel = (
            gram_all.reshape(n_row, n_pl, block, chunk).transpose(0, 2, 1, 3).reshape(n_row * block, modes)
        )
        weighted_part = outer_rows(mode_shapes, gram_panel).astype(jnp.bfloat16)
        weighted_all = ex(weighted_part, ("pcol",), same=True)
        weighted = weighted_all.transpose(1, 0, 2).reshape(weighted_part.shape[0], modes)
        panel_piece = lax.ppermute(mode_shapes, ("prow", "pcol"), swap)
        panel = ex(panel_piece, ("pl",), same=True).reshape(-1, modes)
        return outer_rows(weighted, panel)

    return body


def solution(mesh):
    in_specs = (
        P(("prow", "pcol"), "pl"),
        P(None, ("prow", "pcol")),
        P(("prow", "pl"), None),
        P(),
        P(),
    )
    out_specs = P(("prow", "pl"), "pcol")
    axes = tuple(mesh.axis_names)
    body = make_body(axes, dict(mesh.shape))
    return jax.shard_map(body, mesh=mesh, in_specs=in_specs, out_specs=out_specs, check_vma=False)
```

time: 489 us -> 504 us (1.031)
  the two profiles are of different devices: /device:TPU:39 before, /device:TPU:167 now
where the time goes in v2:
time: 504 us
  Pallas kernels  469 us (93%)
  matrix products  17.5 us (3%)
  local copies, waits for them, and re-layouts  6.87 us (1%)
  other arithmetic  6.05 us (1%)
    pallas_call x6, Pallas kernels, exchange(): pl.pallas_call(kernel, out_shape=jax.ShapeDtypeStruct((count,) + tuple(bl...  469 us
    dot_general x3, matrix products, outer_rows(): lax.dot_general(left_rows, right_rows, (((1,), (1,)), ((), ())), preferre...  10.5 us
  transfers between devices with their start and end apart: 1, of which 0 were waited for; matrix products, arithmetic and copies ran while one was open for 5% of the time, Pallas kernels for 45%

profile of v2, /device:TPU:167, one launch (start us, length us, event | category | flops | bytes accessed | tf_op | source)
XLA Modules:
  0.0 503.6 jit_solution(18022938397279878785)
XLA Ops:
  0.0 0.0 copy-start
  0.0 4.4 collective-permute-start
  4.4 0.0 copy-done
  4.4 7.1 %fusion.17 = f32[2048,256]{1,0:T(8,128)} fusion(bf16[2048,2048]{1,0:T(8,128)(2,1)} %param.6, bf16[2048,256]{1,0:T(8,128)(2,1)S(1)} %copy-done), kind=kOutput, calls=%fused_computation.21 | convolution fusion | flops 2147483648 | bytes 11534336 | tf_op jit(solution)/shard_map/dot_general | solution.py:104
  11.5 50.6 %shard_map.55 = f32[16,128,256]{2,1,0:T(8,128)} custom-call(f32[16,128,256]{2,1,0:T(8,128)} %bitcast.35), custom_call_target="tpu_custom_call" | custom-call | tf_op jit(solution)/shard_map/pallas_call | solution.py:81
  62.2 0.0 copy-start.1
  62.2 0.0 copy-start.2
  62.2 2.4 reduce_sum.18.x_ref
  64.5 54.5 %shard_map.56 = bf16[16,128,256]{2,1,0:T(8,128)(2,1)} custom-call(bf16[128,256]{1,0:T(8,128)(2,1)} %reduce_sum.18.x_ref), custom_call_target="tpu_custom_call" | custom-call | tf_op jit(solution)/shard_map/pallas_call | solution.py:81
  119.1 0.0 copy-done.1
  119.1 0.0 copy-done.2
  119.1 1.8 fusion.1
  120.9 1.7 fusion
  122.6 2.5 copy.8
  125.1 39.7 %shard_map.57 = f32[16,128,128]{2,1,0:T(8,128)} custom-call(f32[16,128,128]{2,1,0:T(8,128)} %bitcast.30), custom_call_target="tpu_custom_call" | custom-call | tf_op jit(solution)/shard_map/pallas_call | solution.py:81
  164.8 1.9 reduce_sum.19.x_ref
  166.7 59.8 %shard_map.58 = bf16[64,128,128]{2,1,0:T(8,128)(2,1)} custom-call(bf16[128,128]{1,0:T(8,128)(2,1)} %reduce_sum.19.x_ref), custom_call_target="tpu_custom_call" | custom-call | tf_op jit(solution)/shard_map/pallas_call | solution.py:81
  226.5 0.0 copy-start.3
  226.5 3.0 copy.9
  229.5 0.0 copy-done.3
  229.6 1.5 fusion.9.x_ref
  231.1 22.5 %shard_map.59 = bf16[4,128,512]{2,1,0:T(8,128)(2,1)} custom-call(bf16[128,512]{1,0:T(8,128)(2,1)} %fusion.9.x_ref), custom_call_target="tpu_custom_call" | custom-call | tf_op jit(solution)/shard_map/pallas_call | solution.py:81
  253.6 1.3 copy.11
  254.9 0.0 collective-permute-done.x_ref
  254.9 241.4 %shard_map.60 = bf16[16,128,2048]{2,1,0:T(8,128)(2,1)} custom-call(bf16[128,2048]{1,0:T(8,128)(2,1)} %collective-permute-done.x_ref), custom_call_target="tpu_custom_call" | custom-call | tf_op jit(solution)/shard_map/pallas_call | solution.py:81
  496.3 7.3 %fusion.18 = f32[128,2048]{1,0:T(8,128)} fusion(bf16[128,2048]{0,1:T(8,128)(2,1)S(1)} %bitcast.32, bf16[2048,2048]{1,0:T(8,128)(2,1)} %bitcast.28), kind=kOutput, calls=%fused_computation.22 | convolution fusion | flops 1073741824 | bytes 9961472 | tf_op jit(solution)/shard_map/dot_general | solution.py:22
  (1 shorter events, 0.0 us)
Async XLA Ops:
  0.0 4.4 copy-start
  0.0 254.9 %collective-permute-start = (bf16[128,2048]{1,0:T(8,128)(2,1)}, bf16[128,2048]{1,0:T(8,128)(2,1)}, u32[]{:S(2)}, u32[]{:S(2)}) collective-permute-start(bf16[128,2048]{1,0:T(8,128)(2,1)} %param.7), channel_id=1, source_target_pairs={{0,0},{64,16},{128,32},{192,48},{16,64},{80,80},{144,96},{208,112}... | collective-permute-start | bytes 1572872 | tf_op jit(solution)/shard_map/ppermute | solution.py:131
  62.2 56.9 %copy-start.1 = (f32[2048]{0:T(1024)S(1)}, f32[2048]{0:T(1024)}, u32[]{:S(2)}) copy-start(f32[2048]{0:T(1024)} %param.8) | copy-start | bytes 24580
  62.2 56.9 %copy-start.2 = (f32[2048]{0:T(1024)S(1)}, f32[2048]{0:T(1024)}, u32[]{:S(2)}) copy-start(f32[2048]{0:T(1024)} %param.9) | copy-start | bytes 24580
  226.5 3.0 copy-start.3

commit v3 on v2

--- a/solution.py
+++ b/solution.py
@@ -65,6 +65,11 @@
 
     local = pltpu.make_async_copy(source(me), out_ref.at[me], local_sem)
     local.start()
+    barrier = pltpu.get_barrier_semaphore()
+    for offset in range(1, count):
+        peer = lax.rem(me + offset, count)
+        pl.semaphore_signal(barrier, inc=1, device_id=device(peer), device_id_type=MESH)
+    pl.semaphore_wait(barrier, count - 1)
     for offset in range(1, count):
         copy(offset).start()
     local.wait()
@@ -74,7 +79,7 @@
         landing(offset).wait_recv()
 
 
-def exchange(x, group, axes, sizes, same):
+def exchange(x, group, axes, sizes, same, kernel_id):
     count = math.prod(sizes[a] for a in group)
     block = x.shape if same else x.shape[1:]
     kernel = functools.partial(exchange_kernel, axes=axes, sizes=sizes, group=group, same=same)
@@ -88,7 +93,7 @@
             pltpu.SemaphoreType.DMA((count,)),
             pltpu.SemaphoreType.DMA(()),
         ],
-        compiler_params=pltpu.CompilerParams(has_side_effects=True),
+        compiler_params=pltpu.CompilerParams(collective_id=kernel_id, has_side_effects=True),
     )(x)
 
 
@@ -102,9 +107,9 @@
         modes = modal_at_loads.shape[0]
         block = modes // (n_row * n_col)
         partial_load = jnp.dot(modal_at_loads, factor_cols, preferred_element_type=jnp.float32)
-        pieces = ex(partial_load.reshape(n_row * n_col, block, -1), ("prow", "pcol"), same=False)
+        pieces = ex(partial_load.reshape(n_row * n_col, block, -1), ("prow", "pcol"), same=False, kernel_id=0)
         own_rows = jnp.sum(pieces, axis=0).astype(jnp.bfloat16)
-        modal_load = ex(own_rows, ("prow", "pcol"), same=True).reshape(modes, -1)
+        modal_load = ex(own_rows, ("prow", "pcol"), same=True, kernel_id=1).reshape(modes, -1)
         modal_wide = modal_load.astype(jnp.float32)
         pseudo = jnp.concatenate(
             [
@@ -119,17 +124,17 @@
         partial_gram = outer_rows(own_pseudo, pseudo)
         chunk = modes // n_pl
         by_chunk = partial_gram.reshape(block, n_pl, chunk).transpose(1, 0, 2)
-        gram_sums = ex(by_chunk, ("pl",), same=False)
+        gram_sums = ex(by_chunk, ("pl",), same=False, kernel_id=2)
         gram_piece = jnp.sum(gram_sums, axis=0).astype(jnp.bfloat16)
-        gram_all = ex(gram_piece, ("prow", "pl"), same=True)
+        gram_all = ex(gram_piece, ("prow", "pl"), same=True, kernel_id=3)
         gram_panel = (
             gram_all.reshape(n_row, n_pl, block, chunk).transpose(0, 2, 1, 3).reshape(n_row * block, modes)
         )
         weighted_part = outer_rows(mode_shapes, gram_panel).astype(jnp.bfloat16)
-        weighted_all = ex(weighted_part, ("pcol",), same=True)
+        weighted_all = ex(weighted_part, ("pcol",), same=True, kernel_id=4)
         weighted = weighted_all.transpose(1, 0, 2).reshape(weighted_part.shape[0], modes)
         panel_piece = lax.ppermute(mode_shapes, ("prow", "pcol"), swap)
-        panel = ex(panel_piece, ("pl",), same=True).reshape(-1, modes)
+        panel = lax.all_gather(panel_piece, "pl", axis=0, tiled=True)
         return outer_rows(weighted, panel)
 
     return body

time: 504 us -> 319 us (0.63)
  the two profiles are of different devices: /device:TPU:167 before, /device:TPU:39 now
where the time goes in v3:
time: 319 us; the launch traced here: 317 us
  Pallas kernels  263 us (82%)
  matrix products  16.6 us (5%)
  between operations  13.5 us (4%)
  waiting for transfers between devices  7.1 us (2%)
  local copies, waits for them, and re-layouts  6.46 us (2%)
  other arithmetic  6.23 us (2%)
  starting transfers between devices  3.89 us (1%)
    pallas_call x5, Pallas kernels, exchange(): pl.pallas_call(kernel, out_shape=jax.ShapeDtypeStruct((count,) + tuple(bl...  263 us
    dot_general x3, matrix products, outer_rows(): lax.dot_general(left_rows, right_rows, (((1,), (1,)), ((), ())), preferre...  9.48 us
    dot_general x1, matrix products, body(): jnp.dot(modal_at_loads, factor_cols, preferred_element_type=jnp.float32)  7.1 us
    ppermute x1, waiting for transfers between devices, body(): panel_piece = lax.ppermute(mode_shapes, ('prow', 'pcol'), swap)  7.06 us
  transfers between devices with their start and end apart: 2, of which 1 were waited for; matrix products, arithmetic and copies ran while one was open for 7% of the time, Pallas kernels for 83%

profile of v3, /device:TPU:39, one launch (start us, length us, event | category | flops | bytes accessed | tf_op | source)
XLA Modules:
  0.0 316.7 jit_solution(14850727324529975946)
XLA Ops:
  6.5 0.0 copy-start
  6.5 0.0 all-gather.2.cloned.1.call-start
  6.5 3.9 %collective-permute-start = (bf16[128,2048]{1,0:T(8,128)(2,1)}, bf16[128,2048]{1,0:T(8,128)(2,1)S(1)}, u32[]{:S(2)}, u32[]{:S(2)}) collective-permute-start(bf16[128,2048]{1,0:T(8,128)(2,1)} %param.7), channel_id=1, source_target_pairs={{0,0},{64,16},{128,32},{192,48},{16,64},{80,80},{144,96},{208,112}... | collective-permute-start | bytes 1572872 | tf_op jit(solution)/shard_map/ppermute | solution.py:136
  10.4 7.1 %collective-permute-done = bf16[128,2048]{1,0:T(8,128)(2,1)S(1)} collective-permute-done((bf16[128,2048]{1,0:T(8,128)(2,1)}, bf16[128,2048]{1,0:T(8,128)(2,1)S(1)}, u32[]{:S(2)}, u32[]{:S(2)}) %collective-permute-start) | collective-permute-done | bytes 524320 | tf_op jit(solution)/shard_map/ppermute | solution.py:136
  17.5 0.0 copy-start.1
  17.5 0.8 copy-done.1
  18.3 0.0 all-gather.2.cloned.1.call-update
  18.3 0.0 copy-done
  18.4 7.1 %fusion.17 = f32[2048,256]{1,0:T(8,128)} fusion(bf16[2048,2048]{1,0:T(8,128)(2,1)} %param.6, bf16[2048,256]{1,0:T(8,128)(2,1)S(1)} %copy-done), kind=kOutput, calls=%fused_computation.21 | convolution fusion | flops 2147483648 | bytes 11534336 | tf_op jit(solution)/shard_map/dot_general | solution.py:109
  25.5 108.4 %shard_map.55 = f32[16,128,256]{2,1,0:T(8,128)} custom-call(f32[16,128,256]{2,1,0:T(8,128)} %bitcast.33), custom_call_target="tpu_custom_call" | custom-call | tf_op jit(solution)/shard_map/pallas_call | solution.py:86
  133.9 0.0 copy-start.2
  133.9 0.0 copy-start.3
  133.9 2.4 reduce_sum.18.x_ref
  136.3 33.5 %shard_map.56 = bf16[16,128,256]{2,1,0:T(8,128)(2,1)} custom-call(bf16[128,256]{1,0:T(8,128)(2,1)} %reduce_sum.18.x_ref), custom_call_target="tpu_custom_call" | custom-call | tf_op jit(solution)/shard_map/pallas_call | solution.py:86
  169.7 0.0 copy-done.2
  169.7 0.0 copy-done.3
  169.8 1.9 fusion.1
  171.7 0.7 fusion
  172.4 1.3 copy.8
  173.8 53.7 %shard_map.57 = f32[16,128,128]{2,1,0:T(8,128)} custom-call(f32[16,128,128]{2,1,0:T(8,128)} %bitcast.28), custom_call_target="tpu_custom_call" | custom-call | tf_op jit(solution)/shard_map/pallas_call | solution.py:86
  227.5 1.9 reduce_sum.19.x_ref
  229.4 56.4 %shard_map.58 = bf16[64,128,128]{2,1,0:T(8,128)(2,1)} custom-call(bf16[128,128]{1,0:T(8,128)(2,1)} %reduce_sum.19.x_ref), custom_call_target="tpu_custom_call" | custom-call | tf_op jit(solution)/shard_map/pallas_call | solution.py:86
  285.9 0.0 copy-start.4
  285.9 3.0 copy.9
  288.9 0.0 copy-done.4
  288.9 1.5 fusion.9.x_ref
  290.4 10.9 %shard_map.59 = bf16[4,128,512]{2,1,0:T(8,128)(2,1)} custom-call(bf16[128,512]{1,0:T(8,128)(2,1)} %fusion.9.x_ref), custom_call_target="tpu_custom_call" | custom-call | tf_op jit(solution)/shard_map/pallas_call | solution.py:86
  301.3 1.3 copy.11
  302.6 0.0 all-gather.2.cloned.1.call-done
  302.6 7.3 %fusion.18 = f32[128,2048]{1,0:T(8,128)} fusion(bf16[128,2048]{0,1:T(8,128)(2,1)S(1)} %bitcast.30, bf16[2048,2048]{1,0:T(8,128)(2,1)} %all-gather.2.cloned.1.call-done), kind=kOutput, calls=%fused_computation.22 | convolution fusion | flops 1073741824 | bytes 9961472 | tf_op jit(solution)/shard_map/dot_general | solution.py:22
  (1 shorter events, 0.0 us)
Async XLA Ops:
  6.5 11.8 %copy-start = (bf16[2048,256]{1,0:T(8,128)(2,1)S(1)}, bf16[2048,256]{1,0:T(8,128)(2,1)}, u32[]{:S(2)}) copy-start(bf16[2048,256]{1,0:T(8,128)(2,1)} %param.5) | copy-start | bytes 3145732
  6.5 296.1 %all-gather.2.cloned.1.call-start = ((), (), s32[]{:S(2)}) async-start(), calls=%async_computation | async-start | bytes 8912896 | tf_op jit(solution)/shard_map/all_gather | solution.py:137
  6.5 11.0 %collective-permute-start = (bf16[128,2048]{1,0:T(8,128)(2,1)}, bf16[128,2048]{1,0:T(8,128)(2,1)S(1)}, u32[]{:S(2)}, u32[]{:S(2)}) collective-permute-start(bf16[128,2048]{1,0:T(8,128)(2,1)} %param.7), channel_id=1, source_target_pairs={{0,0},{64,16},{128,32},{192,48},{16,64},{80,80},{144,96},{208,112}... | collective-permute-start | bytes 1572872 | tf_op jit(solution)/shard_map/ppermute | solution.py:136
  17.5 0.8 copy-start.1
  133.9 35.9 %copy-start.2 = (f32[2048]{0:T(1024)S(1)}, f32[2048]{0:T(1024)}, u32[]{:S(2)}) copy-start(f32[2048]{0:T(1024)} %param.8) | copy-start | bytes 24580
  133.9 35.9 %copy-start.3 = (f32[2048]{0:T(1024)S(1)}, f32[2048]{0:T(1024)}, u32[]{:S(2)}) copy-start(f32[2048]{0:T(1024)} %param.9) | copy-start | bytes 24580
  285.9 3.0 copy-start.4
Sparse Core Ops, SparseCore 0:
  18.5 203.8 all-gather.1

commit v4 on v3

--- a/solution.py
+++ b/solution.py
@@ -100,6 +100,7 @@
 def make_body(axes, sizes):
     n_row, n_col, n_pl = sizes["prow"], sizes["pcol"], sizes["pl"]
     swap = [(c * n_col + r, r * n_col + c) for r in range(n_row) for c in range(n_col)]
+    sibling = [(r, r ^ 1) for r in range(n_row)]
     ex = functools.partial(exchange, axes=axes, sizes=sizes)
 
     def body(factor_cols, modal_at_loads, mode_shapes, natural_freq, damping):
@@ -121,11 +122,11 @@
         row, col = lax.axis_index("prow"), lax.axis_index("pcol")
         first_row = (col * n_row + row) * block
         own_pseudo = lax.dynamic_slice_in_dim(pseudo, first_row, block, 0)
-        partial_gram = outer_rows(own_pseudo, pseudo)
+        partial_gram = outer_rows(own_pseudo, pseudo).astype(jnp.bfloat16)
         chunk = modes // n_pl
         by_chunk = partial_gram.reshape(block, n_pl, chunk).transpose(1, 0, 2)
         gram_sums = ex(by_chunk, ("pl",), same=False, kernel_id=2)
-        gram_piece = jnp.sum(gram_sums, axis=0).astype(jnp.bfloat16)
+        gram_piece = jnp.sum(gram_sums.astype(jnp.float32), axis=0).astype(jnp.bfloat16)
         gram_all = ex(gram_piece, ("prow", "pl"), same=True, kernel_id=3)
         gram_panel = (
             gram_all.reshape(n_row, n_pl, block, chunk).transpose(0, 2, 1, 3).reshape(n_row * block, modes)
@@ -133,9 +134,16 @@
         weighted_part = outer_rows(mode_shapes, gram_panel).astype(jnp.bfloat16)
         weighted_all = ex(weighted_part, ("pcol",), same=True, kernel_id=4)
         weighted = weighted_all.transpose(1, 0, 2).reshape(weighted_part.shape[0], modes)
-        panel_piece = lax.ppermute(mode_shapes, ("prow", "pcol"), swap)
-        panel = lax.all_gather(panel_piece, "pl", axis=0, tiled=True)
-        return outer_rows(weighted, panel)
+        half = modes // 2
+        send_half = lax.dynamic_slice_in_dim(mode_shapes, (col % 2) * half, half, 1)
+        panel_piece = lax.ppermute(send_half, ("prow", "pcol"), swap)
+        panel_mine = lax.all_gather(panel_piece, "pl", axis=0, tiled=True)
+        panel_mine, weighted = lax.optimization_barrier((panel_mine, weighted))
+        panel_other = lax.ppermute(panel_mine, "prow", sibling)
+        core = row % 2
+        weighted_mine = lax.dynamic_slice_in_dim(weighted, core * half, half, 1)
+        weighted_other = lax.dynamic_slice_in_dim(weighted, (1 - core) * half, half, 1)
+        return outer_rows(weighted_mine, panel_mine) + outer_rows(weighted_other, panel_other)
 
     return body
 

time: 319 us -> 271 us (0.85)
  Pallas kernels: 263 us -> 210 us
  waiting for transfers between devices: 7.1 us -> 11.2 us
    pallas_call x5, Pallas kernels: 263 us -> 210 us  [exchange(): pl.pallas_call(kernel, out_shape=jax.ShapeDtypeStruct((count,) + tuple(bl...]
    ppermute x1 -> x2, waiting for transfers between devices: 7.06 us -> 11.2 us  [the longest x1 7.13 us: body(): panel_other = lax.ppermute(panel_mine, 'prow', sibling)]
    dot_general x3 -> x4, matrix products: 9.48 us -> 8.51 us  [outer_rows(): lax.dot_general(left_rows, right_rows, (((1,), (1,)), ((), ())), preferre...]
  transfers between devices with their start and end apart: 2 -> 3, of which waited for: 1 -> 2; matrix products, arithmetic and copies ran while one was open for 7% -> 8% of each run, Pallas kernels for 83% -> 78%
where the time goes in v4:
time: 271 us; the launch traced here: 269 us
  Pallas kernels  210 us (77%)
  matrix products  15.6 us (6%)
  between operations  13.6 us (5%)
  waiting for transfers between devices  11.2 us (4%)
  local copies, waits for them, and re-layouts  7.4 us (3%)
  other arithmetic  5.91 us (2%)
  starting transfers between devices  5.22 us (2%)
    pallas_call x5, Pallas kernels, exchange(): pl.pallas_call(kernel, out_shape=jax.ShapeDtypeStruct((count,) + tuple(bl...  210 us
    dot_general x4, matrix products, outer_rows(): lax.dot_general(left_rows, right_rows, (((1,), (1,)), ((), ())), preferre...  8.51 us
    ppermute x1, waiting for transfers between devices, body(): panel_other = lax.ppermute(panel_mine, 'prow', sibling)  7.13 us
    dot_general x1, matrix products, body(): jnp.dot(modal_at_loads, factor_cols, preferred_element_type=jnp.float32)  7.06 us
  transfers between devices with their start and end apart: 3, of which 2 were waited for; matrix products, arithmetic and copies ran while one was open for 8% of the time, Pallas kernels for 78%

profile of v4, /device:TPU:39, one launch (start us, length us, event | category | flops | bytes accessed | tf_op | source)
XLA Modules:
  0.0 269.2 jit_solution(8139638268856845604)
XLA Ops:
  6.5 0.0 copy-start
  6.5 0.0 all-gather.2.cloned.1.call-start
  6.5 1.1 constant_dynamic-slice_fusion
  7.6 3.8 %collective-permute-start = (bf16[128,1024]{1,0:T(8,128)(2,1)S(1)}, bf16[128,1024]{1,0:T(8,128)(2,1)S(1)}, u32[]{:S(2)}, u32[]{:S(2)}) collective-permute-start(bf16[128,1024]{1,0:T(8,128)(2,1)S(1)} %constant_dynamic-slice_fusion), channel_id=1, source_target_pairs={{0,0},{64,16},{128,32},{192,48},{16,64},{80,80},{144,96},{208,112}... | collective-permute-start | bytes 786440 | tf_op jit(solution)/shard_map/ppermute | solution.py:139
  11.4 4.0 %collective-permute-done = bf16[128,1024]{1,0:T(8,128)(2,1)S(1)} collective-permute-done((bf16[128,1024]{1,0:T(8,128)(2,1)S(1)}, bf16[128,1024]{1,0:T(8,128)(2,1)S(1)}, u32[]{:S(2)}, u32[]{:S(2)}) %collective-permute-start) | collective-permute-done | bytes 262176 | tf_op jit(solution)/shard_map/ppermute | solution.py:139
  15.4 0.0 copy-start.2
  15.4 0.7 copy-done.2
  16.1 0.0 all-gather.2.cloned.1.call-update
  16.2 0.0 copy-done
  16.2 7.1 %fusion.21 = f32[2048,256]{1,0:T(8,128)} fusion(bf16[2048,2048]{1,0:T(8,128)(2,1)} %param.6, bf16[2048,256]{1,0:T(8,128)(2,1)S(1)} %copy-done), kind=kOutput, calls=%fused_computation.28 | convolution fusion | flops 2147483648 | bytes 11534336 | tf_op jit(solution)/shard_map/dot_general | solution.py:110
  23.2 89.4 %shard_map.55 = f32[16,128,256]{2,1,0:T(8,128)} custom-call(f32[16,128,256]{2,1,0:T(8,128)} %bitcast.30), custom_call_target="tpu_custom_call" | custom-call | tf_op jit(solution)/shard_map/pallas_call | solution.py:86
  112.7 0.0 copy-start.4
  112.7 0.0 copy-start.5
  112.7 2.4 reduce_sum.21.x_ref
  115.1 37.8 %shard_map.56 = bf16[16,128,256]{2,1,0:T(8,128)(2,1)} custom-call(bf16[128,256]{1,0:T(8,128)(2,1)} %reduce_sum.21.x_ref), custom_call_target="tpu_custom_call" | custom-call | tf_op jit(solution)/shard_map/pallas_call | solution.py:86
  152.9 0.0 copy-done.4
  152.9 0.0 copy-done.5
  152.9 1.8 fusion
  154.7 0.8 convolution_convert_fusion
  155.5 0.3 copy.7
  155.8 1.0 copy.8
  156.8 15.8 %shard_map.57 = bf16[16,128,128]{2,1,0:T(8,128)(2,1)} custom-call(bf16[16,128,128]{2,1,0:T(8,128)(2,1)} %bitcast.32), custom_call_target="tpu_custom_call" | custom-call | tf_op jit(solution)/shard_map/pallas_call | solution.py:86
  172.6 1.7 reduce_sum.22.x_ref
  174.3 58.1 %shard_map.58 = bf16[64,128,128]{2,1,0:T(8,128)(2,1)} custom-call(bf16[128,128]{1,0:T(8,128)(2,1)} %reduce_sum.22.x_ref), custom_call_target="tpu_custom_call" | custom-call | tf_op jit(solution)/shard_map/pallas_call | solution.py:86
  232.4 0.0 copy-start.3
  232.5 3.0 %copy.9 = bf16[4,16,128,128]{3,1,2,0:T(8,128)(2,1)S(1)} copy(bf16[4,16,128,128]{3,2,1,0:T(8,128)(2,1)} %bitcast.27) | data formatting | bytes 4194304 | tf_op jit(solution)/shard_map/reshape | solution.py:132
  235.5 0.0 copy-done.3
  235.5 1.5 fusion.8.x_ref
  237.0 9.3 %shard_map.59 = bf16[4,128,512]{2,1,0:T(8,128)(2,1)} custom-call(bf16[128,512]{1,0:T(8,128)(2,1)} %fusion.8.x_ref), custom_call_target="tpu_custom_call" | custom-call | tf_op jit(solution)/shard_map/pallas_call | solution.py:86
  246.2 1.3 copy.11
  247.5 0.0 all-gather.2.cloned.1.call-done
  247.6 1.5 collective-permute-start.1
  249.0 0.0 copy-start.1
  249.0 7.1 %collective-permute-done.1 = bf16[2048,1024]{1,0:T(8,128)(2,1)} collective-permute-done((bf16[2048,1024]{1,0:T(8,128)(2,1)}, bf16[2048,1024]{1,0:T(8,128)(2,1)}, u32[]{:S(2)}, u32[]{:S(2)}) %collective-permute-start.1) | collective-permute-done | bytes 4194336 | tf_op jit(solution)/shard_map/ppermute | solution.py:142
  256.2 3.7 %fusion.11 = f32[128,2048]{1,0:T(8,128)S(1)} fusion(bf16[2048,1024]{1,0:T(8,128)(2,1)} %collective-permute-done.1, bf16[128,2048]{0,1:T(8,128)(2,1)S(1)} %bitcast.33, s32[]{:T(128)S(6)} %select_n.28), kind=kOutput, calls=%fused_computation.14 | convolution fusion | flops 536870912 | bytes 5505028 | tf_op jit(solution)/shard_map/dot_general | solution.py:22
  259.9 0.0 copy-done.1
  259.9 2.5 convolution_add_fusion
  (1 shorter events, 0.0 us)
Async XLA Ops:
  6.5 9.6 %copy-start = (bf16[2048,256]{1,0:T(8,128)(2,1)S(1)}, bf16[2048,256]{1,0:T(8,128)(2,1)}, u32[]{:S(2)}) copy-start(bf16[2048,256]{1,0:T(8,128)(2,1)} %param.5) | copy-start | bytes 3145732
  6.5 241.0 %all-gather.2.cloned.1.call-start = ((), (), s32[]{:S(2)}) async-start(), calls=%async_computation | async-start | bytes 4456448 | tf_op jit(solution)/shard_map/all_gather | solution.py:140
  7.6 7.8 %collective-permute-start = (bf16[128,1024]{1,0:T(8,128)(2,1)S(1)}, bf16[128,1024]{1,0:T(8,128)(2,1)S(1)}, u32[]{:S(2)}, u32[]{:S(2)}) collective-permute-start(bf16[128,1024]{1,0:T(8,128)(2,1)S(1)} %constant_dynamic-slice_fusion), channel_id=1, source_target_pairs={{0,0},{64,16},{128,32},{192,48},{16,64},{80,80},{144,96},{208,112}... | collective-permute-start | bytes 786440 | tf_op jit(solution)/shard_map/ppermute | solution.py:139
  15.4 0.7 copy-start.2
  112.7 40.2 %copy-start.4 = (f32[2048]{0:T(1024)S(1)}, f32[2048]{0:T(1024)}, u32[]{:S(2)}) copy-start(f32[2048]{0:T(1024)} %param.8) | copy-start | bytes 24580
  112.7 40.2 %copy-start.5 = (f32[2048]{0:T(1024)S(1)}, f32[2048]{0:T(1024)}, u32[]{:S(2)}) copy-start(f32[2048]{0:T(1024)} %param.9) | copy-start | bytes 24580
  232.4 3.0 %copy-start.3 = (bf16[128,2048]{1,0:T(8,128)(2,1)S(1)}, bf16[128,2048]{1,0:T(8,128)(2,1)}, u32[]{:S(2)}) copy-start(bf16[128,2048]{1,0:T(8,128)(2,1)} %param.7) | copy-start | bytes 1572868
  247.6 8.6 %collective-permute-start.1 = (bf16[2048,1024]{1,0:T(8,128)(2,1)}, bf16[2048,1024]{1,0:T(8,128)(2,1)}, u32[]{:S(2)}, u32[]{:S(2)}) collective-permute-start(bf16[2048,1024]{1,0:T(8,128)(2,1)} %all-gather.2.cloned.1.call-done), channel_id=1, source_target_pairs={{0,64},{64,0},{128,192},{192,128},{1,65},{65,1},{129,193},{193,129... | collective-permute-start | bytes 12582920 | tf_op jit(solution)/shard_map/ppermute | solution.py:142
  249.0 10.8 %copy-start.1 = (bf16[2048,1024]{1,0:T(8,128)(2,1)S(1)}, bf16[2048,1024]{1,0:T(8,128)(2,1)}, u32[]{:S(2)}) copy-start(bf16[2048,1024]{1,0:T(8,128)(2,1)} %all-gather.2.cloned.1.call-done) | copy-start | bytes 12582916
Sparse Core Ops, SparseCore 0:
  16.3 137.9 all-gather.1

commit v5 on v4

--- a/solution.py
+++ b/solution.py
@@ -24,18 +24,33 @@
     )
 
 
-def exchange_kernel(x_ref, out_ref, send_sem, recv_sem, local_sem, *, axes, sizes, group, same):
+def factor_table(sizes):
+    return {
+        "zh": ("prow", sizes["prow"] // 2, 2),
+        "core": ("prow", 2, 1),
+        "pcol": ("pcol", sizes["pcol"], 1),
+        "pl": ("pl", sizes["pl"], 1),
+    }
+
+
+def exchange_kernel(x_ref, out_ref, send_sem, recv_sem, local_sem, *, axes, factors, group, same):
     coords = {a: lax.axis_index(a) for a in axes}
-    count = math.prod(sizes[a] for a in group)
+
+    def value(f):
+        axis, size, stride = factors[f]
+        return lax.rem(coords[axis] // stride, size)
+
+    count = math.prod(factors[f][1] for f in group)
     me = 0
-    for a in group:
-        me = me * sizes[a] + coords[a]
+    for f in group:
+        me = me * factors[f][1] + value(f)
 
     def device(member):
         place = dict(coords)
-        for a in reversed(group):
-            place[a] = lax.rem(member, sizes[a])
-            member = member // sizes[a]
+        for f in reversed(group):
+            axis, size, stride = factors[f]
+            place[axis] = place[axis] + (lax.rem(member, size) - value(f)) * stride
+            member = member // size
         return tuple(place[a] for a in axes)
 
     def source(member):
@@ -79,38 +94,52 @@
         landing(offset).wait_recv()
 
 
-def exchange(x, group, axes, sizes, same, kernel_id):
-    count = math.prod(sizes[a] for a in group)
-    block = x.shape if same else x.shape[1:]
-    kernel = functools.partial(exchange_kernel, axes=axes, sizes=sizes, group=group, same=same)
-    return pl.pallas_call(
-        kernel,
-        out_shape=jax.ShapeDtypeStruct((count,) + tuple(block), x.dtype),
-        in_specs=[pl.BlockSpec(memory_space=pl.ANY)],
-        out_specs=pl.BlockSpec(memory_space=pl.ANY),
-        scratch_shapes=[
-            pltpu.SemaphoreType.DMA((count,)),
-            pltpu.SemaphoreType.DMA((count,)),
-            pltpu.SemaphoreType.DMA(()),
-        ],
-        compiler_params=pltpu.CompilerParams(collective_id=kernel_id, has_side_effects=True),
-    )(x)
+class Exchanger:
+    def __init__(self, axes, sizes):
+        self.axes, self.factors, self.calls = axes, factor_table(sizes), 0
+
+    def __call__(self, x, group, same):
+        count = math.prod(self.factors[f][1] for f in group)
+        block = x.shape if same else x.shape[1:]
+        if count == 1:
+            return x[None] if same else x
+        kernel = functools.partial(
+            exchange_kernel, axes=self.axes, factors=self.factors, group=group, same=same
+        )
+        self.calls += 1
+        return pl.pallas_call(
+            kernel,
+            out_shape=jax.ShapeDtypeStruct((count,) + tuple(block), x.dtype),
+            in_specs=[pl.BlockSpec(memory_space=pl.ANY)],
+            out_specs=pl.BlockSpec(memory_space=pl.ANY),
+            scratch_shapes=[
+                pltpu.SemaphoreType.DMA((count,)),
+                pltpu.SemaphoreType.DMA((count,)),
+                pltpu.SemaphoreType.DMA(()),
+            ],
+            compiler_params=pltpu.CompilerParams(collective_id=self.calls, has_side_effects=True),
+        )(x)
 
 
 def make_body(axes, sizes):
     n_row, n_col, n_pl = sizes["prow"], sizes["pcol"], sizes["pl"]
     swap = [(c * n_col + r, r * n_col + c) for r in range(n_row) for c in range(n_col)]
     sibling = [(r, r ^ 1) for r in range(n_row)]
-    ex = functools.partial(exchange, axes=axes, sizes=sizes)
+    n_zh = n_row // 2
 
     def body(factor_cols, modal_at_loads, mode_shapes, natural_freq, damping):
+        ex = Exchanger(axes, sizes)
         in_phase, quadrature = transfer_pair(natural_freq, damping)
         modes = modal_at_loads.shape[0]
         block = modes // (n_row * n_col)
         partial_load = jnp.dot(modal_at_loads, factor_cols, preferred_element_type=jnp.float32)
-        pieces = ex(partial_load.reshape(n_row * n_col, block, -1), ("prow", "pcol"), same=False, kernel_id=0)
-        own_rows = jnp.sum(pieces, axis=0).astype(jnp.bfloat16)
-        modal_load = ex(own_rows, ("prow", "pcol"), same=True, kernel_id=1).reshape(modes, -1)
+        width = partial_load.shape[1]
+        sums = jnp.sum(ex(partial_load.reshape(2, modes // 2, width), ("core",), same=False), axis=0)
+        sums = jnp.sum(ex(sums.reshape(n_col, -1, width), ("pcol",), same=False), axis=0)
+        sums = jnp.sum(ex(sums.reshape(n_zh, -1, width), ("zh",), same=False), axis=0)
+        gathered = ex(sums.astype(jnp.bfloat16), ("zh",), same=True).reshape(-1, width)
+        gathered = ex(gathered, ("pcol",), same=True).reshape(-1, width)
+        modal_load = ex(gathered, ("core",), same=True).reshape(modes, width)
         modal_wide = modal_load.astype(jnp.float32)
         pseudo = jnp.concatenate(
             [
@@ -125,14 +154,12 @@
         partial_gram = outer_rows(own_pseudo, pseudo).astype(jnp.bfloat16)
         chunk = modes // n_pl
         by_chunk = partial_gram.reshape(block, n_pl, chunk).transpose(1, 0, 2)
-        gram_sums = ex(by_chunk, ("pl",), same=False, kernel_id=2)
+        gram_sums = ex(by_chunk, ("pl",), same=False)
         gram_piece = jnp.sum(gram_sums.astype(jnp.float32), axis=0).astype(jnp.bfloat16)
-        gram_all = ex(gram_piece, ("prow", "pl"), same=True, kernel_id=3)
-        gram_panel = (
-            gram_all.reshape(n_row, n_pl, block, chunk).transpose(0, 2, 1, 3).reshape(n_row * block, modes)
-        )
+        gram_all = ex(ex(ex(gram_piece, ("zh",), same=True), ("pl",), same=True), ("core",), same=True)
+        gram_panel = gram_all.transpose(2, 0, 3, 1, 4).reshape(n_row * block, modes)
         weighted_part = outer_rows(mode_shapes, gram_panel).astype(jnp.bfloat16)
-        weighted_all = ex(weighted_part, ("pcol",), same=True, kernel_id=4)
+        weighted_all = ex(weighted_part, ("pcol",), same=True)
         weighted = weighted_all.transpose(1, 0, 2).reshape(weighted_part.shape[0], modes)
         half = modes // 2
         send_half = lax.dynamic_slice_in_dim(mode_shapes, (col % 2) * half, half, 1)

time: 271 us -> 268 us (0.989)
  Pallas kernels: 210 us -> 203 us
  other arithmetic: 5.91 us -> 9.98 us
    pallas_call x5 -> x11, Pallas kernels: 210 us -> 203 us  [__call__(): pl.pallas_call(kernel, out_shape=jax.ShapeDtypeStruct((count,) + tuple(bl...]
    reduce_sum x1 -> x3, other arithmetic: 2.39 us -> 6.46 us  [the longest x1 2.82 us: body(): jnp.sum(ex(partial_load.reshape(2, modes // 2, width), ('core',), same=Fa...]
    reshape x1 -> x0, local copies, waits for them, and re-layouts: 3 us -> none  [body(): gram_all.reshape(n_row, n_pl, block, chunk).transpose(0, 2, 1, 3)]
    transpose x0 -> x1, local copies, waits for them, and re-layouts: none -> 3 us  [body(): gram_panel = gram_all.transpose(2, 0, 3, 1, 4).reshape(n_row * block, modes)]
  transfers between devices with their start and end apart: 3 -> 3, of which waited for: 2 -> 2; matrix products, arithmetic and copies ran while one was open for 8% -> 9% of each run, Pallas kernels for 78% -> 76%
where the time goes in v5:
time: 268 us
  Pallas kernels  203 us (76%)
  matrix products  15.6 us (6%)
  between operations  13.6 us (5%)
  waiting for transfers between devices  11.2 us (4%)
  other arithmetic  9.98 us (4%)
  local copies, waits for them, and re-layouts  7.4 us (3%)
  starting transfers between devices  7.17 us (3%)
    pallas_call x11, Pallas kernels, __call__(): pl.pallas_call(kernel, out_shape=jax.ShapeDtypeStruct((count,) + tuple(bl...  203 us
    dot_general x4, matrix products, outer_rows(): lax.dot_general(left_rows, right_rows, (((1,), (1,)), ((), ())), preferre...  8.51 us
    ppermute x1, waiting for transfers between devices, body(): panel_other = lax.ppermute(panel_mine, 'prow', sibling)  7.13 us
    dot_general x1, matrix products, body(): jnp.dot(modal_at_loads, factor_cols, preferred_element_type=jnp.float32)  7.06 us
  transfers between devices with their start and end apart: 3, of which 2 were waited for; matrix products, arithmetic and copies ran while one was open for 9% of the time, Pallas kernels for 76%

profile of v5, /device:TPU:39, one launch (start us, length us, event | category | flops | bytes accessed | tf_op | source)
XLA Modules:
  0.0 267.5 jit_solution(13246010273603011083)
XLA Ops:
  6.5 0.0 copy-start
  6.5 0.0 all-gather.2.cloned.1.call-start
  6.5 1.1 constant_dynamic-slice_fusion
  7.6 3.8 %collective-permute-start = (bf16[128,1024]{1,0:T(8,128)(2,1)S(1)}, bf16[128,1024]{1,0:T(8,128)(2,1)S(1)}, u32[]{:S(2)}, u32[]{:S(2)}) collective-permute-start(bf16[128,1024]{1,0:T(8,128)(2,1)S(1)} %constant_dynamic-slice_fusion), channel_id=1, source_target_pairs={{0,0},{64,16},{128,32},{192,48},{16,64},{80,80},{144,96},{208,112}... | collective-permute-start | bytes 786440 | tf_op jit(solution)/shard_map/ppermute | solution.py:166
  11.4 4.0 %collective-permute-done = bf16[128,1024]{1,0:T(8,128)(2,1)S(1)} collective-permute-done((bf16[128,1024]{1,0:T(8,128)(2,1)S(1)}, bf16[128,1024]{1,0:T(8,128)(2,1)S(1)}, u32[]{:S(2)}, u32[]{:S(2)}) %collective-permute-start) | collective-permute-done | bytes 262176 | tf_op jit(solution)/shard_map/ppermute | solution.py:166
  15.4 0.0 copy-start.2
  15.4 0.7 copy-done.2
  16.1 0.0 all-gather.2.cloned.1.call-update
  16.2 0.0 copy-done
  16.2 7.1 %fusion.21 = f32[2048,256]{1,0:T(8,128)} fusion(bf16[2048,2048]{1,0:T(8,128)(2,1)} %param.6, bf16[2048,256]{1,0:T(8,128)(2,1)S(1)} %copy-done), kind=kOutput, calls=%fused_computation.28 | convolution fusion | flops 2147483648 | bytes 11534336 | tf_op jit(solution)/shard_map/dot_general | solution.py:135
  23.2 32.9 %shard_map.55 = f32[2,1024,256]{2,1,0:T(8,128)} custom-call(f32[2,1024,256]{2,1,0:T(8,128)} %bitcast.35), custom_call_target="tpu_custom_call" | custom-call | tf_op jit(solution)/shard_map/pallas_call | solution.py:110
  56.2 2.8 %reduce_sum.39 = f32[1024,256]{1,0:T(8,128)} reduce(f32[2,1024,256]{2,1,0:T(8,128)} %shard_map.55, f32[]{:T(128)} %constant.41.clone.1), dimensions={0}, to_apply=%region_0.0 | reduce | flops 262144 | bytes 3145732 | tf_op jit(solution)/shard_map/reduce_sum | solution.py:137
  59.0 29.9 %shard_map.56 = f32[4,256,256]{2,1,0:T(8,128)} custom-call(f32[4,256,256]{2,1,0:T(8,128)} %bitcast.31), custom_call_target="tpu_custom_call" | custom-call | tf_op jit(solution)/shard_map/pallas_call | solution.py:110
  88.9 0.0 copy-start.4
  88.9 0.0 copy-start.5
  88.9 2.0 reduce_sum.40
  91.0 15.7 %shard_map.57 = f32[2,128,256]{2,1,0:T(8,128)} custom-call(f32[2,128,256]{2,1,0:T(8,128)} %bitcast.40), custom_call_target="tpu_custom_call" | custom-call | tf_op jit(solution)/shard_map/pallas_call | solution.py:110
  106.7 1.6 reduce_sum.41.x_ref
  108.3 7.4 %shard_map.58 = bf16[2,128,256]{2,1,0:T(8,128)(2,1)} custom-call(bf16[128,256]{1,0:T(8,128)(2,1)} %reduce_sum.41.x_ref), custom_call_target="tpu_custom_call" | custom-call | tf_op jit(solution)/shard_map/pallas_call | solution.py:110
  115.8 8.2 %shard_map.59 = bf16[4,256,256]{2,1,0:T(8,128)(2,1)} custom-call(bf16[256,256]{1,0:T(8,128)(2,1)} %bitcast.41), custom_call_target="tpu_custom_call" | custom-call | tf_op jit(solution)/shard_map/pallas_call | solution.py:110
  124.0 17.2 %shard_map.60 = bf16[2,1024,256]{2,1,0:T(8,128)(2,1)} custom-call(bf16[1024,256]{1,0:T(8,128)(2,1)} %bitcast.32), custom_call_target="tpu_custom_call" | custom-call | tf_op jit(solution)/shard_map/pallas_call | solution.py:110
  141.2 0.0 copy-done.4
  141.2 0.0 copy-done.5
  141.2 1.8 fusion
  143.0 0.8 convolution_convert_fusion
  143.8 0.3 copy.7
  144.1 1.0 copy.8
  145.1 15.7 %shard_map.61 = bf16[16,128,128]{2,1,0:T(8,128)(2,1)} custom-call(bf16[16,128,128]{2,1,0:T(8,128)(2,1)} %bitcast.37), custom_call_target="tpu_custom_call" | custom-call | tf_op jit(solution)/shard_map/pallas_call | solution.py:110
  160.8 1.7 reduce_sum.42.x_ref
  162.5 7.0 %shard_map.62.x_ref = bf16[2,128,128]{2,1,0:T(8,128)(2,1)} custom-call(bf16[128,128]{1,0:T(8,128)(2,1)} %reduce_sum.42.x_ref), custom_call_target="tpu_custom_call" | custom-call | tf_op jit(solution)/shard_map/pallas_call | solution.py:110
  169.6 27.5 %shard_map.63.x_ref = bf16[16,2,128,128]{3,2,1,0:T(8,128)(2,1)} custom-call(bf16[2,128,128]{2,1,0:T(8,128)(2,1)} %shard_map.62.x_ref), custom_call_target="tpu_custom_call" | custom-call | tf_op jit(solution)/shard_map/pallas_call | solution.py:110
  197.0 33.1 %shard_map.64 = bf16[2,16,2,128,128]{4,3,2,1,0:T(8,128)(2,1)} custom-call(bf16[16,2,128,128]{3,2,1,0:T(8,128)(2,1)} %shard_map.63.x_ref), custom_call_target="tpu_custom_call" | custom-call | tf_op jit(solution)/shard_map/pallas_call | solution.py:110
  230.1 0.0 copy-start.3
  230.1 3.0 %copy.9 = bf16[2,2,128,16,128]{4,3,2,1,0:T(8,128)(2,1)S(1)} copy(bf16[2,2,128,16,128]{4,2,0,3,1:T(8,128)(2,1)} %bitcast.30) | data formatting | bytes 4194304 | tf_op jit(solution)/shard_map/transpose | solution.py:160
  233.1 0.0 copy-done.3
  233.1 1.5 fusion.8.x_ref
  234.6 7.9 %shard_map.65 = bf16[4,128,512]{2,1,0:T(8,128)(2,1)} custom-call(bf16[128,512]{1,0:T(8,128)(2,1)} %fusion.8.x_ref), custom_call_target="tpu_custom_call" | custom-call | tf_op jit(solution)/shard_map/pallas_call | solution.py:110
  242.6 1.3 copy.11
  243.9 0.0 all-gather.2.cloned.1.call-done
  243.9 3.4 %collective-permute-start.1 = (bf16[2048,1024]{1,0:T(8,128)(2,1)}, bf16[2048,1024]{1,0:T(8,128)(2,1)}, u32[]{:S(2)}, u32[]{:S(2)}) collective-permute-start(bf16[2048,1024]{1,0:T(8,128)(2,1)} %all-gather.2.cloned.1.call-done), channel_id=1, source_target_pairs={{0,64},{64,0},{128,192},{192,128},{1,65},{65,1},{129,193},{193,129... | collective-permute-start | bytes 12582920 | tf_op jit(solution)/shard_map/ppermute | solution.py:169
  247.3 0.0 copy-start.1
  247.3 7.1 %collective-permute-done.1 = bf16[2048,1024]{1,0:T(8,128)(2,1)} collective-permute-done((bf16[2048,1024]{1,0:T(8,128)(2,1)}, bf16[2048,1024]{1,0:T(8,128)(2,1)}, u32[]{:S(2)}, u32[]{:S(2)}) %collective-permute-start.1) | collective-permute-done | bytes 4194336 | tf_op jit(solution)/shard_map/ppermute | solution.py:169
  254.4 3.7 %fusion.11 = f32[128,2048]{1,0:T(8,128)S(1)} fusion(bf16[2048,1024]{1,0:T(8,128)(2,1)} %collective-permute-done.1, bf16[128,2048]{0,1:T(8,128)(2,1)S(1)} %bitcast.38, s32[]{:T(128)S(6)} %select_n.28), kind=kOutput, calls=%fused_computation.14 | convolution fusion | flops 536870912 | bytes 5505028 | tf_op jit(solution)/shard_map/dot_general | solution.py:22
  258.1 0.0 copy-done.1
  258.1 2.5 convolution_add_fusion
  (1 shorter events, 0.0 us)
Async XLA Ops:
  6.5 9.6 %copy-start = (bf16[2048,256]{1,0:T(8,128)(2,1)S(1)}, bf16[2048,256]{1,0:T(8,128)(2,1)}, u32[]{:S(2)}) copy-start(bf16[2048,256]{1,0:T(8,128)(2,1)} %param.5) | copy-start | bytes 3145732
  6.5 237.4 %all-gather.2.cloned.1.call-start = ((), (), s32[]{:S(2)}) async-start(), calls=%async_computation | async-start | bytes 4456448 | tf_op jit(solution)/shard_map/all_gather | solution.py:167
  7.6 7.8 %collective-permute-start = (bf16[128,1024]{1,0:T(8,128)(2,1)S(1)}, bf16[128,1024]{1,0:T(8,128)(2,1)S(1)}, u32[]{:S(2)}, u32[]{:S(2)}) collective-permute-start(bf16[128,1024]{1,0:T(8,128)(2,1)S(1)} %constant_dynamic-slice_fusion), channel_id=1, source_target_pairs={{0,0},{64,16},{128,32},{192,48},{16,64},{80,80},{144,96},{208,112}... | collective-permute-start | bytes 786440 | tf_op jit(solution)/shard_map/ppermute | solution.py:166
  15.4 0.7 copy-start.2
  88.9 52.3 %copy-start.4 = (f32[2048]{0:T(1024)S(1)}, f32[2048]{0:T(1024)}, u32[]{:S(2)}) copy-start(f32[2048]{0:T(1024)} %param.8) | copy-start | bytes 24580
  88.9 52.3 %copy-start.5 = (f32[2048]{0:T(1024)S(1)}, f32[2048]{0:T(1024)}, u32[]{:S(2)}) copy-start(f32[2048]{0:T(1024)} %param.9) | copy-start | bytes 24580
  230.1 3.0 %copy-start.3 = (bf16[128,2048]{1,0:T(8,128)(2,1)S(1)}, bf16[128,2048]{1,0:T(8,128)(2,1)}, u32[]{:S(2)}) copy-start(bf16[128,2048]{1,0:T(8,128)(2,1)} %param.7) | copy-start | bytes 1572868
  243.9 10.5 %collective-permute-start.1 = (bf16[2048,1024]{1,0:T(8,128)(2,1)}, bf16[2048,1024]{1,0:T(8,128)(2,1)}, u32[]{:S(2)}, u32[]{:S(2)}) collective-permute-start(bf16[2048,1024]{1,0:T(8,128)(2,1)} %all-gather.2.cloned.1.call-done), channel_id=1, source_target_pairs={{0,64},{64,0},{128,192},{192,128},{1,65},{65,1},{129,193},{193,129... | collective-permute-start | bytes 12582920 | tf_op jit(solution)/shard_map/ppermute | solution.py:169
  247.3 10.8 %copy-start.1 = (bf16[2048,1024]{1,0:T(8,128)(2,1)S(1)}, bf16[2048,1024]{1,0:T(8,128)(2,1)}, u32[]{:S(2)}) copy-start(bf16[2048,1024]{1,0:T(8,128)(2,1)} %all-gather.2.cloned.1.call-done) | copy-start | bytes 12582916
Sparse Core Ops, SparseCore 0:
  16.3 85.4 all-gather.1

commit v6 on v5

--- a/solution.py
+++ b/solution.py
@@ -127,19 +127,28 @@
     sibling = [(r, r ^ 1) for r in range(n_row)]
     n_zh = n_row // 2
 
+    def beside_sibling(part, core):
+        other = lax.ppermute(part, "prow", sibling)
+        first, second = jnp.where(core == 0, part, other), jnp.where(core == 0, other, part)
+        return jnp.concatenate([first, second], axis=0)
+
     def body(factor_cols, modal_at_loads, mode_shapes, natural_freq, damping):
         ex = Exchanger(axes, sizes)
         in_phase, quadrature = transfer_pair(natural_freq, damping)
         modes = modal_at_loads.shape[0]
         block = modes // (n_row * n_col)
+        row, col = lax.axis_index("prow"), lax.axis_index("pcol")
         partial_load = jnp.dot(modal_at_loads, factor_cols, preferred_element_type=jnp.float32)
         width = partial_load.shape[1]
-        sums = jnp.sum(ex(partial_load.reshape(2, modes // 2, width), ("core",), same=False), axis=0)
+        core = row % 2
+        mine = lax.dynamic_slice_in_dim(partial_load, core * (modes // 2), modes // 2, 0)
+        theirs = lax.dynamic_slice_in_dim(partial_load, (1 - core) * (modes // 2), modes // 2, 0)
+        sums = mine + lax.ppermute(theirs, "prow", sibling)
         sums = jnp.sum(ex(sums.reshape(n_col, -1, width), ("pcol",), same=False), axis=0)
         sums = jnp.sum(ex(sums.reshape(n_zh, -1, width), ("zh",), same=False), axis=0)
         gathered = ex(sums.astype(jnp.bfloat16), ("zh",), same=True).reshape(-1, width)
         gathered = ex(gathered, ("pcol",), same=True).reshape(-1, width)
-        modal_load = ex(gathered, ("core",), same=True).reshape(modes, width)
+        modal_load = beside_sibling(gathered, core)
         modal_wide = modal_load.astype(jnp.float32)
         pseudo = jnp.concatenate(
             [
@@ -148,7 +157,6 @@
             ],
             axis=1,
         )
-        row, col = lax.axis_index("prow"), lax.axis_index("pcol")
         first_row = (col * n_row + row) * block
         own_pseudo = lax.dynamic_slice_in_dim(pseudo, first_row, block, 0)
         partial_gram = outer_rows(own_pseudo, pseudo).astype(jnp.bfloat16)
@@ -156,7 +164,8 @@
         by_chunk = partial_gram.reshape(block, n_pl, chunk).transpose(1, 0, 2)
         gram_sums = ex(by_chunk, ("pl",), same=False)
         gram_piece = jnp.sum(gram_sums.astype(jnp.float32), axis=0).astype(jnp.bfloat16)
-        gram_all = ex(ex(ex(gram_piece, ("zh",), same=True), ("pl",), same=True), ("core",), same=True)
+        gram_all = ex(ex(gram_piece, ("zh",), same=True), ("pl",), same=True)
+        gram_all = beside_sibling(gram_all[None], core)
         gram_panel = gram_all.transpose(2, 0, 3, 1, 4).reshape(n_row * block, modes)
         weighted_part = outer_rows(mode_shapes, gram_panel).astype(jnp.bfloat16)
         weighted_all = ex(weighted_part, ("pcol",), same=True)
@@ -167,7 +176,6 @@
         panel_mine = lax.all_gather(panel_piece, "pl", axis=0, tiled=True)
         panel_mine, weighted = lax.optimization_barrier((panel_mine, weighted))
         panel_other = lax.ppermute(panel_mine, "prow", sibling)
-        core = row % 2
         weighted_mine = lax.dynamic_slice_in_dim(weighted, core * half, half, 1)
         weighted_other = lax.dynamic_slice_in_dim(weighted, (1 - core) * half, half, 1)
         return outer_rows(weighted_mine, panel_mine) + outer_rows(weighted_other, panel_other)

time: 268 us -> 203 us (0.76)
  Pallas kernels: 203 us -> 131 us
  waiting for transfers between devices: 11.2 us -> 18.3 us
  matrix products: 15.6 us -> 12.1 us
    pallas_call x11 -> x8, Pallas kernels: 203 us -> 131 us  [__call__(): pl.pallas_call(kernel, out_shape=jax.ShapeDtypeStruct((count,) + tuple(bl...]
    ppermute x0 -> x3, waiting for transfers between devices: none -> 7.22 us  [the longest x2 4.23 us: beside_sibling(): other = lax.ppermute(part, 'prow', sibling)]
    ppermute x0 -> x3, starting transfers between devices: none -> 3.69 us  [the longest x2 3.69 us: beside_sibling(): other = lax.ppermute(part, 'prow', sibling)]
    reduce_sum x1 -> x0, other arithmetic: 2.82 us -> none  [body(): jnp.sum(ex(partial_load.reshape(2, modes // 2, width), ('core',), same=Fa...]
  transfers between devices with their start and end apart: 3 -> 6, of which waited for: 2 -> 5; matrix products, arithmetic and copies ran while one was open for 9% -> 13% of each run, Pallas kernels for 76% -> 65%
where the time goes in v6:
time: 203 us
  Pallas kernels  131 us (65%)
  waiting for transfers between devices  18.3 us (9%)
  between operations  13.6 us (7%)
  other arithmetic  12.3 us (6%)
  matrix products  12.1 us (6%)
  starting transfers between devices  8.66 us (4%)
  local copies, waits for them, and re-layouts  6.79 us (3%)
    pallas_call x8, Pallas kernels, __call__(): pl.pallas_call(kernel, out_shape=jax.ShapeDtypeStruct((count,) + tuple(bl...  131 us
    ppermute x1, waiting for transfers between devices, body(): panel_other = lax.ppermute(panel_mine, 'prow', sibling)  7 us
    dot_general x4, matrix products, outer_rows(): lax.dot_general(left_rows, right_rows, (((1,), (1,)), ((), ())), preferre...  6.34 us
    dot_general x1, matrix products, body(): jnp.dot(modal_at_loads, factor_cols, preferred_element_type=jnp.float32)  5.73 us
    ppermute x2, waiting for transfers between devices, beside_sibling(): other = lax.ppermute(part, 'prow', sibling)  4.23 us
  transfers between devices with their start and end apart: 6, of which 5 were waited for; matrix products, arithmetic and copies ran while one was open for 13% of the time, Pallas kernels for 65%

profile of v6, /device:TPU:39, one launch (start us, length us, event | category | flops | bytes accessed | tf_op | source)
XLA Modules:
  0.0 202.6 jit_solution(14663505453333248942)
XLA Ops:
  6.5 0.0 copy-start
  6.5 0.0 all-gather.2.cloned.1.call-start
  6.5 1.1 constant_dynamic-slice_fusion.1
  7.6 3.8 %collective-permute-start = (bf16[128,1024]{1,0:T(8,128)(2,1)S(1)}, bf16[128,1024]{1,0:T(8,128)(2,1)S(1)}, u32[]{:S(2)}, u32[]{:S(2)}) collective-permute-start(bf16[128,1024]{1,0:T(8,128)(2,1)S(1)} %constant_dynamic-slice_fusion.1), channel_id=1, source_target_pairs={{0,0},{64,16},{128,32},{192,48},{16,64},{80,80},{144,96},{208,112}... | collective-permute-start | bytes 786440 | tf_op jit(solution)/shard_map/ppermute | solution.py:175
  11.4 4.0 %collective-permute-done = bf16[128,1024]{1,0:T(8,128)(2,1)S(1)} collective-permute-done((bf16[128,1024]{1,0:T(8,128)(2,1)S(1)}, bf16[128,1024]{1,0:T(8,128)(2,1)S(1)}, u32[]{:S(2)}, u32[]{:S(2)}) %collective-permute-start) | collective-permute-done | bytes 262176 | tf_op jit(solution)/shard_map/ppermute | solution.py:175
  15.4 0.0 copy-start.2
  15.4 0.7 copy-done.2
  16.1 0.0 all-gather.2.cloned.1.call-update
  16.2 0.0 copy-done
  16.2 5.7 %fusion.21 = f32[2048,256]{1,0:T(8,128)S(1)} fusion(bf16[2048,2048]{1,0:T(8,128)(2,1)} %param.6, bf16[2048,256]{1,0:T(8,128)(2,1)S(1)} %copy-done), kind=kOutput, calls=%fused_computation.36 | convolution fusion | flops 2147483648 | bytes 11534336 | tf_op jit(solution)/shard_map/dot_general | solution.py:141
  21.9 1.0 constant_dynamic-slice_fusion
  23.0 0.0 collective-permute-start.1
  23.0 3.0 %collective-permute-done.1 = f32[1024,256]{1,0:T(8,128)} collective-permute-done((f32[1024,256]{1,0:T(8,128)}, f32[1024,256]{1,0:T(8,128)}, u32[]{:S(2)}, u32[]{:S(2)}) %collective-permute-start.1) | collective-permute-done | bytes 1048608 | tf_op jit(solution)/shard_map/ppermute | solution.py:146
  26.0 2.3 %dynamic-slice_add_fusion = f32[1024,256]{1,0:T(8,128)} fusion(f32[1024,256]{1,0:T(8,128)} %collective-permute-done.1, f32[2048,256]{1,0:T(8,128)S(1)} %fusion.21, s32[]{:T(128)S(6)} %select_n.54), kind=kLoop, calls=%fused_computation.16 | loop fusion | flops 262144 | bytes 3145732 | tf_op jit(solution)/shard_map/add | solution.py:146
  28.3 0.0 copy-start.4
  28.3 0.0 copy-start.5
  28.3 29.9 %shard_map.55 = f32[4,256,256]{2,1,0:T(8,128)} custom-call(f32[4,256,256]{2,1,0:T(8,128)} %bitcast.32), custom_call_target="tpu_custom_call" | custom-call | tf_op jit(solution)/shard_map/pallas_call | solution.py:110
  58.3 2.0 reduce_sum.30
  60.3 16.1 %shard_map.56 = f32[2,128,256]{2,1,0:T(8,128)} custom-call(f32[2,128,256]{2,1,0:T(8,128)} %bitcast.40), custom_call_target="tpu_custom_call" | custom-call | tf_op jit(solution)/shard_map/pallas_call | solution.py:110
  76.4 1.6 reduce_sum.31.x_ref
  78.0 9.6 %shard_map.57 = bf16[2,128,256]{2,1,0:T(8,128)(2,1)} custom-call(bf16[128,256]{1,0:T(8,128)(2,1)} %reduce_sum.31.x_ref), custom_call_target="tpu_custom_call" | custom-call | tf_op jit(solution)/shard_map/pallas_call | solution.py:110
  87.6 9.4 %shard_map.58 = bf16[4,256,256]{2,1,0:T(8,128)(2,1)} custom-call(bf16[256,256]{1,0:T(8,128)(2,1)} %bitcast.41), custom_call_target="tpu_custom_call" | custom-call | tf_op jit(solution)/shard_map/pallas_call | solution.py:110
  97.1 2.8 %collective-permute-start.2 = (bf16[1024,256]{1,0:T(8,128)(2,1)}, bf16[1024,256]{1,0:T(8,128)(2,1)S(1)}, u32[]{:S(2)}, u32[]{:S(2)}) collective-permute-start(bf16[1024,256]{1,0:T(8,128)(2,1)} %bitcast.33), channel_id=1, source_target_pairs={{0,64},{64,0},{128,192},{192,128},{1,65},{65,1},{129,193},{193,129... | collective-permute-start | bytes 1572872 | tf_op jit(solution)/shard_map/ppermute | solution.py:131
  99.9 0.0 copy-done.4
  99.9 0.0 copy-done.5
  99.9 1.7 collective-permute-done.2
  101.6 1.1 broadcast_select_fusion.3
  102.8 1.9 fusion
  104.7 0.8 convolution_convert_fusion
  105.5 0.3 copy.7
  105.8 1.0 copy.8
  106.8 17.9 %shard_map.59 = bf16[16,128,128]{2,1,0:T(8,128)(2,1)} custom-call(bf16[16,128,128]{2,1,0:T(8,128)(2,1)} %bitcast.37), custom_call_target="tpu_custom_call" | custom-call | tf_op jit(solution)/shard_map/pallas_call | solution.py:110
  124.7 1.7 reduce_sum.32.x_ref
  126.4 7.0 %shard_map.60.x_ref = bf16[2,128,128]{2,1,0:T(8,128)(2,1)} custom-call(bf16[128,128]{1,0:T(8,128)(2,1)} %reduce_sum.32.x_ref), custom_call_target="tpu_custom_call" | custom-call | tf_op jit(solution)/shard_map/pallas_call | solution.py:110
  133.5 30.7 %shard_map.61 = bf16[16,2,128,128]{3,2,1,0:T(8,128)(2,1)} custom-call(bf16[2,128,128]{2,1,0:T(8,128)(2,1)} %shard_map.60.x_ref), custom_call_target="tpu_custom_call" | custom-call | tf_op jit(solution)/shard_map/pallas_call | solution.py:110
  164.2 0.9 collective-permute-start.3
  165.0 2.5 %collective-permute-done.3 = bf16[1,16,2,128,128]{4,3,2,1,0:T(8,128)(2,1)S(1)} collective-permute-done((bf16[1,16,2,128,128]{4,3,2,1,0:T(8,128)(2,1)}, bf16[1,16,2,128,128]{4,3,2,1,0:T(8,128)(2,1)S(1)}, u32[]{:S(2)}, u32[]{:S(2)}) %collective-permute-start.3) | collective-permute-done | bytes 1048608 | tf_op jit(solution)/shard_map/ppermute | solution.py:131
  167.5 1.4 broadcast_select_fusion.1
  168.9 0.2 maximum_bitcast_fusion
  169.1 0.0 copy-start.3
  169.1 1.4 copy.9
  170.5 0.0 copy-done.3
  170.5 1.5 fusion.8.x_ref
  172.0 10.1 %shard_map.62 = bf16[4,128,512]{2,1,0:T(8,128)(2,1)} custom-call(bf16[128,512]{1,0:T(8,128)(2,1)} %fusion.8.x_ref), custom_call_target="tpu_custom_call" | custom-call | tf_op jit(solution)/shard_map/pallas_call | solution.py:110
  182.1 1.3 copy.11
  183.4 0.0 all-gather.2.cloned.1.call-done
  183.5 0.0 copy-start.1
  183.5 1.2 collective-permute-start.4
  184.7 7.0 %collective-permute-done.4 = bf16[2048,1024]{1,0:T(8,128)(2,1)S(1)} collective-permute-done((bf16[2048,1024]{1,0:T(8,128)(2,1)}, bf16[2048,1024]{1,0:T(8,128)(2,1)S(1)}, u32[]{:S(2)}, u32[]{:S(2)}) %collective-permute-start.4) | collective-permute-done | bytes 4194336 | tf_op jit(solution)/shard_map/ppermute | solution.py:178
  191.7 1.5 fusion.11
  193.2 0.0 copy-done.1
  193.2 2.5 %convolution_add_fusion = f32[128,2048]{1,0:T(8,128)} fusion(f32[128,2048]{1,0:T(8,128)S(1)} %fusion.11, bf16[2048,1024]{1,0:T(8,128)(2,1)S(1)} %copy-done.1, bf16[128,2048]{0,1:T(8,128)(2,1)S(1)} %bitcast.39, s32[]{:T(128)S(6)} %select_n.54), kind=kOutput, calls=%fused_computation.2 | convolution fusion | flops 537133056 | bytes 6553604 | tf_op jit(solution)/shard_map/dot_general | solution.py:22
  (1 shorter events, 0.0 us)
Async XLA Ops:
  6.5 9.6 %copy-start = (bf16[2048,256]{1,0:T(8,128)(2,1)S(1)}, bf16[2048,256]{1,0:T(8,128)(2,1)}, u32[]{:S(2)}) copy-start(bf16[2048,256]{1,0:T(8,128)(2,1)} %param.5) | copy-start | bytes 3145732
  6.5 176.9 %all-gather.2.cloned.1.call-start = ((), (), s32[]{:S(2)}) async-start(), calls=%async_computation | async-start | bytes 4456448 | tf_op jit(solution)/shard_map/all_gather | solution.py:176
  7.6 7.8 %collective-permute-start = (bf16[128,1024]{1,0:T(8,128)(2,1)S(1)}, bf16[128,1024]{1,0:T(8,128)(2,1)S(1)}, u32[]{:S(2)}, u32[]{:S(2)}) collective-permute-start(bf16[128,1024]{1,0:T(8,128)(2,1)S(1)} %constant_dynamic-slice_fusion.1), channel_id=1, source_target_pairs={{0,0},{64,16},{128,32},{192,48},{16,64},{80,80},{144,96},{208,112}... | collective-permute-start | bytes 786440 | tf_op jit(solution)/shard_map/ppermute | solution.py:175
  15.4 0.7 copy-start.2
  23.0 3.0 %collective-permute-start.1 = (f32[1024,256]{1,0:T(8,128)}, f32[1024,256]{1,0:T(8,128)}, u32[]{:S(2)}, u32[]{:S(2)}) collective-permute-start(f32[1024,256]{1,0:T(8,128)} %constant_dynamic-slice_fusion), channel_id=1, source_target_pairs={{0,64},{64,0},{128,192},{192,128},{1,65},{65,1},{129,193},{193,129... | collective-permute-start | bytes 3145736 | tf_op jit(solution)/shard_map/ppermute | solution.py:146
  28.3 71.6 %copy-start.4 = (f32[2048]{0:T(1024)S(1)}, f32[2048]{0:T(1024)}, u32[]{:S(2)}) copy-start(f32[2048]{0:T(1024)} %param.8) | copy-start | bytes 24580
  28.3 71.6 %copy-start.5 = (f32[2048]{0:T(1024)S(1)}, f32[2048]{0:T(1024)}, u32[]{:S(2)}) copy-start(f32[2048]{0:T(1024)} %param.9) | copy-start | bytes 24580
  97.1 4.6 %collective-permute-start.2 = (bf16[1024,256]{1,0:T(8,128)(2,1)}, bf16[1024,256]{1,0:T(8,128)(2,1)S(1)}, u32[]{:S(2)}, u32[]{:S(2)}) collective-permute-start(bf16[1024,256]{1,0:T(8,128)(2,1)} %bitcast.33), channel_id=1, source_target_pairs={{0,64},{64,0},{128,192},{192,128},{1,65},{65,1},{129,193},{193,129... | collective-permute-start | bytes 1572872 | tf_op jit(solution)/shard_map/ppermute | solution.py:131
  164.2 3.4 %collective-permute-start.3 = (bf16[1,16,2,128,128]{4,3,2,1,0:T(8,128)(2,1)}, bf16[1,16,2,128,128]{4,3,2,1,0:T(8,128)(2,1)S(1)}, u32[]{:S(2)}, u32[]{:S(2)}) collective-permute-start(bf16[1,16,2,128,128]{4,3,2,1,0:T(8,128)(2,1)} %bitcast.31), channel_id=1, source_target_pairs={{0,64},{64,0},{128,192},{192,128},{1,65},{65,1},{129,193},{193,129... | collective-permute-start | bytes 3145736 | tf_op jit(solution)/shard_map/ppermute | solution.py:131
  169.1 1.4 copy-start.3
  183.5 9.7 %copy-start.1 = (bf16[2048,1024]{1,0:T(8,128)(2,1)S(1)}, bf16[2048,1024]{1,0:T(8,128)(2,1)}, u32[]{:S(2)}) copy-start(bf16[2048,1024]{1,0:T(8,128)(2,1)} %all-gather.2.cloned.1.call-done) | copy-start | bytes 12582916
  183.5 8.2 %collective-permute-start.4 = (bf16[2048,1024]{1,0:T(8,128)(2,1)}, bf16[2048,1024]{1,0:T(8,128)(2,1)S(1)}, u32[]{:S(2)}, u32[]{:S(2)}) collective-permute-start(bf16[2048,1024]{1,0:T(8,128)(2,1)} %all-gather.2.cloned.1.call-done), channel_id=1, source_target_pairs={{0,64},{64,0},{128,192},{192,128},{1,65},{65,1},{129,193},{193,129... | collective-permute-start | bytes 12582920 | tf_op jit(solution)/shard_map/ppermute | solution.py:178
Sparse Core Ops, SparseCore 0:
  16.3 86.5 all-gather.1

commit v7 on v6

--- a/solution.py
+++ b/solution.py
@@ -145,8 +145,7 @@
         theirs = lax.dynamic_slice_in_dim(partial_load, (1 - core) * (modes // 2), modes // 2, 0)
         sums = mine + lax.ppermute(theirs, "prow", sibling)
         sums = jnp.sum(ex(sums.reshape(n_col, -1, width), ("pcol",), same=False), axis=0)
-        sums = jnp.sum(ex(sums.reshape(n_zh, -1, width), ("zh",), same=False), axis=0)
-        gathered = ex(sums.astype(jnp.bfloat16), ("zh",), same=True).reshape(-1, width)
+        gathered = jnp.sum(ex(sums, ("zh",), same=True), axis=0).astype(jnp.bfloat16)
         gathered = ex(gathered, ("pcol",), same=True).reshape(-1, width)
         modal_load = beside_sibling(gathered, core)
         modal_wide = modal_load.astype(jnp.float32)
@@ -167,15 +166,15 @@
         gram_all = ex(ex(gram_piece, ("zh",), same=True), ("pl",), same=True)
         gram_all = beside_sibling(gram_all[None], core)
         gram_panel = gram_all.transpose(2, 0, 3, 1, 4).reshape(n_row * block, modes)
-        weighted_part = outer_rows(mode_shapes, gram_panel).astype(jnp.bfloat16)
-        weighted_all = ex(weighted_part, ("pcol",), same=True)
-        weighted = weighted_all.transpose(1, 0, 2).reshape(weighted_part.shape[0], modes)
         half = modes // 2
         send_half = lax.dynamic_slice_in_dim(mode_shapes, (col % 2) * half, half, 1)
         panel_piece = lax.ppermute(send_half, ("prow", "pcol"), swap)
         panel_mine = lax.all_gather(panel_piece, "pl", axis=0, tiled=True)
-        panel_mine, weighted = lax.optimization_barrier((panel_mine, weighted))
+        panel_mine, gram_panel = lax.optimization_barrier((panel_mine, gram_panel))
         panel_other = lax.ppermute(panel_mine, "prow", sibling)
+        weighted_part = outer_rows(mode_shapes, gram_panel).astype(jnp.bfloat16)
+        weighted_all = ex(weighted_part, ("pcol",), same=True)
+        weighted = weighted_all.transpose(1, 0, 2).reshape(weighted_part.shape[0], modes)
         weighted_mine = lax.dynamic_slice_in_dim(weighted, core * half, half, 1)
         weighted_other = lax.dynamic_slice_in_dim(weighted, (1 - core) * half, half, 1)
         return outer_rows(weighted_mine, panel_mine) + outer_rows(weighted_other, panel_other)

time: 203 us -> 201 us (level)
  waiting for transfers between devices: 18.3 us -> 11.3 us
  matrix products: 12.1 us -> 15.4 us
    ppermute x1, waiting for transfers between devices: 7 us -> 0.01 us  [body(): panel_other = lax.ppermute(panel_mine, 'prow', sibling)]
    dot_general x4, matrix products: 6.34 us -> 9.71 us  [outer_rows(): lax.dot_general(left_rows, right_rows, (((1,), (1,)), ((), ())), preferre...]
    pallas_call x8 -> x7, Pallas kernels: 131 us -> 133 us  [__call__(): pl.pallas_call(kernel, out_shape=jax.ShapeDtypeStruct((count,) + tuple(bl...]
  transfers between devices with their start and end apart: 6 -> 6, of which waited for: 5 -> 4; matrix products, arithmetic and copies ran while one was open for 13% -> 14% of each run, Pallas kernels for 65% -> 67%
where the time goes in v7:
time: 201 us; the launch traced here: 200 us
  Pallas kernels  133 us (66%)
  matrix products  15.4 us (8%)
  between operations  13.6 us (7%)
  other arithmetic  12.5 us (6%)
  waiting for transfers between devices  11.3 us (6%)
  local copies, waits for them, and re-layouts  7.34 us (4%)
  starting transfers between devices  6.71 us (3%)
    pallas_call x7, Pallas kernels, __call__(): pl.pallas_call(kernel, out_shape=jax.ShapeDtypeStruct((count,) + tuple(bl...  133 us
    dot_general x4, matrix products, outer_rows(): lax.dot_general(left_rows, right_rows, (((1,), (1,)), ((), ())), preferre...  9.71 us
    dot_general x1, matrix products, body(): jnp.dot(modal_at_loads, factor_cols, preferred_element_type=jnp.float32)  5.73 us
    ppermute x2, waiting for transfers between devices, beside_sibling(): other = lax.ppermute(part, 'prow', sibling)  4.23 us
    ppermute x1, waiting for transfers between devices, body(): panel_piece = lax.ppermute(send_half, ('prow', 'pcol'), swap)  4.04 us
  transfers between devices with their start and end apart: 6, of which 4 were waited for; matrix products, arithmetic and copies ran while one was open for 14% of the time, Pallas kernels for 67%

profile of v7, /device:TPU:39, one launch (start us, length us, event | category | flops | bytes accessed | tf_op | source)
XLA Modules:
  0.0 200.2 jit_solution(15067574834325318454)
XLA Ops:
  6.5 0.0 copy-start
  6.5 0.0 all-gather.2.cloned.1.call-start
  6.5 1.1 constant_dynamic-slice_fusion.1
  7.6 3.8 %collective-permute-start = (bf16[128,1024]{1,0:T(8,128)(2,1)S(1)}, bf16[128,1024]{1,0:T(8,128)(2,1)S(1)}, u32[]{:S(2)}, u32[]{:S(2)}) collective-permute-start(bf16[128,1024]{1,0:T(8,128)(2,1)S(1)} %constant_dynamic-slice_fusion.1), channel_id=1, source_target_pairs={{0,0},{64,16},{128,32},{192,48},{16,64},{80,80},{144,96},{208,112}... | collective-permute-start | bytes 786440 | tf_op jit(solution)/shard_map/ppermute | solution.py:171
  11.4 4.0 %collective-permute-done = bf16[128,1024]{1,0:T(8,128)(2,1)S(1)} collective-permute-done((bf16[128,1024]{1,0:T(8,128)(2,1)S(1)}, bf16[128,1024]{1,0:T(8,128)(2,1)S(1)}, u32[]{:S(2)}, u32[]{:S(2)}) %collective-permute-start) | collective-permute-done | bytes 262176 | tf_op jit(solution)/shard_map/ppermute | solution.py:171
  15.4 0.0 copy-start.2
  15.4 0.7 copy-done.2
  16.1 0.0 all-gather.2.cloned.1.call-update
  16.2 0.0 copy-done
  16.2 5.7 %fusion.13 = f32[2048,256]{1,0:T(8,128)S(1)} fusion(bf16[2048,2048]{1,0:T(8,128)(2,1)} %param.6, bf16[2048,256]{1,0:T(8,128)(2,1)S(1)} %copy-done), kind=kOutput, calls=%fused_computation.34 | convolution fusion | flops 2147483648 | bytes 11534336 | tf_op jit(solution)/shard_map/dot_general | solution.py:141
  21.9 1.0 constant_dynamic-slice_fusion
  23.0 0.0 collective-permute-start.1
  23.0 3.0 %collective-permute-done.1 = f32[1024,256]{1,0:T(8,128)} collective-permute-done((f32[1024,256]{1,0:T(8,128)}, f32[1024,256]{1,0:T(8,128)}, u32[]{:S(2)}, u32[]{:S(2)}) %collective-permute-start.1) | collective-permute-done | bytes 1048608 | tf_op jit(solution)/shard_map/ppermute | solution.py:146
  26.0 2.3 %dynamic-slice_add_fusion = f32[1024,256]{1,0:T(8,128)} fusion(f32[1024,256]{1,0:T(8,128)} %collective-permute-done.1, f32[2048,256]{1,0:T(8,128)S(1)} %fusion.13, s32[]{:T(128)S(6)} %select_n.54), kind=kLoop, calls=%fused_computation.14 | loop fusion | flops 262144 | bytes 3145732 | tf_op jit(solution)/shard_map/add | solution.py:146
  28.3 29.9 %shard_map.55 = f32[4,256,256]{2,1,0:T(8,128)} custom-call(f32[4,256,256]{2,1,0:T(8,128)} %bitcast.29), custom_call_target="tpu_custom_call" | custom-call | tf_op jit(solution)/shard_map/pallas_call | solution.py:110
  58.3 0.0 copy-start.3
  58.3 0.0 copy-start.4
  58.3 2.0 %reduce_sum.30.x_ref = f32[256,256]{1,0:T(8,128)} reduce(f32[4,256,256]{2,1,0:T(8,128)} %shard_map.55, f32[]{:T(128)} %constant.42.clone.1), dimensions={0}, to_apply=%region_0.1 | reduce | flops 196608 | bytes 1310724 | tf_op jit(solution)/shard_map/reduce_sum | solution.py:147
  60.3 26.5 %shard_map.56 = f32[2,256,256]{2,1,0:T(8,128)} custom-call(f32[256,256]{1,0:T(8,128)} %reduce_sum.30.x_ref), custom_call_target="tpu_custom_call" | custom-call | tf_op jit(solution)/shard_map/pallas_call | solution.py:110
  86.8 1.8 reduce_sum.31.x_ref
  88.6 9.3 %shard_map.57 = bf16[4,256,256]{2,1,0:T(8,128)(2,1)} custom-call(bf16[256,256]{1,0:T(8,128)(2,1)} %reduce_sum.31.x_ref), custom_call_target="tpu_custom_call" | custom-call | tf_op jit(solution)/shard_map/pallas_call | solution.py:110
  97.9 1.4 collective-permute-start.2
  99.3 0.0 copy-done.3
  99.3 0.0 copy-done.4
  99.3 1.7 collective-permute-done.2
  101.0 1.1 broadcast_select_fusion.3
  102.2 1.9 fusion
  104.1 0.8 convolution_convert_fusion
  104.9 0.3 copy.7
  105.2 1.0 copy.8
  106.2 18.4 %shard_map.58 = bf16[16,128,128]{2,1,0:T(8,128)(2,1)} custom-call(bf16[16,128,128]{2,1,0:T(8,128)(2,1)} %bitcast.33), custom_call_target="tpu_custom_call" | custom-call | tf_op jit(solution)/shard_map/pallas_call | solution.py:110
  124.7 1.7 reduce_sum.32.x_ref
  126.4 7.0 %shard_map.59.x_ref = bf16[2,128,128]{2,1,0:T(8,128)(2,1)} custom-call(bf16[128,128]{1,0:T(8,128)(2,1)} %reduce_sum.32.x_ref), custom_call_target="tpu_custom_call" | custom-call | tf_op jit(solution)/shard_map/pallas_call | solution.py:110
  133.4 31.6 %shard_map.60 = bf16[16,2,128,128]{3,2,1,0:T(8,128)(2,1)} custom-call(bf16[2,128,128]{2,1,0:T(8,128)(2,1)} %shard_map.59.x_ref), custom_call_target="tpu_custom_call" | custom-call | tf_op jit(solution)/shard_map/pallas_call | solution.py:110
  165.1 0.9 collective-permute-start.3
  165.9 2.5 %collective-permute-done.3 = bf16[1,16,2,128,128]{4,3,2,1,0:T(8,128)(2,1)S(1)} collective-permute-done((bf16[1,16,2,128,128]{4,3,2,1,0:T(8,128)(2,1)}, bf16[1,16,2,128,128]{4,3,2,1,0:T(8,128)(2,1)S(1)}, u32[]{:S(2)}, u32[]{:S(2)}) %collective-permute-start.3) | collective-permute-done | bytes 1048608 | tf_op jit(solution)/shard_map/ppermute | solution.py:131
  168.4 1.4 broadcast_select_fusion.1
  169.8 0.2 maximum_bitcast_fusion
  170.0 1.4 copy.9
  171.4 0.5 copy.15
  171.9 0.0 all-gather.2.cloned.1.call-done
  171.9 0.6 collective-permute-start.4
  172.6 2.5 %fusion.2.x_ref = bf16[128,512]{1,0:T(8,128)(2,1)} fusion(bf16[512,2048]{1,0:T(8,128)(2,1)S(1)} %bitcast.26, bf16[128,2048]{1,0:T(8,128)(2,1)} %param.7), kind=kOutput, calls=%fused_computation.12 | convolution fusion | flops 268500992 | bytes 2752512 | tf_op jit(solution)/shard_map/dot_general | solution.py:22
  175.1 10.5 %shard_map.61 = bf16[4,128,512]{2,1,0:T(8,128)(2,1)} custom-call(bf16[128,512]{1,0:T(8,128)(2,1)} %fusion.2.x_ref), custom_call_target="tpu_custom_call" | custom-call | tf_op jit(solution)/shard_map/pallas_call | solution.py:110
  185.6 1.3 copy.11
  186.9 0.0 collective-permute-done.4
  186.9 0.0 copy-start.1
  186.9 3.8 %fusion.3 = f32[128,2048]{1,0:T(8,128)S(1)} fusion(bf16[2048,1024]{1,0:T(8,128)(2,1)} %collective-permute-done.4, bf16[128,2048]{0,1:T(8,128)(2,1)S(1)} %bitcast.34, s32[]{:T(128)S(6)} %select_n.55), kind=kOutput, calls=%fused_computation.19 | convolution fusion | flops 536870912 | bytes 5505028 | tf_op jit(solution)/shard_map/dot_general | solution.py:22
  190.8 0.0 copy-done.1
  190.8 2.5 %convolution_add_fusion = f32[128,2048]{1,0:T(8,128)} fusion(f32[128,2048]{1,0:T(8,128)S(1)} %fusion.3, bf16[2048,1024]{1,0:T(8,128)(2,1)S(1)} %copy-done.1, bf16[128,2048]{0,1:T(8,128)(2,1)S(1)} %bitcast.35, s32[]{:T(128)S(6)} %select_n.54), kind=kOutput, calls=%fused_computation.2 | convolution fusion | flops 537133056 | bytes 6553604 | tf_op jit(solution)/shard_map/dot_general | solution.py:22
  (1 shorter events, 0.0 us)
Async XLA Ops:
  6.5 9.7 %copy-start = (bf16[2048,256]{1,0:T(8,128)(2,1)S(1)}, bf16[2048,256]{1,0:T(8,128)(2,1)}, u32[]{:S(2)}) copy-start(bf16[2048,256]{1,0:T(8,128)(2,1)} %param.5) | copy-start | bytes 3145732
  6.5 165.4 %all-gather.2.cloned.1.call-start = ((), (), s32[]{:S(2)}) async-start(), calls=%async_computation | async-start | bytes 4456448 | tf_op jit(solution)/shard_map/all_gather | solution.py:172
  7.6 7.8 %collective-permute-start = (bf16[128,1024]{1,0:T(8,128)(2,1)S(1)}, bf16[128,1024]{1,0:T(8,128)(2,1)S(1)}, u32[]{:S(2)}, u32[]{:S(2)}) collective-permute-start(bf16[128,1024]{1,0:T(8,128)(2,1)S(1)} %constant_dynamic-slice_fusion.1), channel_id=1, source_target_pairs={{0,0},{64,16},{128,32},{192,48},{16,64},{80,80},{144,96},{208,112}... | collective-permute-start | bytes 786440 | tf_op jit(solution)/shard_map/ppermute | solution.py:171
  15.4 0.7 copy-start.2
  23.0 3.0 %collective-permute-start.1 = (f32[1024,256]{1,0:T(8,128)}, f32[1024,256]{1,0:T(8,128)}, u32[]{:S(2)}, u32[]{:S(2)}) collective-permute-start(f32[1024,256]{1,0:T(8,128)} %constant_dynamic-slice_fusion), channel_id=1, source_target_pairs={{0,64},{64,0},{128,192},{192,128},{1,65},{65,1},{129,193},{193,129... | collective-permute-start | bytes 3145736 | tf_op jit(solution)/shard_map/ppermute | solution.py:146
  58.3 41.0 %copy-start.3 = (f32[2048]{0:T(1024)S(1)}, f32[2048]{0:T(1024)}, u32[]{:S(2)}) copy-start(f32[2048]{0:T(1024)} %param.8) | copy-start | bytes 24580
  58.3 41.0 %copy-start.4 = (f32[2048]{0:T(1024)S(1)}, f32[2048]{0:T(1024)}, u32[]{:S(2)}) copy-start(f32[2048]{0:T(1024)} %param.9) | copy-start | bytes 24580
  97.9 3.2 %collective-permute-start.2 = (bf16[1024,256]{1,0:T(8,128)(2,1)}, bf16[1024,256]{1,0:T(8,128)(2,1)S(1)}, u32[]{:S(2)}, u32[]{:S(2)}) collective-permute-start(bf16[1024,256]{1,0:T(8,128)(2,1)} %bitcast.30), channel_id=1, source_target_pairs={{0,64},{64,0},{128,192},{192,128},{1,65},{65,1},{129,193},{193,129... | collective-permute-start | bytes 1572872 | tf_op jit(solution)/shard_map/ppermute | solution.py:131
  165.1 3.4 %collective-permute-start.3 = (bf16[1,16,2,128,128]{4,3,2,1,0:T(8,128)(2,1)}, bf16[1,16,2,128,128]{4,3,2,1,0:T(8,128)(2,1)S(1)}, u32[]{:S(2)}, u32[]{:S(2)}) collective-permute-start(bf16[1,16,2,128,128]{4,3,2,1,0:T(8,128)(2,1)} %bitcast.28), channel_id=1, source_target_pairs={{0,64},{64,0},{128,192},{192,128},{1,65},{65,1},{129,193},{193,129... | collective-permute-start | bytes 3145736 | tf_op jit(solution)/shard_map/ppermute | solution.py:131
  171.9 15.0 %collective-permute-start.4 = (bf16[2048,1024]{1,0:T(8,128)(2,1)}, bf16[2048,1024]{1,0:T(8,128)(2,1)}, u32[]{:S(2)}, u32[]{:S(2)}) collective-permute-start(bf16[2048,1024]{1,0:T(8,128)(2,1)} %all-gather.2.cloned.1.call-done), channel_id=1, source_target_pairs={{0,64},{64,0},{128,192},{192,128},{1,65},{65,1},{129,193},{193,129... | collective-permute-start | bytes 12582920 | tf_op jit(solution)/shard_map/ppermute | solution.py:174
  186.9 3.9 %copy-start.1 = (bf16[2048,1024]{1,0:T(8,128)(2,1)S(1)}, bf16[2048,1024]{1,0:T(8,128)(2,1)}, u32[]{:S(2)}) copy-start(bf16[2048,1024]{1,0:T(8,128)(2,1)} %all-gather.2.cloned.1.call-done) | copy-start | bytes 12582916
Sparse Core Ops, SparseCore 0:
  16.3 90.1 all-gather.1

commit v8 on v7

--- a/solution.py
+++ b/solution.py
@@ -143,9 +143,12 @@
         core = row % 2
         mine = lax.dynamic_slice_in_dim(partial_load, core * (modes // 2), modes // 2, 0)
         theirs = lax.dynamic_slice_in_dim(partial_load, (1 - core) * (modes // 2), modes // 2, 0)
-        sums = mine + lax.ppermute(theirs, "prow", sibling)
-        sums = jnp.sum(ex(sums.reshape(n_col, -1, width), ("pcol",), same=False), axis=0)
-        gathered = jnp.sum(ex(sums, ("zh",), same=True), axis=0).astype(jnp.bfloat16)
+        wide = lambda part: part.astype(jnp.float32)
+        sums = mine + wide(lax.ppermute(theirs.astype(jnp.bfloat16), "prow", sibling))
+        pieces = ex(sums.astype(jnp.bfloat16).reshape(n_col, -1, width), ("pcol",), same=False)
+        sums = jnp.sum(wide(pieces), axis=0)
+        pieces = ex(sums.astype(jnp.bfloat16), ("zh",), same=True)
+        gathered = jnp.sum(wide(pieces), axis=0).astype(jnp.bfloat16)
         gathered = ex(gathered, ("pcol",), same=True).reshape(-1, width)
         modal_load = beside_sibling(gathered, core)
         modal_wide = modal_load.astype(jnp.float32)

time: 201 us -> 190 us (0.945)
  Pallas kernels: 133 us -> 122 us
    pallas_call x7, Pallas kernels: 133 us -> 122 us  [__call__(): pl.pallas_call(kernel, out_shape=jax.ShapeDtypeStruct((count,) + tuple(bl...]
    add x1 -> x0, other arithmetic: 2.33 us -> none  [body(): sums = mine + lax.ppermute(theirs, 'prow', sibling)]
  transfers between devices with their start and end apart: 6 -> 6, of which waited for: 4 -> 4; matrix products, arithmetic and copies ran while one was open for 14% -> 14% of each run, Pallas kernels for 67% -> 65%
where the time goes in v8:
time: 190 us; the launch traced here: 189 us
  Pallas kernels  122 us (64%)
  matrix products  15.4 us (8%)
  between operations  13.6 us (7%)
  other arithmetic  11.8 us (6%)
  waiting for transfers between devices  10.6 us (6%)
  starting transfers between devices  8.19 us (4%)
  local copies, waits for them, and re-layouts  7.14 us (4%)
    pallas_call x7, Pallas kernels, __call__(): pl.pallas_call(kernel, out_shape=jax.ShapeDtypeStruct((count,) + tuple(bl...  122 us
    dot_general x4, matrix products, outer_rows(): lax.dot_general(left_rows, right_rows, (((1,), (1,)), ((), ())), preferre...  9.7 us
    dot_general x1, matrix products, body(): jnp.dot(modal_at_loads, factor_cols, preferred_element_type=jnp.float32)  5.73 us
    ppermute x2, waiting for transfers between devices, beside_sibling(): other = lax.ppermute(part, 'prow', sibling)  4.23 us
    ppermute x1, waiting for transfers between devices, body(): panel_piece = lax.ppermute(send_half, ('prow', 'pcol'), swap)  4.04 us
  transfers between devices with their start and end apart: 6, of which 4 were waited for; matrix products, arithmetic and copies ran while one was open for 14% of the time, Pallas kernels for 65%

profile of v8, /device:TPU:39, one launch (start us, length us, event | category | flops | bytes accessed | tf_op | source)
XLA Modules:
  0.0 188.9 jit_solution(14977398230842366395)
XLA Ops:
  6.5 0.0 copy-start
  6.5 0.0 all-gather.2.cloned.1.call-start
  6.5 1.1 constant_dynamic-slice_fusion
  7.6 3.8 %collective-permute-start = (bf16[128,1024]{1,0:T(8,128)(2,1)S(1)}, bf16[128,1024]{1,0:T(8,128)(2,1)S(1)}, u32[]{:S(2)}, u32[]{:S(2)}) collective-permute-start(bf16[128,1024]{1,0:T(8,128)(2,1)S(1)} %constant_dynamic-slice_fusion), channel_id=1, source_target_pairs={{0,0},{64,16},{128,32},{192,48},{16,64},{80,80},{144,96},{208,112}... | collective-permute-start | bytes 786440 | tf_op jit(solution)/shard_map/ppermute | solution.py:174
  11.4 4.0 %collective-permute-done = bf16[128,1024]{1,0:T(8,128)(2,1)S(1)} collective-permute-done((bf16[128,1024]{1,0:T(8,128)(2,1)S(1)}, bf16[128,1024]{1,0:T(8,128)(2,1)S(1)}, u32[]{:S(2)}, u32[]{:S(2)}) %collective-permute-start) | collective-permute-done | bytes 262176 | tf_op jit(solution)/shard_map/ppermute | solution.py:174
  15.4 0.0 copy-start.2
  15.4 0.7 copy-done.2
  16.1 0.0 all-gather.2.cloned.1.call-update
  16.2 0.0 copy-done
  16.2 5.7 %fusion.13 = f32[2048,256]{1,0:T(8,128)S(1)} fusion(bf16[2048,2048]{1,0:T(8,128)(2,1)} %param.6, bf16[2048,256]{1,0:T(8,128)(2,1)S(1)} %copy-done), kind=kOutput, calls=%fused_computation.34 | convolution fusion | flops 2147483648 | bytes 11534336 | tf_op jit(solution)/shard_map/dot_general | solution.py:141
  21.9 0.9 dynamic-slice_convert_fusion
  22.8 0.0 collective-permute-start.1
  22.8 2.2 %collective-permute-done.1 = bf16[1024,256]{1,0:T(8,128)(2,1)} collective-permute-done((bf16[1024,256]{1,0:T(8,128)(2,1)}, bf16[1024,256]{1,0:T(8,128)(2,1)}, u32[]{:S(2)}, u32[]{:S(2)}) %collective-permute-start.1) | collective-permute-done | bytes 524320 | tf_op jit(solution)/shard_map/ppermute | solution.py:147
  25.0 2.0 %add_convert_fusion = bf16[1024,256]{1,0:T(8,128)(2,1)} fusion(bf16[1024,256]{1,0:T(8,128)(2,1)} %collective-permute-done.1, f32[2048,256]{1,0:T(8,128)S(1)} %fusion.13, s32[]{:T(128)S(6)} %select_n.54), kind=kLoop, calls=%fused_computation.14 | loop fusion | flops 786432 | bytes 2097156 | tf_op jit(solution)/shard_map/convert_element_type | solution.py:148
  27.0 0.0 copy-start.3
  27.0 0.0 copy-start.4
  27.0 24.3 %shard_map.55 = bf16[4,256,256]{2,1,0:T(8,128)(2,1)} custom-call(bf16[4,256,256]{2,1,0:T(8,128)(2,1)} %bitcast.30), custom_call_target="tpu_custom_call" | custom-call | tf_op jit(solution)/shard_map/pallas_call | solution.py:110
  51.3 1.8 reduce_sum.36.x_ref
  53.1 17.1 %shard_map.56 = bf16[2,256,256]{2,1,0:T(8,128)(2,1)} custom-call(bf16[256,256]{1,0:T(8,128)(2,1)} %reduce_sum.36.x_ref), custom_call_target="tpu_custom_call" | custom-call | tf_op jit(solution)/shard_map/pallas_call | solution.py:110
  70.3 1.7 reduce_sum.37.x_ref
  71.9 9.2 %shard_map.57 = bf16[4,256,256]{2,1,0:T(8,128)(2,1)} custom-call(bf16[256,256]{1,0:T(8,128)(2,1)} %reduce_sum.37.x_ref), custom_call_target="tpu_custom_call" | custom-call | tf_op jit(solution)/shard_map/pallas_call | solution.py:110
  81.2 1.6 collective-permute-start.2
  82.8 0.0 copy-done.3
  82.8 0.0 copy-done.4
  82.8 1.7 collective-permute-done.2
  84.5 1.1 broadcast_select_fusion.3
  85.6 1.9 %fusion = (bf16[2048,256]{1,0:T(8,128)(2,1)S(1)}, bf16[2048,256]{1,0:T(8,128)(2,1)S(1)}) fusion(f32[2048]{0:T(1024)S(1)} %get-tuple-element.15, bf16[1024,256]{1,0:T(8,128)(2,1)S(1)} %get-tuple-element.14, bf16[1024,256]{1,0:T(8,128)(2,1)S(1)} %get-tuple-element.13, f32[2048]{0:T(1024)S(1)} %get-tuple-element.16), kind=kLoop, calls=%fused_computation.7 | loop fusion | flops 4194304 | bytes 3162112 | tf_op jit(solution)/shard_map/convert_element_type | solution.py:157
  87.6 0.8 convolution_convert_fusion
  88.4 0.3 copy.7
  88.7 1.0 copy.8
  89.7 27.3 %shard_map.58 = bf16[16,128,128]{2,1,0:T(8,128)(2,1)} custom-call(bf16[16,128,128]{2,1,0:T(8,128)(2,1)} %bitcast.33), custom_call_target="tpu_custom_call" | custom-call | tf_op jit(solution)/shard_map/pallas_call | solution.py:110
  117.0 1.7 reduce_sum.38.x_ref
  118.8 7.0 %shard_map.59.x_ref = bf16[2,128,128]{2,1,0:T(8,128)(2,1)} custom-call(bf16[128,128]{1,0:T(8,128)(2,1)} %reduce_sum.38.x_ref), custom_call_target="tpu_custom_call" | custom-call | tf_op jit(solution)/shard_map/pallas_call | solution.py:110
  125.8 27.4 %shard_map.60 = bf16[16,2,128,128]{3,2,1,0:T(8,128)(2,1)} custom-call(bf16[2,128,128]{2,1,0:T(8,128)(2,1)} %shard_map.59.x_ref), custom_call_target="tpu_custom_call" | custom-call | tf_op jit(solution)/shard_map/pallas_call | solution.py:110
  153.2 2.2 %collective-permute-start.3 = (bf16[1,16,2,128,128]{4,3,2,1,0:T(8,128)(2,1)}, bf16[1,16,2,128,128]{4,3,2,1,0:T(8,128)(2,1)S(1)}, u32[]{:S(2)}, u32[]{:S(2)}) collective-permute-start(bf16[1,16,2,128,128]{4,3,2,1,0:T(8,128)(2,1)} %bitcast.28), channel_id=1, source_target_pairs={{0,64},{64,0},{128,192},{192,128},{1,65},{65,1},{129,193},{193,129... | collective-permute-start | bytes 3145736 | tf_op jit(solution)/shard_map/ppermute | solution.py:131
  155.4 2.5 %collective-permute-done.3 = bf16[1,16,2,128,128]{4,3,2,1,0:T(8,128)(2,1)S(1)} collective-permute-done((bf16[1,16,2,128,128]{4,3,2,1,0:T(8,128)(2,1)}, bf16[1,16,2,128,128]{4,3,2,1,0:T(8,128)(2,1)S(1)}, u32[]{:S(2)}, u32[]{:S(2)}) %collective-permute-start.3) | collective-permute-done | bytes 1048608 | tf_op jit(solution)/shard_map/ppermute | solution.py:131
  157.9 1.4 broadcast_select_fusion.1
  159.3 0.2 maximum_bitcast_fusion
  159.5 1.4 copy.9
  160.8 0.5 copy.15
  161.4 0.0 all-gather.2.cloned.1.call-done
  161.4 0.6 collective-permute-start.4
  162.1 2.5 %fusion.2.x_ref = bf16[128,512]{1,0:T(8,128)(2,1)} fusion(bf16[512,2048]{1,0:T(8,128)(2,1)S(1)} %bitcast.26, bf16[128,2048]{1,0:T(8,128)(2,1)} %param.7), kind=kOutput, calls=%fused_computation.12 | convolution fusion | flops 268500992 | bytes 2752512 | tf_op jit(solution)/shard_map/dot_general | solution.py:22
  164.6 9.7 %shard_map.61 = bf16[4,128,512]{2,1,0:T(8,128)(2,1)} custom-call(bf16[128,512]{1,0:T(8,128)(2,1)} %fusion.2.x_ref), custom_call_target="tpu_custom_call" | custom-call | tf_op jit(solution)/shard_map/pallas_call | solution.py:110
  174.3 1.3 copy.11
  175.6 0.0 collective-permute-done.4
  175.6 0.0 copy-start.1
  175.6 3.8 %fusion.3 = f32[128,2048]{1,0:T(8,128)S(1)} fusion(bf16[2048,1024]{1,0:T(8,128)(2,1)} %collective-permute-done.4, bf16[128,2048]{0,1:T(8,128)(2,1)S(1)} %bitcast.34, s32[]{:T(128)S(6)} %select_n.55), kind=kOutput, calls=%fused_computation.20 | convolution fusion | flops 536870912 | bytes 5505028 | tf_op jit(solution)/shard_map/dot_general | solution.py:22
  179.5 0.0 copy-done.1
  179.5 2.5 %convolution_add_fusion = f32[128,2048]{1,0:T(8,128)} fusion(f32[128,2048]{1,0:T(8,128)S(1)} %fusion.3, bf16[2048,1024]{1,0:T(8,128)(2,1)S(1)} %copy-done.1, bf16[128,2048]{0,1:T(8,128)(2,1)S(1)} %bitcast.35, s32[]{:T(128)S(6)} %select_n.54), kind=kOutput, calls=%fused_computation.2 | convolution fusion | flops 537133056 | bytes 6553604 | tf_op jit(solution)/shard_map/dot_general | solution.py:22
  (1 shorter events, 0.0 us)
Async XLA Ops:
  6.5 9.7 %copy-start = (bf16[2048,256]{1,0:T(8,128)(2,1)S(1)}, bf16[2048,256]{1,0:T(8,128)(2,1)}, u32[]{:S(2)}) copy-start(bf16[2048,256]{1,0:T(8,128)(2,1)} %param.5) | copy-start | bytes 3145732
  6.5 154.9 %all-gather.2.cloned.1.call-start = ((), (), s32[]{:S(2)}) async-start(), calls=%async_computation | async-start | bytes 4456448 | tf_op jit(solution)/shard_map/all_gather | solution.py:175
  7.6 7.8 %collective-permute-start = (bf16[128,1024]{1,0:T(8,128)(2,1)S(1)}, bf16[128,1024]{1,0:T(8,128)(2,1)S(1)}, u32[]{:S(2)}, u32[]{:S(2)}) collective-permute-start(bf16[128,1024]{1,0:T(8,128)(2,1)S(1)} %constant_dynamic-slice_fusion), channel_id=1, source_target_pairs={{0,0},{64,16},{128,32},{192,48},{16,64},{80,80},{144,96},{208,112}... | collective-permute-start | bytes 786440 | tf_op jit(solution)/shard_map/ppermute | solution.py:174
  15.4 0.7 copy-start.2
  22.8 2.3 %collective-permute-start.1 = (bf16[1024,256]{1,0:T(8,128)(2,1)}, bf16[1024,256]{1,0:T(8,128)(2,1)}, u32[]{:S(2)}, u32[]{:S(2)}) collective-permute-start(bf16[1024,256]{1,0:T(8,128)(2,1)} %dynamic-slice_convert_fusion), channel_id=1, source_target_pairs={{0,64},{64,0},{128,192},{192,128},{1,65},{65,1},{129,193},{193,129... | collective-permute-start | bytes 1572872 | tf_op jit(solution)/shard_map/ppermute | solution.py:147
  27.0 55.8 %copy-start.3 = (f32[2048]{0:T(1024)S(1)}, f32[2048]{0:T(1024)}, u32[]{:S(2)}) copy-start(f32[2048]{0:T(1024)} %param.8) | copy-start | bytes 24580
  27.0 55.8 %copy-start.4 = (f32[2048]{0:T(1024)S(1)}, f32[2048]{0:T(1024)}, u32[]{:S(2)}) copy-start(f32[2048]{0:T(1024)} %param.9) | copy-start | bytes 24580
  81.2 3.3 %collective-permute-start.2 = (bf16[1024,256]{1,0:T(8,128)(2,1)}, bf16[1024,256]{1,0:T(8,128)(2,1)S(1)}, u32[]{:S(2)}, u32[]{:S(2)}) collective-permute-start(bf16[1024,256]{1,0:T(8,128)(2,1)} %bitcast.29), channel_id=1, source_target_pairs={{0,64},{64,0},{128,192},{192,128},{1,65},{65,1},{129,193},{193,129... | collective-permute-start | bytes 1572872 | tf_op jit(solution)/shard_map/ppermute | solution.py:131
  153.2 4.7 %collective-permute-start.3 = (bf16[1,16,2,128,128]{4,3,2,1,0:T(8,128)(2,1)}, bf16[1,16,2,128,128]{4,3,2,1,0:T(8,128)(2,1)S(1)}, u32[]{:S(2)}, u32[]{:S(2)}) collective-permute-start(bf16[1,16,2,128,128]{4,3,2,1,0:T(8,128)(2,1)} %bitcast.28), channel_id=1, source_target_pairs={{0,64},{64,0},{128,192},{192,128},{1,65},{65,1},{129,193},{193,129... | collective-permute-start | bytes 3145736 | tf_op jit(solution)/shard_map/ppermute | solution.py:131
  161.4 14.2 %collective-permute-start.4 = (bf16[2048,1024]{1,0:T(8,128)(2,1)}, bf16[2048,1024]{1,0:T(8,128)(2,1)}, u32[]{:S(2)}, u32[]{:S(2)}) collective-permute-start(bf16[2048,1024]{1,0:T(8,128)(2,1)} %all-gather.2.cloned.1.call-done), channel_id=1, source_target_pairs={{0,64},{64,0},{128,192},{192,128},{1,65},{65,1},{129,193},{193,129... | collective-permute-start | bytes 12582920 | tf_op jit(solution)/shard_map/ppermute | solution.py:177
  175.6 3.9 %copy-start.1 = (bf16[2048,1024]{1,0:T(8,128)(2,1)S(1)}, bf16[2048,1024]{1,0:T(8,128)(2,1)}, u32[]{:S(2)}) copy-start(bf16[2048,1024]{1,0:T(8,128)(2,1)} %all-gather.2.cloned.1.call-done) | copy-start | bytes 12582916
Sparse Core Ops, SparseCore 0:
  16.3 94.1 all-gather.1

commit v9 on v8

--- a/solution.py
+++ b/solution.py
@@ -30,6 +30,8 @@
         "core": ("prow", 2, 1),
         "pcol": ("pcol", sizes["pcol"], 1),
         "pl": ("pl", sizes["pl"], 1),
+        "plz": ("pl", sizes["pl"] // 4, 4),
+        "plx": ("pl", 4, 1),
     }
 
 
@@ -163,12 +165,13 @@
         own_pseudo = lax.dynamic_slice_in_dim(pseudo, first_row, block, 0)
         partial_gram = outer_rows(own_pseudo, pseudo).astype(jnp.bfloat16)
         chunk = modes // n_pl
-        by_chunk = partial_gram.reshape(block, n_pl, chunk).transpose(1, 0, 2)
-        gram_sums = ex(by_chunk, ("pl",), same=False)
-        gram_piece = jnp.sum(gram_sums.astype(jnp.float32), axis=0).astype(jnp.bfloat16)
-        gram_all = ex(ex(gram_piece, ("zh",), same=True), ("pl",), same=True)
+        n_z = n_pl // 4
+        by_x = partial_gram.reshape(block, n_z, 4, chunk).transpose(2, 1, 0, 3)
+        sums = jnp.sum(ex(by_x, ("plx",), same=False).astype(jnp.float32), axis=0)
+        gram_piece = jnp.sum(ex(sums, ("plz",), same=False), axis=0).astype(jnp.bfloat16)
+        gram_all = ex(ex(ex(gram_piece, ("zh",), same=True), ("plz",), same=True), ("plx",), same=True)
         gram_all = beside_sibling(gram_all[None], core)
-        gram_panel = gram_all.transpose(2, 0, 3, 1, 4).reshape(n_row * block, modes)
+        gram_panel = gram_all.transpose(3, 0, 4, 2, 1, 5).reshape(n_row * block, modes)
         half = modes // 2
         send_half = lax.dynamic_slice_in_dim(mode_shapes, (col % 2) * half, half, 1)
         panel_piece = lax.ppermute(send_half, ("prow", "pcol"), swap)

time: 190 us -> 192 us (1.011); the launches traced: 189 us -> 188 us
  Pallas kernels: 122 us -> 113 us
  local copies, waits for them, and re-layouts: 7.14 us -> 11.4 us
  starting transfers between devices: 8.19 us -> 10.8 us
    pallas_call x7 -> x9, Pallas kernels: 122 us -> 113 us  [__call__(): pl.pallas_call(kernel, out_shape=jax.ShapeDtypeStruct((count,) + tuple(bl...]
    reshape x1 -> x2, local copies, waits for them, and re-layouts: 1.01 us -> 4.31 us  [the longest x1 3.29 us: body(): gram_all.transpose(3, 0, 4, 2, 1, 5).reshape(n_row * block, modes)]
    ppermute x2, starting transfers between devices: 3.78 us -> 6.37 us  [beside_sibling(): other = lax.ppermute(part, 'prow', sibling)]
  transfers between devices with their start and end apart: 6 -> 6, of which waited for: 4 -> 4; matrix products, arithmetic and copies ran while one was open for 14% -> 17% of each run, Pallas kernels for 65% -> 60%
where the time goes in v9:
time: 192 us; the launch traced here: 188 us
  Pallas kernels  113 us (59%)
  matrix products  15.4 us (8%)
  between operations  13.6 us (7%)
  other arithmetic  13.5 us (7%)
  local copies, waits for them, and re-layouts  11.4 us (6%)
  starting transfers between devices  10.8 us (6%)
  waiting for transfers between devices  10.6 us (6%)
    pallas_call x9, Pallas kernels, __call__(): pl.pallas_call(kernel, out_shape=jax.ShapeDtypeStruct((count,) + tuple(bl...  113 us
    dot_general x4, matrix products, outer_rows(): lax.dot_general(left_rows, right_rows, (((1,), (1,)), ((), ())), preferre...  9.71 us
    ppermute x2, starting transfers between devices, beside_sibling(): other = lax.ppermute(part, 'prow', sibling)  6.37 us
    dot_general x1, matrix products, body(): jnp.dot(modal_at_loads, factor_cols, preferred_element_type=jnp.float32)  5.73 us
    ppermute x2, waiting for transfers between devices, beside_sibling(): other = lax.ppermute(part, 'prow', sibling)  4.23 us
    ppermute x1, waiting for transfers between devices, body(): panel_piece = lax.ppermute(send_half, ('prow', 'pcol'), swap)  4.04 us
  transfers between devices with their start and end apart: 6, of which 4 were waited for; matrix products, arithmetic and copies ran while one was open for 17% of the time, Pallas kernels for 60%

profile of v9, /device:TPU:39, one launch (start us, length us, event | category | flops | bytes accessed | tf_op | source)
XLA Modules:
  0.0 187.9 jit_solution(18075204344715110316)
XLA Ops:
  6.5 0.0 copy-start
  6.5 0.0 all-gather.2.cloned.1.call-start
  6.5 1.1 constant_dynamic-slice_fusion
  7.6 3.8 %collective-permute-start = (bf16[128,1024]{1,0:T(8,128)(2,1)S(1)}, bf16[128,1024]{1,0:T(8,128)(2,1)S(1)}, u32[]{:S(2)}, u32[]{:S(2)}) collective-permute-start(bf16[128,1024]{1,0:T(8,128)(2,1)S(1)} %constant_dynamic-slice_fusion), channel_id=1, source_target_pairs={{0,0},{64,16},{128,32},{192,48},{16,64},{80,80},{144,96},{208,112}... | collective-permute-start | bytes 786440 | tf_op jit(solution)/shard_map/ppermute | solution.py:177
  11.4 4.0 %collective-permute-done = bf16[128,1024]{1,0:T(8,128)(2,1)S(1)} collective-permute-done((bf16[128,1024]{1,0:T(8,128)(2,1)S(1)}, bf16[128,1024]{1,0:T(8,128)(2,1)S(1)}, u32[]{:S(2)}, u32[]{:S(2)}) %collective-permute-start) | collective-permute-done | bytes 262176 | tf_op jit(solution)/shard_map/ppermute | solution.py:177
  15.4 0.0 copy-start.2
  15.4 0.7 copy-done.2
  16.1 0.0 all-gather.2.cloned.1.call-update
  16.1 0.0 copy-done
  16.2 5.7 %fusion.13 = f32[2048,256]{1,0:T(8,128)S(1)} fusion(bf16[2048,2048]{1,0:T(8,128)(2,1)} %param.6, bf16[2048,256]{1,0:T(8,128)(2,1)S(1)} %copy-done), kind=kOutput, calls=%fused_computation.34 | convolution fusion | flops 2147483648 | bytes 11534336 | tf_op jit(solution)/shard_map/dot_general | solution.py:143
  21.9 0.9 dynamic-slice_convert_fusion
  22.8 0.0 collective-permute-start.1
  22.8 2.2 %collective-permute-done.1 = bf16[1024,256]{1,0:T(8,128)(2,1)} collective-permute-done((bf16[1024,256]{1,0:T(8,128)(2,1)}, bf16[1024,256]{1,0:T(8,128)(2,1)}, u32[]{:S(2)}, u32[]{:S(2)}) %collective-permute-start.1) | collective-permute-done | bytes 524320 | tf_op jit(solution)/shard_map/ppermute | solution.py:149
  25.0 2.0 %add_convert_fusion = bf16[1024,256]{1,0:T(8,128)(2,1)} fusion(bf16[1024,256]{1,0:T(8,128)(2,1)} %collective-permute-done.1, f32[2048,256]{1,0:T(8,128)S(1)} %fusion.13, s32[]{:T(128)S(6)} %select_n.54), kind=kLoop, calls=%fused_computation.14 | loop fusion | flops 786432 | bytes 2097156 | tf_op jit(solution)/shard_map/convert_element_type | solution.py:150
  27.0 0.0 copy-start.3
  27.0 0.0 copy-start.4
  27.0 24.3 %shard_map.55 = bf16[4,256,256]{2,1,0:T(8,128)(2,1)} custom-call(bf16[4,256,256]{2,1,0:T(8,128)(2,1)} %bitcast.23), custom_call_target="tpu_custom_call" | custom-call | tf_op jit(solution)/shard_map/pallas_call | solution.py:112
  51.3 1.8 reduce_sum.42.x_ref
  53.1 17.1 %shard_map.56 = bf16[2,256,256]{2,1,0:T(8,128)(2,1)} custom-call(bf16[256,256]{1,0:T(8,128)(2,1)} %reduce_sum.42.x_ref), custom_call_target="tpu_custom_call" | custom-call | tf_op jit(solution)/shard_map/pallas_call | solution.py:112
  70.2 1.7 reduce_sum.43.x_ref
  71.9 9.2 %shard_map.57 = bf16[4,256,256]{2,1,0:T(8,128)(2,1)} custom-call(bf16[256,256]{1,0:T(8,128)(2,1)} %reduce_sum.43.x_ref), custom_call_target="tpu_custom_call" | custom-call | tf_op jit(solution)/shard_map/pallas_call | solution.py:112
  81.1 1.6 collective-permute-start.2
  82.7 0.0 copy-done.3
  82.7 0.0 copy-done.4
  82.8 1.7 collective-permute-done.2
  84.5 1.1 broadcast_select_fusion.3
  85.6 1.9 %fusion = (bf16[2048,256]{1,0:T(8,128)(2,1)S(1)}, bf16[2048,256]{1,0:T(8,128)(2,1)S(1)}) fusion(f32[2048]{0:T(1024)S(1)} %get-tuple-element.15, bf16[1024,256]{1,0:T(8,128)(2,1)S(1)} %get-tuple-element.14, bf16[1024,256]{1,0:T(8,128)(2,1)S(1)} %get-tuple-element.13, f32[2048]{0:T(1024)S(1)} %get-tuple-element.16), kind=kLoop, calls=%fused_computation.7 | loop fusion | flops 4194304 | bytes 3162112 | tf_op jit(solution)/shard_map/convert_element_type | solution.py:159
  87.6 0.8 convolution_convert_fusion
  88.4 0.3 copy.7
  88.6 1.0 copy.8
  89.7 16.0 %shard_map.58 = bf16[4,4,128,128]{3,2,1,0:T(8,128)(2,1)} custom-call(bf16[4,4,128,128]{3,2,1,0:T(8,128)(2,1)} %bitcast.26), custom_call_target="tpu_custom_call" | custom-call | tf_op jit(solution)/shard_map/pallas_call | solution.py:112
  105.7 1.8 convert_reduce_fusion.x_ref
  107.5 9.5 %shard_map.59 = f32[4,128,128]{2,1,0:T(8,128)} custom-call(f32[4,128,128]{2,1,0:T(8,128)} %convert_reduce_fusion.x_ref), custom_call_target="tpu_custom_call" | custom-call | tf_op jit(solution)/shard_map/pallas_call | solution.py:112
  117.0 1.6 reduce_sum.45.x_ref
  118.6 7.0 %shard_map.60.x_ref = bf16[2,128,128]{2,1,0:T(8,128)(2,1)} custom-call(bf16[128,128]{1,0:T(8,128)(2,1)} %reduce_sum.45.x_ref), custom_call_target="tpu_custom_call" | custom-call | tf_op jit(solution)/shard_map/pallas_call | solution.py:112
  125.7 5.8 %shard_map.61.x_ref = bf16[4,2,128,128]{3,2,1,0:T(8,128)(2,1)} custom-call(bf16[2,128,128]{2,1,0:T(8,128)(2,1)} %shard_map.60.x_ref), custom_call_target="tpu_custom_call" | custom-call | tf_op jit(solution)/shard_map/pallas_call | solution.py:112
  131.5 11.9 %shard_map.62 = bf16[4,4,2,128,128]{4,3,2,1,0:T(8,128)(2,1)} custom-call(bf16[4,2,128,128]{3,2,1,0:T(8,128)(2,1)} %shard_map.61.x_ref), custom_call_target="tpu_custom_call" | custom-call | tf_op jit(solution)/shard_map/pallas_call | solution.py:112
  143.4 4.8 %collective-permute-start.3 = (bf16[1,4,4,2,128,128]{5,4,3,2,1,0:T(8,128)(2,1)}, bf16[1,4,4,2,128,128]{5,4,3,2,1,0:T(8,128)(2,1)S(1)}, u32[]{:S(2)}, u32[]{:S(2)}) collective-permute-start(bf16[1,4,4,2,128,128]{5,4,3,2,1,0:T(8,128)(2,1)} %bitcast.21), channel_id=1, source_target_pairs={{0,64},{64,0},{128,192},{192,128},{1,65},{65,1},{129,193},{193,129... | collective-permute-start | bytes 3145736 | tf_op jit(solution)/shard_map/ppermute | solution.py:133
  148.1 2.5 %collective-permute-done.3 = bf16[1,4,4,2,128,128]{5,4,3,2,1,0:T(8,128)(2,1)S(1)} collective-permute-done((bf16[1,4,4,2,128,128]{5,4,3,2,1,0:T(8,128)(2,1)}, bf16[1,4,4,2,128,128]{5,4,3,2,1,0:T(8,128)(2,1)S(1)}, u32[]{:S(2)}, u32[]{:S(2)}) %collective-permute-start.3) | collective-permute-done | bytes 1048608 | tf_op jit(solution)/shard_map/ppermute | solution.py:133
  150.6 1.4 broadcast_select_fusion.1
  152.0 0.2 maximum_bitcast_fusion
  152.2 2.9 %copy.9 = bf16[2,2,128,4,4,128]{5,4,3,2,1,0:T(4,128)(2,1)} copy(bf16[2,2,128,4,4,128]{5,2,0,3,4,1:T(8,128)(2,1)S(1)} %maximum_bitcast_fusion) | data formatting | bytes 4194304 | tf_op jit(solution)/shard_map/transpose | solution.py:174
  155.1 3.3 %reshape.20 = bf16[512,2048]{1,0:T(8,128)(2,1)S(1)} reshape(bf16[2,2,128,4,4,128]{5,4,3,2,1,0:T(4,128)(2,1)} %copy.9) | data formatting | bytes 4194304 | tf_op jit(solution)/shard_map/reshape | solution.py:174
  158.4 0.0 all-gather.2.cloned.1.call-done
  158.5 0.6 collective-permute-start.4
  159.1 2.5 %fusion.2.x_ref = bf16[128,512]{1,0:T(8,128)(2,1)} fusion(bf16[512,2048]{1,0:T(8,128)(2,1)S(1)} %reshape.20, bf16[128,2048]{1,0:T(8,128)(2,1)} %param.7), kind=kOutput, calls=%fused_computation.11 | convolution fusion | flops 268500992 | bytes 2752512 | tf_op jit(solution)/shard_map/dot_general | solution.py:22
  161.6 11.7 %shard_map.63 = bf16[4,128,512]{2,1,0:T(8,128)(2,1)} custom-call(bf16[128,512]{1,0:T(8,128)(2,1)} %fusion.2.x_ref), custom_call_target="tpu_custom_call" | custom-call | tf_op jit(solution)/shard_map/pallas_call | solution.py:112
  173.3 1.3 copy.11
  174.7 0.0 collective-permute-done.4
  174.7 0.0 copy-start.1
  174.7 3.9 %fusion.3 = f32[128,2048]{1,0:T(8,128)S(1)} fusion(bf16[2048,1024]{1,0:T(8,128)(2,1)} %collective-permute-done.4, bf16[128,2048]{0,1:T(8,128)(2,1)S(1)} %bitcast.27, s32[]{:T(128)S(6)} %select_n.55), kind=kOutput, calls=%fused_computation.20 | convolution fusion | flops 536870912 | bytes 5505028 | tf_op jit(solution)/shard_map/dot_general | solution.py:22
  178.5 0.0 copy-done.1
  178.6 2.5 %convolution_add_fusion = f32[128,2048]{1,0:T(8,128)} fusion(f32[128,2048]{1,0:T(8,128)S(1)} %fusion.3, bf16[2048,1024]{1,0:T(8,128)(2,1)S(1)} %copy-done.1, bf16[128,2048]{0,1:T(8,128)(2,1)S(1)} %bitcast.28, s32[]{:T(128)S(6)} %select_n.54), kind=kOutput, calls=%fused_computation.2 | convolution fusion | flops 537133056 | bytes 6553604 | tf_op jit(solution)/shard_map/dot_general | solution.py:22
  (1 shorter events, 0.0 us)
Async XLA Ops:
  6.5 9.6 %copy-start = (bf16[2048,256]{1,0:T(8,128)(2,1)S(1)}, bf16[2048,256]{1,0:T(8,128)(2,1)}, u32[]{:S(2)}) copy-start(bf16[2048,256]{1,0:T(8,128)(2,1)} %param.5) | copy-start | bytes 3145732
  6.5 151.9 %all-gather.2.cloned.1.call-start = ((), (), s32[]{:S(2)}) async-start(), calls=%async_computation | async-start | bytes 4456448 | tf_op jit(solution)/shard_map/all_gather | solution.py:178
  7.6 7.8 %collective-permute-start = (bf16[128,1024]{1,0:T(8,128)(2,1)S(1)}, bf16[128,1024]{1,0:T(8,128)(2,1)S(1)}, u32[]{:S(2)}, u32[]{:S(2)}) collective-permute-start(bf16[128,1024]{1,0:T(8,128)(2,1)S(1)} %constant_dynamic-slice_fusion), channel_id=1, source_target_pairs={{0,0},{64,16},{128,32},{192,48},{16,64},{80,80},{144,96},{208,112}... | collective-permute-start | bytes 786440 | tf_op jit(solution)/shard_map/ppermute | solution.py:177
  15.4 0.7 copy-start.2
  22.8 2.3 %collective-permute-start.1 = (bf16[1024,256]{1,0:T(8,128)(2,1)}, bf16[1024,256]{1,0:T(8,128)(2,1)}, u32[]{:S(2)}, u32[]{:S(2)}) collective-permute-start(bf16[1024,256]{1,0:T(8,128)(2,1)} %dynamic-slice_convert_fusion), channel_id=1, source_target_pairs={{0,64},{64,0},{128,192},{192,128},{1,65},{65,1},{129,193},{193,129... | collective-permute-start | bytes 1572872 | tf_op jit(solution)/shard_map/ppermute | solution.py:149
  27.0 55.8 %copy-start.3 = (f32[2048]{0:T(1024)S(1)}, f32[2048]{0:T(1024)}, u32[]{:S(2)}) copy-start(f32[2048]{0:T(1024)} %param.8) | copy-start | bytes 24580
  27.0 55.8 %copy-start.4 = (f32[2048]{0:T(1024)S(1)}, f32[2048]{0:T(1024)}, u32[]{:S(2)}) copy-start(f32[2048]{0:T(1024)} %param.9) | copy-start | bytes 24580
  81.1 3.3 %collective-permute-start.2 = (bf16[1024,256]{1,0:T(8,128)(2,1)}, bf16[1024,256]{1,0:T(8,128)(2,1)S(1)}, u32[]{:S(2)}, u32[]{:S(2)}) collective-permute-start(bf16[1024,256]{1,0:T(8,128)(2,1)} %bitcast.22), channel_id=1, source_target_pairs={{0,64},{64,0},{128,192},{192,128},{1,65},{65,1},{129,193},{193,129... | collective-permute-start | bytes 1572872 | tf_op jit(solution)/shard_map/ppermute | solution.py:133
  143.4 7.3 %collective-permute-start.3 = (bf16[1,4,4,2,128,128]{5,4,3,2,1,0:T(8,128)(2,1)}, bf16[1,4,4,2,128,128]{5,4,3,2,1,0:T(8,128)(2,1)S(1)}, u32[]{:S(2)}, u32[]{:S(2)}) collective-permute-start(bf16[1,4,4,2,128,128]{5,4,3,2,1,0:T(8,128)(2,1)} %bitcast.21), channel_id=1, source_target_pairs={{0,64},{64,0},{128,192},{192,128},{1,65},{65,1},{129,193},{193,129... | collective-permute-start | bytes 3145736 | tf_op jit(solution)/shard_map/ppermute | solution.py:133
  158.5 16.2 %collective-permute-start.4 = (bf16[2048,1024]{1,0:T(8,128)(2,1)}, bf16[2048,1024]{1,0:T(8,128)(2,1)}, u32[]{:S(2)}, u32[]{:S(2)}) collective-permute-start(bf16[2048,1024]{1,0:T(8,128)(2,1)} %all-gather.2.cloned.1.call-done), channel_id=1, source_target_pairs={{0,64},{64,0},{128,192},{192,128},{1,65},{65,1},{129,193},{193,129... | collective-permute-start | bytes 12582920 | tf_op jit(solution)/shard_map/ppermute | solution.py:180
  174.7 3.9 %copy-start.1 = (bf16[2048,1024]{1,0:T(8,128)(2,1)S(1)}, bf16[2048,1024]{1,0:T(8,128)(2,1)}, u32[]{:S(2)}) copy-start(bf16[2048,1024]{1,0:T(8,128)(2,1)} %all-gather.2.cloned.1.call-done) | copy-start | bytes 12582916
Sparse Core Ops, SparseCore 0:
  16.2 91.4 all-gather.1

commit v10 on v8

--- a/solution.py
+++ b/solution.py
@@ -92,6 +92,91 @@
         copy(offset).wait_send()
     for offset in range(1, count):
         landing(offset).wait_recv()
+
+
+def modal_sum_kernel(x_ref, out_ref, got, coll, part_out, part_in, send_a, recv_a, send_b, recv_b,
+                     send_c, recv_c, *, axes, factors):
+    coords = {a: lax.axis_index(a) for a in axes}
+
+    def value(f):
+        axis, size, stride = factors[f]
+        return lax.rem(coords[axis] // stride, size)
+
+    def device(f, v):
+        place = dict(coords)
+        axis, size, stride = factors[f]
+        place[axis] = place[axis] + (v - value(f)) * stride
+        return tuple(place[a] for a in axes)
+
+    n = factors["pcol"][1]
+    me, half = value("pcol"), value("zh")
+    partner = device("zh", 1 - half)
+    peer = lambda k: lax.rem(me + k, n)
+    sender = lambda k: lax.rem(me + n - k, n)
+
+    def step(src, dst_at, k, to, sems):
+        return pltpu.make_async_remote_copy(
+            src_ref=src, dst_ref=dst_at, send_sem=sems[0].at[k], recv_sem=sems[1].at[k],
+            device_id=to, device_id_type=MESH,
+        )
+
+    barrier = pltpu.get_barrier_semaphore()
+    for k in range(1, n):
+        pl.semaphore_signal(barrier, inc=1, device_id=device("pcol", peer(k)), device_id_type=MESH)
+    pl.semaphore_signal(barrier, inc=1, device_id=partner, device_id_type=MESH)
+    pl.semaphore_wait(barrier, n)
+
+    for k in range(1, n):
+        step(x_ref.at[peer(k)], got.at[me], k, device("pcol", peer(k)), (send_a, recv_a)).start()
+    for k in range(1, n):
+        step(x_ref.at[peer(k)], got.at[me], k, device("pcol", peer(k)), (send_a, recv_a)).wait_send()
+    for k in range(1, n):
+        step(x_ref.at[me], got.at[sender(k)], k, device("pcol", sender(k)), (send_a, recv_a)).wait_recv()
+    total = x_ref[me].astype(jnp.float32)
+    for k in range(1, n):
+        total = total + got[sender(k)].astype(jnp.float32)
+    part_out[...] = total.astype(part_out.dtype)
+
+    across = pltpu.make_async_remote_copy(
+        src_ref=part_out, dst_ref=part_in, send_sem=send_b, recv_sem=recv_b,
+        device_id=partner, device_id_type=MESH,
+    )
+    across.start()
+    across.wait_send()
+    across.wait_recv()
+    coll[me] = (part_out[...].astype(jnp.float32) + part_in[...].astype(jnp.float32)).astype(coll.dtype)
+
+    for k in range(1, n):
+        step(coll.at[me], coll.at[me], k, device("pcol", peer(k)), (send_c, recv_c)).start()
+    for k in range(1, n):
+        step(coll.at[me], coll.at[me], k, device("pcol", peer(k)), (send_c, recv_c)).wait_send()
+    for k in range(1, n):
+        step(coll.at[me], coll.at[sender(k)], k, device("pcol", sender(k)), (send_c, recv_c)).wait_recv()
+    out_ref[...] = coll[...]
+
+
+def modal_sum(x, axes, sizes):
+    n, rows, width = x.shape
+    kernel = functools.partial(modal_sum_kernel, axes=axes, factors=factor_table(sizes))
+    return pl.pallas_call(
+        kernel,
+        out_shape=jax.ShapeDtypeStruct(x.shape, x.dtype),
+        in_specs=[pl.BlockSpec(memory_space=pltpu.VMEM)],
+        out_specs=pl.BlockSpec(memory_space=pltpu.VMEM),
+        scratch_shapes=[
+            pltpu.VMEM(x.shape, x.dtype),
+            pltpu.VMEM(x.shape, x.dtype),
+            pltpu.VMEM((rows, width), x.dtype),
+            pltpu.VMEM((rows, width), x.dtype),
+            pltpu.SemaphoreType.DMA((n,)),
+            pltpu.SemaphoreType.DMA((n,)),
+            pltpu.SemaphoreType.DMA(()),
+            pltpu.SemaphoreType.DMA(()),
+            pltpu.SemaphoreType.DMA((n,)),
+            pltpu.SemaphoreType.DMA((n,)),
+        ],
+        compiler_params=pltpu.CompilerParams(collective_id=0, has_side_effects=True),
+    )(x)
 
 
 class Exchanger:
@@ -145,11 +230,8 @@
         theirs = lax.dynamic_slice_in_dim(partial_load, (1 - core) * (modes // 2), modes // 2, 0)
         wide = lambda part: part.astype(jnp.float32)
         sums = mine + wide(lax.ppermute(theirs.astype(jnp.bfloat16), "prow", sibling))
-        pieces = ex(sums.astype(jnp.bfloat16).reshape(n_col, -1, width), ("pcol",), same=False)
-        sums = jnp.sum(wide(pieces), axis=0)
-        pieces = ex(sums.astype(jnp.bfloat16), ("zh",), same=True)
-        gathered = jnp.sum(wide(pieces), axis=0).astype(jnp.bfloat16)
-        gathered = ex(gathered, ("pcol",), same=True).reshape(-1, width)
+        pieces = sums.astype(jnp.bfloat16).reshape(n_col, -1, width)
+        gathered = modal_sum(pieces, axes, sizes).reshape(-1, width)
         modal_load = beside_sibling(gathered, core)
         modal_wide = modal_load.astype(jnp.float32)
         pseudo = jnp.concatenate(

time: 190 us -> 186 us (0.979)
  other arithmetic: 11.8 us -> 8.32 us
  Pallas kernels: 122 us -> 124 us
    pallas_call x0 -> x1, Pallas kernels: none -> 47.3 us  [modal_sum(): pl.pallas_call(kernel, out_shape=jax.ShapeDtypeStruct(x.shape, x.dtype),...]
    pallas_call x7 -> x4, Pallas kernels: 122 us -> 76.4 us  [__call__(): pl.pallas_call(kernel, out_shape=jax.ShapeDtypeStruct((count,) + tuple(bl...]
    reduce_sum x2 -> x0, other arithmetic: 3.5 us -> none  [the longest x1 1.81 us: body(): sums = jnp.sum(wide(pieces), axis=0)]
  transfers between devices with their start and end apart: 6 -> 6, of which waited for: 4 -> 4; matrix products, arithmetic and copies ran while one was open for 14% -> 12% of each run, Pallas kernels for 65% -> 67%
where the time goes in v10:
time: 186 us; the launch traced here: 185 us
  Pallas kernels  124 us (67%)
  matrix products  15.4 us (8%)
  between operations  13.6 us (7%)
  waiting for transfers between devices  10.6 us (6%)
  other arithmetic  8.32 us (4%)
  local copies, waits for them, and re-layouts  7.15 us (4%)
  starting transfers between devices  6.51 us (4%)
    pallas_call x4, Pallas kernels, __call__(): pl.pallas_call(kernel, out_shape=jax.ShapeDtypeStruct((count,) + tuple(bl...  76.4 us
    pallas_call x1, Pallas kernels, modal_sum(): pl.pallas_call(kernel, out_shape=jax.ShapeDtypeStruct(x.shape, x.dtype),...  47.3 us
    dot_general x4, matrix products, outer_rows(): lax.dot_general(left_rows, right_rows, (((1,), (1,)), ((), ())), preferre...  9.71 us
    dot_general x1, matrix products, body(): jnp.dot(modal_at_loads, factor_cols, preferred_element_type=jnp.float32)  5.73 us
    ppermute x2, waiting for transfers between devices, beside_sibling(): other = lax.ppermute(part, 'prow', sibling)  4.23 us
    ppermute x1, waiting for transfers between devices, body(): panel_piece = lax.ppermute(send_half, ('prow', 'pcol'), swap)  4.04 us
    ppermute x1, starting transfers between devices, body(): panel_piece = lax.ppermute(send_half, ('prow', 'pcol'), swap)  3.77 us
  transfers between devices with their start and end apart: 6, of which 4 were waited for; matrix products, arithmetic and copies ran while one was open for 12% of the time, Pallas kernels for 67%

profile of v10, /device:TPU:39, one launch (start us, length us, event | category | flops | bytes accessed | tf_op | source)
XLA Modules:
  0.0 185.2 jit_solution(8519109950019925669)
XLA Ops:
  6.5 0.0 copy-start
  6.5 0.0 all-gather.2.cloned.1.call-start
  6.5 1.1 constant_dynamic-slice_fusion
  7.6 3.8 %collective-permute-start = (bf16[128,1024]{1,0:T(8,128)(2,1)S(1)}, bf16[128,1024]{1,0:T(8,128)(2,1)S(1)}, u32[]{:S(2)}, u32[]{:S(2)}) collective-permute-start(bf16[128,1024]{1,0:T(8,128)(2,1)S(1)} %constant_dynamic-slice_fusion), channel_id=1, source_target_pairs={{0,0},{64,16},{128,32},{192,48},{16,64},{80,80},{144,96},{208,112}... | collective-permute-start | bytes 786440 | tf_op jit(solution)/shard_map/ppermute | solution.py:256
  11.4 4.0 %collective-permute-done = bf16[128,1024]{1,0:T(8,128)(2,1)S(1)} collective-permute-done((bf16[128,1024]{1,0:T(8,128)(2,1)S(1)}, bf16[128,1024]{1,0:T(8,128)(2,1)S(1)}, u32[]{:S(2)}, u32[]{:S(2)}) %collective-permute-start) | collective-permute-done | bytes 262176 | tf_op jit(solution)/shard_map/ppermute | solution.py:256
  15.4 0.0 copy-start.2
  15.4 0.7 copy-done.2
  16.1 0.0 all-gather.2.cloned.1.call-update
  16.2 0.0 copy-done
  16.2 5.7 %fusion.13 = f32[2048,256]{1,0:T(8,128)S(1)} fusion(bf16[2048,2048]{1,0:T(8,128)(2,1)} %param.6, bf16[2048,256]{1,0:T(8,128)(2,1)S(1)} %copy-done), kind=kOutput, calls=%fused_computation.34 | convolution fusion | flops 2147483648 | bytes 11534336 | tf_op jit(solution)/shard_map/dot_general | solution.py:226
  21.9 0.0 copy-start.3
  21.9 0.0 copy-start.4
  22.0 0.9 dynamic-slice_convert_fusion
  22.8 0.0 collective-permute-start.1
  22.8 2.2 %collective-permute-done.1 = bf16[1024,256]{1,0:T(8,128)(2,1)} collective-permute-done((bf16[1024,256]{1,0:T(8,128)(2,1)}, bf16[1024,256]{1,0:T(8,128)(2,1)}, u32[]{:S(2)}, u32[]{:S(2)}) %collective-permute-start.1) | collective-permute-done | bytes 524320 | tf_op jit(solution)/shard_map/ppermute | solution.py:232
  25.1 2.0 %add_convert_fusion = bf16[1024,256]{1,0:T(8,128)(2,1)} fusion(bf16[1024,256]{1,0:T(8,128)(2,1)} %collective-permute-done.1, f32[2048,256]{1,0:T(8,128)S(1)} %fusion.13, s32[]{:T(128)S(6)} %select_n.54), kind=kLoop, calls=%fused_computation.14 | loop fusion | flops 786432 | bytes 2097156 | tf_op jit(solution)/shard_map/convert_element_type | solution.py:233
  27.0 47.3 %shard_map.55 = bf16[4,256,256]{2,1,0:T(8,128)(2,1)} custom-call(bf16[4,256,256]{2,1,0:T(8,128)(2,1)} %bitcast.30), custom_call_target="tpu_custom_call" | custom-call | tf_op jit(solution)/shard_map/pallas_call | solution.py:161
  74.3 1.2 collective-permute-start.2
  75.5 0.0 copy-done.3
  75.5 0.0 copy-done.4
  75.5 1.7 collective-permute-done.2
  77.3 1.1 broadcast_select_fusion.3
  78.4 1.9 %fusion = (bf16[2048,256]{1,0:T(8,128)(2,1)S(1)}, bf16[2048,256]{1,0:T(8,128)(2,1)S(1)}) fusion(f32[2048]{0:T(1024)S(1)} %get-tuple-element.15, bf16[1024,256]{1,0:T(8,128)(2,1)S(1)} %get-tuple-element.14, bf16[1024,256]{1,0:T(8,128)(2,1)S(1)} %get-tuple-element.13, f32[2048]{0:T(1024)S(1)} %get-tuple-element.16), kind=kLoop, calls=%fused_computation.7 | loop fusion | flops 4194304 | bytes 3162112 | tf_op jit(solution)/shard_map/convert_element_type | solution.py:239
  80.3 0.8 convolution_convert_fusion
  81.2 0.3 copy.7
  81.4 1.0 copy.8
  82.5 28.8 %shard_map.56 = bf16[16,128,128]{2,1,0:T(8,128)(2,1)} custom-call(bf16[16,128,128]{2,1,0:T(8,128)(2,1)} %bitcast.33), custom_call_target="tpu_custom_call" | custom-call | tf_op jit(solution)/shard_map/pallas_call | solution.py:195
  111.3 1.7 reduce_sum.12.x_ref
  113.1 7.4 %shard_map.57.x_ref = bf16[2,128,128]{2,1,0:T(8,128)(2,1)} custom-call(bf16[128,128]{1,0:T(8,128)(2,1)} %reduce_sum.12.x_ref), custom_call_target="tpu_custom_call" | custom-call | tf_op jit(solution)/shard_map/pallas_call | solution.py:195
  120.4 30.4 %shard_map.58 = bf16[16,2,128,128]{3,2,1,0:T(8,128)(2,1)} custom-call(bf16[2,128,128]{2,1,0:T(8,128)(2,1)} %shard_map.57.x_ref), custom_call_target="tpu_custom_call" | custom-call | tf_op jit(solution)/shard_map/pallas_call | solution.py:195
  150.9 0.9 collective-permute-start.3
  151.8 2.5 %collective-permute-done.3 = bf16[1,16,2,128,128]{4,3,2,1,0:T(8,128)(2,1)S(1)} collective-permute-done((bf16[1,16,2,128,128]{4,3,2,1,0:T(8,128)(2,1)}, bf16[1,16,2,128,128]{4,3,2,1,0:T(8,128)(2,1)S(1)}, u32[]{:S(2)}, u32[]{:S(2)}) %collective-permute-start.3) | collective-permute-done | bytes 1048608 | tf_op jit(solution)/shard_map/ppermute | solution.py:216
  154.3 1.4 broadcast_select_fusion.1
  155.6 0.2 maximum_bitcast_fusion
  155.8 1.4 copy.9
  157.2 0.5 copy.15
  157.7 0.0 all-gather.2.cloned.1.call-done
  157.8 0.6 collective-permute-start.4
  158.4 2.5 %fusion.2.x_ref = bf16[128,512]{1,0:T(8,128)(2,1)} fusion(bf16[512,2048]{1,0:T(8,128)(2,1)S(1)} %bitcast.26, bf16[128,2048]{1,0:T(8,128)(2,1)} %param.7), kind=kOutput, calls=%fused_computation.12 | convolution fusion | flops 268500992 | bytes 2752512 | tf_op jit(solution)/shard_map/dot_general | solution.py:22
  160.9 9.7 %shard_map.59 = bf16[4,128,512]{2,1,0:T(8,128)(2,1)} custom-call(bf16[128,512]{1,0:T(8,128)(2,1)} %fusion.2.x_ref), custom_call_target="tpu_custom_call" | custom-call | tf_op jit(solution)/shard_map/pallas_call | solution.py:195
  170.7 1.3 copy.11
  172.0 0.0 collective-permute-done.4
  172.0 0.0 copy-start.1
  172.0 3.9 %fusion.3 = f32[128,2048]{1,0:T(8,128)S(1)} fusion(bf16[2048,1024]{1,0:T(8,128)(2,1)} %collective-permute-done.4, bf16[128,2048]{0,1:T(8,128)(2,1)S(1)} %bitcast.34, s32[]{:T(128)S(6)} %select_n.55), kind=kOutput, calls=%fused_computation.20 | convolution fusion | flops 536870912 | bytes 5505028 | tf_op jit(solution)/shard_map/dot_general | solution.py:22
  175.9 0.0 copy-done.1
  175.9 2.5 %convolution_add_fusion = f32[128,2048]{1,0:T(8,128)} fusion(f32[128,2048]{1,0:T(8,128)S(1)} %fusion.3, bf16[2048,1024]{1,0:T(8,128)(2,1)S(1)} %copy-done.1, bf16[128,2048]{0,1:T(8,128)(2,1)S(1)} %bitcast.35, s32[]{:T(128)S(6)} %select_n.54), kind=kOutput, calls=%fused_computation.2 | convolution fusion | flops 537133056 | bytes 6553604 | tf_op jit(solution)/shard_map/dot_general | solution.py:22
  (1 shorter events, 0.0 us)
Async XLA Ops:
  6.5 9.6 %copy-start = (bf16[2048,256]{1,0:T(8,128)(2,1)S(1)}, bf16[2048,256]{1,0:T(8,128)(2,1)}, u32[]{:S(2)}) copy-start(bf16[2048,256]{1,0:T(8,128)(2,1)} %param.5) | copy-start | bytes 3145732
  6.5 151.2 %all-gather.2.cloned.1.call-start = ((), (), s32[]{:S(2)}) async-start(), calls=%async_computation | async-start | bytes 4456448 | tf_op jit(solution)/shard_map/all_gather | solution.py:257
  7.6 7.8 %collective-permute-start = (bf16[128,1024]{1,0:T(8,128)(2,1)S(1)}, bf16[128,1024]{1,0:T(8,128)(2,1)S(1)}, u32[]{:S(2)}, u32[]{:S(2)}) collective-permute-start(bf16[128,1024]{1,0:T(8,128)(2,1)S(1)} %constant_dynamic-slice_fusion), channel_id=1, source_target_pairs={{0,0},{64,16},{128,32},{192,48},{16,64},{80,80},{144,96},{208,112}... | collective-permute-start | bytes 786440 | tf_op jit(solution)/shard_map/ppermute | solution.py:256
  15.4 0.7 copy-start.2
  21.9 53.6 %copy-start.3 = (f32[2048]{0:T(1024)S(1)}, f32[2048]{0:T(1024)}, u32[]{:S(2)}) copy-start(f32[2048]{0:T(1024)} %param.8) | copy-start | bytes 24580
  21.9 53.6 %copy-start.4 = (f32[2048]{0:T(1024)S(1)}, f32[2048]{0:T(1024)}, u32[]{:S(2)}) copy-start(f32[2048]{0:T(1024)} %param.9) | copy-start | bytes 24580
  22.8 2.3 %collective-permute-start.1 = (bf16[1024,256]{1,0:T(8,128)(2,1)}, bf16[1024,256]{1,0:T(8,128)(2,1)}, u32[]{:S(2)}, u32[]{:S(2)}) collective-permute-start(bf16[1024,256]{1,0:T(8,128)(2,1)} %dynamic-slice_convert_fusion), channel_id=1, source_target_pairs={{0,64},{64,0},{128,192},{192,128},{1,65},{65,1},{129,193},{193,129... | collective-permute-start | bytes 1572872 | tf_op jit(solution)/shard_map/ppermute | solution.py:232
  74.3 3.0 %collective-permute-start.2 = (bf16[1024,256]{1,0:T(8,128)(2,1)}, bf16[1024,256]{1,0:T(8,128)(2,1)S(1)}, u32[]{:S(2)}, u32[]{:S(2)}) collective-permute-start(bf16[1024,256]{1,0:T(8,128)(2,1)} %bitcast.29), channel_id=1, source_target_pairs={{0,64},{64,0},{128,192},{192,128},{1,65},{65,1},{129,193},{193,129... | collective-permute-start | bytes 1572872 | tf_op jit(solution)/shard_map/ppermute | solution.py:216
  150.9 3.4 %collective-permute-start.3 = (bf16[1,16,2,128,128]{4,3,2,1,0:T(8,128)(2,1)}, bf16[1,16,2,128,128]{4,3,2,1,0:T(8,128)(2,1)S(1)}, u32[]{:S(2)}, u32[]{:S(2)}) collective-permute-start(bf16[1,16,2,128,128]{4,3,2,1,0:T(8,128)(2,1)} %bitcast.28), channel_id=1, source_target_pairs={{0,64},{64,0},{128,192},{192,128},{1,65},{65,1},{129,193},{193,129... | collective-permute-start | bytes 3145736 | tf_op jit(solution)/shard_map/ppermute | solution.py:216
  157.8 14.2 %collective-permute-start.4 = (bf16[2048,1024]{1,0:T(8,128)(2,1)}, bf16[2048,1024]{1,0:T(8,128)(2,1)}, u32[]{:S(2)}, u32[]{:S(2)}) collective-permute-start(bf16[2048,1024]{1,0:T(8,128)(2,1)} %all-gather.2.cloned.1.call-done), channel_id=1, source_target_pairs={{0,64},{64,0},{128,192},{192,128},{1,65},{65,1},{129,193},{193,129... | collective-permute-start | bytes 12582920 | tf_op jit(solution)/shard_map/ppermute | solution.py:259
  172.0 3.9 %copy-start.1 = (bf16[2048,1024]{1,0:T(8,128)(2,1)S(1)}, bf16[2048,1024]{1,0:T(8,128)(2,1)}, u32[]{:S(2)}) copy-start(bf16[2048,1024]{1,0:T(8,128)(2,1)} %all-gather.2.cloned.1.call-done) | copy-start | bytes 12582916
Sparse Core Ops, SparseCore 0:
  16.3 94.4 all-gather.1

commit v11 on v10

--- a/solution.py
+++ b/solution.py
@@ -94,8 +94,8 @@
         landing(offset).wait_recv()
 
 
-def modal_sum_kernel(x_ref, out_ref, got, coll, part_out, part_in, send_a, recv_a, send_b, recv_b,
-                     send_c, recv_c, *, axes, factors):
+def fused_sum_kernel(x_ref, out_ref, got, coll, part_out, part_in, send_a, recv_a, send_b, recv_b,
+                     send_c, recv_c, *, axes, factors, over, add_across):
     coords = {a: lax.axis_index(a) for a in axes}
 
     def value(f):
@@ -108,8 +108,8 @@
         place[axis] = place[axis] + (v - value(f)) * stride
         return tuple(place[a] for a in axes)
 
-    n = factors["pcol"][1]
-    me, half = value("pcol"), value("zh")
+    n = factors[over][1]
+    me, half = value(over), value("zh")
     partner = device("zh", 1 - half)
     peer = lambda k: lax.rem(me + k, n)
     sender = lambda k: lax.rem(me + n - k, n)
@@ -122,16 +122,16 @@
 
     barrier = pltpu.get_barrier_semaphore()
     for k in range(1, n):
-        pl.semaphore_signal(barrier, inc=1, device_id=device("pcol", peer(k)), device_id_type=MESH)
+        pl.semaphore_signal(barrier, inc=1, device_id=device(over, peer(k)), device_id_type=MESH)
     pl.semaphore_signal(barrier, inc=1, device_id=partner, device_id_type=MESH)
     pl.semaphore_wait(barrier, n)
 
     for k in range(1, n):
-        step(x_ref.at[peer(k)], got.at[me], k, device("pcol", peer(k)), (send_a, recv_a)).start()
-    for k in range(1, n):
-        step(x_ref.at[peer(k)], got.at[me], k, device("pcol", peer(k)), (send_a, recv_a)).wait_send()
-    for k in range(1, n):
-        step(x_ref.at[me], got.at[sender(k)], k, device("pcol", sender(k)), (send_a, recv_a)).wait_recv()
+        step(x_ref.at[peer(k)], got.at[me], k, device(over, peer(k)), (send_a, recv_a)).start()
+    for k in range(1, n):
+        step(x_ref.at[peer(k)], got.at[me], k, device(over, peer(k)), (send_a, recv_a)).wait_send()
+    for k in range(1, n):
+        step(x_ref.at[me], got.at[sender(k)], k, device(over, sender(k)), (send_a, recv_a)).wait_recv()
     total = x_ref[me].astype(jnp.float32)
     for k in range(1, n):
         total = total + got[sender(k)].astype(jnp.float32)
@@ -144,28 +144,38 @@
     across.start()
     across.wait_send()
     across.wait_recv()
-    coll[me] = (part_out[...].astype(jnp.float32) + part_in[...].astype(jnp.float32)).astype(coll.dtype)
-
-    for k in range(1, n):
-        step(coll.at[me], coll.at[me], k, device("pcol", peer(k)), (send_c, recv_c)).start()
-    for k in range(1, n):
-        step(coll.at[me], coll.at[me], k, device("pcol", peer(k)), (send_c, recv_c)).wait_send()
-    for k in range(1, n):
-        step(coll.at[me], coll.at[sender(k)], k, device("pcol", sender(k)), (send_c, recv_c)).wait_recv()
+    if add_across:
+        mine, theirs = part_out[...].astype(jnp.float32), part_in[...].astype(jnp.float32)
+        coll[me] = (mine + theirs).astype(coll.dtype)
+    else:
+        mine, theirs = part_out[...], part_in[...]
+        first = jnp.where(half == 0, mine, theirs)
+        second = jnp.where(half == 0, theirs, mine)
+        coll[me] = jnp.stack([first, second])
+
+    for k in range(1, n):
+        step(coll.at[me], coll.at[me], k, device(over, peer(k)), (send_c, recv_c)).start()
+    for k in range(1, n):
+        step(coll.at[me], coll.at[me], k, device(over, peer(k)), (send_c, recv_c)).wait_send()
+    for k in range(1, n):
+        step(coll.at[me], coll.at[sender(k)], k, device(over, sender(k)), (send_c, recv_c)).wait_recv()
     out_ref[...] = coll[...]
 
 
-def modal_sum(x, axes, sizes):
+def fused_sum(x, axes, sizes, over, add_across, kernel_id):
     n, rows, width = x.shape
-    kernel = functools.partial(modal_sum_kernel, axes=axes, factors=factor_table(sizes))
+    block = (rows, width) if add_across else (2, rows, width)
+    kernel = functools.partial(
+        fused_sum_kernel, axes=axes, factors=factor_table(sizes), over=over, add_across=add_across
+    )
     return pl.pallas_call(
         kernel,
-        out_shape=jax.ShapeDtypeStruct(x.shape, x.dtype),
+        out_shape=jax.ShapeDtypeStruct((n,) + block, x.dtype),
         in_specs=[pl.BlockSpec(memory_space=pltpu.VMEM)],
         out_specs=pl.BlockSpec(memory_space=pltpu.VMEM),
         scratch_shapes=[
             pltpu.VMEM(x.shape, x.dtype),
-            pltpu.VMEM(x.shape, x.dtype),
+            pltpu.VMEM((n,) + block, x.dtype),
             pltpu.VMEM((rows, width), x.dtype),
             pltpu.VMEM((rows, width), x.dtype),
             pltpu.SemaphoreType.DMA((n,)),
@@ -175,7 +185,7 @@
             pltpu.SemaphoreType.DMA((n,)),
             pltpu.SemaphoreType.DMA((n,)),
         ],
-        compiler_params=pltpu.CompilerParams(collective_id=0, has_side_effects=True),
+        compiler_params=pltpu.CompilerParams(collective_id=kernel_id, has_side_effects=True),
     )(x)
 
 
@@ -231,7 +241,7 @@
         wide = lambda part: part.astype(jnp.float32)
         sums = mine + wide(lax.ppermute(theirs.astype(jnp.bfloat16), "prow", sibling))
         pieces = sums.astype(jnp.bfloat16).reshape(n_col, -1, width)
-        gathered = modal_sum(pieces, axes, sizes).reshape(-1, width)
+        gathered = fused_sum(pieces, axes, sizes, "pcol", True, 100).reshape(-1, width)
         modal_load = beside_sibling(gathered, core)
         modal_wide = modal_load.astype(jnp.float32)
         pseudo = jnp.concatenate(
@@ -246,9 +256,7 @@
         partial_gram = outer_rows(own_pseudo, pseudo).astype(jnp.bfloat16)
         chunk = modes // n_pl
         by_chunk = partial_gram.reshape(block, n_pl, chunk).transpose(1, 0, 2)
-        gram_sums = ex(by_chunk, ("pl",), same=False)
-        gram_piece = jnp.sum(gram_sums.astype(jnp.float32), axis=0).astype(jnp.bfloat16)
-        gram_all = ex(ex(gram_piece, ("zh",), same=True), ("pl",), same=True)
+        gram_all = fused_sum(by_chunk, axes, sizes, "pl", False, 101)
         gram_all = beside_sibling(gram_all[None], core)
         gram_panel = gram_all.transpose(2, 0, 3, 1, 4).reshape(n_row * block, modes)
         half = modes // 2

time: 186 us -> 179 us (0.962)
  Pallas kernels: 124 us -> 117 us
    pallas_call x4 -> x1, Pallas kernels: 76.4 us -> 9.67 us  [__call__(): pl.pallas_call(kernel, out_shape=jax.ShapeDtypeStruct((count,) + tuple(bl...]
    pallas_call x1 -> x2, Pallas kernels: 47.3 us -> 107 us  [fused_sum(): pl.pallas_call(kernel, out_shape=jax.ShapeDtypeStruct((n,) + block, x.dty...]
  transfers between devices with their start and end apart: 6 -> 6, of which waited for: 4 -> 4; matrix products, arithmetic and copies ran while one was open for 12% -> 12% of each run, Pallas kernels for 67% -> 66%
where the time goes in v11:
time: 179 us; the launch traced here: 178 us
  Pallas kernels  117 us (65%)
  matrix products  15.4 us (9%)
  between operations  13.6 us (8%)
  waiting for transfers between devices  10.6 us (6%)
  starting transfers between devices  7.83 us (4%)
  local copies, waits for them, and re-layouts  7.14 us (4%)
  other arithmetic  6.58 us (4%)
    pallas_call x2, Pallas kernels, fused_sum(): pl.pallas_call(kernel, out_shape=jax.ShapeDtypeStruct((n,) + block, x.dty...  107 us
    dot_general x4, matrix products, outer_rows(): lax.dot_general(left_rows, right_rows, (((1,), (1,)), ((), ())), preferre...  9.71 us
    pallas_call x1, Pallas kernels, __call__(): pl.pallas_call(kernel, out_shape=jax.ShapeDtypeStruct((count,) + tuple(bl...  9.67 us
    dot_general x1, matrix products, body(): jnp.dot(modal_at_loads, factor_cols, preferred_element_type=jnp.float32)  5.73 us
    ppermute x2, waiting for transfers between devices, beside_sibling(): other = lax.ppermute(part, 'prow', sibling)  4.23 us
    ppermute x1, waiting for transfers between devices, body(): panel_piece = lax.ppermute(send_half, ('prow', 'pcol'), swap)  4.04 us
    ppermute x1, starting transfers between devices, body(): panel_piece = lax.ppermute(send_half, ('prow', 'pcol'), swap)  3.77 us
  transfers between devices with their start and end apart: 6, of which 4 were waited for; matrix products, arithmetic and copies ran while one was open for 12% of the time, Pallas kernels for 66%

profile of v11, /device:TPU:39, one launch (start us, length us, event | category | flops | bytes accessed | tf_op | source)
XLA Modules:
  0.0 178.0 jit_solution(4717271006732630779)
XLA Ops:
  6.5 0.0 copy-start
  6.5 0.0 all-gather.2.cloned.1.call-start
  6.5 1.1 constant_dynamic-slice_fusion
  7.6 3.8 %collective-permute-start = (bf16[128,1024]{1,0:T(8,128)(2,1)S(1)}, bf16[128,1024]{1,0:T(8,128)(2,1)S(1)}, u32[]{:S(2)}, u32[]{:S(2)}) collective-permute-start(bf16[128,1024]{1,0:T(8,128)(2,1)S(1)} %constant_dynamic-slice_fusion), channel_id=1, source_target_pairs={{0,0},{64,16},{128,32},{192,48},{16,64},{80,80},{144,96},{208,112}... | collective-permute-start | bytes 786440 | tf_op jit(solution)/shard_map/ppermute | solution.py:264
  11.4 4.0 %collective-permute-done = bf16[128,1024]{1,0:T(8,128)(2,1)S(1)} collective-permute-done((bf16[128,1024]{1,0:T(8,128)(2,1)S(1)}, bf16[128,1024]{1,0:T(8,128)(2,1)S(1)}, u32[]{:S(2)}, u32[]{:S(2)}) %collective-permute-start) | collective-permute-done | bytes 262176 | tf_op jit(solution)/shard_map/ppermute | solution.py:264
  15.4 0.0 copy-start.2
  15.4 0.7 copy-done.2
  16.1 0.0 all-gather.2.cloned.1.call-update
  16.2 0.0 copy-done
  16.2 5.7 %fusion.13 = f32[2048,256]{1,0:T(8,128)S(1)} fusion(bf16[2048,2048]{1,0:T(8,128)(2,1)} %param.6, bf16[2048,256]{1,0:T(8,128)(2,1)S(1)} %copy-done), kind=kOutput, calls=%fused_computation.34 | convolution fusion | flops 2147483648 | bytes 11534336 | tf_op jit(solution)/shard_map/dot_general | solution.py:236
  21.9 0.0 copy-start.3
  21.9 0.0 copy-start.4
  22.0 0.9 dynamic-slice_convert_fusion
  22.8 0.0 collective-permute-start.1
  22.8 2.2 %collective-permute-done.1 = bf16[1024,256]{1,0:T(8,128)(2,1)} collective-permute-done((bf16[1024,256]{1,0:T(8,128)(2,1)}, bf16[1024,256]{1,0:T(8,128)(2,1)}, u32[]{:S(2)}, u32[]{:S(2)}) %collective-permute-start.1) | collective-permute-done | bytes 524320 | tf_op jit(solution)/shard_map/ppermute | solution.py:242
  25.1 2.0 %add_convert_fusion = bf16[1024,256]{1,0:T(8,128)(2,1)} fusion(bf16[1024,256]{1,0:T(8,128)(2,1)} %collective-permute-done.1, f32[2048,256]{1,0:T(8,128)S(1)} %fusion.13, s32[]{:T(128)S(6)} %select_n.54), kind=kLoop, calls=%fused_computation.14 | loop fusion | flops 786432 | bytes 2097156 | tf_op jit(solution)/shard_map/convert_element_type | solution.py:243
  27.0 47.3 %shard_map.55 = bf16[4,256,256]{2,1,0:T(8,128)(2,1)} custom-call(bf16[4,256,256]{2,1,0:T(8,128)(2,1)} %bitcast.30), custom_call_target="tpu_custom_call" | custom-call | tf_op jit(solution)/shard_map/pallas_call | solution.py:171
  74.3 1.2 collective-permute-start.2
  75.5 0.0 copy-done.3
  75.5 0.0 copy-done.4
  75.5 1.7 collective-permute-done.2
  77.3 1.1 broadcast_select_fusion.3
  78.4 1.9 %fusion = (bf16[2048,256]{1,0:T(8,128)(2,1)S(1)}, bf16[2048,256]{1,0:T(8,128)(2,1)S(1)}) fusion(f32[2048]{0:T(1024)S(1)} %get-tuple-element.15, bf16[1024,256]{1,0:T(8,128)(2,1)S(1)} %get-tuple-element.14, bf16[1024,256]{1,0:T(8,128)(2,1)S(1)} %get-tuple-element.13, f32[2048]{0:T(1024)S(1)} %get-tuple-element.16), kind=kLoop, calls=%fused_computation.7 | loop fusion | flops 4194304 | bytes 3162112 | tf_op jit(solution)/shard_map/convert_element_type | solution.py:249
  80.3 0.8 convolution_convert_fusion
  81.2 0.3 copy.7
  81.4 1.0 copy.8
  82.4 59.9 %shard_map.56 = bf16[16,2,128,128]{3,2,1,0:T(8,128)(2,1)} custom-call(bf16[16,128,128]{2,1,0:T(8,128)(2,1)} %bitcast.31), custom_call_target="tpu_custom_call" | custom-call | tf_op jit(solution)/shard_map/pallas_call | solution.py:171
  142.4 2.2 %collective-permute-start.3 = (bf16[1,16,2,128,128]{4,3,2,1,0:T(8,128)(2,1)}, bf16[1,16,2,128,128]{4,3,2,1,0:T(8,128)(2,1)S(1)}, u32[]{:S(2)}, u32[]{:S(2)}) collective-permute-start(bf16[1,16,2,128,128]{4,3,2,1,0:T(8,128)(2,1)} %bitcast.28), channel_id=1, source_target_pairs={{0,64},{64,0},{128,192},{192,128},{1,65},{65,1},{129,193},{193,129... | collective-permute-start | bytes 3145736 | tf_op jit(solution)/shard_map/ppermute | solution.py:226
  144.6 2.5 %collective-permute-done.3 = bf16[1,16,2,128,128]{4,3,2,1,0:T(8,128)(2,1)S(1)} collective-permute-done((bf16[1,16,2,128,128]{4,3,2,1,0:T(8,128)(2,1)}, bf16[1,16,2,128,128]{4,3,2,1,0:T(8,128)(2,1)S(1)}, u32[]{:S(2)}, u32[]{:S(2)}) %collective-permute-start.3) | collective-permute-done | bytes 1048608 | tf_op jit(solution)/shard_map/ppermute | solution.py:226
  147.1 1.4 broadcast_select_fusion.1
  148.4 0.2 maximum_bitcast_fusion
  148.6 1.4 copy.9
  150.0 0.5 copy.15
  150.6 0.0 all-gather.2.cloned.1.call-done
  150.6 0.6 collective-permute-start.4
  151.2 2.5 %fusion.2.x_ref = bf16[128,512]{1,0:T(8,128)(2,1)} fusion(bf16[512,2048]{1,0:T(8,128)(2,1)S(1)} %bitcast.26, bf16[128,2048]{1,0:T(8,128)(2,1)} %param.7), kind=kOutput, calls=%fused_computation.12 | convolution fusion | flops 268500992 | bytes 2752512 | tf_op jit(solution)/shard_map/dot_general | solution.py:22
  153.8 9.7 %shard_map.57 = bf16[4,128,512]{2,1,0:T(8,128)(2,1)} custom-call(bf16[128,512]{1,0:T(8,128)(2,1)} %fusion.2.x_ref), custom_call_target="tpu_custom_call" | custom-call | tf_op jit(solution)/shard_map/pallas_call | solution.py:205
  163.4 1.3 copy.11
  164.8 0.0 collective-permute-done.4
  164.8 0.0 copy-start.1
  164.8 3.8 %fusion.3 = f32[128,2048]{1,0:T(8,128)S(1)} fusion(bf16[2048,1024]{1,0:T(8,128)(2,1)} %collective-permute-done.4, bf16[128,2048]{0,1:T(8,128)(2,1)S(1)} %bitcast.34, s32[]{:T(128)S(6)} %select_n.55), kind=kOutput, calls=%fused_computation.20 | convolution fusion | flops 536870912 | bytes 5505028 | tf_op jit(solution)/shard_map/dot_general | solution.py:22
  168.6 0.0 copy-done.1
  168.6 2.5 %convolution_add_fusion = f32[128,2048]{1,0:T(8,128)} fusion(f32[128,2048]{1,0:T(8,128)S(1)} %fusion.3, bf16[2048,1024]{1,0:T(8,128)(2,1)S(1)} %copy-done.1, bf16[128,2048]{0,1:T(8,128)(2,1)S(1)} %bitcast.35, s32[]{:T(128)S(6)} %select_n.54), kind=kOutput, calls=%fused_computation.2 | convolution fusion | flops 537133056 | bytes 6553604 | tf_op jit(solution)/shard_map/dot_general | solution.py:22
  (1 shorter events, 0.0 us)
Async XLA Ops:
  6.5 9.6 %copy-start = (bf16[2048,256]{1,0:T(8,128)(2,1)S(1)}, bf16[2048,256]{1,0:T(8,128)(2,1)}, u32[]{:S(2)}) copy-start(bf16[2048,256]{1,0:T(8,128)(2,1)} %param.5) | copy-start | bytes 3145732
  6.5 144.0 %all-gather.2.cloned.1.call-start = ((), (), s32[]{:S(2)}) async-start(), calls=%async_computation | async-start | bytes 4456448 | tf_op jit(solution)/shard_map/all_gather | solution.py:265
  7.6 7.8 %collective-permute-start = (bf16[128,1024]{1,0:T(8,128)(2,1)S(1)}, bf16[128,1024]{1,0:T(8,128)(2,1)S(1)}, u32[]{:S(2)}, u32[]{:S(2)}) collective-permute-start(bf16[128,1024]{1,0:T(8,128)(2,1)S(1)} %constant_dynamic-slice_fusion), channel_id=1, source_target_pairs={{0,0},{64,16},{128,32},{192,48},{16,64},{80,80},{144,96},{208,112}... | collective-permute-start | bytes 786440 | tf_op jit(solution)/shard_map/ppermute | solution.py:264
  15.4 0.7 copy-start.2
  21.9 53.6 %copy-start.3 = (f32[2048]{0:T(1024)S(1)}, f32[2048]{0:T(1024)}, u32[]{:S(2)}) copy-start(f32[2048]{0:T(1024)} %param.8) | copy-start | bytes 24580
  21.9 53.6 %copy-start.4 = (f32[2048]{0:T(1024)S(1)}, f32[2048]{0:T(1024)}, u32[]{:S(2)}) copy-start(f32[2048]{0:T(1024)} %param.9) | copy-start | bytes 24580
  22.8 2.3 %collective-permute-start.1 = (bf16[1024,256]{1,0:T(8,128)(2,1)}, bf16[1024,256]{1,0:T(8,128)(2,1)}, u32[]{:S(2)}, u32[]{:S(2)}) collective-permute-start(bf16[1024,256]{1,0:T(8,128)(2,1)} %dynamic-slice_convert_fusion), channel_id=1, source_target_pairs={{0,64},{64,0},{128,192},{192,128},{1,65},{65,1},{129,193},{193,129... | collective-permute-start | bytes 1572872 | tf_op jit(solution)/shard_map/ppermute | solution.py:242
  74.3 3.0 %collective-permute-start.2 = (bf16[1024,256]{1,0:T(8,128)(2,1)}, bf16[1024,256]{1,0:T(8,128)(2,1)S(1)}, u32[]{:S(2)}, u32[]{:S(2)}) collective-permute-start(bf16[1024,256]{1,0:T(8,128)(2,1)} %bitcast.29), channel_id=1, source_target_pairs={{0,64},{64,0},{128,192},{192,128},{1,65},{65,1},{129,193},{193,129... | collective-permute-start | bytes 1572872 | tf_op jit(solution)/shard_map/ppermute | solution.py:226
  142.4 4.7 %collective-permute-start.3 = (bf16[1,16,2,128,128]{4,3,2,1,0:T(8,128)(2,1)}, bf16[1,16,2,128,128]{4,3,2,1,0:T(8,128)(2,1)S(1)}, u32[]{:S(2)}, u32[]{:S(2)}) collective-permute-start(bf16[1,16,2,128,128]{4,3,2,1,0:T(8,128)(2,1)} %bitcast.28), channel_id=1, source_target_pairs={{0,64},{64,0},{128,192},{192,128},{1,65},{65,1},{129,193},{193,129... | collective-permute-start | bytes 3145736 | tf_op jit(solution)/shard_map/ppermute | solution.py:226
  150.6 14.2 %collective-permute-start.4 = (bf16[2048,1024]{1,0:T(8,128)(2,1)}, bf16[2048,1024]{1,0:T(8,128)(2,1)}, u32[]{:S(2)}, u32[]{:S(2)}) collective-permute-start(bf16[2048,1024]{1,0:T(8,128)(2,1)} %all-gather.2.cloned.1.call-done), channel_id=1, source_target_pairs={{0,64},{64,0},{128,192},{192,128},{1,65},{65,1},{129,193},{193,129... | collective-permute-start | bytes 12582920 | tf_op jit(solution)/shard_map/ppermute | solution.py:267
  164.8 3.9 %copy-start.1 = (bf16[2048,1024]{1,0:T(8,128)(2,1)S(1)}, bf16[2048,1024]{1,0:T(8,128)(2,1)}, u32[]{:S(2)}) copy-start(bf16[2048,1024]{1,0:T(8,128)(2,1)} %all-gather.2.cloned.1.call-done) | copy-start | bytes 12582916
Sparse Core Ops, SparseCore 0:
  16.3 94.9 all-gather.1

commit v12 on v11

--- a/solution.py
+++ b/solution.py
@@ -160,6 +160,118 @@
     for k in range(1, n):
         step(coll.at[me], coll.at[sender(k)], k, device(over, sender(k)), (send_c, recv_c)).wait_recv()
     out_ref[...] = coll[...]
+
+
+def modal_sum_kernel(mine_ref, theirs_ref, out_ref, sib_in, pieces, got, coll, part_out, part_in,
+                     sib_out, send_s, recv_s, send_a, recv_a, send_b, recv_b, send_c, recv_c,
+                     send_d, recv_d, *, axes, factors):
+    coords = {a: lax.axis_index(a) for a in axes}
+
+    def value(f):
+        axis, size, stride = factors[f]
+        return lax.rem(coords[axis] // stride, size)
+
+    def device(f, v):
+        place = dict(coords)
+        axis, size, stride = factors[f]
+        place[axis] = place[axis] + (v - value(f)) * stride
+        return tuple(place[a] for a in axes)
+
+    n = factors["pcol"][1]
+    me, half, core = value("pcol"), value("zh"), value("core")
+    partner, sibling = device("zh", 1 - half), device("core", 1 - core)
+    peer = lambda k: lax.rem(me + k, n)
+    sender = lambda k: lax.rem(me + n - k, n)
+
+    def step(src, dst_at, k, to, sems):
+        return pltpu.make_async_remote_copy(
+            src_ref=src, dst_ref=dst_at, send_sem=sems[0].at[k], recv_sem=sems[1].at[k],
+            device_id=to, device_id_type=MESH,
+        )
+
+    def one(src, dst, to, send_sem, recv_sem):
+        return pltpu.make_async_remote_copy(
+            src_ref=src, dst_ref=dst, send_sem=send_sem, recv_sem=recv_sem,
+            device_id=to, device_id_type=MESH,
+        )
+
+    barrier = pltpu.get_barrier_semaphore()
+    for k in range(1, n):
+        pl.semaphore_signal(barrier, inc=1, device_id=device("pcol", peer(k)), device_id_type=MESH)
+    pl.semaphore_signal(barrier, inc=1, device_id=partner, device_id_type=MESH)
+    pl.semaphore_signal(barrier, inc=1, device_id=sibling, device_id_type=MESH)
+    pl.semaphore_wait(barrier, n + 1)
+
+    chip = one(theirs_ref, sib_in, sibling, send_s, recv_s)
+    chip.start()
+    chip.wait_send()
+    chip.wait_recv()
+    summed = mine_ref[...] + sib_in[...].astype(jnp.float32)
+    pieces[...] = summed.astype(pieces.dtype).reshape(pieces.shape)
+
+    for k in range(1, n):
+        step(pieces.at[peer(k)], got.at[me], k, device("pcol", peer(k)), (send_a, recv_a)).start()
+    for k in range(1, n):
+        step(pieces.at[peer(k)], got.at[me], k, device("pcol", peer(k)), (send_a, recv_a)).wait_send()
+    for k in range(1, n):
+        step(pieces.at[me], got.at[sender(k)], k, device("pcol", sender(k)), (send_a, recv_a)).wait_recv()
+    total = pieces[me].astype(jnp.float32)
+    for k in range(1, n):
+        total = total + got[sender(k)].astype(jnp.float32)
+    part_out[...] = total.astype(part_out.dtype)
+
+    across = one(part_out, part_in, partner, send_b, recv_b)
+    across.start()
+    across.wait_send()
+    across.wait_recv()
+    coll[me] = (part_out[...].astype(jnp.float32) + part_in[...].astype(jnp.float32)).astype(coll.dtype)
+
+    for k in range(1, n):
+        step(coll.at[me], coll.at[me], k, device("pcol", peer(k)), (send_c, recv_c)).start()
+    for k in range(1, n):
+        step(coll.at[me], coll.at[me], k, device("pcol", peer(k)), (send_c, recv_c)).wait_send()
+    for k in range(1, n):
+        step(coll.at[me], coll.at[sender(k)], k, device("pcol", sender(k)), (send_c, recv_c)).wait_recv()
+
+    join = one(coll, sib_out, sibling, send_d, recv_d)
+    join.start()
+    join.wait_send()
+    join.wait_recv()
+    out_ref[core] = coll[...]
+    out_ref[1 - core] = sib_out[...]
+
+
+def modal_sum(mine, theirs, axes, sizes):
+    n = sizes["pcol"]
+    rows, width = mine.shape
+    block = (n, rows // n, width)
+    kernel = functools.partial(modal_sum_kernel, axes=axes, factors=factor_table(sizes))
+    return pl.pallas_call(
+        kernel,
+        out_shape=jax.ShapeDtypeStruct((2,) + block, jnp.bfloat16),
+        in_specs=[pl.BlockSpec(memory_space=pltpu.VMEM)] * 2,
+        out_specs=pl.BlockSpec(memory_space=pltpu.VMEM),
+        scratch_shapes=[
+            pltpu.VMEM((rows, width), jnp.bfloat16),
+            pltpu.VMEM(block, jnp.bfloat16),
+            pltpu.VMEM(block, jnp.bfloat16),
+            pltpu.VMEM(block, jnp.bfloat16),
+            pltpu.VMEM(block[1:], jnp.bfloat16),
+            pltpu.VMEM(block[1:], jnp.bfloat16),
+            pltpu.VMEM(block, jnp.bfloat16),
+            pltpu.SemaphoreType.DMA(()),
+            pltpu.SemaphoreType.DMA(()),
+            pltpu.SemaphoreType.DMA((n,)),
+            pltpu.SemaphoreType.DMA((n,)),
+            pltpu.SemaphoreType.DMA(()),
+            pltpu.SemaphoreType.DMA(()),
+            pltpu.SemaphoreType.DMA((n,)),
+            pltpu.SemaphoreType.DMA((n,)),
+            pltpu.SemaphoreType.DMA(()),
+            pltpu.SemaphoreType.DMA(()),
+        ],
+        compiler_params=pltpu.CompilerParams(collective_id=102, has_side_effects=True),
+    )(mine, theirs)
 
 
 def fused_sum(x, axes, sizes, over, add_across, kernel_id):
@@ -238,11 +350,7 @@
         core = row % 2
         mine = lax.dynamic_slice_in_dim(partial_load, core * (modes // 2), modes // 2, 0)
         theirs = lax.dynamic_slice_in_dim(partial_load, (1 - core) * (modes // 2), modes // 2, 0)
-        wide = lambda part: part.astype(jnp.float32)
-        sums = mine + wide(lax.ppermute(theirs.astype(jnp.bfloat16), "prow", sibling))
-        pieces = sums.astype(jnp.bfloat16).reshape(n_col, -1, width)
-        gathered = fused_sum(pieces, axes, sizes, "pcol", True, 100).reshape(-1, width)
-        modal_load = beside_sibling(gathered, core)
+        modal_load = modal_sum(mine, theirs.astype(jnp.bfloat16), axes, sizes).reshape(modes, width)
         modal_wide = modal_load.astype(jnp.float32)
         pseudo = jnp.concatenate(
             [

time: 179 us -> 179 us (level)
  Pallas kernels: 117 us -> 126 us
  waiting for transfers between devices: 10.6 us -> 6.58 us
  other arithmetic: 6.58 us -> 3.34 us
  starting transfers between devices: 7.83 us -> 5.04 us
    pallas_call x0 -> x1, Pallas kernels: none -> 52.9 us  [modal_sum(): pl.pallas_call(kernel, out_shape=jax.ShapeDtypeStruct((2,) + block, jnp.b...]
    pallas_call x2 -> x1, Pallas kernels: 107 us -> 61.5 us  [fused_sum(): pl.pallas_call(kernel, out_shape=jax.ShapeDtypeStruct((n,) + block, x.dty...]
    ppermute x2 -> x1, starting transfers between devices: 3.41 us -> 0.82 us  [beside_sibling(): other = lax.ppermute(part, 'prow', sibling)]
    ppermute x1 -> x0, waiting for transfers between devices: 2.25 us -> none  [body(): lax.ppermute(theirs.astype(jnp.bfloat16), 'prow', sibling)]
    convert_element_type x1 -> x0, other arithmetic: 1.95 us -> none  [body(): pieces = sums.astype(jnp.bfloat16).reshape(n_col, -1, width)]
    ppermute x2 -> x1, waiting for transfers between devices: 4.23 us -> 2.5 us  [beside_sibling(): other = lax.ppermute(part, 'prow', sibling)]
  transfers between devices with their start and end apart: 6 -> 4, of which waited for: 4 -> 2; matrix products, arithmetic and copies ran while one was open for 12% -> 11% of each run, Pallas kernels for 66% -> 71%
where the time goes in v12:
time: 179 us; the launch traced here: 178 us
  Pallas kernels  126 us (70%)
  matrix products  15.6 us (9%)
  between operations  13.6 us (8%)
  local copies, waits for them, and re-layouts  8.22 us (5%)
  waiting for transfers between devices  6.58 us (4%)
  starting transfers between devices  5.04 us (3%)
  other arithmetic  3.34 us (2%)
    pallas_call x1, Pallas kernels, fused_sum(): pl.pallas_call(kernel, out_shape=jax.ShapeDtypeStruct((n,) + block, x.dty...  61.5 us
    pallas_call x1, Pallas kernels, modal_sum(): pl.pallas_call(kernel, out_shape=jax.ShapeDtypeStruct((2,) + block, jnp.b...  52.9 us
    pallas_call x1, Pallas kernels, __call__(): pl.pallas_call(kernel, out_shape=jax.ShapeDtypeStruct((count,) + tuple(bl...  11.1 us
    dot_general x4, matrix products, outer_rows(): lax.dot_general(left_rows, right_rows, (((1,), (1,)), ((), ())), preferre...  9.71 us
    dot_general x1, matrix products, body(): jnp.dot(modal_at_loads, factor_cols, preferred_element_type=jnp.float32)  5.86 us
    ppermute x1, waiting for transfers between devices, body(): panel_piece = lax.ppermute(send_half, ('prow', 'pcol'), swap)  4.04 us
    ppermute x1, starting transfers between devices, body(): panel_piece = lax.ppermute(send_half, ('prow', 'pcol'), swap)  3.77 us
  transfers between devices with their start and end apart: 4, of which 2 were waited for; matrix products, arithmetic and copies ran while one was open for 11% of the time, Pallas kernels for 71%

profile of v12, /device:TPU:39, one launch (start us, length us, event | category | flops | bytes accessed | tf_op | source)
XLA Modules:
  0.0 177.8 jit_solution(1852602074027106382)
XLA Ops:
  6.5 0.0 copy-start
  6.5 0.0 all-gather.2.cloned.1.call-start
  6.5 1.1 constant_dynamic-slice_fusion.1
  7.6 3.8 %collective-permute-start = (bf16[128,1024]{1,0:T(8,128)(2,1)S(1)}, bf16[128,1024]{1,0:T(8,128)(2,1)S(1)}, u32[]{:S(2)}, u32[]{:S(2)}) collective-permute-start(bf16[128,1024]{1,0:T(8,128)(2,1)S(1)} %constant_dynamic-slice_fusion.1), channel_id=1, source_target_pairs={{0,0},{64,16},{128,32},{192,48},{16,64},{80,80},{144,96},{208,112}... | collective-permute-start | bytes 786440 | tf_op jit(solution)/shard_map/ppermute | solution.py:372
  11.4 4.0 %collective-permute-done = bf16[128,1024]{1,0:T(8,128)(2,1)S(1)} collective-permute-done((bf16[128,1024]{1,0:T(8,128)(2,1)S(1)}, bf16[128,1024]{1,0:T(8,128)(2,1)S(1)}, u32[]{:S(2)}, u32[]{:S(2)}) %collective-permute-start) | collective-permute-done | bytes 262176 | tf_op jit(solution)/shard_map/ppermute | solution.py:372
  15.4 0.0 copy-start.2
  15.4 0.7 copy-done.2
  16.1 0.0 all-gather.2.cloned.1.call-update
  16.2 0.0 copy-done
  16.2 5.9 %fusion.13 = f32[2048,256]{1,0:T(8,128)S(1)} fusion(bf16[2048,2048]{1,0:T(8,128)(2,1)} %param.6, bf16[2048,256]{1,0:T(8,128)(2,1)S(1)} %copy-done), kind=kOutput, calls=%fused_computation.31 | convolution fusion | flops 2147483648 | bytes 11534336 | tf_op jit(solution)/shard_map/dot_general | solution.py:348
  22.1 0.9 dynamic-slice_convert_fusion.theirs_ref
  23.0 0.0 copy-start.3
  23.0 0.0 copy-start.4
  23.0 1.0 constant_dynamic-slice_fusion.mine_ref
  24.0 52.9 %shard_map.55 = bf16[2,4,256,256]{3,2,1,0:T(8,128)(2,1)} custom-call(f32[1024,256]{1,0:T(8,128)} %constant_dynamic-slice_fusion.mine_ref, bf16[1024,256]{1,0:T(8,128)(2,1)} %dynamic-slice_convert_fusion.theirs_ref), custom_call_target="tpu_custom_call" | custom-call | tf_op jit(solution)/shard_map/pallas_call | solution.py:249
  76.9 0.0 copy-done.3
  76.9 0.0 copy-done.4
  77.0 1.8 fusion
  78.8 0.8 convolution_convert_fusion
  79.6 0.3 copy.7
  79.8 1.0 copy.8
  80.9 61.5 %shard_map.56 = bf16[16,2,128,128]{3,2,1,0:T(8,128)(2,1)} custom-call(bf16[16,128,128]{2,1,0:T(8,128)(2,1)} %bitcast.29), custom_call_target="tpu_custom_call" | custom-call | tf_op jit(solution)/shard_map/pallas_call | solution.py:283
  142.3 0.8 collective-permute-start.1
  143.2 2.5 %collective-permute-done.1 = bf16[1,16,2,128,128]{4,3,2,1,0:T(8,128)(2,1)S(1)} collective-permute-done((bf16[1,16,2,128,128]{4,3,2,1,0:T(8,128)(2,1)}, bf16[1,16,2,128,128]{4,3,2,1,0:T(8,128)(2,1)S(1)}, u32[]{:S(2)}, u32[]{:S(2)}) %collective-permute-start.1) | collective-permute-done | bytes 1048608 | tf_op jit(solution)/shard_map/ppermute | solution.py:338
  145.7 1.4 broadcast_select_fusion.1
  147.0 0.2 maximum_bitcast_fusion
  147.2 1.4 copy.9
  148.6 0.5 copy.15
  149.1 0.0 all-gather.2.cloned.1.call-done
  149.2 0.5 collective-permute-start.2
  149.6 2.5 %fusion.2.x_ref = bf16[128,512]{1,0:T(8,128)(2,1)} fusion(bf16[512,2048]{1,0:T(8,128)(2,1)S(1)} %bitcast.26, bf16[128,2048]{1,0:T(8,128)(2,1)} %param.7), kind=kOutput, calls=%fused_computation.12 | convolution fusion | flops 268500992 | bytes 2752512 | tf_op jit(solution)/shard_map/dot_general | solution.py:22
  152.2 11.1 %shard_map.57 = bf16[4,128,512]{2,1,0:T(8,128)(2,1)} custom-call(bf16[128,512]{1,0:T(8,128)(2,1)} %fusion.2.x_ref), custom_call_target="tpu_custom_call" | custom-call | tf_op jit(solution)/shard_map/pallas_call | solution.py:317
  163.3 1.3 copy.11
  164.6 0.0 collective-permute-done.2
  164.6 0.0 copy-start.1
  164.6 3.8 %fusion.3 = f32[128,2048]{1,0:T(8,128)S(1)} fusion(bf16[2048,1024]{1,0:T(8,128)(2,1)} %collective-permute-done.2, bf16[128,2048]{0,1:T(8,128)(2,1)S(1)} %bitcast.32, s32[]{:T(128)S(6)} %select_n.42), kind=kOutput, calls=%fused_computation.16 | convolution fusion | flops 536870912 | bytes 5505028 | tf_op jit(solution)/shard_map/dot_general | solution.py:22
  168.5 0.0 copy-done.1
  168.5 2.5 %convolution_add_fusion = f32[128,2048]{1,0:T(8,128)} fusion(f32[128,2048]{1,0:T(8,128)S(1)} %fusion.3, bf16[2048,1024]{1,0:T(8,128)(2,1)S(1)} %copy-done.1, bf16[128,2048]{0,1:T(8,128)(2,1)S(1)} %bitcast.33, s32[]{:T(128)S(6)} %select_n.41), kind=kOutput, calls=%fused_computation.2 | convolution fusion | flops 537133056 | bytes 6553604 | tf_op jit(solution)/shard_map/dot_general | solution.py:22
  (1 shorter events, 0.0 us)
Async XLA Ops:
  6.5 9.7 %copy-start = (bf16[2048,256]{1,0:T(8,128)(2,1)S(1)}, bf16[2048,256]{1,0:T(8,128)(2,1)}, u32[]{:S(2)}) copy-start(bf16[2048,256]{1,0:T(8,128)(2,1)} %param.5) | copy-start | bytes 3145732
  6.5 142.6 %all-gather.2.cloned.1.call-start = ((), (), s32[]{:S(2)}) async-start(), calls=%async_computation | async-start | bytes 4456448 | tf_op jit(solution)/shard_map/all_gather | solution.py:373
  7.6 7.8 %collective-permute-start = (bf16[128,1024]{1,0:T(8,128)(2,1)S(1)}, bf16[128,1024]{1,0:T(8,128)(2,1)S(1)}, u32[]{:S(2)}, u32[]{:S(2)}) collective-permute-start(bf16[128,1024]{1,0:T(8,128)(2,1)S(1)} %constant_dynamic-slice_fusion.1), channel_id=1, source_target_pairs={{0,0},{64,16},{128,32},{192,48},{16,64},{80,80},{144,96},{208,112}... | collective-permute-start | bytes 786440 | tf_op jit(solution)/shard_map/ppermute | solution.py:372
  15.4 0.7 copy-start.2
  23.0 54.0 %copy-start.3 = (f32[2048]{0:T(1024)S(1)}, f32[2048]{0:T(1024)}, u32[]{:S(2)}) copy-start(f32[2048]{0:T(1024)} %param.8) | copy-start | bytes 24580
  23.0 54.0 %copy-start.4 = (f32[2048]{0:T(1024)S(1)}, f32[2048]{0:T(1024)}, u32[]{:S(2)}) copy-start(f32[2048]{0:T(1024)} %param.9) | copy-start | bytes 24580
  142.3 3.3 %collective-permute-start.1 = (bf16[1,16,2,128,128]{4,3,2,1,0:T(8,128)(2,1)}, bf16[1,16,2,128,128]{4,3,2,1,0:T(8,128)(2,1)S(1)}, u32[]{:S(2)}, u32[]{:S(2)}) collective-permute-start(bf16[1,16,2,128,128]{4,3,2,1,0:T(8,128)(2,1)} %bitcast.28), channel_id=1, source_target_pairs={{0,64},{64,0},{128,192},{192,128},{1,65},{65,1},{129,193},{193,129... | collective-permute-start | bytes 3145736 | tf_op jit(solution)/shard_map/ppermute | solution.py:338
  149.2 15.4 %collective-permute-start.2 = (bf16[2048,1024]{1,0:T(8,128)(2,1)}, bf16[2048,1024]{1,0:T(8,128)(2,1)}, u32[]{:S(2)}, u32[]{:S(2)}) collective-permute-start(bf16[2048,1024]{1,0:T(8,128)(2,1)} %all-gather.2.cloned.1.call-done), channel_id=1, source_target_pairs={{0,64},{64,0},{128,192},{192,128},{1,65},{65,1},{129,193},{193,129... | collective-permute-start | bytes 12582920 | tf_op jit(solution)/shard_map/ppermute | solution.py:375
  164.6 3.9 %copy-start.1 = (bf16[2048,1024]{1,0:T(8,128)(2,1)S(1)}, bf16[2048,1024]{1,0:T(8,128)(2,1)}, u32[]{:S(2)}) copy-start(bf16[2048,1024]{1,0:T(8,128)(2,1)} %all-gather.2.cloned.1.call-done) | copy-start | bytes 12582916
Sparse Core Ops, SparseCore 0:
  16.3 95.5 all-gather.1

commit v13 on v12

--- a/solution.py
+++ b/solution.py
@@ -272,6 +272,137 @@
         ],
         compiler_params=pltpu.CompilerParams(collective_id=102, has_side_effects=True),
     )(mine, theirs)
+
+
+def gram_weighted_kernel(x_ref, shapes_ref, out_ref, got, coll, sib_coll, part_out, part_in, wbuf,
+                         send_a, recv_a, send_b, recv_b, send_c, recv_c, send_d, recv_d, send_e,
+                         recv_e, *, axes, factors):
+    coords = {a: lax.axis_index(a) for a in axes}
+
+    def value(f):
+        axis, size, stride = factors[f]
+        return lax.rem(coords[axis] // stride, size)
+
+    def device(f, v):
+        place = dict(coords)
+        axis, size, stride = factors[f]
+        place[axis] = place[axis] + (v - value(f)) * stride
+        return tuple(place[a] for a in axes)
+
+    n, n_col = factors["pl"][1], factors["pcol"][1]
+    me, half, core, col = value("pl"), value("zh"), value("core"), value("pcol")
+    partner, sibling = device("zh", 1 - half), device("core", 1 - core)
+
+    def step(src, dst_at, k, to, sems):
+        return pltpu.make_async_remote_copy(
+            src_ref=src, dst_ref=dst_at, send_sem=sems[0].at[k], recv_sem=sems[1].at[k],
+            device_id=to, device_id_type=MESH,
+        )
+
+    def one(src, dst, to, send_sem, recv_sem):
+        return pltpu.make_async_remote_copy(
+            src_ref=src, dst_ref=dst, send_sem=send_sem, recv_sem=recv_sem,
+            device_id=to, device_id_type=MESH,
+        )
+
+    barrier = pltpu.get_barrier_semaphore()
+    for k in range(1, n):
+        pl.semaphore_signal(barrier, inc=1, device_id=device("pl", lax.rem(me + k, n)), device_id_type=MESH)
+    for k in range(1, n_col):
+        pl.semaphore_signal(
+            barrier, inc=1, device_id=device("pcol", lax.rem(col + k, n_col)), device_id_type=MESH
+        )
+    pl.semaphore_signal(barrier, inc=1, device_id=partner, device_id_type=MESH)
+    pl.semaphore_signal(barrier, inc=1, device_id=sibling, device_id_type=MESH)
+    pl.semaphore_wait(barrier, n + n_col)
+
+    peer = lambda k: lax.rem(me + k, n)
+    sender = lambda k: lax.rem(me + n - k, n)
+    for k in range(1, n):
+        step(x_ref.at[peer(k)], got.at[me], k, device("pl", peer(k)), (send_a, recv_a)).start()
+    for k in range(1, n):
+        step(x_ref.at[peer(k)], got.at[me], k, device("pl", peer(k)), (send_a, recv_a)).wait_send()
+    for k in range(1, n):
+        step(x_ref.at[me], got.at[sender(k)], k, device("pl", sender(k)), (send_a, recv_a)).wait_recv()
+    total = x_ref[me].astype(jnp.float32)
+    for k in range(1, n):
+        total = total + got[sender(k)].astype(jnp.float32)
+    part_out[...] = total.astype(part_out.dtype)
+
+    across = one(part_out, part_in, partner, send_b, recv_b)
+    across.start()
+    across.wait_send()
+    across.wait_recv()
+    mine, theirs = part_out[...], part_in[...]
+    coll[me] = jnp.stack([jnp.where(half == 0, mine, theirs), jnp.where(half == 0, theirs, mine)])
+
+    for k in range(1, n):
+        step(coll.at[me], coll.at[me], k, device("pl", peer(k)), (send_c, recv_c)).start()
+    for k in range(1, n):
+        step(coll.at[me], coll.at[me], k, device("pl", peer(k)), (send_c, recv_c)).wait_send()
+    for k in range(1, n):
+        step(coll.at[me], coll.at[sender(k)], k, device("pl", sender(k)), (send_c, recv_c)).wait_recv()
+
+    join = one(coll, sib_coll, sibling, send_d, recv_d)
+    join.start()
+    join.wait_send()
+    join.wait_recv()
+
+    chunk = coll.shape[-1]
+    parts = []
+    for h in range(2):
+        for k in range(2):
+            acc = jnp.zeros((shapes_ref.shape[0], coll.shape[2]), jnp.float32)
+            for l in range(n):
+                block = jnp.where(core == k, coll[l, h], sib_coll[l, h])
+                acc = acc + lax.dot_general(
+                    shapes_ref[:, l * chunk:(l + 1) * chunk], block,
+                    (((1,), (1,)), ((), ())), preferred_element_type=jnp.float32,
+                )
+            parts.append(acc)
+    wbuf[col] = jnp.concatenate(parts, axis=1).astype(wbuf.dtype)
+
+    wpeer = lambda k: lax.rem(col + k, n_col)
+    wsender = lambda k: lax.rem(col + n_col - k, n_col)
+    for k in range(1, n_col):
+        step(wbuf.at[col], wbuf.at[col], k, device("pcol", wpeer(k)), (send_e, recv_e)).start()
+    for k in range(1, n_col):
+        step(wbuf.at[col], wbuf.at[col], k, device("pcol", wpeer(k)), (send_e, recv_e)).wait_send()
+    for k in range(1, n_col):
+        step(wbuf.at[col], wbuf.at[wsender(k)], k, device("pcol", wsender(k)), (send_e, recv_e)).wait_recv()
+    out_ref[...] = wbuf[...]
+
+
+def gram_weighted(x, mode_shapes, axes, sizes):
+    n, rows, width = x.shape
+    n_col = sizes["pcol"]
+    wshape = (n_col, mode_shapes.shape[0], 4 * rows)
+    kernel = functools.partial(gram_weighted_kernel, axes=axes, factors=factor_table(sizes))
+    return pl.pallas_call(
+        kernel,
+        out_shape=jax.ShapeDtypeStruct(wshape, jnp.bfloat16),
+        in_specs=[pl.BlockSpec(memory_space=pltpu.VMEM)] * 2,
+        out_specs=pl.BlockSpec(memory_space=pltpu.VMEM),
+        scratch_shapes=[
+            pltpu.VMEM(x.shape, x.dtype),
+            pltpu.VMEM((n, 2, rows, width), x.dtype),
+            pltpu.VMEM((n, 2, rows, width), x.dtype),
+            pltpu.VMEM((rows, width), x.dtype),
+            pltpu.VMEM((rows, width), x.dtype),
+            pltpu.VMEM(wshape, jnp.bfloat16),
+            pltpu.SemaphoreType.DMA((n,)),
+            pltpu.SemaphoreType.DMA((n,)),
+            pltpu.SemaphoreType.DMA(()),
+            pltpu.SemaphoreType.DMA(()),
+            pltpu.SemaphoreType.DMA((n,)),
+            pltpu.SemaphoreType.DMA((n,)),
+            pltpu.SemaphoreType.DMA(()),
+            pltpu.SemaphoreType.DMA(()),
+            pltpu.SemaphoreType.DMA((n_col,)),
+            pltpu.SemaphoreType.DMA((n_col,)),
+        ],
+        compiler_params=pltpu.CompilerParams(collective_id=103, has_side_effects=True),
+    )(x, mode_shapes)
 
 
 def fused_sum(x, axes, sizes, over, add_across, kernel_id):
@@ -364,18 +495,14 @@
         partial_gram = outer_rows(own_pseudo, pseudo).astype(jnp.bfloat16)
         chunk = modes // n_pl
         by_chunk = partial_gram.reshape(block, n_pl, chunk).transpose(1, 0, 2)
-        gram_all = fused_sum(by_chunk, axes, sizes, "pl", False, 101)
-        gram_all = beside_sibling(gram_all[None], core)
-        gram_panel = gram_all.transpose(2, 0, 3, 1, 4).reshape(n_row * block, modes)
         half = modes // 2
         send_half = lax.dynamic_slice_in_dim(mode_shapes, (col % 2) * half, half, 1)
         panel_piece = lax.ppermute(send_half, ("prow", "pcol"), swap)
         panel_mine = lax.all_gather(panel_piece, "pl", axis=0, tiled=True)
-        panel_mine, gram_panel = lax.optimization_barrier((panel_mine, gram_panel))
+        weighted_all = gram_weighted(by_chunk, mode_shapes, axes, sizes)
+        panel_mine, weighted_all = lax.optimization_barrier((panel_mine, weighted_all))
         panel_other = lax.ppermute(panel_mine, "prow", sibling)
-        weighted_part = outer_rows(mode_shapes, gram_panel).astype(jnp.bfloat16)
-        weighted_all = ex(weighted_part, ("pcol",), same=True)
-        weighted = weighted_all.transpose(1, 0, 2).reshape(weighted_part.shape[0], modes)
+        weighted = weighted_all.transpose(1, 0, 2).reshape(mode_shapes.shape[0], modes)
         weighted_mine = lax.dynamic_slice_in_dim(weighted, core * half, half, 1)
         weighted_other = lax.dynamic_slice_in_dim(weighted, (1 - core) * half, half, 1)
         return outer_rows(weighted_mine, panel_mine) + outer_rows(weighted_other, panel_other)

time: 179 us -> 177 us (0.989)
  waiting for transfers between devices: 6.58 us -> 9.88 us
  matrix products: 15.6 us -> 12.9 us
  Pallas kernels: 126 us -> 128 us
  local copies, waits for them, and re-layouts: 8.22 us -> 6.31 us
    ppermute x1, waiting for transfers between devices: 0.01 us -> 5.8 us  [body(): panel_other = lax.ppermute(panel_mine, 'prow', sibling)]
    dot_general x4 -> x3, matrix products: 9.71 us -> 7.02 us  [outer_rows(): lax.dot_general(left_rows, right_rows, (((1,), (1,)), ((), ())), preferre...]
    ppermute x1 -> x0, waiting for transfers between devices: 2.5 us -> none  [beside_sibling(): other = lax.ppermute(part, 'prow', sibling)]
    pallas_call x2 -> x1, Pallas kernels: 72.6 us -> 75 us  [gram_weighted(): pl.pallas_call(kernel, out_shape=jax.ShapeDtypeStruct(wshape, jnp.bfloat1...]
  transfers between devices with their start and end apart: 4 -> 3, of which waited for: 2 -> 2; matrix products, arithmetic and copies ran while one was open for 11% -> 7% of each run, Pallas kernels for 71% -> 72%
where the time goes in v13:
time: 177 us
  Pallas kernels  128 us (72%)
  between operations  13.6 us (8%)
  matrix products  12.9 us (7%)
  waiting for transfers between devices  9.88 us (6%)
  local copies, waits for them, and re-layouts  6.31 us (4%)
  starting transfers between devices  4.57 us (3%)
  other arithmetic  1.79 us (1%)
    pallas_call x1, Pallas kernels, gram_weighted(): pl.pallas_call(kernel, out_shape=jax.ShapeDtypeStruct(wshape, jnp.bfloat1...  75 us
    pallas_call x1, Pallas kernels, modal_sum(): pl.pallas_call(kernel, out_shape=jax.ShapeDtypeStruct((2,) + block, jnp.b...  52.9 us
    dot_general x3, matrix products, outer_rows(): lax.dot_general(left_rows, right_rows, (((1,), (1,)), ((), ())), preferre...  7.02 us
    dot_general x1, matrix products, body(): jnp.dot(modal_at_loads, factor_cols, preferred_element_type=jnp.float32)  5.86 us
    ppermute x1, waiting for transfers between devices, body(): panel_other = lax.ppermute(panel_mine, 'prow', sibling)  5.8 us
    ppermute x1, waiting for transfers between devices, body(): panel_piece = lax.ppermute(send_half, ('prow', 'pcol'), swap)  4.04 us
    ppermute x1, starting transfers between devices, body(): panel_piece = lax.ppermute(send_half, ('prow', 'pcol'), swap)  3.77 us
  transfers between devices with their start and end apart: 3, of which 2 were waited for; matrix products, arithmetic and copies ran while one was open for 7% of the time, Pallas kernels for 72%

profile of v13, /device:TPU:39, one launch (start us, length us, event | category | flops | bytes accessed | tf_op | source)
XLA Modules:
  0.0 176.8 jit_solution(15723984492279913729)
XLA Ops:
  6.5 0.0 copy-start
  6.5 0.0 all-gather.2.cloned.1.call-start
  6.5 1.1 constant_dynamic-slice_fusion.1
  7.6 3.8 %collective-permute-start = (bf16[128,1024]{1,0:T(8,128)(2,1)S(1)}, bf16[128,1024]{1,0:T(8,128)(2,1)S(1)}, u32[]{:S(2)}, u32[]{:S(2)}) collective-permute-start(bf16[128,1024]{1,0:T(8,128)(2,1)S(1)} %constant_dynamic-slice_fusion.1), channel_id=1, source_target_pairs={{0,0},{64,16},{128,32},{192,48},{16,64},{80,80},{144,96},{208,112}... | collective-permute-start | bytes 786440 | tf_op jit(solution)/shard_map/ppermute | solution.py:500
  11.4 4.0 %collective-permute-done = bf16[128,1024]{1,0:T(8,128)(2,1)S(1)} collective-permute-done((bf16[128,1024]{1,0:T(8,128)(2,1)S(1)}, bf16[128,1024]{1,0:T(8,128)(2,1)S(1)}, u32[]{:S(2)}, u32[]{:S(2)}) %collective-permute-start) | collective-permute-done | bytes 262176 | tf_op jit(solution)/shard_map/ppermute | solution.py:500
  15.4 0.0 copy-start.2
  15.4 0.7 copy-done.2
  16.1 0.0 all-gather.2.cloned.1.call-update
  16.2 0.0 copy-done
  16.2 5.9 %fusion.12 = f32[2048,256]{1,0:T(8,128)S(1)} fusion(bf16[2048,2048]{1,0:T(8,128)(2,1)} %param.6, bf16[2048,256]{1,0:T(8,128)(2,1)S(1)} %copy-done), kind=kOutput, calls=%fused_computation.25 | convolution fusion | flops 2147483648 | bytes 11534336 | tf_op jit(solution)/shard_map/dot_general | solution.py:479
  22.1 0.0 copy-start.3
  22.1 0.0 copy-start.4
  22.1 0.9 dynamic-slice_convert_fusion.theirs_ref
  23.0 1.0 constant_dynamic-slice_fusion.mine_ref
  24.0 52.9 %shard_map.55 = bf16[2,4,256,256]{3,2,1,0:T(8,128)(2,1)} custom-call(f32[1024,256]{1,0:T(8,128)} %constant_dynamic-slice_fusion.mine_ref, bf16[1024,256]{1,0:T(8,128)(2,1)} %dynamic-slice_convert_fusion.theirs_ref), custom_call_target="tpu_custom_call" | custom-call | tf_op jit(solution)/shard_map/pallas_call | solution.py:249
  76.9 0.0 copy-done.3
  76.9 0.0 copy-done.4
  77.0 1.8 %fusion = (bf16[2048,256]{1,0:T(8,128)(2,1)S(1)}, bf16[2048,256]{1,0:T(8,128)(2,1)S(1)}) fusion(bf16[2,4,256,256]{3,2,1,0:T(8,128)(2,1)} %shard_map.55, f32[2048]{0:T(1024)S(1)} %get-tuple-element.11, f32[2048]{0:T(1024)S(1)} %get-tuple-element.12), kind=kLoop, calls=%fused_computation.7 | loop fusion | flops 2621440 | bytes 3162112 | tf_op jit(solution)/shard_map/convert_element_type | solution.py:488
  78.7 0.8 convolution_convert_fusion
  79.6 0.3 copy.6
  79.8 1.0 copy.7
  80.9 75.0 %shard_map.56 = bf16[4,128,512]{2,1,0:T(8,128)(2,1)} custom-call(bf16[16,128,128]{2,1,0:T(8,128)(2,1)} %bitcast.13, bf16[128,2048]{1,0:T(8,128)(2,1)} %shapes_ref.1), custom_call_target="tpu_custom_call" | custom-call | tf_op jit(solution)/shard_map/pallas_call | solution.py:381
  155.8 0.0 all-gather.2.cloned.1.call-done
  155.8 0.8 collective-permute-start.1
  156.6 1.3 copy.8
  158.0 0.0 copy-start.1
  158.0 5.8 %collective-permute-done.1 = bf16[2048,1024]{1,0:T(8,128)(2,1)} collective-permute-done((bf16[2048,1024]{1,0:T(8,128)(2,1)}, bf16[2048,1024]{1,0:T(8,128)(2,1)}, u32[]{:S(2)}, u32[]{:S(2)}) %collective-permute-start.1) | collective-permute-done | bytes 4194336 | tf_op jit(solution)/shard_map/ppermute | solution.py:504
  163.8 3.7 %fusion.2 = f32[128,2048]{1,0:T(8,128)S(1)} fusion(bf16[2048,1024]{1,0:T(8,128)(2,1)} %collective-permute-done.1, bf16[128,2048]{0,1:T(8,128)(2,1)S(1)} %bitcast.15, s32[]{:T(128)S(6)} %select_n.29), kind=kOutput, calls=%fused_computation.10 | convolution fusion | flops 536870912 | bytes 5505028 | tf_op jit(solution)/shard_map/dot_general | solution.py:22
  167.5 0.0 copy-done.1
  167.5 2.5 %convolution_add_fusion = f32[128,2048]{1,0:T(8,128)} fusion(f32[128,2048]{1,0:T(8,128)S(1)} %fusion.2, bf16[2048,1024]{1,0:T(8,128)(2,1)S(1)} %copy-done.1, bf16[128,2048]{0,1:T(8,128)(2,1)S(1)} %bitcast.16, s32[]{:T(128)S(6)} %select_n.28), kind=kOutput, calls=%fused_computation.2 | convolution fusion | flops 537133056 | bytes 6553604 | tf_op jit(solution)/shard_map/dot_general | solution.py:22
  (1 shorter events, 0.0 us)
Async XLA Ops:
  6.5 9.6 %copy-start = (bf16[2048,256]{1,0:T(8,128)(2,1)S(1)}, bf16[2048,256]{1,0:T(8,128)(2,1)}, u32[]{:S(2)}) copy-start(bf16[2048,256]{1,0:T(8,128)(2,1)} %param.5) | copy-start | bytes 3145732
  6.5 149.3 %all-gather.2.cloned.1.call-start = ((), (), s32[]{:S(2)}) async-start(), calls=%async_computation | async-start | bytes 4456448 | tf_op jit(solution)/shard_map/all_gather | solution.py:501
  7.6 7.8 %collective-permute-start = (bf16[128,1024]{1,0:T(8,128)(2,1)S(1)}, bf16[128,1024]{1,0:T(8,128)(2,1)S(1)}, u32[]{:S(2)}, u32[]{:S(2)}) collective-permute-start(bf16[128,1024]{1,0:T(8,128)(2,1)S(1)} %constant_dynamic-slice_fusion.1), channel_id=1, source_target_pairs={{0,0},{64,16},{128,32},{192,48},{16,64},{80,80},{144,96},{208,112}... | collective-permute-start | bytes 786440 | tf_op jit(solution)/shard_map/ppermute | solution.py:500
  15.4 0.7 copy-start.2
  22.1 54.9 %copy-start.3 = (f32[2048]{0:T(1024)S(1)}, f32[2048]{0:T(1024)}, u32[]{:S(2)}) copy-start(f32[2048]{0:T(1024)} %param.8) | copy-start | bytes 24580
  22.1 54.9 %copy-start.4 = (f32[2048]{0:T(1024)S(1)}, f32[2048]{0:T(1024)}, u32[]{:S(2)}) copy-start(f32[2048]{0:T(1024)} %param.9) | copy-start | bytes 24580
  155.8 7.9 %collective-permute-start.1 = (bf16[2048,1024]{1,0:T(8,128)(2,1)}, bf16[2048,1024]{1,0:T(8,128)(2,1)}, u32[]{:S(2)}, u32[]{:S(2)}) collective-permute-start(bf16[2048,1024]{1,0:T(8,128)(2,1)} %all-gather.2.cloned.1.call-done), channel_id=1, source_target_pairs={{0,64},{64,0},{128,192},{192,128},{1,65},{65,1},{129,193},{193,129... | collective-permute-start | bytes 12582920 | tf_op jit(solution)/shard_map/ppermute | solution.py:504
  158.0 9.5 %copy-start.1 = (bf16[2048,1024]{1,0:T(8,128)(2,1)S(1)}, bf16[2048,1024]{1,0:T(8,128)(2,1)}, u32[]{:S(2)}) copy-start(bf16[2048,1024]{1,0:T(8,128)(2,1)} %all-gather.2.cloned.1.call-done) | copy-start | bytes 12582916
Sparse Core Ops, SparseCore 0:
  16.3 95.4 all-gather.1

commit v14 on v13

--- a/solution.py
+++ b/solution.py
@@ -505,7 +505,7 @@
         weighted = weighted_all.transpose(1, 0, 2).reshape(mode_shapes.shape[0], modes)
         weighted_mine = lax.dynamic_slice_in_dim(weighted, core * half, half, 1)
         weighted_other = lax.dynamic_slice_in_dim(weighted, (1 - core) * half, half, 1)
-        return outer_rows(weighted_mine, panel_mine) + outer_rows(weighted_other, panel_other)
+        return outer_rows(weighted_other, panel_other) + outer_rows(weighted_mine, panel_mine)
 
     return body
 

time: 177 us -> 176 us (level)
  waiting for transfers between devices: 9.88 us -> 6.18 us
  matrix products: 12.9 us -> 15 us
    ppermute x1, waiting for transfers between devices: 5.8 us -> 2.1 us  [body(): panel_other = lax.ppermute(panel_mine, 'prow', sibling)]
    dot_general x3, matrix products: 7.02 us -> 9.19 us  [outer_rows(): lax.dot_general(left_rows, right_rows, (((1,), (1,)), ((), ())), preferre...]
  transfers between devices with their start and end apart: 3 -> 3, of which waited for: 2 -> 2; matrix products, arithmetic and copies ran while one was open for 7% -> 10% of each run, Pallas kernels for 72% -> 73%
where the time goes in v14:
time: 176 us; the launch traced here: 175 us
  Pallas kernels  128 us (73%)
  matrix products  15 us (9%)
  between operations  13.5 us (8%)
  local copies, waits for them, and re-layouts  6.31 us (4%)
  waiting for transfers between devices  6.18 us (4%)
  starting transfers between devices  4.57 us (3%)
  other arithmetic  1.79 us (1%)
    pallas_call x1, Pallas kernels, gram_weighted(): pl.pallas_call(kernel, out_shape=jax.ShapeDtypeStruct(wshape, jnp.bfloat1...  75 us
    pallas_call x1, Pallas kernels, modal_sum(): pl.pallas_call(kernel, out_shape=jax.ShapeDtypeStruct((2,) + block, jnp.b...  52.9 us
    dot_general x3, matrix products, outer_rows(): lax.dot_general(left_rows, right_rows, (((1,), (1,)), ((), ())), preferre...  9.19 us
    dot_general x1, matrix products, body(): jnp.dot(modal_at_loads, factor_cols, preferred_element_type=jnp.float32)  5.86 us
    ppermute x1, waiting for transfers between devices, body(): panel_piece = lax.ppermute(send_half, ('prow', 'pcol'), swap)  4.04 us
    ppermute x1, starting transfers between devices, body(): panel_piece = lax.ppermute(send_half, ('prow', 'pcol'), swap)  3.77 us
  transfers between devices with their start and end apart: 3, of which 2 were waited for; matrix products, arithmetic and copies ran while one was open for 10% of the time, Pallas kernels for 73%

profile of v14, /device:TPU:39, one launch (start us, length us, event | category | flops | bytes accessed | tf_op | source)
XLA Modules:
  0.0 175.3 jit_solution(16211242867505477482)
XLA Ops:
  6.5 0.0 copy-start
  6.5 0.0 all-gather.2.cloned.1.call-start
  6.5 1.1 constant_dynamic-slice_fusion.1
  7.6 3.8 %collective-permute-start = (bf16[128,1024]{1,0:T(8,128)(2,1)S(1)}, bf16[128,1024]{1,0:T(8,128)(2,1)S(1)}, u32[]{:S(2)}, u32[]{:S(2)}) collective-permute-start(bf16[128,1024]{1,0:T(8,128)(2,1)S(1)} %constant_dynamic-slice_fusion.1), channel_id=1, source_target_pairs={{0,0},{64,16},{128,32},{192,48},{16,64},{80,80},{144,96},{208,112}... | collective-permute-start | bytes 786440 | tf_op jit(solution)/shard_map/ppermute | solution.py:500
  11.4 4.0 %collective-permute-done = bf16[128,1024]{1,0:T(8,128)(2,1)S(1)} collective-permute-done((bf16[128,1024]{1,0:T(8,128)(2,1)S(1)}, bf16[128,1024]{1,0:T(8,128)(2,1)S(1)}, u32[]{:S(2)}, u32[]{:S(2)}) %collective-permute-start) | collective-permute-done | bytes 262176 | tf_op jit(solution)/shard_map/ppermute | solution.py:500
  15.4 0.0 copy-start.1
  15.4 0.7 copy-done.1
  16.1 0.0 all-gather.2.cloned.1.call-update
  16.2 0.0 copy-done
  16.2 5.9 %fusion.12 = f32[2048,256]{1,0:T(8,128)S(1)} fusion(bf16[2048,2048]{1,0:T(8,128)(2,1)} %param.6, bf16[2048,256]{1,0:T(8,128)(2,1)S(1)} %copy-done), kind=kOutput, calls=%fused_computation.25 | convolution fusion | flops 2147483648 | bytes 11534336 | tf_op jit(solution)/shard_map/dot_general | solution.py:479
  22.1 0.0 copy-start.2
  22.1 0.0 copy-start.3
  22.1 0.9 dynamic-slice_convert_fusion.theirs_ref
  23.0 1.0 constant_dynamic-slice_fusion.mine_ref
  24.0 52.9 %shard_map.55 = bf16[2,4,256,256]{3,2,1,0:T(8,128)(2,1)} custom-call(f32[1024,256]{1,0:T(8,128)} %constant_dynamic-slice_fusion.mine_ref, bf16[1024,256]{1,0:T(8,128)(2,1)} %dynamic-slice_convert_fusion.theirs_ref), custom_call_target="tpu_custom_call" | custom-call | tf_op jit(solution)/shard_map/pallas_call | solution.py:249
  76.9 0.0 copy-done.2
  76.9 0.0 copy-done.3
  77.0 1.8 %fusion = (bf16[2048,256]{1,0:T(8,128)(2,1)S(1)}, bf16[2048,256]{1,0:T(8,128)(2,1)S(1)}) fusion(bf16[2,4,256,256]{3,2,1,0:T(8,128)(2,1)} %shard_map.55, f32[2048]{0:T(1024)S(1)} %get-tuple-element.11, f32[2048]{0:T(1024)S(1)} %get-tuple-element.12), kind=kLoop, calls=%fused_computation.7 | loop fusion | flops 2621440 | bytes 3162112 | tf_op jit(solution)/shard_map/convert_element_type | solution.py:488
  78.7 0.8 convolution_convert_fusion
  79.6 0.3 copy.6
  79.8 1.0 copy.7
  80.8 75.0 %shard_map.56 = bf16[4,128,512]{2,1,0:T(8,128)(2,1)} custom-call(bf16[16,128,128]{2,1,0:T(8,128)(2,1)} %bitcast.13, bf16[128,2048]{1,0:T(8,128)(2,1)} %shapes_ref.1), custom_call_target="tpu_custom_call" | custom-call | tf_op jit(solution)/shard_map/pallas_call | solution.py:381
  155.8 0.0 all-gather.2.cloned.1.call-done
  155.8 0.8 collective-permute-start.1
  156.6 1.3 copy.8
  158.0 3.7 %fusion.2 = f32[128,2048]{1,0:T(8,128)S(1)} fusion(bf16[2048,1024]{1,0:T(8,128)(2,1)} %all-gather.2.cloned.1.call-done, bf16[128,2048]{0,1:T(8,128)(2,1)S(1)} %bitcast.15, s32[]{:T(128)S(6)} %select_n.28), kind=kOutput, calls=%fused_computation.10 | convolution fusion | flops 536870912 | bytes 5505028 | tf_op jit(solution)/shard_map/dot_general | solution.py:22
  161.7 2.1 %collective-permute-done.1 = bf16[2048,1024]{1,0:T(8,128)(2,1)} collective-permute-done((bf16[2048,1024]{1,0:T(8,128)(2,1)}, bf16[2048,1024]{1,0:T(8,128)(2,1)}, u32[]{:S(2)}, u32[]{:S(2)}) %collective-permute-start.1) | collective-permute-done | bytes 4194336 | tf_op jit(solution)/shard_map/ppermute | solution.py:504
  163.8 4.7 %convolution_add_fusion = f32[128,2048]{1,0:T(8,128)} fusion(f32[128,2048]{1,0:T(8,128)S(1)} %fusion.2, bf16[2048,1024]{1,0:T(8,128)(2,1)} %collective-permute-done.1, bf16[128,2048]{0,1:T(8,128)(2,1)S(1)} %bitcast.16, s32[]{:T(128)S(6)} %select_n.29), kind=kOutput, calls=%fused_computation.2 | convolution fusion | flops 537133056 | bytes 6553604 | tf_op jit(solution)/shard_map/dot_general | solution.py:22
  (1 shorter events, 0.0 us)
Async XLA Ops:
  6.5 9.6 %copy-start = (bf16[2048,256]{1,0:T(8,128)(2,1)S(1)}, bf16[2048,256]{1,0:T(8,128)(2,1)}, u32[]{:S(2)}) copy-start(bf16[2048,256]{1,0:T(8,128)(2,1)} %param.5) | copy-start | bytes 3145732
  6.5 149.3 %all-gather.2.cloned.1.call-start = ((), (), s32[]{:S(2)}) async-start(), calls=%async_computation | async-start | bytes 4456448 | tf_op jit(solution)/shard_map/all_gather | solution.py:501
  7.6 7.8 %collective-permute-start = (bf16[128,1024]{1,0:T(8,128)(2,1)S(1)}, bf16[128,1024]{1,0:T(8,128)(2,1)S(1)}, u32[]{:S(2)}, u32[]{:S(2)}) collective-permute-start(bf16[128,1024]{1,0:T(8,128)(2,1)S(1)} %constant_dynamic-slice_fusion.1), channel_id=1, source_target_pairs={{0,0},{64,16},{128,32},{192,48},{16,64},{80,80},{144,96},{208,112}... | collective-permute-start | bytes 786440 | tf_op jit(solution)/shard_map/ppermute | solution.py:500
  15.4 0.7 copy-start.1
  22.1 54.9 %copy-start.2 = (f32[2048]{0:T(1024)S(1)}, f32[2048]{0:T(1024)}, u32[]{:S(2)}) copy-start(f32[2048]{0:T(1024)} %param.8) | copy-start | bytes 24580
  22.1 54.9 %copy-start.3 = (f32[2048]{0:T(1024)S(1)}, f32[2048]{0:T(1024)}, u32[]{:S(2)}) copy-start(f32[2048]{0:T(1024)} %param.9) | copy-start | bytes 24580
  155.8 7.9 %collective-permute-start.1 = (bf16[2048,1024]{1,0:T(8,128)(2,1)}, bf16[2048,1024]{1,0:T(8,128)(2,1)}, u32[]{:S(2)}, u32[]{:S(2)}) collective-permute-start(bf16[2048,1024]{1,0:T(8,128)(2,1)} %all-gather.2.cloned.1.call-done), channel_id=1, source_target_pairs={{0,64},{64,0},{128,192},{192,128},{1,65},{65,1},{129,193},{193,129... | collective-permute-start | bytes 12582920 | tf_op jit(solution)/shard_map/ppermute | solution.py:504
Sparse Core Ops, SparseCore 0:
  16.3 95.4 all-gather.1

commit v15 on v14

--- a/solution.py
+++ b/solution.py
@@ -348,18 +348,14 @@
     join.wait_send()
     join.wait_recv()
 
-    chunk = coll.shape[-1]
+    shapes = shapes_ref[...]
     parts = []
     for h in range(2):
-        for k in range(2):
-            acc = jnp.zeros((shapes_ref.shape[0], coll.shape[2]), jnp.float32)
-            for l in range(n):
-                block = jnp.where(core == k, coll[l, h], sib_coll[l, h])
-                acc = acc + lax.dot_general(
-                    shapes_ref[:, l * chunk:(l + 1) * chunk], block,
-                    (((1,), (1,)), ((), ())), preferred_element_type=jnp.float32,
-                )
-            parts.append(acc)
+        own, other = (
+            jnp.einsum("laj,lij->lai", shapes, blocks[:, h], preferred_element_type=jnp.float32).sum(0)
+            for blocks in (coll, sib_coll)
+        )
+        parts += [jnp.where(core == 0, own, other), jnp.where(core == 0, other, own)]
     wbuf[col] = jnp.concatenate(parts, axis=1).astype(wbuf.dtype)
 
     wpeer = lambda k: lax.rem(col + k, n_col)
@@ -377,6 +373,7 @@
     n, rows, width = x.shape
     n_col = sizes["pcol"]
     wshape = (n_col, mode_shapes.shape[0], 4 * rows)
+    by_chunk = mode_shapes.reshape(mode_shapes.shape[0], n, width).transpose(1, 0, 2)
     kernel = functools.partial(gram_weighted_kernel, axes=axes, factors=factor_table(sizes))
     return pl.pallas_call(
         kernel,
@@ -402,7 +399,7 @@
             pltpu.SemaphoreType.DMA((n_col,)),
         ],
         compiler_params=pltpu.CompilerParams(collective_id=103, has_side_effects=True),
-    )(x, mode_shapes)
+    )(x, by_chunk)
 
 
 def fused_sum(x, axes, sizes, over, add_across, kernel_id):

time: 176 us -> 176 us (level)
  local copies, waits for them, and re-layouts: 6.31 us -> 8.64 us
  Pallas kernels: 128 us -> 126 us
  transfers between devices with their start and end apart: 3 -> 3, of which waited for: 2 -> 2; matrix products, arithmetic and copies ran while one was open for 10% -> 11% of each run, Pallas kernels for 73% -> 72%
where the time goes in v15:
time: 176 us
  Pallas kernels  126 us (72%)
  matrix products  15.1 us (9%)
  between operations  13.6 us (8%)
  local copies, waits for them, and re-layouts  8.64 us (5%)
  waiting for transfers between devices  6.18 us (4%)
  starting transfers between devices  4.56 us (3%)
  other arithmetic  1.78 us (1%)
    pallas_call x1, Pallas kernels, gram_weighted(): pl.pallas_call(kernel, out_shape=jax.ShapeDtypeStruct(wshape, jnp.bfloat1...  74.3 us
    pallas_call x1, Pallas kernels, modal_sum(): pl.pallas_call(kernel, out_shape=jax.ShapeDtypeStruct((2,) + block, jnp.b...  51.6 us
    dot_general x3, matrix products, outer_rows(): lax.dot_general(left_rows, right_rows, (((1,), (1,)), ((), ())), preferre...  9.19 us
    dot_general x1, matrix products, body(): jnp.dot(modal_at_loads, factor_cols, preferred_element_type=jnp.float32)  5.86 us
    ppermute x1, waiting for transfers between devices, body(): panel_piece = lax.ppermute(send_half, ('prow', 'pcol'), swap)  4.04 us
    ppermute x1, starting transfers between devices, body(): panel_piece = lax.ppermute(send_half, ('prow', 'pcol'), swap)  3.77 us
  transfers between devices with their start and end apart: 3, of which 2 were waited for; matrix products, arithmetic and copies ran while one was open for 11% of the time, Pallas kernels for 72%

profile of v15, /device:TPU:39, one launch (start us, length us, event | category | flops | bytes accessed | tf_op | source)
XLA Modules:
  0.0 175.7 jit_solution(4918530505229535008)
XLA Ops:
  6.5 0.0 copy-start
  6.5 0.0 all-gather.2.cloned.1.call-start
  6.5 1.1 constant_dynamic-slice_fusion.1
  7.6 3.8 %collective-permute-start = (bf16[128,1024]{1,0:T(8,128)(2,1)S(1)}, bf16[128,1024]{1,0:T(8,128)(2,1)S(1)}, u32[]{:S(2)}, u32[]{:S(2)}) collective-permute-start(bf16[128,1024]{1,0:T(8,128)(2,1)S(1)} %constant_dynamic-slice_fusion.1), channel_id=1, source_target_pairs={{0,0},{64,16},{128,32},{192,48},{16,64},{80,80},{144,96},{208,112}... | collective-permute-start | bytes 786440 | tf_op jit(solution)/shard_map/ppermute | solution.py:497
  11.4 4.0 %collective-permute-done = bf16[128,1024]{1,0:T(8,128)(2,1)S(1)} collective-permute-done((bf16[128,1024]{1,0:T(8,128)(2,1)S(1)}, bf16[128,1024]{1,0:T(8,128)(2,1)S(1)}, u32[]{:S(2)}, u32[]{:S(2)}) %collective-permute-start) | collective-permute-done | bytes 262176 | tf_op jit(solution)/shard_map/ppermute | solution.py:497
  15.4 0.0 copy-start.1
  15.4 0.7 copy-done.1
  16.1 0.0 all-gather.2.cloned.1.call-update
  16.2 1.3 copy.8
  17.5 0.0 copy-done
  17.5 5.9 %fusion.12 = f32[2048,256]{1,0:T(8,128)S(1)} fusion(bf16[2048,2048]{1,0:T(8,128)(2,1)} %param.6, bf16[2048,256]{1,0:T(8,128)(2,1)S(1)} %copy-done), kind=kOutput, calls=%fused_computation.25 | convolution fusion | flops 2147483648 | bytes 11534336 | tf_op jit(solution)/shard_map/dot_general | solution.py:476
  23.4 0.0 copy-start.2
  23.4 0.0 copy-start.3
  23.4 0.9 dynamic-slice_convert_fusion.theirs_ref
  24.3 1.0 constant_dynamic-slice_fusion.mine_ref
  25.3 51.6 %shard_map.55 = bf16[2,4,256,256]{3,2,1,0:T(8,128)(2,1)} custom-call(f32[1024,256]{1,0:T(8,128)} %constant_dynamic-slice_fusion.mine_ref, bf16[1024,256]{1,0:T(8,128)(2,1)} %dynamic-slice_convert_fusion.theirs_ref), custom_call_target="tpu_custom_call" | custom-call | tf_op jit(solution)/shard_map/pallas_call | solution.py:249
  77.0 0.0 copy-done.2
  77.0 0.0 copy-done.3
  77.0 1.8 %fusion = (bf16[2048,256]{1,0:T(8,128)(2,1)S(1)}, bf16[2048,256]{1,0:T(8,128)(2,1)S(1)}) fusion(bf16[2,4,256,256]{3,2,1,0:T(8,128)(2,1)} %shard_map.55, f32[2048]{0:T(1024)S(1)} %get-tuple-element.11, f32[2048]{0:T(1024)S(1)} %get-tuple-element.12), kind=kLoop, calls=%fused_computation.7 | loop fusion | flops 2621440 | bytes 3162112 | tf_op jit(solution)/shard_map/convert_element_type | solution.py:485
  78.8 0.8 convolution_convert_fusion
  79.6 0.3 copy.6
  79.9 1.0 copy.7
  80.9 1.0 copy.9
  81.9 74.3 %shard_map.56 = bf16[4,128,512]{2,1,0:T(8,128)(2,1)} custom-call(bf16[16,128,128]{2,1,0:T(8,128)(2,1)} %bitcast.15, bf16[16,128,128]{2,1,0:T(8,128)(2,1)} %bitcast.16), custom_call_target="tpu_custom_call" | custom-call | tf_op jit(solution)/shard_map/pallas_call | solution.py:378
  156.2 0.0 all-gather.2.cloned.1.call-done
  156.2 0.8 collective-permute-start.1
  157.0 1.3 copy.10
  158.3 3.7 %fusion.2 = f32[128,2048]{1,0:T(8,128)S(1)} fusion(bf16[2048,1024]{1,0:T(8,128)(2,1)} %all-gather.2.cloned.1.call-done, bf16[128,2048]{0,1:T(8,128)(2,1)S(1)} %bitcast.19, s32[]{:T(128)S(6)} %select_n.28), kind=kOutput, calls=%fused_computation.10 | convolution fusion | flops 536870912 | bytes 5505028 | tf_op jit(solution)/shard_map/dot_general | solution.py:22
  162.0 2.1 %collective-permute-done.1 = bf16[2048,1024]{1,0:T(8,128)(2,1)} collective-permute-done((bf16[2048,1024]{1,0:T(8,128)(2,1)}, bf16[2048,1024]{1,0:T(8,128)(2,1)}, u32[]{:S(2)}, u32[]{:S(2)}) %collective-permute-start.1) | collective-permute-done | bytes 4194336 | tf_op jit(solution)/shard_map/ppermute | solution.py:501
  164.1 4.7 %convolution_add_fusion = f32[128,2048]{1,0:T(8,128)} fusion(f32[128,2048]{1,0:T(8,128)S(1)} %fusion.2, bf16[2048,1024]{1,0:T(8,128)(2,1)} %collective-permute-done.1, bf16[128,2048]{0,1:T(8,128)(2,1)S(1)} %bitcast.20, s32[]{:T(128)S(6)} %select_n.29), kind=kOutput, calls=%fused_computation.2 | convolution fusion | flops 537133056 | bytes 6553604 | tf_op jit(solution)/shard_map/dot_general | solution.py:22
  (1 shorter events, 0.0 us)
Async XLA Ops:
  6.5 11.0 %copy-start = (bf16[2048,256]{1,0:T(8,128)(2,1)S(1)}, bf16[2048,256]{1,0:T(8,128)(2,1)}, u32[]{:S(2)}) copy-start(bf16[2048,256]{1,0:T(8,128)(2,1)} %param.5) | copy-start | bytes 3145732
  6.5 149.7 %all-gather.2.cloned.1.call-start = ((), (), s32[]{:S(2)}) async-start(), calls=%async_computation | async-start | bytes 4456448 | tf_op jit(solution)/shard_map/all_gather | solution.py:498
  7.6 7.8 %collective-permute-start = (bf16[128,1024]{1,0:T(8,128)(2,1)S(1)}, bf16[128,1024]{1,0:T(8,128)(2,1)S(1)}, u32[]{:S(2)}, u32[]{:S(2)}) collective-permute-start(bf16[128,1024]{1,0:T(8,128)(2,1)S(1)} %constant_dynamic-slice_fusion.1), channel_id=1, source_target_pairs={{0,0},{64,16},{128,32},{192,48},{16,64},{80,80},{144,96},{208,112}... | collective-permute-start | bytes 786440 | tf_op jit(solution)/shard_map/ppermute | solution.py:497
  15.4 0.7 copy-start.1
  23.4 53.6 %copy-start.2 = (f32[2048]{0:T(1024)S(1)}, f32[2048]{0:T(1024)}, u32[]{:S(2)}) copy-start(f32[2048]{0:T(1024)} %param.8) | copy-start | bytes 24580
  23.4 53.6 %copy-start.3 = (f32[2048]{0:T(1024)S(1)}, f32[2048]{0:T(1024)}, u32[]{:S(2)}) copy-start(f32[2048]{0:T(1024)} %param.9) | copy-start | bytes 24580
  156.2 7.9 %collective-permute-start.1 = (bf16[2048,1024]{1,0:T(8,128)(2,1)}, bf16[2048,1024]{1,0:T(8,128)(2,1)}, u32[]{:S(2)}, u32[]{:S(2)}) collective-permute-start(bf16[2048,1024]{1,0:T(8,128)(2,1)} %all-gather.2.cloned.1.call-done), channel_id=1, source_target_pairs={{0,64},{64,0},{128,192},{192,128},{1,65},{65,1},{129,193},{193,129... | collective-permute-start | bytes 12582920 | tf_op jit(solution)/shard_map/ppermute | solution.py:501
Sparse Core Ops, SparseCore 0:
  16.3 95.1 all-gather.1

commit v16 on v14

--- a/solution.py
+++ b/solution.py
@@ -370,7 +370,9 @@
         step(wbuf.at[col], wbuf.at[col], k, device("pcol", wpeer(k)), (send_e, recv_e)).wait_send()
     for k in range(1, n_col):
         step(wbuf.at[col], wbuf.at[wsender(k)], k, device("pcol", wsender(k)), (send_e, recv_e)).wait_recv()
-    out_ref[...] = wbuf[...]
+    width_w = wbuf.shape[2]
+    for c in range(n_col):
+        out_ref[:, c * width_w:(c + 1) * width_w] = wbuf[c]
 
 
 def gram_weighted(x, mode_shapes, axes, sizes):
@@ -380,7 +382,7 @@
     kernel = functools.partial(gram_weighted_kernel, axes=axes, factors=factor_table(sizes))
     return pl.pallas_call(
         kernel,
-        out_shape=jax.ShapeDtypeStruct(wshape, jnp.bfloat16),
+        out_shape=jax.ShapeDtypeStruct((wshape[1], n_col * wshape[2]), jnp.bfloat16),
         in_specs=[pl.BlockSpec(memory_space=pltpu.VMEM)] * 2,
         out_specs=pl.BlockSpec(memory_space=pltpu.VMEM),
         scratch_shapes=[
@@ -476,11 +478,12 @@
         modes = modal_at_loads.shape[0]
         block = modes // (n_row * n_col)
         row, col = lax.axis_index("prow"), lax.axis_index("pcol")
-        partial_load = jnp.dot(modal_at_loads, factor_cols, preferred_element_type=jnp.float32)
-        width = partial_load.shape[1]
+        width = factor_cols.shape[1]
         core = row % 2
-        mine = lax.dynamic_slice_in_dim(partial_load, core * (modes // 2), modes // 2, 0)
-        theirs = lax.dynamic_slice_in_dim(partial_load, (1 - core) * (modes // 2), modes // 2, 0)
+        own_modes = lax.dynamic_slice_in_dim(modal_at_loads, core * (modes // 2), modes // 2, 0)
+        sib_modes = lax.dynamic_slice_in_dim(modal_at_loads, (1 - core) * (modes // 2), modes // 2, 0)
+        mine = jnp.dot(own_modes, factor_cols, preferred_element_type=jnp.float32)
+        theirs = jnp.dot(sib_modes, factor_cols, preferred_element_type=jnp.float32)
         modal_load = modal_sum(mine, theirs.astype(jnp.bfloat16), axes, sizes).reshape(modes, width)
         modal_wide = modal_load.astype(jnp.float32)
         pseudo = jnp.concatenate(
@@ -499,10 +502,9 @@
         send_half = lax.dynamic_slice_in_dim(mode_shapes, (col % 2) * half, half, 1)
         panel_piece = lax.ppermute(send_half, ("prow", "pcol"), swap)
         panel_mine = lax.all_gather(panel_piece, "pl", axis=0, tiled=True)
-        weighted_all = gram_weighted(by_chunk, mode_shapes, axes, sizes)
-        panel_mine, weighted_all = lax.optimization_barrier((panel_mine, weighted_all))
+        weighted = gram_weighted(by_chunk, mode_shapes, axes, sizes)
+        panel_mine, weighted = lax.optimization_barrier((panel_mine, weighted))
         panel_other = lax.ppermute(panel_mine, "prow", sibling)
-        weighted = weighted_all.transpose(1, 0, 2).reshape(mode_shapes.shape[0], modes)
         weighted_mine = lax.dynamic_slice_in_dim(weighted, core * half, half, 1)
         weighted_other = lax.dynamic_slice_in_dim(weighted, (1 - core) * half, half, 1)
         return outer_rows(weighted_other, panel_other) + outer_rows(weighted_mine, panel_mine)

time: 176 us -> 174 us (0.989)
  local copies, waits for them, and re-layouts: 6.31 us -> 3.2 us
    dot_general x3, matrix products: 9.19 us -> 7.08 us  [outer_rows(): lax.dot_general(left_rows, right_rows, (((1,), (1,)), ((), ())), preferre...]
    dot_general x1 -> x2, matrix products: 5.86 us -> 6.69 us  [the longest x1 4.57 us: body(): mine = jnp.dot(own_modes, factor_cols, preferred_element_type=jnp.float32)]
  transfers between devices with their start and end apart: 3 -> 3, of which waited for: 2 -> 2; matrix products, arithmetic and copies ran while one was open for 10% -> 8% of each run, Pallas kernels for 73% -> 75%
where the time goes in v16:
time: 174 us; the launch traced here: 173 us
  Pallas kernels  129 us (74%)
  matrix products  13.8 us (8%)
  between operations  13.5 us (8%)
  waiting for transfers between devices  7.28 us (4%)
  starting transfers between devices  4.57 us (3%)
  local copies, waits for them, and re-layouts  3.2 us (2%)
  other arithmetic  1.79 us (1%)
    pallas_call x1, Pallas kernels, gram_weighted(): pl.pallas_call(kernel, out_shape=jax.ShapeDtypeStruct((wshape[1], n_col *...  75.2 us
    pallas_call x1, Pallas kernels, modal_sum(): pl.pallas_call(kernel, out_shape=jax.ShapeDtypeStruct((2,) + block, jnp.b...  53.9 us
    dot_general x3, matrix products, outer_rows(): lax.dot_general(left_rows, right_rows, (((1,), (1,)), ((), ())), preferre...  7.08 us
    dot_general x1, matrix products, body(): mine = jnp.dot(own_modes, factor_cols, preferred_element_type=jnp.float32)  4.57 us
    ppermute x1, waiting for transfers between devices, body(): panel_piece = lax.ppermute(send_half, ('prow', 'pcol'), swap)  4.04 us
    ppermute x1, starting transfers between devices, body(): panel_piece = lax.ppermute(send_half, ('prow', 'pcol'), swap)  3.77 us
  transfers between devices with their start and end apart: 3, of which 2 were waited for; matrix products, arithmetic and copies ran while one was open for 8% of the time, Pallas kernels for 75%

profile of v16, /device:TPU:39, one launch (start us, length us, event | category | flops | bytes accessed | tf_op | source)
XLA Modules:
  0.0 173.3 jit_solution(14720992952641260667)
XLA Ops:
  6.5 0.0 copy-start
  6.5 0.0 all-gather.2.cloned.1.call-start
  6.5 1.1 constant_dynamic-slice_fusion
  7.6 3.8 %collective-permute-start = (bf16[128,1024]{1,0:T(8,128)(2,1)S(1)}, bf16[128,1024]{1,0:T(8,128)(2,1)S(1)}, u32[]{:S(2)}, u32[]{:S(2)}) collective-permute-start(bf16[128,1024]{1,0:T(8,128)(2,1)S(1)} %constant_dynamic-slice_fusion), channel_id=1, source_target_pairs={{0,0},{64,16},{128,32},{192,48},{16,64},{80,80},{144,96},{208,112}... | collective-permute-start | bytes 786440 | tf_op jit(solution)/shard_map/ppermute | solution.py:503
  11.4 4.0 %collective-permute-done = bf16[128,1024]{1,0:T(8,128)(2,1)S(1)} collective-permute-done((bf16[128,1024]{1,0:T(8,128)(2,1)S(1)}, bf16[128,1024]{1,0:T(8,128)(2,1)S(1)}, u32[]{:S(2)}, u32[]{:S(2)}) %collective-permute-start) | collective-permute-done | bytes 262176 | tf_op jit(solution)/shard_map/ppermute | solution.py:503
  15.4 0.0 copy-start.2
  15.4 0.7 copy-done.2
  16.1 0.0 all-gather.2.cloned.1.call-update
  16.2 0.0 copy-done
  16.2 0.0 copy-start.5
  16.2 4.6 %fusion.2.mine_ref = f32[1024,256]{1,0:T(8,128)} fusion(bf16[2048,256]{1,0:T(8,128)(2,1)S(1)} %copy-done, bf16[2048,2048]{1,0:T(8,128)(2,1)} %param.6, s32[]{:T(128)S(6)} %select_n.28), kind=kOutput, calls=%fused_computation.2 | convolution fusion | flops 1073741824 | bytes 6291460 | tf_op jit(solution)/shard_map/dot_general | solution.py:485
  20.8 0.1 copy-done.5
  20.9 0.0 copy-start.3
  20.9 0.0 copy-start.4
  20.9 2.1 %fusion.6.theirs_ref = bf16[1024,256]{1,0:T(8,128)(2,1)} fusion(bf16[2048,256]{1,0:T(8,128)(2,1)S(1)} %copy-done, bf16[2048,2048]{1,0:T(8,128)(2,1)S(1)} %copy-done.5, s32[]{:T(128)S(6)} %select_n.29), kind=kOutput, calls=%fused_computation.13 | convolution fusion | flops 1074003968 | bytes 5767172 | tf_op jit(solution)/shard_map/dot_general | solution.py:486
  23.0 53.9 %shard_map.55 = bf16[2,4,256,256]{3,2,1,0:T(8,128)(2,1)} custom-call(f32[1024,256]{1,0:T(8,128)} %fusion.2.mine_ref, bf16[1024,256]{1,0:T(8,128)(2,1)} %fusion.6.theirs_ref), custom_call_target="tpu_custom_call" | custom-call | tf_op jit(solution)/shard_map/pallas_call | solution.py:249
  76.9 0.0 copy-done.3
  76.9 0.0 copy-done.4
  77.0 1.8 %fusion.4 = (bf16[2048,256]{1,0:T(8,128)(2,1)S(1)}, bf16[2048,256]{1,0:T(8,128)(2,1)S(1)}) fusion(bf16[2,4,256,256]{3,2,1,0:T(8,128)(2,1)} %shard_map.55, f32[2048]{0:T(1024)S(1)} %get-tuple-element.11, f32[2048]{0:T(1024)S(1)} %get-tuple-element.12), kind=kLoop, calls=%fused_computation.11 | loop fusion | flops 2621440 | bytes 3162112 | tf_op jit(solution)/shard_map/convert_element_type | solution.py:491
  78.8 0.8 convolution_convert_fusion
  79.6 0.3 copy.6
  79.8 1.0 copy.7
  80.9 75.2 %shard_map.56 = bf16[128,2048]{1,0:T(8,128)(2,1)} custom-call(bf16[16,128,128]{2,1,0:T(8,128)(2,1)} %bitcast.10, bf16[128,2048]{1,0:T(8,128)(2,1)} %shapes_ref.1), custom_call_target="tpu_custom_call" | custom-call | tf_op jit(solution)/shard_map/pallas_call | solution.py:383
  156.1 0.0 copy-start.1
  156.1 0.0 all-gather.2.cloned.1.call-done
  156.1 0.8 collective-permute-start.1
  157.0 3.8 %fusion.9 = f32[128,2048]{1,0:T(8,128)S(1)} fusion(bf16[2048,1024]{1,0:T(8,128)(2,1)} %all-gather.2.cloned.1.call-done, bf16[128,2048]{1,0:T(8,128)(2,1)} %shard_map.56, s32[]{:T(128)S(6)} %select_n.28), kind=kOutput, calls=%fused_computation.14 | convolution fusion | flops 536870912 | bytes 5505028 | tf_op jit(solution)/shard_map/dot_general | solution.py:22
  160.7 3.2 %collective-permute-done.1 = bf16[2048,1024]{1,0:T(8,128)(2,1)S(1)} collective-permute-done((bf16[2048,1024]{1,0:T(8,128)(2,1)}, bf16[2048,1024]{1,0:T(8,128)(2,1)S(1)}, u32[]{:S(2)}, u32[]{:S(2)}) %collective-permute-start.1) | collective-permute-done | bytes 4194336 | tf_op jit(solution)/shard_map/ppermute | solution.py:507
  164.0 0.0 copy-done.1
  164.0 2.5 %convolution_add_fusion = f32[128,2048]{1,0:T(8,128)} fusion(f32[128,2048]{1,0:T(8,128)S(1)} %fusion.9, bf16[2048,1024]{1,0:T(8,128)(2,1)S(1)} %collective-permute-done.1, bf16[128,2048]{1,0:T(8,128)(2,1)S(1)} %copy-done.1, s32[]{:T(128)S(6)} %select_n.29), kind=kOutput, calls=%fused_computation.6 | convolution fusion | flops 537133056 | bytes 6553604 | tf_op jit(solution)/shard_map/dot_general | solution.py:22
  (1 shorter events, 0.0 us)
Async XLA Ops:
  6.5 9.6 %copy-start = (bf16[2048,256]{1,0:T(8,128)(2,1)S(1)}, bf16[2048,256]{1,0:T(8,128)(2,1)}, u32[]{:S(2)}) copy-start(bf16[2048,256]{1,0:T(8,128)(2,1)} %param.5) | copy-start | bytes 3145732
  6.5 149.6 %all-gather.2.cloned.1.call-start = ((), (), s32[]{:S(2)}) async-start(), calls=%async_computation | async-start | bytes 4456448 | tf_op jit(solution)/shard_map/all_gather | solution.py:504
  7.6 7.8 %collective-permute-start = (bf16[128,1024]{1,0:T(8,128)(2,1)S(1)}, bf16[128,1024]{1,0:T(8,128)(2,1)S(1)}, u32[]{:S(2)}, u32[]{:S(2)}) collective-permute-start(bf16[128,1024]{1,0:T(8,128)(2,1)S(1)} %constant_dynamic-slice_fusion), channel_id=1, source_target_pairs={{0,0},{64,16},{128,32},{192,48},{16,64},{80,80},{144,96},{208,112}... | collective-permute-start | bytes 786440 | tf_op jit(solution)/shard_map/ppermute | solution.py:503
  15.4 0.7 copy-start.2
  16.2 4.7 %copy-start.5 = (bf16[2048,2048]{1,0:T(8,128)(2,1)S(1)}, bf16[2048,2048]{1,0:T(8,128)(2,1)}, u32[]{:S(2)}) copy-start(bf16[2048,2048]{1,0:T(8,128)(2,1)} %param.6) | copy-start | bytes 25165828
  20.9 56.0 %copy-start.3 = (f32[2048]{0:T(1024)S(1)}, f32[2048]{0:T(1024)}, u32[]{:S(2)}) copy-start(f32[2048]{0:T(1024)} %param.8) | copy-start | bytes 24580
  20.9 56.0 %copy-start.4 = (f32[2048]{0:T(1024)S(1)}, f32[2048]{0:T(1024)}, u32[]{:S(2)}) copy-start(f32[2048]{0:T(1024)} %param.9) | copy-start | bytes 24580
  156.1 7.8 %copy-start.1 = (bf16[128,2048]{1,0:T(8,128)(2,1)S(1)}, bf16[128,2048]{1,0:T(8,128)(2,1)}, u32[]{:S(2)}) copy-start(bf16[128,2048]{1,0:T(8,128)(2,1)} %shard_map.56) | copy-start | bytes 1572868
  156.1 7.8 %collective-permute-start.1 = (bf16[2048,1024]{1,0:T(8,128)(2,1)}, bf16[2048,1024]{1,0:T(8,128)(2,1)S(1)}, u32[]{:S(2)}, u32[]{:S(2)}) collective-permute-start(bf16[2048,1024]{1,0:T(8,128)(2,1)} %all-gather.2.cloned.1.call-done), channel_id=1, source_target_pairs={{0,64},{64,0},{128,192},{192,128},{1,65},{65,1},{129,193},{193,129... | collective-permute-start | bytes 12582920 | tf_op jit(solution)/shard_map/ppermute | solution.py:507
Sparse Core Ops, SparseCore 0:
  16.3 94.9 all-gather.1

commit v17 on v16

--- a/solution.py
+++ b/solution.py
@@ -343,23 +343,26 @@
     for k in range(1, n):
         step(coll.at[me], coll.at[sender(k)], k, device("pl", sender(k)), (send_c, recv_c)).wait_recv()
 
+    chunk = coll.shape[-1]
+
+    def weighted_block(blocks, h):
+        acc = jnp.zeros((shapes_ref.shape[0], blocks.shape[2]), jnp.float32)
+        for l in range(n):
+            acc = acc + lax.dot_general(
+                shapes_ref[:, l * chunk:(l + 1) * chunk], blocks[l, h],
+                (((1,), (1,)), ((), ())), preferred_element_type=jnp.float32,
+            )
+        return acc
+
     join = one(coll, sib_coll, sibling, send_d, recv_d)
     join.start()
+    own = [weighted_block(coll, h) for h in range(2)]
     join.wait_send()
     join.wait_recv()
-
-    chunk = coll.shape[-1]
+    other = [weighted_block(sib_coll, h) for h in range(2)]
     parts = []
     for h in range(2):
-        for k in range(2):
-            acc = jnp.zeros((shapes_ref.shape[0], coll.shape[2]), jnp.float32)
-            for l in range(n):
-                block = jnp.where(core == k, coll[l, h], sib_coll[l, h])
-                acc = acc + lax.dot_general(
-                    shapes_ref[:, l * chunk:(l + 1) * chunk], block,
-                    (((1,), (1,)), ((), ())), preferred_element_type=jnp.float32,
-                )
-            parts.append(acc)
+        parts += [jnp.where(core == 0, own[h], other[h]), jnp.where(core == 0, other[h], own[h])]
     wbuf[col] = jnp.concatenate(parts, axis=1).astype(wbuf.dtype)
 
     wpeer = lambda k: lax.rem(col + k, n_col)

time: 174 us -> 173 us (level)
  transfers between devices with their start and end apart: 3 -> 3, of which waited for: 2 -> 2; matrix products, arithmetic and copies ran while one was open for 8% -> 8% of each run, Pallas kernels for 75% -> 74%
where the time goes in v17:
time: 173 us
  Pallas kernels  128 us (74%)
  matrix products  13.8 us (8%)
  between operations  13.5 us (8%)
  waiting for transfers between devices  7.29 us (4%)
  starting transfers between devices  4.57 us (3%)
  local copies, waits for them, and re-layouts  3.2 us (2%)
  other arithmetic  1.79 us (1%)
    pallas_call x1, Pallas kernels, gram_weighted(): pl.pallas_call(kernel, out_shape=jax.ShapeDtypeStruct((wshape[1], n_col *...  74.5 us
    pallas_call x1, Pallas kernels, modal_sum(): pl.pallas_call(kernel, out_shape=jax.ShapeDtypeStruct((2,) + block, jnp.b...  53.9 us
    dot_general x3, matrix products, outer_rows(): lax.dot_general(left_rows, right_rows, (((1,), (1,)), ((), ())), preferre...  7.07 us
    dot_general x1, matrix products, body(): mine = jnp.dot(own_modes, factor_cols, preferred_element_type=jnp.float32)  4.57 us
    ppermute x1, waiting for transfers between devices, body(): panel_piece = lax.ppermute(send_half, ('prow', 'pcol'), swap)  4.04 us
    ppermute x1, starting transfers between devices, body(): panel_piece = lax.ppermute(send_half, ('prow', 'pcol'), swap)  3.77 us
  transfers between devices with their start and end apart: 3, of which 2 were waited for; matrix products, arithmetic and copies ran while one was open for 8% of the time, Pallas kernels for 74%

profile of v17, /device:TPU:39, one launch (start us, length us, event | category | flops | bytes accessed | tf_op | source)
XLA Modules:
  0.0 172.6 jit_solution(6763378121735676553)
XLA Ops:
  6.5 0.0 copy-start
  6.5 0.0 all-gather.2.cloned.1.call-start
  6.5 1.1 constant_dynamic-slice_fusion
  7.6 3.8 %collective-permute-start = (bf16[128,1024]{1,0:T(8,128)(2,1)S(1)}, bf16[128,1024]{1,0:T(8,128)(2,1)S(1)}, u32[]{:S(2)}, u32[]{:S(2)}) collective-permute-start(bf16[128,1024]{1,0:T(8,128)(2,1)S(1)} %constant_dynamic-slice_fusion), channel_id=1, source_target_pairs={{0,0},{64,16},{128,32},{192,48},{16,64},{80,80},{144,96},{208,112}... | collective-permute-start | bytes 786440 | tf_op jit(solution)/shard_map/ppermute | solution.py:506
  11.4 4.0 %collective-permute-done = bf16[128,1024]{1,0:T(8,128)(2,1)S(1)} collective-permute-done((bf16[128,1024]{1,0:T(8,128)(2,1)S(1)}, bf16[128,1024]{1,0:T(8,128)(2,1)S(1)}, u32[]{:S(2)}, u32[]{:S(2)}) %collective-permute-start) | collective-permute-done | bytes 262176 | tf_op jit(solution)/shard_map/ppermute | solution.py:506
  15.4 0.0 copy-start.2
  15.4 0.7 copy-done.2
  16.1 0.0 all-gather.2.cloned.1.call-update
  16.2 0.0 copy-done
  16.2 0.0 copy-start.5
  16.2 4.6 %fusion.2.mine_ref = f32[1024,256]{1,0:T(8,128)} fusion(bf16[2048,256]{1,0:T(8,128)(2,1)S(1)} %copy-done, bf16[2048,2048]{1,0:T(8,128)(2,1)} %param.6, s32[]{:T(128)S(6)} %select_n.28), kind=kOutput, calls=%fused_computation.2 | convolution fusion | flops 1073741824 | bytes 6291460 | tf_op jit(solution)/shard_map/dot_general | solution.py:488
  20.8 0.1 copy-done.5
  20.9 0.0 copy-start.3
  20.9 0.0 copy-start.4
  20.9 2.1 %fusion.6.theirs_ref = bf16[1024,256]{1,0:T(8,128)(2,1)} fusion(bf16[2048,256]{1,0:T(8,128)(2,1)S(1)} %copy-done, bf16[2048,2048]{1,0:T(8,128)(2,1)S(1)} %copy-done.5, s32[]{:T(128)S(6)} %select_n.29), kind=kOutput, calls=%fused_computation.13 | convolution fusion | flops 1074003968 | bytes 5767172 | tf_op jit(solution)/shard_map/dot_general | solution.py:489
  23.0 53.9 %shard_map.55 = bf16[2,4,256,256]{3,2,1,0:T(8,128)(2,1)} custom-call(f32[1024,256]{1,0:T(8,128)} %fusion.2.mine_ref, bf16[1024,256]{1,0:T(8,128)(2,1)} %fusion.6.theirs_ref), custom_call_target="tpu_custom_call" | custom-call | tf_op jit(solution)/shard_map/pallas_call | solution.py:249
  76.9 0.0 copy-done.3
  76.9 0.0 copy-done.4
  77.0 1.8 %fusion.4 = (bf16[2048,256]{1,0:T(8,128)(2,1)S(1)}, bf16[2048,256]{1,0:T(8,128)(2,1)S(1)}) fusion(bf16[2,4,256,256]{3,2,1,0:T(8,128)(2,1)} %shard_map.55, f32[2048]{0:T(1024)S(1)} %get-tuple-element.11, f32[2048]{0:T(1024)S(1)} %get-tuple-element.12), kind=kLoop, calls=%fused_computation.11 | loop fusion | flops 2621440 | bytes 3162112 | tf_op jit(solution)/shard_map/convert_element_type | solution.py:494
  78.8 0.8 convolution_convert_fusion
  79.6 0.3 copy.6
  79.8 1.0 copy.7
  80.9 74.5 %shard_map.56 = bf16[128,2048]{1,0:T(8,128)(2,1)} custom-call(bf16[16,128,128]{2,1,0:T(8,128)(2,1)} %bitcast.10, bf16[128,2048]{1,0:T(8,128)(2,1)} %shapes_ref.1), custom_call_target="tpu_custom_call" | custom-call | tf_op jit(solution)/shard_map/pallas_call | solution.py:386
  155.4 0.0 copy-start.1
  155.4 0.0 all-gather.2.cloned.1.call-done
  155.4 0.8 collective-permute-start.1
  156.2 3.8 %fusion.9 = f32[128,2048]{1,0:T(8,128)S(1)} fusion(bf16[2048,1024]{1,0:T(8,128)(2,1)} %all-gather.2.cloned.1.call-done, bf16[128,2048]{1,0:T(8,128)(2,1)} %shard_map.56, s32[]{:T(128)S(6)} %select_n.28), kind=kOutput, calls=%fused_computation.14 | convolution fusion | flops 536870912 | bytes 5505028 | tf_op jit(solution)/shard_map/dot_general | solution.py:22
  160.0 3.2 %collective-permute-done.1 = bf16[2048,1024]{1,0:T(8,128)(2,1)S(1)} collective-permute-done((bf16[2048,1024]{1,0:T(8,128)(2,1)}, bf16[2048,1024]{1,0:T(8,128)(2,1)S(1)}, u32[]{:S(2)}, u32[]{:S(2)}) %collective-permute-start.1) | collective-permute-done | bytes 4194336 | tf_op jit(solution)/shard_map/ppermute | solution.py:510
  163.2 0.0 copy-done.1
  163.2 2.5 %convolution_add_fusion = f32[128,2048]{1,0:T(8,128)} fusion(f32[128,2048]{1,0:T(8,128)S(1)} %fusion.9, bf16[2048,1024]{1,0:T(8,128)(2,1)S(1)} %collective-permute-done.1, bf16[128,2048]{1,0:T(8,128)(2,1)S(1)} %copy-done.1, s32[]{:T(128)S(6)} %select_n.29), kind=kOutput, calls=%fused_computation.6 | convolution fusion | flops 537133056 | bytes 6553604 | tf_op jit(solution)/shard_map/dot_general | solution.py:22
  (1 shorter events, 0.0 us)
Async XLA Ops:
  6.5 9.6 %copy-start = (bf16[2048,256]{1,0:T(8,128)(2,1)S(1)}, bf16[2048,256]{1,0:T(8,128)(2,1)}, u32[]{:S(2)}) copy-start(bf16[2048,256]{1,0:T(8,128)(2,1)} %param.5) | copy-start | bytes 3145732
  6.5 148.9 %all-gather.2.cloned.1.call-start = ((), (), s32[]{:S(2)}) async-start(), calls=%async_computation | async-start | bytes 4456448 | tf_op jit(solution)/shard_map/all_gather | solution.py:507
  7.6 7.8 %collective-permute-start = (bf16[128,1024]{1,0:T(8,128)(2,1)S(1)}, bf16[128,1024]{1,0:T(8,128)(2,1)S(1)}, u32[]{:S(2)}, u32[]{:S(2)}) collective-permute-start(bf16[128,1024]{1,0:T(8,128)(2,1)S(1)} %constant_dynamic-slice_fusion), channel_id=1, source_target_pairs={{0,0},{64,16},{128,32},{192,48},{16,64},{80,80},{144,96},{208,112}... | collective-permute-start | bytes 786440 | tf_op jit(solution)/shard_map/ppermute | solution.py:506
  15.4 0.7 copy-start.2
  16.2 4.7 %copy-start.5 = (bf16[2048,2048]{1,0:T(8,128)(2,1)S(1)}, bf16[2048,2048]{1,0:T(8,128)(2,1)}, u32[]{:S(2)}) copy-start(bf16[2048,2048]{1,0:T(8,128)(2,1)} %param.6) | copy-start | bytes 25165828
  20.9 56.0 %copy-start.3 = (f32[2048]{0:T(1024)S(1)}, f32[2048]{0:T(1024)}, u32[]{:S(2)}) copy-start(f32[2048]{0:T(1024)} %param.8) | copy-start | bytes 24580
  20.9 56.0 %copy-start.4 = (f32[2048]{0:T(1024)S(1)}, f32[2048]{0:T(1024)}, u32[]{:S(2)}) copy-start(f32[2048]{0:T(1024)} %param.9) | copy-start | bytes 24580
  155.4 7.8 %copy-start.1 = (bf16[128,2048]{1,0:T(8,128)(2,1)S(1)}, bf16[128,2048]{1,0:T(8,128)(2,1)}, u32[]{:S(2)}) copy-start(bf16[128,2048]{1,0:T(8,128)(2,1)} %shard_map.56) | copy-start | bytes 1572868
  155.4 7.8 %collective-permute-start.1 = (bf16[2048,1024]{1,0:T(8,128)(2,1)}, bf16[2048,1024]{1,0:T(8,128)(2,1)S(1)}, u32[]{:S(2)}, u32[]{:S(2)}) collective-permute-start(bf16[2048,1024]{1,0:T(8,128)(2,1)} %all-gather.2.cloned.1.call-done), channel_id=1, source_target_pairs={{0,64},{64,0},{128,192},{192,128},{1,65},{65,1},{129,193},{193,129... | collective-permute-start | bytes 12582920 | tf_op jit(solution)/shard_map/ppermute | solution.py:510
Sparse Core Ops, SparseCore 0:
  16.3 94.9 all-gather.1

commit v18 on v17

--- a/solution.py
+++ b/solution.py
@@ -274,9 +274,9 @@
     )(mine, theirs)
 
 
-def gram_weighted_kernel(x_ref, shapes_ref, out_ref, got, coll, sib_coll, part_out, part_in, wbuf,
-                         send_a, recv_a, send_b, recv_b, send_c, recv_c, send_d, recv_d, send_e,
-                         recv_e, *, axes, factors):
+def gram_weighted_kernel(own_ref, pseudo_ref, shapes_ref, out_ref, x_ref, got, coll, sib_coll,
+                         part_out, part_in, wbuf, send_a, recv_a, send_b, recv_b, send_c, recv_c,
+                         send_d, recv_d, send_e, recv_e, *, axes, factors):
     coords = {a: lax.axis_index(a) for a in axes}
 
     def value(f):
@@ -304,6 +304,13 @@
             src_ref=src, dst_ref=dst, send_sem=send_sem, recv_sem=recv_sem,
             device_id=to, device_id_type=MESH,
         )
+
+    partial = lax.dot_general(
+        own_ref[...], pseudo_ref[...], (((1,), (1,)), ((), ())), preferred_element_type=jnp.float32
+    ).astype(x_ref.dtype)
+    width_x = x_ref.shape[2]
+    for l in range(n):
+        x_ref[l] = partial[:, l * width_x:(l + 1) * width_x]
 
     barrier = pltpu.get_barrier_semaphore()
     for k in range(1, n):
@@ -378,17 +385,20 @@
         out_ref[:, c * width_w:(c + 1) * width_w] = wbuf[c]
 
 
-def gram_weighted(x, mode_shapes, axes, sizes):
-    n, rows, width = x.shape
+def gram_weighted(own_pseudo, pseudo, mode_shapes, axes, sizes):
+    n, rows = sizes["pl"], own_pseudo.shape[0]
+    width = pseudo.shape[0] // n
+    x = jax.ShapeDtypeStruct((n, rows, width), jnp.bfloat16)
     n_col = sizes["pcol"]
     wshape = (n_col, mode_shapes.shape[0], 4 * rows)
     kernel = functools.partial(gram_weighted_kernel, axes=axes, factors=factor_table(sizes))
     return pl.pallas_call(
         kernel,
         out_shape=jax.ShapeDtypeStruct((wshape[1], n_col * wshape[2]), jnp.bfloat16),
-        in_specs=[pl.BlockSpec(memory_space=pltpu.VMEM)] * 2,
+        in_specs=[pl.BlockSpec(memory_space=pltpu.VMEM)] * 3,
         out_specs=pl.BlockSpec(memory_space=pltpu.VMEM),
         scratch_shapes=[
+            pltpu.VMEM(x.shape, x.dtype),
             pltpu.VMEM(x.shape, x.dtype),
             pltpu.VMEM((n, 2, rows, width), x.dtype),
             pltpu.VMEM((n, 2, rows, width), x.dtype),
@@ -407,7 +417,7 @@
             pltpu.SemaphoreType.DMA((n_col,)),
         ],
         compiler_params=pltpu.CompilerParams(collective_id=103, has_side_effects=True),
-    )(x, mode_shapes)
+    )(own_pseudo, pseudo, mode_shapes)
 
 
 def fused_sum(x, axes, sizes, over, add_across, kernel_id):
@@ -498,14 +508,11 @@
         )
         first_row = (col * n_row + row) * block
         own_pseudo = lax.dynamic_slice_in_dim(pseudo, first_row, block, 0)
-        partial_gram = outer_rows(own_pseudo, pseudo).astype(jnp.bfloat16)
-        chunk = modes // n_pl
-        by_chunk = partial_gram.reshape(block, n_pl, chunk).transpose(1, 0, 2)
         half = modes // 2
         send_half = lax.dynamic_slice_in_dim(mode_shapes, (col % 2) * half, half, 1)
         panel_piece = lax.ppermute(send_half, ("prow", "pcol"), swap)
         panel_mine = lax.all_gather(panel_piece, "pl", axis=0, tiled=True)
-        weighted = gram_weighted(by_chunk, mode_shapes, axes, sizes)
+        weighted = gram_weighted(own_pseudo, pseudo, mode_shapes, axes, sizes)
         panel_mine, weighted = lax.optimization_barrier((panel_mine, weighted))
         panel_other = lax.ppermute(panel_mine, "prow", sibling)
         weighted_mine = lax.dynamic_slice_in_dim(weighted, core * half, half, 1)

time: 173 us -> 173 us (level)
  other arithmetic: 1.79 us -> 3.95 us
    concatenate x0 -> x2, other arithmetic: none -> 2.16 us  [body(): jnp.concatenate([(in_phase[:, None] * modal_wide).astype(jnp.bfloat16), (...]
    dot_general x3 -> x2, matrix products: 7.07 us -> 6.27 us  [outer_rows(): lax.dot_general(left_rows, right_rows, (((1,), (1,)), ((), ())), preferre...]
where the time goes in v18:
time: 173 us; the launch traced here: 172 us
  Pallas kernels  128 us (74%)
  between operations  13.5 us (8%)
  matrix products  13 us (8%)
  waiting for transfers between devices  7.29 us (4%)
  starting transfers between devices  4.57 us (3%)
  other arithmetic  3.95 us (2%)
  local copies, waits for them, and re-layouts  1.93 us (1%)
    pallas_call x1, Pallas kernels, gram_weighted(): pl.pallas_call(kernel, out_shape=jax.ShapeDtypeStruct((wshape[1], n_col *...  74.1 us
    pallas_call x1, Pallas kernels, modal_sum(): pl.pallas_call(kernel, out_shape=jax.ShapeDtypeStruct((2,) + block, jnp.b...  53.9 us
    dot_general x2, matrix products, outer_rows(): lax.dot_general(left_rows, right_rows, (((1,), (1,)), ((), ())), preferre...  6.27 us
    dot_general x1, matrix products, body(): mine = jnp.dot(own_modes, factor_cols, preferred_element_type=jnp.float32)  4.57 us
    ppermute x1, waiting for transfers between devices, body(): panel_piece = lax.ppermute(send_half, ('prow', 'pcol'), swap)  4.04 us
    ppermute x1, starting transfers between devices, body(): panel_piece = lax.ppermute(send_half, ('prow', 'pcol'), swap)  3.77 us
  transfers between devices with their start and end apart: 3, of which 2 were waited for; matrix products, arithmetic and copies ran while one was open for 8% of the time, Pallas kernels for 74%

profile of v18, /device:TPU:39, one launch (start us, length us, event | category | flops | bytes accessed | tf_op | source)
XLA Modules:
  0.0 172.2 jit_solution(8647792962357143853)
XLA Ops:
  6.5 0.0 copy-start
  6.5 0.0 all-gather.2.cloned.1.call-start
  6.5 1.1 constant_dynamic-slice_fusion
  7.6 3.8 %collective-permute-start = (bf16[128,1024]{1,0:T(8,128)(2,1)S(1)}, bf16[128,1024]{1,0:T(8,128)(2,1)S(1)}, u32[]{:S(2)}, u32[]{:S(2)}) collective-permute-start(bf16[128,1024]{1,0:T(8,128)(2,1)S(1)} %constant_dynamic-slice_fusion), channel_id=1, source_target_pairs={{0,0},{64,16},{128,32},{192,48},{16,64},{80,80},{144,96},{208,112}... | collective-permute-start | bytes 786440 | tf_op jit(solution)/shard_map/ppermute | solution.py:513
  11.4 4.0 %collective-permute-done = bf16[128,1024]{1,0:T(8,128)(2,1)S(1)} collective-permute-done((bf16[128,1024]{1,0:T(8,128)(2,1)S(1)}, bf16[128,1024]{1,0:T(8,128)(2,1)S(1)}, u32[]{:S(2)}, u32[]{:S(2)}) %collective-permute-start) | collective-permute-done | bytes 262176 | tf_op jit(solution)/shard_map/ppermute | solution.py:513
  15.4 0.0 copy-start.2
  15.4 0.7 copy-done.2
  16.1 0.0 all-gather.2.cloned.1.call-update
  16.2 0.0 copy-done
  16.2 0.0 copy-start.5
  16.2 4.6 %fusion.2.mine_ref = f32[1024,256]{1,0:T(8,128)} fusion(bf16[2048,256]{1,0:T(8,128)(2,1)S(1)} %copy-done, bf16[2048,2048]{1,0:T(8,128)(2,1)} %param.6, s32[]{:T(128)S(6)} %select_n.28), kind=kOutput, calls=%fused_computation.2 | convolution fusion | flops 1073741824 | bytes 6291460 | tf_op jit(solution)/shard_map/dot_general | solution.py:498
  20.8 0.1 copy-done.5
  20.9 0.0 copy-start.3
  20.9 0.0 copy-start.4
  20.9 2.1 %fusion.6.theirs_ref = bf16[1024,256]{1,0:T(8,128)(2,1)} fusion(bf16[2048,256]{1,0:T(8,128)(2,1)S(1)} %copy-done, bf16[2048,2048]{1,0:T(8,128)(2,1)S(1)} %copy-done.5, s32[]{:T(128)S(6)} %select_n.29), kind=kOutput, calls=%fused_computation.12 | convolution fusion | flops 1074003968 | bytes 5767172 | tf_op jit(solution)/shard_map/dot_general | solution.py:499
  23.0 53.9 %shard_map.55 = bf16[2,4,256,256]{3,2,1,0:T(8,128)(2,1)} custom-call(f32[1024,256]{1,0:T(8,128)} %fusion.2.mine_ref, bf16[1024,256]{1,0:T(8,128)(2,1)} %fusion.6.theirs_ref), custom_call_target="tpu_custom_call" | custom-call | tf_op jit(solution)/shard_map/pallas_call | solution.py:249
  76.9 0.0 copy-done.3
  76.9 0.0 copy-done.4
  77.0 1.8 %fusion.5 = (bf16[2048,256]{1,0:T(8,128)(2,1)S(1)}, bf16[2048,256]{1,0:T(8,128)(2,1)S(1)}) fusion(bf16[2,4,256,256]{3,2,1,0:T(8,128)(2,1)} %shard_map.55, f32[2048]{0:T(1024)S(1)} %get-tuple-element.11, f32[2048]{0:T(1024)S(1)} %get-tuple-element.12), kind=kLoop, calls=%fused_computation.11 | loop fusion | flops 2621440 | bytes 3162112 | tf_op jit(solution)/shard_map/convert_element_type | solution.py:505
  78.8 0.7 fusion.12.own_ref
  79.4 1.5 pad_maximum_fusion.pseudo_ref
  80.9 74.1 %shard_map.56 = bf16[128,2048]{1,0:T(8,128)(2,1)} custom-call(bf16[128,512]{1,0:T(8,128)(2,1)} %fusion.12.own_ref, bf16[2048,512]{1,0:T(8,128)(2,1)} %pad_maximum_fusion.pseudo_ref, bf16[128,2048]{1,0:T(8,128)(2,1)} %shapes_ref.1), custom_call_target="tpu_custom_call" | custom-call | tf_op jit(solution)/shard_map/pallas_call | solution.py:395
  155.0 0.0 copy-start.1
  155.0 0.0 all-gather.2.cloned.1.call-done
  155.0 0.8 collective-permute-start.1
  155.9 3.8 %fusion.9 = f32[128,2048]{1,0:T(8,128)S(1)} fusion(bf16[2048,1024]{1,0:T(8,128)(2,1)} %all-gather.2.cloned.1.call-done, bf16[128,2048]{1,0:T(8,128)(2,1)} %shard_map.56, s32[]{:T(128)S(6)} %select_n.28), kind=kOutput, calls=%fused_computation.13 | convolution fusion | flops 536870912 | bytes 5505028 | tf_op jit(solution)/shard_map/dot_general | solution.py:22
  159.6 3.2 %collective-permute-done.1 = bf16[2048,1024]{1,0:T(8,128)(2,1)S(1)} collective-permute-done((bf16[2048,1024]{1,0:T(8,128)(2,1)}, bf16[2048,1024]{1,0:T(8,128)(2,1)S(1)}, u32[]{:S(2)}, u32[]{:S(2)}) %collective-permute-start.1) | collective-permute-done | bytes 4194336 | tf_op jit(solution)/shard_map/ppermute | solution.py:517
  162.8 0.0 copy-done.1
  162.9 2.5 %convolution_add_fusion = f32[128,2048]{1,0:T(8,128)} fusion(f32[128,2048]{1,0:T(8,128)S(1)} %fusion.9, bf16[2048,1024]{1,0:T(8,128)(2,1)S(1)} %collective-permute-done.1, bf16[128,2048]{1,0:T(8,128)(2,1)S(1)} %copy-done.1, s32[]{:T(128)S(6)} %select_n.29), kind=kOutput, calls=%fused_computation.6 | convolution fusion | flops 537133056 | bytes 6553604 | tf_op jit(solution)/shard_map/dot_general | solution.py:22
  (1 shorter events, 0.0 us)
Async XLA Ops:
  6.5 9.6 %copy-start = (bf16[2048,256]{1,0:T(8,128)(2,1)S(1)}, bf16[2048,256]{1,0:T(8,128)(2,1)}, u32[]{:S(2)}) copy-start(bf16[2048,256]{1,0:T(8,128)(2,1)} %param.5) | copy-start | bytes 3145732
  6.5 148.5 %all-gather.2.cloned.1.call-start = ((), (), s32[]{:S(2)}) async-start(), calls=%async_computation | async-start | bytes 4456448 | tf_op jit(solution)/shard_map/all_gather | solution.py:514
  7.6 7.8 %collective-permute-start = (bf16[128,1024]{1,0:T(8,128)(2,1)S(1)}, bf16[128,1024]{1,0:T(8,128)(2,1)S(1)}, u32[]{:S(2)}, u32[]{:S(2)}) collective-permute-start(bf16[128,1024]{1,0:T(8,128)(2,1)S(1)} %constant_dynamic-slice_fusion), channel_id=1, source_target_pairs={{0,0},{64,16},{128,32},{192,48},{16,64},{80,80},{144,96},{208,112}... | collective-permute-start | bytes 786440 | tf_op jit(solution)/shard_map/ppermute | solution.py:513
  15.4 0.7 copy-start.2
  16.2 4.7 %copy-start.5 = (bf16[2048,2048]{1,0:T(8,128)(2,1)S(1)}, bf16[2048,2048]{1,0:T(8,128)(2,1)}, u32[]{:S(2)}) copy-start(bf16[2048,2048]{1,0:T(8,128)(2,1)} %param.6) | copy-start | bytes 25165828
  20.9 56.0 %copy-start.3 = (f32[2048]{0:T(1024)S(1)}, f32[2048]{0:T(1024)}, u32[]{:S(2)}) copy-start(f32[2048]{0:T(1024)} %param.8) | copy-start | bytes 24580
  20.9 56.0 %copy-start.4 = (f32[2048]{0:T(1024)S(1)}, f32[2048]{0:T(1024)}, u32[]{:S(2)}) copy-start(f32[2048]{0:T(1024)} %param.9) | copy-start | bytes 24580
  155.0 7.8 %copy-start.1 = (bf16[128,2048]{1,0:T(8,128)(2,1)S(1)}, bf16[128,2048]{1,0:T(8,128)(2,1)}, u32[]{:S(2)}) copy-start(bf16[128,2048]{1,0:T(8,128)(2,1)} %shard_map.56) | copy-start | bytes 1572868
  155.0 7.8 %collective-permute-start.1 = (bf16[2048,1024]{1,0:T(8,128)(2,1)}, bf16[2048,1024]{1,0:T(8,128)(2,1)S(1)}, u32[]{:S(2)}, u32[]{:S(2)}) collective-permute-start(bf16[2048,1024]{1,0:T(8,128)(2,1)} %all-gather.2.cloned.1.call-done), channel_id=1, source_target_pairs={{0,64},{64,0},{128,192},{192,128},{1,65},{65,1},{129,193},{193,129... | collective-permute-start | bytes 12582920 | tf_op jit(solution)/shard_map/ppermute | solution.py:517
Sparse Core Ops, SparseCore 0:
  16.3 94.9 all-gather.1

commit v19 on v17

--- a/solution.py
+++ b/solution.py
@@ -195,6 +195,7 @@
             device_id=to, device_id_type=MESH,
         )
 
+    pending = []
     barrier = pltpu.get_barrier_semaphore()
     for k in range(1, n):
         pl.semaphore_signal(barrier, inc=1, device_id=device("pcol", peer(k)), device_id_type=MESH)
@@ -204,7 +205,7 @@
 
     chip = one(theirs_ref, sib_in, sibling, send_s, recv_s)
     chip.start()
-    chip.wait_send()
+    pending.append(chip)
     chip.wait_recv()
     summed = mine_ref[...] + sib_in[...].astype(jnp.float32)
     pieces[...] = summed.astype(pieces.dtype).reshape(pieces.shape)
@@ -212,7 +213,7 @@
     for k in range(1, n):
         step(pieces.at[peer(k)], got.at[me], k, device("pcol", peer(k)), (send_a, recv_a)).start()
     for k in range(1, n):
-        step(pieces.at[peer(k)], got.at[me], k, device("pcol", peer(k)), (send_a, recv_a)).wait_send()
+        pending.append(step(pieces.at[peer(k)], got.at[me], k, device("pcol", peer(k)), (send_a, recv_a)))
     for k in range(1, n):
         step(pieces.at[me], got.at[sender(k)], k, device("pcol", sender(k)), (send_a, recv_a)).wait_recv()
     total = pieces[me].astype(jnp.float32)
@@ -222,23 +223,25 @@
 
     across = one(part_out, part_in, partner, send_b, recv_b)
     across.start()
-    across.wait_send()
+    pending.append(across)
     across.wait_recv()
     coll[me] = (part_out[...].astype(jnp.float32) + part_in[...].astype(jnp.float32)).astype(coll.dtype)
 
     for k in range(1, n):
         step(coll.at[me], coll.at[me], k, device("pcol", peer(k)), (send_c, recv_c)).start()
     for k in range(1, n):
-        step(coll.at[me], coll.at[me], k, device("pcol", peer(k)), (send_c, recv_c)).wait_send()
+        pending.append(step(coll.at[me], coll.at[me], k, device("pcol", peer(k)), (send_c, recv_c)))
     for k in range(1, n):
         step(coll.at[me], coll.at[sender(k)], k, device("pcol", sender(k)), (send_c, recv_c)).wait_recv()
 
     join = one(coll, sib_out, sibling, send_d, recv_d)
     join.start()
-    join.wait_send()
+    pending.append(join)
     join.wait_recv()
     out_ref[core] = coll[...]
     out_ref[1 - core] = sib_out[...]
+    for sent in pending:
+        sent.wait_send()
 
 
 def modal_sum(mine, theirs, axes, sizes):
@@ -305,6 +308,7 @@
             device_id=to, device_id_type=MESH,
         )
 
+    pending = []
     barrier = pltpu.get_barrier_semaphore()
     for k in range(1, n):
         pl.semaphore_signal(barrier, inc=1, device_id=device("pl", lax.rem(me + k, n)), device_id_type=MESH)
@@ -321,7 +325,7 @@
     for k in range(1, n):
         step(x_ref.at[peer(k)], got.at[me], k, device("pl", peer(k)), (send_a, recv_a)).start()
     for k in range(1, n):
-        step(x_ref.at[peer(k)], got.at[me], k, device("pl", peer(k)), (send_a, recv_a)).wait_send()
+        pending.append(step(x_ref.at[peer(k)], got.at[me], k, device("pl", peer(k)), (send_a, recv_a)))
     for k in range(1, n):
         step(x_ref.at[me], got.at[sender(k)], k, device("pl", sender(k)), (send_a, recv_a)).wait_recv()
     total = x_ref[me].astype(jnp.float32)
@@ -331,7 +335,7 @@
 
     across = one(part_out, part_in, partner, send_b, recv_b)
     across.start()
-    across.wait_send()
+    pending.append(across)
     across.wait_recv()
     mine, theirs = part_out[...], part_in[...]
     coll[me] = jnp.stack([jnp.where(half == 0, mine, theirs), jnp.where(half == 0, theirs, mine)])
@@ -339,7 +343,7 @@
     for k in range(1, n):
         step(coll.at[me], coll.at[me], k, device("pl", peer(k)), (send_c, recv_c)).start()
     for k in range(1, n):
-        step(coll.at[me], coll.at[me], k, device("pl", peer(k)), (send_c, recv_c)).wait_send()
+        pending.append(step(coll.at[me], coll.at[me], k, device("pl", peer(k)), (send_c, recv_c)))
     for k in range(1, n):
         step(coll.at[me], coll.at[sender(k)], k, device("pl", sender(k)), (send_c, recv_c)).wait_recv()
 
@@ -357,7 +361,7 @@
     join = one(coll, sib_coll, sibling, send_d, recv_d)
     join.start()
     own = [weighted_block(coll, h) for h in range(2)]
-    join.wait_send()
+    pending.append(join)
     join.wait_recv()
     other = [weighted_block(sib_coll, h) for h in range(2)]
     parts = []
@@ -370,12 +374,14 @@
     for k in range(1, n_col):
         step(wbuf.at[col], wbuf.at[col], k, device("pcol", wpeer(k)), (send_e, recv_e)).start()
     for k in range(1, n_col):
-        step(wbuf.at[col], wbuf.at[col], k, device("pcol", wpeer(k)), (send_e, recv_e)).wait_send()
+        pending.append(step(wbuf.at[col], wbuf.at[col], k, device("pcol", wpeer(k)), (send_e, recv_e)))
     for k in range(1, n_col):
         step(wbuf.at[col], wbuf.at[wsender(k)], k, device("pcol", wsender(k)), (send_e, recv_e)).wait_recv()
     width_w = wbuf.shape[2]
     for c in range(n_col):
         out_ref[:, c * width_w:(c + 1) * width_w] = wbuf[c]
+    for sent in pending:
+        sent.wait_send()
 
 
 def gram_weighted(x, mode_shapes, axes, sizes):

time: 173 us -> 171 us (0.988)
  Pallas kernels: 128 us -> 125 us
    pallas_call x1, Pallas kernels: 74.5 us -> 71.9 us  [gram_weighted(): pl.pallas_call(kernel, out_shape=jax.ShapeDtypeStruct((wshape[1], n_col *...]
where the time goes in v19:
time: 171 us; the launch traced here: 169 us
  Pallas kernels  125 us (73%)
  matrix products  13.8 us (8%)
  between operations  13.5 us (8%)
  waiting for transfers between devices  7.61 us (4%)
  starting transfers between devices  3.9 us (2%)
  local copies, waits for them, and re-layouts  3.2 us (2%)
  other arithmetic  1.79 us (1%)
    pallas_call x1, Pallas kernels, gram_weighted(): pl.pallas_call(kernel, out_shape=jax.ShapeDtypeStruct((wshape[1], n_col *...  71.9 us
    pallas_call x1, Pallas kernels, modal_sum(): pl.pallas_call(kernel, out_shape=jax.ShapeDtypeStruct((2,) + block, jnp.b...  53.3 us
    dot_general x3, matrix products, outer_rows(): lax.dot_general(left_rows, right_rows, (((1,), (1,)), ((), ())), preferre...  7.08 us
    dot_general x1, matrix products, body(): mine = jnp.dot(own_modes, factor_cols, preferred_element_type=jnp.float32)  4.57 us
    ppermute x1, waiting for transfers between devices, body(): panel_piece = lax.ppermute(send_half, ('prow', 'pcol'), swap)  4.04 us
    ppermute x1, starting transfers between devices, body(): panel_piece = lax.ppermute(send_half, ('prow', 'pcol'), swap)  3.77 us
    ppermute x1, waiting for transfers between devices, body(): panel_other = lax.ppermute(panel_mine, 'prow', sibling)  3.53 us
  transfers between devices with their start and end apart: 3, of which 2 were waited for; matrix products, arithmetic and copies ran while one was open for 8% of the time, Pallas kernels for 74%

profile of v19, /device:TPU:39, one launch (start us, length us, event | category | flops | bytes accessed | tf_op | source)
XLA Modules:
  0.0 169.0 jit_solution(14167976513419675193)
XLA Ops:
  6.5 0.0 copy-start
  6.5 0.0 all-gather.2.cloned.1.call-start
  6.5 1.1 constant_dynamic-slice_fusion
  7.6 3.8 %collective-permute-start = (bf16[128,1024]{1,0:T(8,128)(2,1)S(1)}, bf16[128,1024]{1,0:T(8,128)(2,1)S(1)}, u32[]{:S(2)}, u32[]{:S(2)}) collective-permute-start(bf16[128,1024]{1,0:T(8,128)(2,1)S(1)} %constant_dynamic-slice_fusion), channel_id=1, source_target_pairs={{0,0},{64,16},{128,32},{192,48},{16,64},{80,80},{144,96},{208,112}... | collective-permute-start | bytes 786440 | tf_op jit(solution)/shard_map/ppermute | solution.py:512
  11.4 4.0 %collective-permute-done = bf16[128,1024]{1,0:T(8,128)(2,1)S(1)} collective-permute-done((bf16[128,1024]{1,0:T(8,128)(2,1)S(1)}, bf16[128,1024]{1,0:T(8,128)(2,1)S(1)}, u32[]{:S(2)}, u32[]{:S(2)}) %collective-permute-start) | collective-permute-done | bytes 262176 | tf_op jit(solution)/shard_map/ppermute | solution.py:512
  15.4 0.0 copy-start.2
  15.4 0.7 copy-done.2
  16.1 0.0 all-gather.2.cloned.1.call-update
  16.2 0.0 copy-done
  16.2 0.0 copy-start.5
  16.2 4.6 %fusion.2.mine_ref = f32[1024,256]{1,0:T(8,128)} fusion(bf16[2048,256]{1,0:T(8,128)(2,1)S(1)} %copy-done, bf16[2048,2048]{1,0:T(8,128)(2,1)} %param.6, s32[]{:T(128)S(6)} %select_n.28), kind=kOutput, calls=%fused_computation.2 | convolution fusion | flops 1073741824 | bytes 6291460 | tf_op jit(solution)/shard_map/dot_general | solution.py:494
  20.8 0.1 copy-done.5
  20.9 0.0 copy-start.3
  20.9 0.0 copy-start.4
  20.9 2.1 %fusion.6.theirs_ref = bf16[1024,256]{1,0:T(8,128)(2,1)} fusion(bf16[2048,256]{1,0:T(8,128)(2,1)S(1)} %copy-done, bf16[2048,2048]{1,0:T(8,128)(2,1)S(1)} %copy-done.5, s32[]{:T(128)S(6)} %select_n.29), kind=kOutput, calls=%fused_computation.13 | convolution fusion | flops 1074003968 | bytes 5767172 | tf_op jit(solution)/shard_map/dot_general | solution.py:495
  23.0 53.3 %shard_map.55 = bf16[2,4,256,256]{3,2,1,0:T(8,128)(2,1)} custom-call(f32[1024,256]{1,0:T(8,128)} %fusion.2.mine_ref, bf16[1024,256]{1,0:T(8,128)(2,1)} %fusion.6.theirs_ref), custom_call_target="tpu_custom_call" | custom-call | tf_op jit(solution)/shard_map/pallas_call | solution.py:252
  76.3 0.0 copy-done.3
  76.4 0.0 copy-done.4
  76.4 1.8 %fusion.4 = (bf16[2048,256]{1,0:T(8,128)(2,1)S(1)}, bf16[2048,256]{1,0:T(8,128)(2,1)S(1)}) fusion(bf16[2,4,256,256]{3,2,1,0:T(8,128)(2,1)} %shard_map.55, f32[2048]{0:T(1024)S(1)} %get-tuple-element.11, f32[2048]{0:T(1024)S(1)} %get-tuple-element.12), kind=kLoop, calls=%fused_computation.11 | loop fusion | flops 2621440 | bytes 3162112 | tf_op jit(solution)/shard_map/convert_element_type | solution.py:500
  78.2 0.8 convolution_convert_fusion
  79.0 0.3 copy.6
  79.3 1.0 copy.7
  80.3 71.9 %shard_map.56 = bf16[128,2048]{1,0:T(8,128)(2,1)} custom-call(bf16[16,128,128]{2,1,0:T(8,128)(2,1)} %bitcast.10, bf16[128,2048]{1,0:T(8,128)(2,1)} %shapes_ref.1), custom_call_target="tpu_custom_call" | custom-call | tf_op jit(solution)/shard_map/pallas_call | solution.py:392
  152.2 0.0 copy-start.1
  152.2 0.0 all-gather.2.cloned.1.call-done
  152.2 0.1 collective-permute-start.1
  152.3 3.8 %fusion.9 = f32[128,2048]{1,0:T(8,128)S(1)} fusion(bf16[2048,1024]{1,0:T(8,128)(2,1)} %all-gather.2.cloned.1.call-done, bf16[128,2048]{1,0:T(8,128)(2,1)} %shard_map.56, s32[]{:T(128)S(6)} %select_n.28), kind=kOutput, calls=%fused_computation.14 | convolution fusion | flops 536870912 | bytes 5505028 | tf_op jit(solution)/shard_map/dot_general | solution.py:22
  156.1 3.5 %collective-permute-done.1 = bf16[2048,1024]{1,0:T(8,128)(2,1)S(1)} collective-permute-done((bf16[2048,1024]{1,0:T(8,128)(2,1)}, bf16[2048,1024]{1,0:T(8,128)(2,1)S(1)}, u32[]{:S(2)}, u32[]{:S(2)}) %collective-permute-start.1) | collective-permute-done | bytes 4194336 | tf_op jit(solution)/shard_map/ppermute | solution.py:516
  159.7 0.0 copy-done.1
  159.7 2.5 %convolution_add_fusion = f32[128,2048]{1,0:T(8,128)} fusion(f32[128,2048]{1,0:T(8,128)S(1)} %fusion.9, bf16[2048,1024]{1,0:T(8,128)(2,1)S(1)} %collective-permute-done.1, bf16[128,2048]{1,0:T(8,128)(2,1)S(1)} %copy-done.1, s32[]{:T(128)S(6)} %select_n.29), kind=kOutput, calls=%fused_computation.6 | convolution fusion | flops 537133056 | bytes 6553604 | tf_op jit(solution)/shard_map/dot_general | solution.py:22
  (1 shorter events, 0.0 us)
Async XLA Ops:
  6.5 9.6 %copy-start = (bf16[2048,256]{1,0:T(8,128)(2,1)S(1)}, bf16[2048,256]{1,0:T(8,128)(2,1)}, u32[]{:S(2)}) copy-start(bf16[2048,256]{1,0:T(8,128)(2,1)} %param.5) | copy-start | bytes 3145732
  6.5 145.7 %all-gather.2.cloned.1.call-start = ((), (), s32[]{:S(2)}) async-start(), calls=%async_computation | async-start | bytes 4456448 | tf_op jit(solution)/shard_map/all_gather | solution.py:513
  7.6 7.8 %collective-permute-start = (bf16[128,1024]{1,0:T(8,128)(2,1)S(1)}, bf16[128,1024]{1,0:T(8,128)(2,1)S(1)}, u32[]{:S(2)}, u32[]{:S(2)}) collective-permute-start(bf16[128,1024]{1,0:T(8,128)(2,1)S(1)} %constant_dynamic-slice_fusion), channel_id=1, source_target_pairs={{0,0},{64,16},{128,32},{192,48},{16,64},{80,80},{144,96},{208,112}... | collective-permute-start | bytes 786440 | tf_op jit(solution)/shard_map/ppermute | solution.py:512
  15.4 0.7 copy-start.2
  16.2 4.7 %copy-start.5 = (bf16[2048,2048]{1,0:T(8,128)(2,1)S(1)}, bf16[2048,2048]{1,0:T(8,128)(2,1)}, u32[]{:S(2)}) copy-start(bf16[2048,2048]{1,0:T(8,128)(2,1)} %param.6) | copy-start | bytes 25165828
  20.9 55.5 %copy-start.3 = (f32[2048]{0:T(1024)S(1)}, f32[2048]{0:T(1024)}, u32[]{:S(2)}) copy-start(f32[2048]{0:T(1024)} %param.8) | copy-start | bytes 24580
  20.9 55.5 %copy-start.4 = (f32[2048]{0:T(1024)S(1)}, f32[2048]{0:T(1024)}, u32[]{:S(2)}) copy-start(f32[2048]{0:T(1024)} %param.9) | copy-start | bytes 24580
  152.2 7.5 %copy-start.1 = (bf16[128,2048]{1,0:T(8,128)(2,1)S(1)}, bf16[128,2048]{1,0:T(8,128)(2,1)}, u32[]{:S(2)}) copy-start(bf16[128,2048]{1,0:T(8,128)(2,1)} %shard_map.56) | copy-start | bytes 1572868
  152.2 7.5 %collective-permute-start.1 = (bf16[2048,1024]{1,0:T(8,128)(2,1)}, bf16[2048,1024]{1,0:T(8,128)(2,1)S(1)}, u32[]{:S(2)}, u32[]{:S(2)}) collective-permute-start(bf16[2048,1024]{1,0:T(8,128)(2,1)} %all-gather.2.cloned.1.call-done), channel_id=1, source_target_pairs={{0,64},{64,0},{128,192},{192,128},{1,65},{65,1},{129,193},{193,129... | collective-permute-start | bytes 12582920 | tf_op jit(solution)/shard_map/ppermute | solution.py:516
Sparse Core Ops, SparseCore 0:
  16.3 93.9 all-gather.1

commit v20 on v19

--- a/solution.py
+++ b/solution.py
@@ -344,8 +344,19 @@
         step(coll.at[me], coll.at[me], k, device("pl", peer(k)), (send_c, recv_c)).start()
     for k in range(1, n):
         pending.append(step(coll.at[me], coll.at[me], k, device("pl", peer(k)), (send_c, recv_c)))
+
+    def to_sibling(chunk_at):
+        return pltpu.make_async_remote_copy(
+            src_ref=coll.at[chunk_at], dst_ref=sib_coll.at[chunk_at], send_sem=send_d.at[chunk_at],
+            recv_sem=recv_d.at[chunk_at], device_id=sibling, device_id_type=MESH,
+        )
+
+    to_sibling(me).start()
+    pending.append(to_sibling(me))
     for k in range(1, n):
         step(coll.at[me], coll.at[sender(k)], k, device("pl", sender(k)), (send_c, recv_c)).wait_recv()
+        to_sibling(sender(k)).start()
+        pending.append(to_sibling(sender(k)))
 
     chunk = coll.shape[-1]
 
@@ -358,11 +369,9 @@
             )
         return acc
 
-    join = one(coll, sib_coll, sibling, send_d, recv_d)
-    join.start()
     own = [weighted_block(coll, h) for h in range(2)]
-    pending.append(join)
-    join.wait_recv()
+    for l in range(n):
+        to_sibling(l).wait_recv()
     other = [weighted_block(sib_coll, h) for h in range(2)]
     parts = []
     for h in range(2):
@@ -407,8 +416,8 @@
             pltpu.SemaphoreType.DMA(()),
             pltpu.SemaphoreType.DMA((n,)),
             pltpu.SemaphoreType.DMA((n,)),
-            pltpu.SemaphoreType.DMA(()),
-            pltpu.SemaphoreType.DMA(()),
+            pltpu.SemaphoreType.DMA((n,)),
+            pltpu.SemaphoreType.DMA((n,)),
             pltpu.SemaphoreType.DMA((n_col,)),
             pltpu.SemaphoreType.DMA((n_col,)),
         ],

time: 171 us -> 170 us (level)
  no operation moved by 1% of the time
where the time goes in v20:
time: 170 us; the launch traced here: 169 us
  Pallas kernels  125 us (74%)
  matrix products  13.8 us (8%)
  between operations  13.5 us (8%)
  waiting for transfers between devices  7.28 us (4%)
  starting transfers between devices  4.25 us (2%)
  local copies, waits for them, and re-layouts  3.2 us (2%)
  other arithmetic  1.79 us (1%)
    pallas_call x1, Pallas kernels, gram_weighted(): pl.pallas_call(kernel, out_shape=jax.ShapeDtypeStruct((wshape[1], n_col *...  72.2 us
    pallas_call x1, Pallas kernels, modal_sum(): pl.pallas_call(kernel, out_shape=jax.ShapeDtypeStruct((2,) + block, jnp.b...  53.3 us
    dot_general x3, matrix products, outer_rows(): lax.dot_general(left_rows, right_rows, (((1,), (1,)), ((), ())), preferre...  7.08 us
    dot_general x1, matrix products, body(): mine = jnp.dot(own_modes, factor_cols, preferred_element_type=jnp.float32)  4.57 us
    ppermute x1, waiting for transfers between devices, body(): panel_piece = lax.ppermute(send_half, ('prow', 'pcol'), swap)  4.04 us
    ppermute x1, starting transfers between devices, body(): panel_piece = lax.ppermute(send_half, ('prow', 'pcol'), swap)  3.77 us
  transfers between devices with their start and end apart: 3, of which 2 were waited for; matrix products, arithmetic and copies ran while one was open for 8% of the time, Pallas kernels for 74%

profile of v20, /device:TPU:39, one launch (start us, length us, event | category | flops | bytes accessed | tf_op | source)
XLA Modules:
  0.0 169.3 jit_solution(13673387057568127039)
XLA Ops:
  6.5 0.0 copy-start
  6.5 0.0 all-gather.2.cloned.1.call-start
  6.5 1.1 constant_dynamic-slice_fusion
  7.6 3.8 %collective-permute-start = (bf16[128,1024]{1,0:T(8,128)(2,1)S(1)}, bf16[128,1024]{1,0:T(8,128)(2,1)S(1)}, u32[]{:S(2)}, u32[]{:S(2)}) collective-permute-start(bf16[128,1024]{1,0:T(8,128)(2,1)S(1)} %constant_dynamic-slice_fusion), channel_id=1, source_target_pairs={{0,0},{64,16},{128,32},{192,48},{16,64},{80,80},{144,96},{208,112}... | collective-permute-start | bytes 786440 | tf_op jit(solution)/shard_map/ppermute | solution.py:521
  11.4 4.0 %collective-permute-done = bf16[128,1024]{1,0:T(8,128)(2,1)S(1)} collective-permute-done((bf16[128,1024]{1,0:T(8,128)(2,1)S(1)}, bf16[128,1024]{1,0:T(8,128)(2,1)S(1)}, u32[]{:S(2)}, u32[]{:S(2)}) %collective-permute-start) | collective-permute-done | bytes 262176 | tf_op jit(solution)/shard_map/ppermute | solution.py:521
  15.4 0.0 copy-start.2
  15.4 0.7 copy-done.2
  16.1 0.0 all-gather.2.cloned.1.call-update
  16.2 0.0 copy-done
  16.2 0.0 copy-start.5
  16.2 4.6 %fusion.2.mine_ref = f32[1024,256]{1,0:T(8,128)} fusion(bf16[2048,256]{1,0:T(8,128)(2,1)S(1)} %copy-done, bf16[2048,2048]{1,0:T(8,128)(2,1)} %param.6, s32[]{:T(128)S(6)} %select_n.28), kind=kOutput, calls=%fused_computation.2 | convolution fusion | flops 1073741824 | bytes 6291460 | tf_op jit(solution)/shard_map/dot_general | solution.py:503
  20.8 0.1 copy-done.5
  20.9 0.0 copy-start.3
  20.9 0.0 copy-start.4
  20.9 2.1 %fusion.6.theirs_ref = bf16[1024,256]{1,0:T(8,128)(2,1)} fusion(bf16[2048,256]{1,0:T(8,128)(2,1)S(1)} %copy-done, bf16[2048,2048]{1,0:T(8,128)(2,1)S(1)} %copy-done.5, s32[]{:T(128)S(6)} %select_n.29), kind=kOutput, calls=%fused_computation.13 | convolution fusion | flops 1074003968 | bytes 5767172 | tf_op jit(solution)/shard_map/dot_general | solution.py:504
  23.0 53.3 %shard_map.55 = bf16[2,4,256,256]{3,2,1,0:T(8,128)(2,1)} custom-call(f32[1024,256]{1,0:T(8,128)} %fusion.2.mine_ref, bf16[1024,256]{1,0:T(8,128)(2,1)} %fusion.6.theirs_ref), custom_call_target="tpu_custom_call" | custom-call | tf_op jit(solution)/shard_map/pallas_call | solution.py:252
  76.3 0.0 copy-done.3
  76.4 0.0 copy-done.4
  76.4 1.8 %fusion.4 = (bf16[2048,256]{1,0:T(8,128)(2,1)S(1)}, bf16[2048,256]{1,0:T(8,128)(2,1)S(1)}) fusion(bf16[2,4,256,256]{3,2,1,0:T(8,128)(2,1)} %shard_map.55, f32[2048]{0:T(1024)S(1)} %get-tuple-element.11, f32[2048]{0:T(1024)S(1)} %get-tuple-element.12), kind=kLoop, calls=%fused_computation.11 | loop fusion | flops 2621440 | bytes 3162112 | tf_op jit(solution)/shard_map/convert_element_type | solution.py:509
  78.2 0.8 convolution_convert_fusion
  79.0 0.3 copy.6
  79.3 1.0 copy.7
  80.3 72.2 %shard_map.56 = bf16[128,2048]{1,0:T(8,128)(2,1)} custom-call(bf16[16,128,128]{2,1,0:T(8,128)(2,1)} %bitcast.10, bf16[128,2048]{1,0:T(8,128)(2,1)} %shapes_ref.1), custom_call_target="tpu_custom_call" | custom-call | tf_op jit(solution)/shard_map/pallas_call | solution.py:401
  152.5 0.0 copy-start.1
  152.5 0.0 all-gather.2.cloned.1.call-done
  152.5 0.5 collective-permute-start.1
  153.0 3.8 %fusion.9 = f32[128,2048]{1,0:T(8,128)S(1)} fusion(bf16[2048,1024]{1,0:T(8,128)(2,1)} %all-gather.2.cloned.1.call-done, bf16[128,2048]{1,0:T(8,128)(2,1)} %shard_map.56, s32[]{:T(128)S(6)} %select_n.28), kind=kOutput, calls=%fused_computation.14 | convolution fusion | flops 536870912 | bytes 5505028 | tf_op jit(solution)/shard_map/dot_general | solution.py:22
  156.8 3.2 %collective-permute-done.1 = bf16[2048,1024]{1,0:T(8,128)(2,1)S(1)} collective-permute-done((bf16[2048,1024]{1,0:T(8,128)(2,1)}, bf16[2048,1024]{1,0:T(8,128)(2,1)S(1)}, u32[]{:S(2)}, u32[]{:S(2)}) %collective-permute-start.1) | collective-permute-done | bytes 4194336 | tf_op jit(solution)/shard_map/ppermute | solution.py:525
  160.0 0.0 copy-done.1
  160.0 2.5 %convolution_add_fusion = f32[128,2048]{1,0:T(8,128)} fusion(f32[128,2048]{1,0:T(8,128)S(1)} %fusion.9, bf16[2048,1024]{1,0:T(8,128)(2,1)S(1)} %collective-permute-done.1, bf16[128,2048]{1,0:T(8,128)(2,1)S(1)} %copy-done.1, s32[]{:T(128)S(6)} %select_n.29), kind=kOutput, calls=%fused_computation.6 | convolution fusion | flops 537133056 | bytes 6553604 | tf_op jit(solution)/shard_map/dot_general | solution.py:22
  (1 shorter events, 0.0 us)
Async XLA Ops:
  6.5 9.6 %copy-start = (bf16[2048,256]{1,0:T(8,128)(2,1)S(1)}, bf16[2048,256]{1,0:T(8,128)(2,1)}, u32[]{:S(2)}) copy-start(bf16[2048,256]{1,0:T(8,128)(2,1)} %param.5) | copy-start | bytes 3145732
  6.5 146.0 %all-gather.2.cloned.1.call-start = ((), (), s32[]{:S(2)}) async-start(), calls=%async_computation | async-start | bytes 4456448 | tf_op jit(solution)/shard_map/all_gather | solution.py:522
  7.6 7.8 %collective-permute-start = (bf16[128,1024]{1,0:T(8,128)(2,1)S(1)}, bf16[128,1024]{1,0:T(8,128)(2,1)S(1)}, u32[]{:S(2)}, u32[]{:S(2)}) collective-permute-start(bf16[128,1024]{1,0:T(8,128)(2,1)S(1)} %constant_dynamic-slice_fusion), channel_id=1, source_target_pairs={{0,0},{64,16},{128,32},{192,48},{16,64},{80,80},{144,96},{208,112}... | collective-permute-start | bytes 786440 | tf_op jit(solution)/shard_map/ppermute | solution.py:521
  15.4 0.7 copy-start.2
  16.2 4.7 %copy-start.5 = (bf16[2048,2048]{1,0:T(8,128)(2,1)S(1)}, bf16[2048,2048]{1,0:T(8,128)(2,1)}, u32[]{:S(2)}) copy-start(bf16[2048,2048]{1,0:T(8,128)(2,1)} %param.6) | copy-start | bytes 25165828
  20.9 55.5 %copy-start.3 = (f32[2048]{0:T(1024)S(1)}, f32[2048]{0:T(1024)}, u32[]{:S(2)}) copy-start(f32[2048]{0:T(1024)} %param.8) | copy-start | bytes 24580
  20.9 55.5 %copy-start.4 = (f32[2048]{0:T(1024)S(1)}, f32[2048]{0:T(1024)}, u32[]{:S(2)}) copy-start(f32[2048]{0:T(1024)} %param.9) | copy-start | bytes 24580
  152.5 7.5 %copy-start.1 = (bf16[128,2048]{1,0:T(8,128)(2,1)S(1)}, bf16[128,2048]{1,0:T(8,128)(2,1)}, u32[]{:S(2)}) copy-start(bf16[128,2048]{1,0:T(8,128)(2,1)} %shard_map.56) | copy-start | bytes 1572868
  152.5 7.5 %collective-permute-start.1 = (bf16[2048,1024]{1,0:T(8,128)(2,1)}, bf16[2048,1024]{1,0:T(8,128)(2,1)S(1)}, u32[]{:S(2)}, u32[]{:S(2)}) collective-permute-start(bf16[2048,1024]{1,0:T(8,128)(2,1)} %all-gather.2.cloned.1.call-done), channel_id=1, source_target_pairs={{0,64},{64,0},{128,192},{192,128},{1,65},{65,1},{129,193},{193,129... | collective-permute-start | bytes 12582920 | tf_op jit(solution)/shard_map/ppermute | solution.py:525
Sparse Core Ops, SparseCore 0:
  16.3 93.9 all-gather.1

commit v21 on v20

--- a/solution.py
+++ b/solution.py
@@ -231,13 +231,21 @@
         step(coll.at[me], coll.at[me], k, device("pcol", peer(k)), (send_c, recv_c)).start()
     for k in range(1, n):
         pending.append(step(coll.at[me], coll.at[me], k, device("pcol", peer(k)), (send_c, recv_c)))
+
+    def to_sibling(piece):
+        return pltpu.make_async_remote_copy(
+            src_ref=coll.at[piece], dst_ref=sib_out.at[piece], send_sem=send_d.at[piece],
+            recv_sem=recv_d.at[piece], device_id=sibling, device_id_type=MESH,
+        )
+
+    to_sibling(me).start()
+    pending.append(to_sibling(me))
     for k in range(1, n):
         step(coll.at[me], coll.at[sender(k)], k, device("pcol", sender(k)), (send_c, recv_c)).wait_recv()
-
-    join = one(coll, sib_out, sibling, send_d, recv_d)
-    join.start()
-    pending.append(join)
-    join.wait_recv()
+        to_sibling(sender(k)).start()
+        pending.append(to_sibling(sender(k)))
+    for piece in range(n):
+        to_sibling(piece).wait_recv()
     out_ref[core] = coll[...]
     out_ref[1 - core] = sib_out[...]
     for sent in pending:
@@ -270,8 +278,8 @@
             pltpu.SemaphoreType.DMA(()),
             pltpu.SemaphoreType.DMA((n,)),
             pltpu.SemaphoreType.DMA((n,)),
-            pltpu.SemaphoreType.DMA(()),
-            pltpu.SemaphoreType.DMA(()),
+            pltpu.SemaphoreType.DMA((n,)),
+            pltpu.SemaphoreType.DMA((n,)),
         ],
         compiler_params=pltpu.CompilerParams(collective_id=102, has_side_effects=True),
     )(mine, theirs)

time: 170 us -> 171 us (level)
  no operation moved by 1% of the time
where the time goes in v21:
time: 171 us; the launch traced here: 169 us
  Pallas kernels  125 us (73%)
  matrix products  13.8 us (8%)
  between operations  13.5 us (8%)
  waiting for transfers between devices  7.28 us (4%)
  starting transfers between devices  4.25 us (2%)
  local copies, waits for them, and re-layouts  3.2 us (2%)
  other arithmetic  1.78 us (1%)
    pallas_call x1, Pallas kernels, gram_weighted(): pl.pallas_call(kernel, out_shape=jax.ShapeDtypeStruct((wshape[1], n_col *...  72.4 us
    pallas_call x1, Pallas kernels, modal_sum(): pl.pallas_call(kernel, out_shape=jax.ShapeDtypeStruct((2,) + block, jnp.b...  53 us
    dot_general x3, matrix products, outer_rows(): lax.dot_general(left_rows, right_rows, (((1,), (1,)), ((), ())), preferre...  7.09 us
    dot_general x1, matrix products, body(): mine = jnp.dot(own_modes, factor_cols, preferred_element_type=jnp.float32)  4.57 us
    ppermute x1, waiting for transfers between devices, body(): panel_piece = lax.ppermute(send_half, ('prow', 'pcol'), swap)  4.04 us
    ppermute x1, starting transfers between devices, body(): panel_piece = lax.ppermute(send_half, ('prow', 'pcol'), swap)  3.77 us
  transfers between devices with their start and end apart: 3, of which 2 were waited for; matrix products, arithmetic and copies ran while one was open for 8% of the time, Pallas kernels for 74%

profile of v21, /device:TPU:39, one launch (start us, length us, event | category | flops | bytes accessed | tf_op | source)
XLA Modules:
  0.0 169.3 jit_solution(9716300353252755699)
XLA Ops:
  6.5 0.0 copy-start
  6.5 0.0 all-gather.2.cloned.1.call-start
  6.5 1.1 constant_dynamic-slice_fusion
  7.6 3.8 %collective-permute-start = (bf16[128,1024]{1,0:T(8,128)(2,1)S(1)}, bf16[128,1024]{1,0:T(8,128)(2,1)S(1)}, u32[]{:S(2)}, u32[]{:S(2)}) collective-permute-start(bf16[128,1024]{1,0:T(8,128)(2,1)S(1)} %constant_dynamic-slice_fusion), channel_id=1, source_target_pairs={{0,0},{64,16},{128,32},{192,48},{16,64},{80,80},{144,96},{208,112}... | collective-permute-start | bytes 786440 | tf_op jit(solution)/shard_map/ppermute | solution.py:529
  11.4 4.0 %collective-permute-done = bf16[128,1024]{1,0:T(8,128)(2,1)S(1)} collective-permute-done((bf16[128,1024]{1,0:T(8,128)(2,1)S(1)}, bf16[128,1024]{1,0:T(8,128)(2,1)S(1)}, u32[]{:S(2)}, u32[]{:S(2)}) %collective-permute-start) | collective-permute-done | bytes 262176 | tf_op jit(solution)/shard_map/ppermute | solution.py:529
  15.4 0.0 copy-start.2
  15.4 0.7 copy-done.2
  16.1 0.0 all-gather.2.cloned.1.call-update
  16.2 0.0 copy-done
  16.2 0.0 copy-start.5
  16.2 4.6 %fusion.2.mine_ref = f32[1024,256]{1,0:T(8,128)} fusion(bf16[2048,256]{1,0:T(8,128)(2,1)S(1)} %copy-done, bf16[2048,2048]{1,0:T(8,128)(2,1)} %param.6, s32[]{:T(128)S(6)} %select_n.28), kind=kOutput, calls=%fused_computation.2 | convolution fusion | flops 1073741824 | bytes 6291460 | tf_op jit(solution)/shard_map/dot_general | solution.py:511
  20.8 0.1 copy-done.5
  20.9 0.0 copy-start.3
  20.9 0.0 copy-start.4
  20.9 2.1 %fusion.6.theirs_ref = bf16[1024,256]{1,0:T(8,128)(2,1)} fusion(bf16[2048,256]{1,0:T(8,128)(2,1)S(1)} %copy-done, bf16[2048,2048]{1,0:T(8,128)(2,1)S(1)} %copy-done.5, s32[]{:T(128)S(6)} %select_n.29), kind=kOutput, calls=%fused_computation.13 | convolution fusion | flops 1074003968 | bytes 5767172 | tf_op jit(solution)/shard_map/dot_general | solution.py:512
  23.0 53.0 %shard_map.55 = bf16[2,4,256,256]{3,2,1,0:T(8,128)(2,1)} custom-call(f32[1024,256]{1,0:T(8,128)} %fusion.2.mine_ref, bf16[1024,256]{1,0:T(8,128)(2,1)} %fusion.6.theirs_ref), custom_call_target="tpu_custom_call" | custom-call | tf_op jit(solution)/shard_map/pallas_call | solution.py:260
  76.0 0.0 copy-done.3
  76.0 0.0 copy-done.4
  76.1 1.8 %fusion.4 = (bf16[2048,256]{1,0:T(8,128)(2,1)S(1)}, bf16[2048,256]{1,0:T(8,128)(2,1)S(1)}) fusion(bf16[2,4,256,256]{3,2,1,0:T(8,128)(2,1)} %shard_map.55, f32[2048]{0:T(1024)S(1)} %get-tuple-element.11, f32[2048]{0:T(1024)S(1)} %get-tuple-element.12), kind=kLoop, calls=%fused_computation.11 | loop fusion | flops 2621440 | bytes 3162112 | tf_op jit(solution)/shard_map/convert_element_type | solution.py:517
  77.9 0.8 convolution_convert_fusion
  78.7 0.3 copy.6
  79.0 1.0 copy.7
  80.0 72.4 %shard_map.56 = bf16[128,2048]{1,0:T(8,128)(2,1)} custom-call(bf16[16,128,128]{2,1,0:T(8,128)(2,1)} %bitcast.10, bf16[128,2048]{1,0:T(8,128)(2,1)} %shapes_ref.1), custom_call_target="tpu_custom_call" | custom-call | tf_op jit(solution)/shard_map/pallas_call | solution.py:409
  152.4 0.0 copy-start.1
  152.4 0.0 all-gather.2.cloned.1.call-done
  152.5 0.5 collective-permute-start.1
  152.9 3.8 %fusion.9 = f32[128,2048]{1,0:T(8,128)S(1)} fusion(bf16[2048,1024]{1,0:T(8,128)(2,1)} %all-gather.2.cloned.1.call-done, bf16[128,2048]{1,0:T(8,128)(2,1)} %shard_map.56, s32[]{:T(128)S(6)} %select_n.28), kind=kOutput, calls=%fused_computation.14 | convolution fusion | flops 536870912 | bytes 5505028 | tf_op jit(solution)/shard_map/dot_general | solution.py:22
  156.7 3.2 %collective-permute-done.1 = bf16[2048,1024]{1,0:T(8,128)(2,1)S(1)} collective-permute-done((bf16[2048,1024]{1,0:T(8,128)(2,1)}, bf16[2048,1024]{1,0:T(8,128)(2,1)S(1)}, u32[]{:S(2)}, u32[]{:S(2)}) %collective-permute-start.1) | collective-permute-done | bytes 4194336 | tf_op jit(solution)/shard_map/ppermute | solution.py:533
  159.9 0.0 copy-done.1
  159.9 2.5 %convolution_add_fusion = f32[128,2048]{1,0:T(8,128)} fusion(f32[128,2048]{1,0:T(8,128)S(1)} %fusion.9, bf16[2048,1024]{1,0:T(8,128)(2,1)S(1)} %collective-permute-done.1, bf16[128,2048]{1,0:T(8,128)(2,1)S(1)} %copy-done.1, s32[]{:T(128)S(6)} %select_n.29), kind=kOutput, calls=%fused_computation.6 | convolution fusion | flops 537133056 | bytes 6553604 | tf_op jit(solution)/shard_map/dot_general | solution.py:22
  (1 shorter events, 0.0 us)
Async XLA Ops:
  6.5 9.6 %copy-start = (bf16[2048,256]{1,0:T(8,128)(2,1)S(1)}, bf16[2048,256]{1,0:T(8,128)(2,1)}, u32[]{:S(2)}) copy-start(bf16[2048,256]{1,0:T(8,128)(2,1)} %param.5) | copy-start | bytes 3145732
  6.5 145.9 %all-gather.2.cloned.1.call-start = ((), (), s32[]{:S(2)}) async-start(), calls=%async_computation | async-start | bytes 4456448 | tf_op jit(solution)/shard_map/all_gather | solution.py:530
  7.6 7.8 %collective-permute-start = (bf16[128,1024]{1,0:T(8,128)(2,1)S(1)}, bf16[128,1024]{1,0:T(8,128)(2,1)S(1)}, u32[]{:S(2)}, u32[]{:S(2)}) collective-permute-start(bf16[128,1024]{1,0:T(8,128)(2,1)S(1)} %constant_dynamic-slice_fusion), channel_id=1, source_target_pairs={{0,0},{64,16},{128,32},{192,48},{16,64},{80,80},{144,96},{208,112}... | collective-permute-start | bytes 786440 | tf_op jit(solution)/shard_map/ppermute | solution.py:529
  15.4 0.7 copy-start.2
  16.2 4.7 %copy-start.5 = (bf16[2048,2048]{1,0:T(8,128)(2,1)S(1)}, bf16[2048,2048]{1,0:T(8,128)(2,1)}, u32[]{:S(2)}) copy-start(bf16[2048,2048]{1,0:T(8,128)(2,1)} %param.6) | copy-start | bytes 25165828
  20.9 55.1 %copy-start.3 = (f32[2048]{0:T(1024)S(1)}, f32[2048]{0:T(1024)}, u32[]{:S(2)}) copy-start(f32[2048]{0:T(1024)} %param.8) | copy-start | bytes 24580
  20.9 55.1 %copy-start.4 = (f32[2048]{0:T(1024)S(1)}, f32[2048]{0:T(1024)}, u32[]{:S(2)}) copy-start(f32[2048]{0:T(1024)} %param.9) | copy-start | bytes 24580
  152.4 7.5 %copy-start.1 = (bf16[128,2048]{1,0:T(8,128)(2,1)S(1)}, bf16[128,2048]{1,0:T(8,128)(2,1)}, u32[]{:S(2)}) copy-start(bf16[128,2048]{1,0:T(8,128)(2,1)} %shard_map.56) | copy-start | bytes 1572868
  152.5 7.5 %collective-permute-start.1 = (bf16[2048,1024]{1,0:T(8,128)(2,1)}, bf16[2048,1024]{1,0:T(8,128)(2,1)S(1)}, u32[]{:S(2)}, u32[]{:S(2)}) collective-permute-start(bf16[2048,1024]{1,0:T(8,128)(2,1)} %all-gather.2.cloned.1.call-done), channel_id=1, source_target_pairs={{0,64},{64,0},{128,192},{192,128},{1,65},{65,1},{129,193},{193,129... | collective-permute-start | bytes 12582920 | tf_op jit(solution)/shard_map/ppermute | solution.py:533
Sparse Core Ops, SparseCore 0:
  16.3 94.5 all-gather.1

commit v22 on v20

--- a/solution.py
+++ b/solution.py
@@ -351,14 +351,22 @@
             recv_sem=recv_d.at[chunk_at], device_id=sibling, device_id_type=MESH,
         )
 
+    chunk = coll.shape[-1]
+
+    def chunk_dot(blocks, at, h):
+        columns = shapes_ref[:, pl.ds(pl.multiple_of(at * chunk, chunk), chunk)]
+        return lax.dot_general(
+            columns, blocks[at, h], (((1,), (1,)), ((), ())), preferred_element_type=jnp.float32
+        )
+
     to_sibling(me).start()
     pending.append(to_sibling(me))
+    own = [chunk_dot(coll, me, h) for h in range(2)]
     for k in range(1, n):
         step(coll.at[me], coll.at[sender(k)], k, device("pl", sender(k)), (send_c, recv_c)).wait_recv()
         to_sibling(sender(k)).start()
         pending.append(to_sibling(sender(k)))
-
-    chunk = coll.shape[-1]
+        own = [own[h] + chunk_dot(coll, sender(k), h) for h in range(2)]
 
     def weighted_block(blocks, h):
         acc = jnp.zeros((shapes_ref.shape[0], blocks.shape[2]), jnp.float32)
@@ -369,7 +377,6 @@
             )
         return acc
 
-    own = [weighted_block(coll, h) for h in range(2)]
     for l in range(n):
         to_sibling(l).wait_recv()
     other = [weighted_block(sib_coll, h) for h in range(2)]

time: 170 us -> 170 us (level)
  transfers between devices with their start and end apart: 3 -> 3, of which waited for: 2 -> 2; matrix products, arithmetic and copies ran while one was open for 8% -> 9% of each run, Pallas kernels for 74% -> 74%
where the time goes in v22:
time: 170 us; the launch traced here: 169 us
  Pallas kernels  125 us (74%)
  matrix products  13.8 us (8%)
  between operations  13.5 us (8%)
  waiting for transfers between devices  7.37 us (4%)
  starting transfers between devices  4.14 us (2%)
  local copies, waits for them, and re-layouts  3.2 us (2%)
  other arithmetic  1.79 us (1%)
    pallas_call x1, Pallas kernels, gram_weighted(): pl.pallas_call(kernel, out_shape=jax.ShapeDtypeStruct((wshape[1], n_col *...  71.4 us
    pallas_call x1, Pallas kernels, modal_sum(): pl.pallas_call(kernel, out_shape=jax.ShapeDtypeStruct((2,) + block, jnp.b...  53.3 us
    dot_general x3, matrix products, outer_rows(): lax.dot_general(left_rows, right_rows, (((1,), (1,)), ((), ())), preferre...  7.08 us
    dot_general x1, matrix products, body(): mine = jnp.dot(own_modes, factor_cols, preferred_element_type=jnp.float32)  4.57 us
    ppermute x1, waiting for transfers between devices, body(): panel_piece = lax.ppermute(send_half, ('prow', 'pcol'), swap)  4.04 us
    ppermute x1, starting transfers between devices, body(): panel_piece = lax.ppermute(send_half, ('prow', 'pcol'), swap)  3.77 us
  transfers between devices with their start and end apart: 3, of which 2 were waited for; matrix products, arithmetic and copies ran while one was open for 9% of the time, Pallas kernels for 74%

profile of v22, /device:TPU:39, one launch (start us, length us, event | category | flops | bytes accessed | tf_op | source)
XLA Modules:
  0.0 168.5 jit_solution(4857122845689236776)
XLA Ops:
  6.5 0.0 copy-start
  6.5 0.0 all-gather.2.cloned.1.call-start
  6.5 1.1 constant_dynamic-slice_fusion
  7.6 3.8 %collective-permute-start = (bf16[128,1024]{1,0:T(8,128)(2,1)S(1)}, bf16[128,1024]{1,0:T(8,128)(2,1)S(1)}, u32[]{:S(2)}, u32[]{:S(2)}) collective-permute-start(bf16[128,1024]{1,0:T(8,128)(2,1)S(1)} %constant_dynamic-slice_fusion), channel_id=1, source_target_pairs={{0,0},{64,16},{128,32},{192,48},{16,64},{80,80},{144,96},{208,112}... | collective-permute-start | bytes 786440 | tf_op jit(solution)/shard_map/ppermute | solution.py:528
  11.4 4.0 %collective-permute-done = bf16[128,1024]{1,0:T(8,128)(2,1)S(1)} collective-permute-done((bf16[128,1024]{1,0:T(8,128)(2,1)S(1)}, bf16[128,1024]{1,0:T(8,128)(2,1)S(1)}, u32[]{:S(2)}, u32[]{:S(2)}) %collective-permute-start) | collective-permute-done | bytes 262176 | tf_op jit(solution)/shard_map/ppermute | solution.py:528
  15.4 0.0 copy-start.2
  15.4 0.7 copy-done.2
  16.1 0.0 all-gather.2.cloned.1.call-update
  16.2 0.0 copy-done
  16.2 0.0 copy-start.5
  16.2 4.6 %fusion.2.mine_ref = f32[1024,256]{1,0:T(8,128)} fusion(bf16[2048,256]{1,0:T(8,128)(2,1)S(1)} %copy-done, bf16[2048,2048]{1,0:T(8,128)(2,1)} %param.6, s32[]{:T(128)S(6)} %select_n.28), kind=kOutput, calls=%fused_computation.2 | convolution fusion | flops 1073741824 | bytes 6291460 | tf_op jit(solution)/shard_map/dot_general | solution.py:510
  20.8 0.1 copy-done.5
  20.9 0.0 copy-start.3
  20.9 0.0 copy-start.4
  20.9 2.1 %fusion.6.theirs_ref = bf16[1024,256]{1,0:T(8,128)(2,1)} fusion(bf16[2048,256]{1,0:T(8,128)(2,1)S(1)} %copy-done, bf16[2048,2048]{1,0:T(8,128)(2,1)S(1)} %copy-done.5, s32[]{:T(128)S(6)} %select_n.29), kind=kOutput, calls=%fused_computation.13 | convolution fusion | flops 1074003968 | bytes 5767172 | tf_op jit(solution)/shard_map/dot_general | solution.py:511
  23.0 53.3 %shard_map.55 = bf16[2,4,256,256]{3,2,1,0:T(8,128)(2,1)} custom-call(f32[1024,256]{1,0:T(8,128)} %fusion.2.mine_ref, bf16[1024,256]{1,0:T(8,128)(2,1)} %fusion.6.theirs_ref), custom_call_target="tpu_custom_call" | custom-call | tf_op jit(solution)/shard_map/pallas_call | solution.py:252
  76.3 0.0 copy-done.3
  76.4 0.0 copy-done.4
  76.4 1.8 %fusion.4 = (bf16[2048,256]{1,0:T(8,128)(2,1)S(1)}, bf16[2048,256]{1,0:T(8,128)(2,1)S(1)}) fusion(bf16[2,4,256,256]{3,2,1,0:T(8,128)(2,1)} %shard_map.55, f32[2048]{0:T(1024)S(1)} %get-tuple-element.11, f32[2048]{0:T(1024)S(1)} %get-tuple-element.12), kind=kLoop, calls=%fused_computation.11 | loop fusion | flops 2621440 | bytes 3162112 | tf_op jit(solution)/shard_map/convert_element_type | solution.py:516
  78.2 0.8 convolution_convert_fusion
  79.0 0.3 copy.6
  79.3 1.0 copy.7
  80.3 71.4 %shard_map.56 = bf16[128,2048]{1,0:T(8,128)(2,1)} custom-call(bf16[16,128,128]{2,1,0:T(8,128)(2,1)} %bitcast.10, bf16[128,2048]{1,0:T(8,128)(2,1)} %shapes_ref.1), custom_call_target="tpu_custom_call" | custom-call | tf_op jit(solution)/shard_map/pallas_call | solution.py:408
  151.7 0.0 copy-start.1
  151.7 0.0 all-gather.2.cloned.1.call-done
  151.7 0.4 collective-permute-start.1
  152.1 3.8 %fusion.9 = f32[128,2048]{1,0:T(8,128)S(1)} fusion(bf16[2048,1024]{1,0:T(8,128)(2,1)} %all-gather.2.cloned.1.call-done, bf16[128,2048]{1,0:T(8,128)(2,1)} %shard_map.56, s32[]{:T(128)S(6)} %select_n.28), kind=kOutput, calls=%fused_computation.14 | convolution fusion | flops 536870912 | bytes 5505028 | tf_op jit(solution)/shard_map/dot_general | solution.py:22
  155.9 3.3 %collective-permute-done.1 = bf16[2048,1024]{1,0:T(8,128)(2,1)S(1)} collective-permute-done((bf16[2048,1024]{1,0:T(8,128)(2,1)}, bf16[2048,1024]{1,0:T(8,128)(2,1)S(1)}, u32[]{:S(2)}, u32[]{:S(2)}) %collective-permute-start.1) | collective-permute-done | bytes 4194336 | tf_op jit(solution)/shard_map/ppermute | solution.py:532
  159.2 0.0 copy-done.1
  159.2 2.5 %convolution_add_fusion = f32[128,2048]{1,0:T(8,128)} fusion(f32[128,2048]{1,0:T(8,128)S(1)} %fusion.9, bf16[2048,1024]{1,0:T(8,128)(2,1)S(1)} %collective-permute-done.1, bf16[128,2048]{1,0:T(8,128)(2,1)S(1)} %copy-done.1, s32[]{:T(128)S(6)} %select_n.29), kind=kOutput, calls=%fused_computation.6 | convolution fusion | flops 537133056 | bytes 6553604 | tf_op jit(solution)/shard_map/dot_general | solution.py:22
  (1 shorter events, 0.0 us)
Async XLA Ops:
  6.5 9.6 %copy-start = (bf16[2048,256]{1,0:T(8,128)(2,1)S(1)}, bf16[2048,256]{1,0:T(8,128)(2,1)}, u32[]{:S(2)}) copy-start(bf16[2048,256]{1,0:T(8,128)(2,1)} %param.5) | copy-start | bytes 3145732
  6.5 145.2 %all-gather.2.cloned.1.call-start = ((), (), s32[]{:S(2)}) async-start(), calls=%async_computation | async-start | bytes 4456448 | tf_op jit(solution)/shard_map/all_gather | solution.py:529
  7.6 7.8 %collective-permute-start = (bf16[128,1024]{1,0:T(8,128)(2,1)S(1)}, bf16[128,1024]{1,0:T(8,128)(2,1)S(1)}, u32[]{:S(2)}, u32[]{:S(2)}) collective-permute-start(bf16[128,1024]{1,0:T(8,128)(2,1)S(1)} %constant_dynamic-slice_fusion), channel_id=1, source_target_pairs={{0,0},{64,16},{128,32},{192,48},{16,64},{80,80},{144,96},{208,112}... | collective-permute-start | bytes 786440 | tf_op jit(solution)/shard_map/ppermute | solution.py:528
  15.4 0.7 copy-start.2
  16.2 4.7 %copy-start.5 = (bf16[2048,2048]{1,0:T(8,128)(2,1)S(1)}, bf16[2048,2048]{1,0:T(8,128)(2,1)}, u32[]{:S(2)}) copy-start(bf16[2048,2048]{1,0:T(8,128)(2,1)} %param.6) | copy-start | bytes 25165828
  20.9 55.5 %copy-start.3 = (f32[2048]{0:T(1024)S(1)}, f32[2048]{0:T(1024)}, u32[]{:S(2)}) copy-start(f32[2048]{0:T(1024)} %param.8) | copy-start | bytes 24580
  20.9 55.5 %copy-start.4 = (f32[2048]{0:T(1024)S(1)}, f32[2048]{0:T(1024)}, u32[]{:S(2)}) copy-start(f32[2048]{0:T(1024)} %param.9) | copy-start | bytes 24580
  151.7 7.5 %copy-start.1 = (bf16[128,2048]{1,0:T(8,128)(2,1)S(1)}, bf16[128,2048]{1,0:T(8,128)(2,1)}, u32[]{:S(2)}) copy-start(bf16[128,2048]{1,0:T(8,128)(2,1)} %shard_map.56) | copy-start | bytes 1572868
  151.7 7.5 %collective-permute-start.1 = (bf16[2048,1024]{1,0:T(8,128)(2,1)}, bf16[2048,1024]{1,0:T(8,128)(2,1)S(1)}, u32[]{:S(2)}, u32[]{:S(2)}) collective-permute-start(bf16[2048,1024]{1,0:T(8,128)(2,1)} %all-gather.2.cloned.1.call-done), channel_id=1, source_target_pairs={{0,64},{64,0},{128,192},{192,128},{1,65},{65,1},{129,193},{193,129... | collective-permute-start | bytes 12582920 | tf_op jit(solution)/shard_map/ppermute | solution.py:532
Sparse Core Ops, SparseCore 0:
  16.3 93.9 all-gather.1

commit v23 on v20

--- a/solution.py
+++ b/solution.py
@@ -207,7 +207,7 @@
     chip.start()
     pending.append(chip)
     chip.wait_recv()
-    summed = mine_ref[...] + sib_in[...].astype(jnp.float32)
+    summed = mine_ref[...].astype(jnp.float32) + sib_in[...].astype(jnp.float32)
     pieces[...] = summed.astype(pieces.dtype).reshape(pieces.shape)
 
     for k in range(1, n):
@@ -502,7 +502,8 @@
         sib_modes = lax.dynamic_slice_in_dim(modal_at_loads, (1 - core) * (modes // 2), modes // 2, 0)
         mine = jnp.dot(own_modes, factor_cols, preferred_element_type=jnp.float32)
         theirs = jnp.dot(sib_modes, factor_cols, preferred_element_type=jnp.float32)
-        modal_load = modal_sum(mine, theirs.astype(jnp.bfloat16), axes, sizes).reshape(modes, width)
+        bf16 = jnp.bfloat16
+        modal_load = modal_sum(mine.astype(bf16), theirs.astype(bf16), axes, sizes).reshape(modes, width)
         modal_wide = modal_load.astype(jnp.float32)
         pseudo = jnp.concatenate(
             [

time: 170 us -> 170 us (level)
    dot_general x1, matrix products: 4.57 us -> 2.07 us  [body(): mine = jnp.dot(own_modes, factor_cols, preferred_element_type=jnp.float32)]
    dot_general x1, matrix products: 2.12 us -> 4.44 us  [body(): theirs = jnp.dot(sib_modes, factor_cols, preferred_element_type=jnp.float32)]
where the time goes in v23:
time: 170 us; the launch traced here: 169 us
  Pallas kernels  126 us (74%)
  matrix products  13.6 us (8%)
  between operations  13.5 us (8%)
  waiting for transfers between devices  7.28 us (4%)
  starting transfers between devices  4.25 us (2%)
  local copies, waits for them, and re-layouts  3.33 us (2%)
  other arithmetic  1.79 us (1%)
    pallas_call x1, Pallas kernels, gram_weighted(): pl.pallas_call(kernel, out_shape=jax.ShapeDtypeStruct((wshape[1], n_col *...  72.3 us
    pallas_call x1, Pallas kernels, modal_sum(): pl.pallas_call(kernel, out_shape=jax.ShapeDtypeStruct((2,) + block, jnp.b...  53.2 us
    dot_general x3, matrix products, outer_rows(): lax.dot_general(left_rows, right_rows, (((1,), (1,)), ((), ())), preferre...  7.08 us
    dot_general x1, matrix products, body(): theirs = jnp.dot(sib_modes, factor_cols, preferred_element_type=jnp.float32)  4.44 us
    ppermute x1, waiting for transfers between devices, body(): panel_piece = lax.ppermute(send_half, ('prow', 'pcol'), swap)  4.04 us
    ppermute x1, starting transfers between devices, body(): panel_piece = lax.ppermute(send_half, ('prow', 'pcol'), swap)  3.77 us
  transfers between devices with their start and end apart: 3, of which 2 were waited for; matrix products, arithmetic and copies ran while one was open for 8% of the time, Pallas kernels for 74%

profile of v23, /device:TPU:39, one launch (start us, length us, event | category | flops | bytes accessed | tf_op | source)
XLA Modules:
  0.0 169.3 jit_solution(3982619442088085551)
XLA Ops:
  6.5 0.0 copy-start
  6.5 0.0 all-gather.2.cloned.1.call-start
  6.5 1.1 constant_dynamic-slice_fusion
  7.6 3.8 %collective-permute-start = (bf16[128,1024]{1,0:T(8,128)(2,1)S(1)}, bf16[128,1024]{1,0:T(8,128)(2,1)S(1)}, u32[]{:S(2)}, u32[]{:S(2)}) collective-permute-start(bf16[128,1024]{1,0:T(8,128)(2,1)S(1)} %constant_dynamic-slice_fusion), channel_id=1, source_target_pairs={{0,0},{64,16},{128,32},{192,48},{16,64},{80,80},{144,96},{208,112}... | collective-permute-start | bytes 786440 | tf_op jit(solution)/shard_map/ppermute | solution.py:522
  11.4 4.0 %collective-permute-done = bf16[128,1024]{1,0:T(8,128)(2,1)S(1)} collective-permute-done((bf16[128,1024]{1,0:T(8,128)(2,1)S(1)}, bf16[128,1024]{1,0:T(8,128)(2,1)S(1)}, u32[]{:S(2)}, u32[]{:S(2)}) %collective-permute-start) | collective-permute-done | bytes 262176 | tf_op jit(solution)/shard_map/ppermute | solution.py:522
  15.4 0.0 copy-start.2
  15.4 0.7 copy-done.2
  16.1 0.0 all-gather.2.cloned.1.call-update
  16.2 0.0 copy-done
  16.2 0.0 copy-start.5
  16.2 4.4 %fusion.9.theirs_ref = bf16[1024,256]{1,0:T(8,128)(2,1)} fusion(bf16[2048,256]{1,0:T(8,128)(2,1)S(1)} %copy-done, bf16[2048,2048]{1,0:T(8,128)(2,1)} %param.6, s32[]{:T(128)S(6)} %select_n.29), kind=kOutput, calls=%fused_computation.14 | convolution fusion | flops 1074003968 | bytes 5767172 | tf_op jit(solution)/shard_map/dot_general | solution.py:504
  20.6 0.3 copy-done.5
  20.9 0.0 copy-start.3
  20.9 0.0 copy-start.4
  20.9 2.1 %fusion.6.mine_ref = bf16[1024,256]{1,0:T(8,128)(2,1)} fusion(bf16[2048,256]{1,0:T(8,128)(2,1)S(1)} %copy-done, bf16[2048,2048]{1,0:T(8,128)(2,1)S(1)} %copy-done.5, s32[]{:T(128)S(6)} %select_n.28), kind=kOutput, calls=%fused_computation.13 | convolution fusion | flops 1074003968 | bytes 5767172 | tf_op jit(solution)/shard_map/dot_general | solution.py:503
  23.0 53.2 %shard_map.55 = bf16[2,4,256,256]{3,2,1,0:T(8,128)(2,1)} custom-call(bf16[1024,256]{1,0:T(8,128)(2,1)} %fusion.6.mine_ref, bf16[1024,256]{1,0:T(8,128)(2,1)} %fusion.9.theirs_ref), custom_call_target="tpu_custom_call" | custom-call | tf_op jit(solution)/shard_map/pallas_call | solution.py:252
  76.2 0.0 copy-done.3
  76.2 0.0 copy-done.4
  76.2 1.8 %fusion.4 = (bf16[2048,256]{1,0:T(8,128)(2,1)S(1)}, bf16[2048,256]{1,0:T(8,128)(2,1)S(1)}) fusion(bf16[2,4,256,256]{3,2,1,0:T(8,128)(2,1)} %shard_map.55, f32[2048]{0:T(1024)S(1)} %get-tuple-element.11, f32[2048]{0:T(1024)S(1)} %get-tuple-element.12), kind=kLoop, calls=%fused_computation.11 | loop fusion | flops 2621440 | bytes 3162112 | tf_op jit(solution)/shard_map/convert_element_type | solution.py:510
  78.0 0.8 convolution_convert_fusion
  78.8 0.3 copy.6
  79.1 1.0 copy.7
  80.1 72.3 %shard_map.56 = bf16[128,2048]{1,0:T(8,128)(2,1)} custom-call(bf16[16,128,128]{2,1,0:T(8,128)(2,1)} %bitcast.10, bf16[128,2048]{1,0:T(8,128)(2,1)} %shapes_ref.1), custom_call_target="tpu_custom_call" | custom-call | tf_op jit(solution)/shard_map/pallas_call | solution.py:401
  152.4 0.0 copy-start.1
  152.4 0.0 all-gather.2.cloned.1.call-done
  152.5 0.5 collective-permute-start.1
  153.0 3.8 %fusion.12 = f32[128,2048]{1,0:T(8,128)S(1)} fusion(bf16[2048,1024]{1,0:T(8,128)(2,1)} %all-gather.2.cloned.1.call-done, bf16[128,2048]{1,0:T(8,128)(2,1)} %shard_map.56, s32[]{:T(128)S(6)} %select_n.28), kind=kOutput, calls=%fused_computation.15 | convolution fusion | flops 536870912 | bytes 5505028 | tf_op jit(solution)/shard_map/dot_general | solution.py:22
  156.7 3.2 %collective-permute-done.1 = bf16[2048,1024]{1,0:T(8,128)(2,1)S(1)} collective-permute-done((bf16[2048,1024]{1,0:T(8,128)(2,1)}, bf16[2048,1024]{1,0:T(8,128)(2,1)S(1)}, u32[]{:S(2)}, u32[]{:S(2)}) %collective-permute-start.1) | collective-permute-done | bytes 4194336 | tf_op jit(solution)/shard_map/ppermute | solution.py:526
  160.0 0.0 copy-done.1
  160.0 2.5 %convolution_add_fusion = f32[128,2048]{1,0:T(8,128)} fusion(f32[128,2048]{1,0:T(8,128)S(1)} %fusion.12, bf16[2048,1024]{1,0:T(8,128)(2,1)S(1)} %collective-permute-done.1, bf16[128,2048]{1,0:T(8,128)(2,1)S(1)} %copy-done.1, s32[]{:T(128)S(6)} %select_n.29), kind=kOutput, calls=%fused_computation.6 | convolution fusion | flops 537133056 | bytes 6553604 | tf_op jit(solution)/shard_map/dot_general | solution.py:22
  (1 shorter events, 0.0 us)
Async XLA Ops:
  6.5 9.6 %copy-start = (bf16[2048,256]{1,0:T(8,128)(2,1)S(1)}, bf16[2048,256]{1,0:T(8,128)(2,1)}, u32[]{:S(2)}) copy-start(bf16[2048,256]{1,0:T(8,128)(2,1)} %param.5) | copy-start | bytes 3145732
  6.5 145.9 %all-gather.2.cloned.1.call-start = ((), (), s32[]{:S(2)}) async-start(), calls=%async_computation | async-start | bytes 4456448 | tf_op jit(solution)/shard_map/all_gather | solution.py:523
  7.6 7.8 %collective-permute-start = (bf16[128,1024]{1,0:T(8,128)(2,1)S(1)}, bf16[128,1024]{1,0:T(8,128)(2,1)S(1)}, u32[]{:S(2)}, u32[]{:S(2)}) collective-permute-start(bf16[128,1024]{1,0:T(8,128)(2,1)S(1)} %constant_dynamic-slice_fusion), channel_id=1, source_target_pairs={{0,0},{64,16},{128,32},{192,48},{16,64},{80,80},{144,96},{208,112}... | collective-permute-start | bytes 786440 | tf_op jit(solution)/shard_map/ppermute | solution.py:522
  15.4 0.7 copy-start.2
  16.2 4.7 %copy-start.5 = (bf16[2048,2048]{1,0:T(8,128)(2,1)S(1)}, bf16[2048,2048]{1,0:T(8,128)(2,1)}, u32[]{:S(2)}) copy-start(bf16[2048,2048]{1,0:T(8,128)(2,1)} %param.6) | copy-start | bytes 25165828
  20.9 55.3 %copy-start.3 = (f32[2048]{0:T(1024)S(1)}, f32[2048]{0:T(1024)}, u32[]{:S(2)}) copy-start(f32[2048]{0:T(1024)} %param.8) | copy-start | bytes 24580
  20.9 55.3 %copy-start.4 = (f32[2048]{0:T(1024)S(1)}, f32[2048]{0:T(1024)}, u32[]{:S(2)}) copy-start(f32[2048]{0:T(1024)} %param.9) | copy-start | bytes 24580
  152.4 7.5 %copy-start.1 = (bf16[128,2048]{1,0:T(8,128)(2,1)S(1)}, bf16[128,2048]{1,0:T(8,128)(2,1)}, u32[]{:S(2)}) copy-start(bf16[128,2048]{1,0:T(8,128)(2,1)} %shard_map.56) | copy-start | bytes 1572868
  152.5 7.5 %collective-permute-start.1 = (bf16[2048,1024]{1,0:T(8,128)(2,1)}, bf16[2048,1024]{1,0:T(8,128)(2,1)S(1)}, u32[]{:S(2)}, u32[]{:S(2)}) collective-permute-start(bf16[2048,1024]{1,0:T(8,128)(2,1)} %all-gather.2.cloned.1.call-done), channel_id=1, source_target_pairs={{0,64},{64,0},{128,192},{192,128},{1,65},{65,1},{129,193},{193,129... | collective-permute-start | bytes 12582920 | tf_op jit(solution)/shard_map/ppermute | solution.py:526
Sparse Core Ops, SparseCore 0:
  16.3 98.0 all-gather.1

commit v24 on v20

--- a/solution.py
+++ b/solution.py
@@ -214,10 +214,9 @@
         step(pieces.at[peer(k)], got.at[me], k, device("pcol", peer(k)), (send_a, recv_a)).start()
     for k in range(1, n):
         pending.append(step(pieces.at[peer(k)], got.at[me], k, device("pcol", peer(k)), (send_a, recv_a)))
+    total = pieces[me].astype(jnp.float32)
     for k in range(1, n):
         step(pieces.at[me], got.at[sender(k)], k, device("pcol", sender(k)), (send_a, recv_a)).wait_recv()
-    total = pieces[me].astype(jnp.float32)
-    for k in range(1, n):
         total = total + got[sender(k)].astype(jnp.float32)
     part_out[...] = total.astype(part_out.dtype)
 
@@ -326,10 +325,9 @@
         step(x_ref.at[peer(k)], got.at[me], k, device("pl", peer(k)), (send_a, recv_a)).start()
     for k in range(1, n):
         pending.append(step(x_ref.at[peer(k)], got.at[me], k, device("pl", peer(k)), (send_a, recv_a)))
+    total = x_ref[me].astype(jnp.float32)
     for k in range(1, n):
         step(x_ref.at[me], got.at[sender(k)], k, device("pl", sender(k)), (send_a, recv_a)).wait_recv()
-    total = x_ref[me].astype(jnp.float32)
-    for k in range(1, n):
         total = total + got[sender(k)].astype(jnp.float32)
     part_out[...] = total.astype(part_out.dtype)
 

time: 170 us -> 171 us (level)
  no operation moved by 1% of the time
where the time goes in v24:
time: 171 us; the launch traced here: 169 us
  Pallas kernels  125 us (73%)
  matrix products  13.8 us (8%)
  between operations  13.5 us (8%)
  waiting for transfers between devices  7.28 us (4%)
  starting transfers between devices  4.25 us (2%)
  local copies, waits for them, and re-layouts  3.2 us (2%)
  other arithmetic  1.79 us (1%)
    pallas_call x1, Pallas kernels, gram_weighted(): pl.pallas_call(kernel, out_shape=jax.ShapeDtypeStruct((wshape[1], n_col *...  72.1 us
    pallas_call x1, Pallas kernels, modal_sum(): pl.pallas_call(kernel, out_shape=jax.ShapeDtypeStruct((2,) + block, jnp.b...  53.3 us
    dot_general x3, matrix products, outer_rows(): lax.dot_general(left_rows, right_rows, (((1,), (1,)), ((), ())), preferre...  7.08 us
    dot_general x1, matrix products, body(): mine = jnp.dot(own_modes, factor_cols, preferred_element_type=jnp.float32)  4.57 us
    ppermute x1, waiting for transfers between devices, body(): panel_piece = lax.ppermute(send_half, ('prow', 'pcol'), swap)  4.04 us
    ppermute x1, starting transfers between devices, body(): panel_piece = lax.ppermute(send_half, ('prow', 'pcol'), swap)  3.77 us
  transfers between devices with their start and end apart: 3, of which 2 were waited for; matrix products, arithmetic and copies ran while one was open for 8% of the time, Pallas kernels for 74%

profile of v24, /device:TPU:39, one launch (start us, length us, event | category | flops | bytes accessed | tf_op | source)
XLA Modules:
  0.0 169.2 jit_solution(5396910682469275875)
XLA Ops:
  6.5 0.0 copy-start
  6.5 0.0 all-gather.2.cloned.1.call-start
  6.5 1.1 constant_dynamic-slice_fusion
  7.6 3.8 %collective-permute-start = (bf16[128,1024]{1,0:T(8,128)(2,1)S(1)}, bf16[128,1024]{1,0:T(8,128)(2,1)S(1)}, u32[]{:S(2)}, u32[]{:S(2)}) collective-permute-start(bf16[128,1024]{1,0:T(8,128)(2,1)S(1)} %constant_dynamic-slice_fusion), channel_id=1, source_target_pairs={{0,0},{64,16},{128,32},{192,48},{16,64},{80,80},{144,96},{208,112}... | collective-permute-start | bytes 786440 | tf_op jit(solution)/shard_map/ppermute | solution.py:519
  11.4 4.0 %collective-permute-done = bf16[128,1024]{1,0:T(8,128)(2,1)S(1)} collective-permute-done((bf16[128,1024]{1,0:T(8,128)(2,1)S(1)}, bf16[128,1024]{1,0:T(8,128)(2,1)S(1)}, u32[]{:S(2)}, u32[]{:S(2)}) %collective-permute-start) | collective-permute-done | bytes 262176 | tf_op jit(solution)/shard_map/ppermute | solution.py:519
  15.4 0.0 copy-start.2
  15.4 0.7 copy-done.2
  16.1 0.0 all-gather.2.cloned.1.call-update
  16.2 0.0 copy-done
  16.2 0.0 copy-start.5
  16.2 4.6 %fusion.2.mine_ref = f32[1024,256]{1,0:T(8,128)} fusion(bf16[2048,256]{1,0:T(8,128)(2,1)S(1)} %copy-done, bf16[2048,2048]{1,0:T(8,128)(2,1)} %param.6, s32[]{:T(128)S(6)} %select_n.28), kind=kOutput, calls=%fused_computation.2 | convolution fusion | flops 1073741824 | bytes 6291460 | tf_op jit(solution)/shard_map/dot_general | solution.py:501
  20.8 0.1 copy-done.5
  20.9 0.0 copy-start.3
  20.9 0.0 copy-start.4
  20.9 2.1 %fusion.6.theirs_ref = bf16[1024,256]{1,0:T(8,128)(2,1)} fusion(bf16[2048,256]{1,0:T(8,128)(2,1)S(1)} %copy-done, bf16[2048,2048]{1,0:T(8,128)(2,1)S(1)} %copy-done.5, s32[]{:T(128)S(6)} %select_n.29), kind=kOutput, calls=%fused_computation.13 | convolution fusion | flops 1074003968 | bytes 5767172 | tf_op jit(solution)/shard_map/dot_general | solution.py:502
  23.0 53.3 %shard_map.55 = bf16[2,4,256,256]{3,2,1,0:T(8,128)(2,1)} custom-call(f32[1024,256]{1,0:T(8,128)} %fusion.2.mine_ref, bf16[1024,256]{1,0:T(8,128)(2,1)} %fusion.6.theirs_ref), custom_call_target="tpu_custom_call" | custom-call | tf_op jit(solution)/shard_map/pallas_call | solution.py:251
  76.3 0.0 copy-done.3
  76.3 0.0 copy-done.4
  76.3 1.8 %fusion.4 = (bf16[2048,256]{1,0:T(8,128)(2,1)S(1)}, bf16[2048,256]{1,0:T(8,128)(2,1)S(1)}) fusion(bf16[2,4,256,256]{3,2,1,0:T(8,128)(2,1)} %shard_map.55, f32[2048]{0:T(1024)S(1)} %get-tuple-element.11, f32[2048]{0:T(1024)S(1)} %get-tuple-element.12), kind=kLoop, calls=%fused_computation.11 | loop fusion | flops 2621440 | bytes 3162112 | tf_op jit(solution)/shard_map/convert_element_type | solution.py:507
  78.1 0.8 convolution_convert_fusion
  78.9 0.3 copy.6
  79.2 1.0 copy.7
  80.2 72.1 %shard_map.56 = bf16[128,2048]{1,0:T(8,128)(2,1)} custom-call(bf16[16,128,128]{2,1,0:T(8,128)(2,1)} %bitcast.10, bf16[128,2048]{1,0:T(8,128)(2,1)} %shapes_ref.1), custom_call_target="tpu_custom_call" | custom-call | tf_op jit(solution)/shard_map/pallas_call | solution.py:399
  152.3 0.0 copy-start.1
  152.3 0.0 all-gather.2.cloned.1.call-done
  152.3 0.5 collective-permute-start.1
  152.8 3.8 %fusion.9 = f32[128,2048]{1,0:T(8,128)S(1)} fusion(bf16[2048,1024]{1,0:T(8,128)(2,1)} %all-gather.2.cloned.1.call-done, bf16[128,2048]{1,0:T(8,128)(2,1)} %shard_map.56, s32[]{:T(128)S(6)} %select_n.28), kind=kOutput, calls=%fused_computation.14 | convolution fusion | flops 536870912 | bytes 5505028 | tf_op jit(solution)/shard_map/dot_general | solution.py:22
  156.6 3.2 %collective-permute-done.1 = bf16[2048,1024]{1,0:T(8,128)(2,1)S(1)} collective-permute-done((bf16[2048,1024]{1,0:T(8,128)(2,1)}, bf16[2048,1024]{1,0:T(8,128)(2,1)S(1)}, u32[]{:S(2)}, u32[]{:S(2)}) %collective-permute-start.1) | collective-permute-done | bytes 4194336 | tf_op jit(solution)/shard_map/ppermute | solution.py:523
  159.8 0.0 copy-done.1
  159.8 2.5 %convolution_add_fusion = f32[128,2048]{1,0:T(8,128)} fusion(f32[128,2048]{1,0:T(8,128)S(1)} %fusion.9, bf16[2048,1024]{1,0:T(8,128)(2,1)S(1)} %collective-permute-done.1, bf16[128,2048]{1,0:T(8,128)(2,1)S(1)} %copy-done.1, s32[]{:T(128)S(6)} %select_n.29), kind=kOutput, calls=%fused_computation.6 | convolution fusion | flops 537133056 | bytes 6553604 | tf_op jit(solution)/shard_map/dot_general | solution.py:22
  (1 shorter events, 0.0 us)
Async XLA Ops:
  6.5 9.6 %copy-start = (bf16[2048,256]{1,0:T(8,128)(2,1)S(1)}, bf16[2048,256]{1,0:T(8,128)(2,1)}, u32[]{:S(2)}) copy-start(bf16[2048,256]{1,0:T(8,128)(2,1)} %param.5) | copy-start | bytes 3145732
  6.5 145.8 %all-gather.2.cloned.1.call-start = ((), (), s32[]{:S(2)}) async-start(), calls=%async_computation | async-start | bytes 4456448 | tf_op jit(solution)/shard_map/all_gather | solution.py:520
  7.6 7.8 %collective-permute-start = (bf16[128,1024]{1,0:T(8,128)(2,1)S(1)}, bf16[128,1024]{1,0:T(8,128)(2,1)S(1)}, u32[]{:S(2)}, u32[]{:S(2)}) collective-permute-start(bf16[128,1024]{1,0:T(8,128)(2,1)S(1)} %constant_dynamic-slice_fusion), channel_id=1, source_target_pairs={{0,0},{64,16},{128,32},{192,48},{16,64},{80,80},{144,96},{208,112}... | collective-permute-start | bytes 786440 | tf_op jit(solution)/shard_map/ppermute | solution.py:519
  15.4 0.7 copy-start.2
  16.2 4.7 %copy-start.5 = (bf16[2048,2048]{1,0:T(8,128)(2,1)S(1)}, bf16[2048,2048]{1,0:T(8,128)(2,1)}, u32[]{:S(2)}) copy-start(bf16[2048,2048]{1,0:T(8,128)(2,1)} %param.6) | copy-start | bytes 25165828
  20.9 55.4 %copy-start.3 = (f32[2048]{0:T(1024)S(1)}, f32[2048]{0:T(1024)}, u32[]{:S(2)}) copy-start(f32[2048]{0:T(1024)} %param.8) | copy-start | bytes 24580
  20.9 55.4 %copy-start.4 = (f32[2048]{0:T(1024)S(1)}, f32[2048]{0:T(1024)}, u32[]{:S(2)}) copy-start(f32[2048]{0:T(1024)} %param.9) | copy-start | bytes 24580
  152.3 7.5 %copy-start.1 = (bf16[128,2048]{1,0:T(8,128)(2,1)S(1)}, bf16[128,2048]{1,0:T(8,128)(2,1)}, u32[]{:S(2)}) copy-start(bf16[128,2048]{1,0:T(8,128)(2,1)} %shard_map.56) | copy-start | bytes 1572868
  152.3 7.5 %collective-permute-start.1 = (bf16[2048,1024]{1,0:T(8,128)(2,1)}, bf16[2048,1024]{1,0:T(8,128)(2,1)S(1)}, u32[]{:S(2)}, u32[]{:S(2)}) collective-permute-start(bf16[2048,1024]{1,0:T(8,128)(2,1)} %all-gather.2.cloned.1.call-done), channel_id=1, source_target_pairs={{0,64},{64,0},{128,192},{192,128},{1,65},{65,1},{129,193},{193,129... | collective-permute-start | bytes 12582920 | tf_op jit(solution)/shard_map/ppermute | solution.py:523
Sparse Core Ops, SparseCore 0:
  16.3 101.1 all-gather.1

commit v25 on v20

--- a/solution.py
+++ b/solution.py
@@ -370,25 +370,35 @@
         return acc
 
     own = [weighted_block(coll, h) for h in range(2)]
+    wpeer = lambda k: lax.rem(col + k, n_col)
+    wsender = lambda k: lax.rem(col + n_col - k, n_col)
+    blocks_w = wbuf.shape[1]
+
+    def w_copy(k, r, to_col, at_col):
+        return pltpu.make_async_remote_copy(
+            src_ref=wbuf.at[col, r], dst_ref=wbuf.at[at_col, r], send_sem=send_e.at[k * blocks_w + r],
+            recv_sem=recv_e.at[k * blocks_w + r], device_id=device("pcol", to_col), device_id_type=MESH,
+        )
+
+    def send_blocks(values, first):
+        for h in range(2):
+            r = 2 * h + first
+            wbuf[col, r] = values[h].astype(wbuf.dtype)
+            for k in range(1, n_col):
+                w_copy(k, r, wpeer(k), col).start()
+                pending.append(w_copy(k, r, wpeer(k), col))
+
+    send_blocks(own, core)
     for l in range(n):
         to_sibling(l).wait_recv()
-    other = [weighted_block(sib_coll, h) for h in range(2)]
-    parts = []
-    for h in range(2):
-        parts += [jnp.where(core == 0, own[h], other[h]), jnp.where(core == 0, other[h], own[h])]
-    wbuf[col] = jnp.concatenate(parts, axis=1).astype(wbuf.dtype)
-
-    wpeer = lambda k: lax.rem(col + k, n_col)
-    wsender = lambda k: lax.rem(col + n_col - k, n_col)
+    send_blocks([weighted_block(sib_coll, h) for h in range(2)], 1 - core)
     for k in range(1, n_col):
-        step(wbuf.at[col], wbuf.at[col], k, device("pcol", wpeer(k)), (send_e, recv_e)).start()
-    for k in range(1, n_col):
-        pending.append(step(wbuf.at[col], wbuf.at[col], k, device("pcol", wpeer(k)), (send_e, recv_e)))
-    for k in range(1, n_col):
-        step(wbuf.at[col], wbuf.at[wsender(k)], k, device("pcol", wsender(k)), (send_e, recv_e)).wait_recv()
-    width_w = wbuf.shape[2]
+        for r in range(blocks_w):
+            w_copy(k, r, wsender(k), wsender(k)).wait_recv()
+    width_w = wbuf.shape[3]
     for c in range(n_col):
-        out_ref[:, c * width_w:(c + 1) * width_w] = wbuf[c]
+        for r in range(blocks_w):
+            out_ref[:, (c * blocks_w + r) * width_w:(c * blocks_w + r + 1) * width_w] = wbuf[c, r]
     for sent in pending:
         sent.wait_send()
 
@@ -396,11 +406,11 @@
 def gram_weighted(x, mode_shapes, axes, sizes):
     n, rows, width = x.shape
     n_col = sizes["pcol"]
-    wshape = (n_col, mode_shapes.shape[0], 4 * rows)
+    wshape = (n_col, 4, mode_shapes.shape[0], rows)
     kernel = functools.partial(gram_weighted_kernel, axes=axes, factors=factor_table(sizes))
     return pl.pallas_call(
         kernel,
-        out_shape=jax.ShapeDtypeStruct((wshape[1], n_col * wshape[2]), jnp.bfloat16),
+        out_shape=jax.ShapeDtypeStruct((wshape[2], n_col * 4 * rows), jnp.bfloat16),
         in_specs=[pl.BlockSpec(memory_space=pltpu.VMEM)] * 2,
         out_specs=pl.BlockSpec(memory_space=pltpu.VMEM),
         scratch_shapes=[
@@ -418,8 +428,8 @@
             pltpu.SemaphoreType.DMA((n,)),
             pltpu.SemaphoreType.DMA((n,)),
             pltpu.SemaphoreType.DMA((n,)),
-            pltpu.SemaphoreType.DMA((n_col,)),
-            pltpu.SemaphoreType.DMA((n_col,)),
+            pltpu.SemaphoreType.DMA((4 * n_col,)),
+            pltpu.SemaphoreType.DMA((4 * n_col,)),
         ],
         compiler_params=pltpu.CompilerParams(collective_id=103, has_side_effects=True),
     )(x, mode_shapes)

time: 170 us -> 168 us (0.988)
  Pallas kernels: 125 us -> 123 us
    pallas_call x1, Pallas kernels: 72.2 us -> 69.7 us  [gram_weighted(): pl.pallas_call(kernel, out_shape=jax.ShapeDtypeStruct((wshape[2], n_col *...]
  transfers between devices with their start and end apart: 3 -> 3, of which waited for: 2 -> 2; matrix products, arithmetic and copies ran while one was open for 8% -> 9% of each run, Pallas kernels for 74% -> 73%
where the time goes in v25:
time: 168 us; the launch traced here: 167 us
  Pallas kernels  123 us (73%)
  matrix products  13.8 us (8%)
  between operations  13.5 us (8%)
  waiting for transfers between devices  7.29 us (4%)
  starting transfers between devices  4.84 us (3%)
  local copies, waits for them, and re-layouts  3.2 us (2%)
  other arithmetic  1.79 us (1%)
    pallas_call x1, Pallas kernels, gram_weighted(): pl.pallas_call(kernel, out_shape=jax.ShapeDtypeStruct((wshape[2], n_col *...  69.7 us
    pallas_call x1, Pallas kernels, modal_sum(): pl.pallas_call(kernel, out_shape=jax.ShapeDtypeStruct((2,) + block, jnp.b...  53.3 us
    dot_general x3, matrix products, outer_rows(): lax.dot_general(left_rows, right_rows, (((1,), (1,)), ((), ())), preferre...  7.07 us
    dot_general x1, matrix products, body(): mine = jnp.dot(own_modes, factor_cols, preferred_element_type=jnp.float32)  4.57 us
    ppermute x1, waiting for transfers between devices, body(): panel_piece = lax.ppermute(send_half, ('prow', 'pcol'), swap)  4.04 us
    ppermute x1, starting transfers between devices, body(): panel_piece = lax.ppermute(send_half, ('prow', 'pcol'), swap)  3.77 us
  transfers between devices with their start and end apart: 3, of which 2 were waited for; matrix products, arithmetic and copies ran while one was open for 9% of the time, Pallas kernels for 73%

profile of v25, /device:TPU:39, one launch (start us, length us, event | category | flops | bytes accessed | tf_op | source)
XLA Modules:
  0.0 167.4 jit_solution(1284524270122958048)
XLA Ops:
  6.5 0.0 copy-start
  6.5 0.0 all-gather.2.cloned.1.call-start
  6.5 1.1 constant_dynamic-slice_fusion
  7.6 3.8 %collective-permute-start = (bf16[128,1024]{1,0:T(8,128)(2,1)S(1)}, bf16[128,1024]{1,0:T(8,128)(2,1)S(1)}, u32[]{:S(2)}, u32[]{:S(2)}) collective-permute-start(bf16[128,1024]{1,0:T(8,128)(2,1)S(1)} %constant_dynamic-slice_fusion), channel_id=1, source_target_pairs={{0,0},{64,16},{128,32},{192,48},{16,64},{80,80},{144,96},{208,112}... | collective-permute-start | bytes 786440 | tf_op jit(solution)/shard_map/ppermute | solution.py:531
  11.4 4.0 %collective-permute-done = bf16[128,1024]{1,0:T(8,128)(2,1)S(1)} collective-permute-done((bf16[128,1024]{1,0:T(8,128)(2,1)S(1)}, bf16[128,1024]{1,0:T(8,128)(2,1)S(1)}, u32[]{:S(2)}, u32[]{:S(2)}) %collective-permute-start) | collective-permute-done | bytes 262176 | tf_op jit(solution)/shard_map/ppermute | solution.py:531
  15.4 0.0 copy-start.2
  15.4 0.7 copy-done.2
  16.1 0.0 all-gather.2.cloned.1.call-update
  16.2 0.0 copy-done
  16.2 0.0 copy-start.5
  16.2 4.6 %fusion.2.mine_ref = f32[1024,256]{1,0:T(8,128)} fusion(bf16[2048,256]{1,0:T(8,128)(2,1)S(1)} %copy-done, bf16[2048,2048]{1,0:T(8,128)(2,1)} %param.6, s32[]{:T(128)S(6)} %select_n.28), kind=kOutput, calls=%fused_computation.2 | convolution fusion | flops 1073741824 | bytes 6291460 | tf_op jit(solution)/shard_map/dot_general | solution.py:513
  20.8 0.1 copy-done.5
  20.9 0.0 copy-start.3
  20.9 0.0 copy-start.4
  20.9 2.1 %fusion.6.theirs_ref = bf16[1024,256]{1,0:T(8,128)(2,1)} fusion(bf16[2048,256]{1,0:T(8,128)(2,1)S(1)} %copy-done, bf16[2048,2048]{1,0:T(8,128)(2,1)S(1)} %copy-done.5, s32[]{:T(128)S(6)} %select_n.29), kind=kOutput, calls=%fused_computation.13 | convolution fusion | flops 1074003968 | bytes 5767172 | tf_op jit(solution)/shard_map/dot_general | solution.py:514
  23.0 53.3 %shard_map.55 = bf16[2,4,256,256]{3,2,1,0:T(8,128)(2,1)} custom-call(f32[1024,256]{1,0:T(8,128)} %fusion.2.mine_ref, bf16[1024,256]{1,0:T(8,128)(2,1)} %fusion.6.theirs_ref), custom_call_target="tpu_custom_call" | custom-call | tf_op jit(solution)/shard_map/pallas_call | solution.py:252
  76.3 0.0 copy-done.3
  76.4 0.0 copy-done.4
  76.4 1.8 %fusion.4 = (bf16[2048,256]{1,0:T(8,128)(2,1)S(1)}, bf16[2048,256]{1,0:T(8,128)(2,1)S(1)}) fusion(bf16[2,4,256,256]{3,2,1,0:T(8,128)(2,1)} %shard_map.55, f32[2048]{0:T(1024)S(1)} %get-tuple-element.11, f32[2048]{0:T(1024)S(1)} %get-tuple-element.12), kind=kLoop, calls=%fused_computation.11 | loop fusion | flops 2621440 | bytes 3162112 | tf_op jit(solution)/shard_map/convert_element_type | solution.py:519
  78.2 0.8 convolution_convert_fusion
  79.0 0.3 copy.6
  79.3 1.0 copy.7
  80.3 69.7 %shard_map.56 = bf16[128,2048]{1,0:T(8,128)(2,1)} custom-call(bf16[16,128,128]{2,1,0:T(8,128)(2,1)} %bitcast.10, bf16[128,2048]{1,0:T(8,128)(2,1)} %shapes_ref.1), custom_call_target="tpu_custom_call" | custom-call | tf_op jit(solution)/shard_map/pallas_call | solution.py:411
  150.0 0.0 copy-start.1
  150.0 0.0 all-gather.2.cloned.1.call-done
  150.0 1.1 collective-permute-start.1
  151.1 3.8 %fusion.9 = f32[128,2048]{1,0:T(8,128)S(1)} fusion(bf16[2048,1024]{1,0:T(8,128)(2,1)} %all-gather.2.cloned.1.call-done, bf16[128,2048]{1,0:T(8,128)(2,1)} %shard_map.56, s32[]{:T(128)S(6)} %select_n.28), kind=kOutput, calls=%fused_computation.14 | convolution fusion | flops 536870912 | bytes 5505028 | tf_op jit(solution)/shard_map/dot_general | solution.py:22
  154.9 3.2 %collective-permute-done.1 = bf16[2048,1024]{1,0:T(8,128)(2,1)S(1)} collective-permute-done((bf16[2048,1024]{1,0:T(8,128)(2,1)}, bf16[2048,1024]{1,0:T(8,128)(2,1)S(1)}, u32[]{:S(2)}, u32[]{:S(2)}) %collective-permute-start.1) | collective-permute-done | bytes 4194336 | tf_op jit(solution)/shard_map/ppermute | solution.py:535
  158.1 0.0 copy-done.1
  158.1 2.5 %convolution_add_fusion = f32[128,2048]{1,0:T(8,128)} fusion(f32[128,2048]{1,0:T(8,128)S(1)} %fusion.9, bf16[2048,1024]{1,0:T(8,128)(2,1)S(1)} %collective-permute-done.1, bf16[128,2048]{1,0:T(8,128)(2,1)S(1)} %copy-done.1, s32[]{:T(128)S(6)} %select_n.29), kind=kOutput, calls=%fused_computation.6 | convolution fusion | flops 537133056 | bytes 6553604 | tf_op jit(solution)/shard_map/dot_general | solution.py:22
  (1 shorter events, 0.0 us)
Async XLA Ops:
  6.5 9.6 %copy-start = (bf16[2048,256]{1,0:T(8,128)(2,1)S(1)}, bf16[2048,256]{1,0:T(8,128)(2,1)}, u32[]{:S(2)}) copy-start(bf16[2048,256]{1,0:T(8,128)(2,1)} %param.5) | copy-start | bytes 3145732
  6.5 143.5 %all-gather.2.cloned.1.call-start = ((), (), s32[]{:S(2)}) async-start(), calls=%async_computation | async-start | bytes 4456448 | tf_op jit(solution)/shard_map/all_gather | solution.py:532
  7.6 7.8 %collective-permute-start = (bf16[128,1024]{1,0:T(8,128)(2,1)S(1)}, bf16[128,1024]{1,0:T(8,128)(2,1)S(1)}, u32[]{:S(2)}, u32[]{:S(2)}) collective-permute-start(bf16[128,1024]{1,0:T(8,128)(2,1)S(1)} %constant_dynamic-slice_fusion), channel_id=1, source_target_pairs={{0,0},{64,16},{128,32},{192,48},{16,64},{80,80},{144,96},{208,112}... | collective-permute-start | bytes 786440 | tf_op jit(solution)/shard_map/ppermute | solution.py:531
  15.4 0.7 copy-start.2
  16.2 4.7 %copy-start.5 = (bf16[2048,2048]{1,0:T(8,128)(2,1)S(1)}, bf16[2048,2048]{1,0:T(8,128)(2,1)}, u32[]{:S(2)}) copy-start(bf16[2048,2048]{1,0:T(8,128)(2,1)} %param.6) | copy-start | bytes 25165828
  20.9 55.5 %copy-start.3 = (f32[2048]{0:T(1024)S(1)}, f32[2048]{0:T(1024)}, u32[]{:S(2)}) copy-start(f32[2048]{0:T(1024)} %param.8) | copy-start | bytes 24580
  20.9 55.5 %copy-start.4 = (f32[2048]{0:T(1024)S(1)}, f32[2048]{0:T(1024)}, u32[]{:S(2)}) copy-start(f32[2048]{0:T(1024)} %param.9) | copy-start | bytes 24580
  150.0 8.1 %copy-start.1 = (bf16[128,2048]{1,0:T(8,128)(2,1)S(1)}, bf16[128,2048]{1,0:T(8,128)(2,1)}, u32[]{:S(2)}) copy-start(bf16[128,2048]{1,0:T(8,128)(2,1)} %shard_map.56) | copy-start | bytes 1572868
  150.0 8.1 %collective-permute-start.1 = (bf16[2048,1024]{1,0:T(8,128)(2,1)}, bf16[2048,1024]{1,0:T(8,128)(2,1)S(1)}, u32[]{:S(2)}, u32[]{:S(2)}) collective-permute-start(bf16[2048,1024]{1,0:T(8,128)(2,1)} %all-gather.2.cloned.1.call-done), channel_id=1, source_target_pairs={{0,64},{64,0},{128,192},{192,128},{1,65},{65,1},{129,193},{193,129... | collective-permute-start | bytes 12582920 | tf_op jit(solution)/shard_map/ppermute | solution.py:535
Sparse Core Ops, SparseCore 0:
  16.3 93.9 all-gather.1

commit v26 on v25

--- a/solution.py
+++ b/solution.py
@@ -389,9 +389,17 @@
                 pending.append(w_copy(k, r, wpeer(k), col))
 
     send_blocks(own, core)
+    other = [jnp.zeros((shapes_ref.shape[0], sib_coll.shape[2]), jnp.float32) for h in range(2)]
     for l in range(n):
         to_sibling(l).wait_recv()
-    send_blocks([weighted_block(sib_coll, h) for h in range(2)], 1 - core)
+        columns = shapes_ref[:, l * chunk:(l + 1) * chunk]
+        other = [
+            other[h] + lax.dot_general(
+                columns, sib_coll[l, h], (((1,), (1,)), ((), ())), preferred_element_type=jnp.float32
+            )
+            for h in range(2)
+        ]
+    send_blocks(other, 1 - core)
     for k in range(1, n_col):
         for r in range(blocks_w):
             w_copy(k, r, wsender(k), wsender(k)).wait_recv()

time: 168 us -> 168 us (level)
  no operation moved by 1% of the time
where the time goes in v26:
time: 168 us; the launch traced here: 167 us
  Pallas kernels  123 us (73%)
  matrix products  13.8 us (8%)
  between operations  13.5 us (8%)
  waiting for transfers between devices  7.29 us (4%)
  starting transfers between devices  5.12 us (3%)
  local copies, waits for them, and re-layouts  3.2 us (2%)
  other arithmetic  1.79 us (1%)
    pallas_call x1, Pallas kernels, gram_weighted(): pl.pallas_call(kernel, out_shape=jax.ShapeDtypeStruct((wshape[2], n_col *...  69.4 us
    pallas_call x1, Pallas kernels, modal_sum(): pl.pallas_call(kernel, out_shape=jax.ShapeDtypeStruct((2,) + block, jnp.b...  53.3 us
    dot_general x3, matrix products, outer_rows(): lax.dot_general(left_rows, right_rows, (((1,), (1,)), ((), ())), preferre...  7.07 us
    dot_general x1, matrix products, body(): mine = jnp.dot(own_modes, factor_cols, preferred_element_type=jnp.float32)  4.57 us
    ppermute x1, waiting for transfers between devices, body(): panel_piece = lax.ppermute(send_half, ('prow', 'pcol'), swap)  4.04 us
    ppermute x1, starting transfers between devices, body(): panel_piece = lax.ppermute(send_half, ('prow', 'pcol'), swap)  3.77 us
  transfers between devices with their start and end apart: 3, of which 2 were waited for; matrix products, arithmetic and copies ran while one was open for 9% of the time, Pallas kernels for 73%

profile of v26, /device:TPU:39, one launch (start us, length us, event | category | flops | bytes accessed | tf_op | source)
XLA Modules:
  0.0 167.4 jit_solution(8498275170834848131)
XLA Ops:
  6.5 0.0 copy-start
  6.5 0.0 all-gather.2.cloned.1.call-start
  6.5 1.1 constant_dynamic-slice_fusion
  7.6 3.8 %collective-permute-start = (bf16[128,1024]{1,0:T(8,128)(2,1)S(1)}, bf16[128,1024]{1,0:T(8,128)(2,1)S(1)}, u32[]{:S(2)}, u32[]{:S(2)}) collective-permute-start(bf16[128,1024]{1,0:T(8,128)(2,1)S(1)} %constant_dynamic-slice_fusion), channel_id=1, source_target_pairs={{0,0},{64,16},{128,32},{192,48},{16,64},{80,80},{144,96},{208,112}... | collective-permute-start | bytes 786440 | tf_op jit(solution)/shard_map/ppermute | solution.py:539
  11.4 4.0 %collective-permute-done = bf16[128,1024]{1,0:T(8,128)(2,1)S(1)} collective-permute-done((bf16[128,1024]{1,0:T(8,128)(2,1)S(1)}, bf16[128,1024]{1,0:T(8,128)(2,1)S(1)}, u32[]{:S(2)}, u32[]{:S(2)}) %collective-permute-start) | collective-permute-done | bytes 262176 | tf_op jit(solution)/shard_map/ppermute | solution.py:539
  15.4 0.0 copy-start.2
  15.4 0.7 copy-done.2
  16.1 0.0 all-gather.2.cloned.1.call-update
  16.2 0.0 copy-done
  16.2 0.0 copy-start.5
  16.2 4.6 %fusion.2.mine_ref = f32[1024,256]{1,0:T(8,128)} fusion(bf16[2048,256]{1,0:T(8,128)(2,1)S(1)} %copy-done, bf16[2048,2048]{1,0:T(8,128)(2,1)} %param.6, s32[]{:T(128)S(6)} %select_n.28), kind=kOutput, calls=%fused_computation.2 | convolution fusion | flops 1073741824 | bytes 6291460 | tf_op jit(solution)/shard_map/dot_general | solution.py:521
  20.8 0.1 copy-done.5
  20.9 0.0 copy-start.3
  20.9 0.0 copy-start.4
  20.9 2.1 %fusion.6.theirs_ref = bf16[1024,256]{1,0:T(8,128)(2,1)} fusion(bf16[2048,256]{1,0:T(8,128)(2,1)S(1)} %copy-done, bf16[2048,2048]{1,0:T(8,128)(2,1)S(1)} %copy-done.5, s32[]{:T(128)S(6)} %select_n.29), kind=kOutput, calls=%fused_computation.13 | convolution fusion | flops 1074003968 | bytes 5767172 | tf_op jit(solution)/shard_map/dot_general | solution.py:522
  23.0 53.3 %shard_map.55 = bf16[2,4,256,256]{3,2,1,0:T(8,128)(2,1)} custom-call(f32[1024,256]{1,0:T(8,128)} %fusion.2.mine_ref, bf16[1024,256]{1,0:T(8,128)(2,1)} %fusion.6.theirs_ref), custom_call_target="tpu_custom_call" | custom-call | tf_op jit(solution)/shard_map/pallas_call | solution.py:252
  76.3 0.0 copy-done.3
  76.4 0.0 copy-done.4
  76.4 1.8 %fusion.4 = (bf16[2048,256]{1,0:T(8,128)(2,1)S(1)}, bf16[2048,256]{1,0:T(8,128)(2,1)S(1)}) fusion(bf16[2,4,256,256]{3,2,1,0:T(8,128)(2,1)} %shard_map.55, f32[2048]{0:T(1024)S(1)} %get-tuple-element.11, f32[2048]{0:T(1024)S(1)} %get-tuple-element.12), kind=kLoop, calls=%fused_computation.11 | loop fusion | flops 2621440 | bytes 3162112 | tf_op jit(solution)/shard_map/convert_element_type | solution.py:527
  78.2 0.8 convolution_convert_fusion
  79.0 0.3 copy.6
  79.3 1.0 copy.7
  80.3 69.4 %shard_map.56 = bf16[128,2048]{1,0:T(8,128)(2,1)} custom-call(bf16[16,128,128]{2,1,0:T(8,128)(2,1)} %bitcast.10, bf16[128,2048]{1,0:T(8,128)(2,1)} %shapes_ref.1), custom_call_target="tpu_custom_call" | custom-call | tf_op jit(solution)/shard_map/pallas_call | solution.py:419
  149.7 0.0 copy-start.1
  149.7 0.0 all-gather.2.cloned.1.call-done
  149.7 1.4 collective-permute-start.1
  151.1 3.8 %fusion.9 = f32[128,2048]{1,0:T(8,128)S(1)} fusion(bf16[2048,1024]{1,0:T(8,128)(2,1)} %all-gather.2.cloned.1.call-done, bf16[128,2048]{1,0:T(8,128)(2,1)} %shard_map.56, s32[]{:T(128)S(6)} %select_n.28), kind=kOutput, calls=%fused_computation.14 | convolution fusion | flops 536870912 | bytes 5505028 | tf_op jit(solution)/shard_map/dot_general | solution.py:22
  154.9 3.2 %collective-permute-done.1 = bf16[2048,1024]{1,0:T(8,128)(2,1)S(1)} collective-permute-done((bf16[2048,1024]{1,0:T(8,128)(2,1)}, bf16[2048,1024]{1,0:T(8,128)(2,1)S(1)}, u32[]{:S(2)}, u32[]{:S(2)}) %collective-permute-start.1) | collective-permute-done | bytes 4194336 | tf_op jit(solution)/shard_map/ppermute | solution.py:543
  158.1 0.0 copy-done.1
  158.1 2.5 %convolution_add_fusion = f32[128,2048]{1,0:T(8,128)} fusion(f32[128,2048]{1,0:T(8,128)S(1)} %fusion.9, bf16[2048,1024]{1,0:T(8,128)(2,1)S(1)} %collective-permute-done.1, bf16[128,2048]{1,0:T(8,128)(2,1)S(1)} %copy-done.1, s32[]{:T(128)S(6)} %select_n.29), kind=kOutput, calls=%fused_computation.6 | convolution fusion | flops 537133056 | bytes 6553604 | tf_op jit(solution)/shard_map/dot_general | solution.py:22
  (1 shorter events, 0.0 us)
Async XLA Ops:
  6.5 9.6 %copy-start = (bf16[2048,256]{1,0:T(8,128)(2,1)S(1)}, bf16[2048,256]{1,0:T(8,128)(2,1)}, u32[]{:S(2)}) copy-start(bf16[2048,256]{1,0:T(8,128)(2,1)} %param.5) | copy-start | bytes 3145732
  6.5 143.2 %all-gather.2.cloned.1.call-start = ((), (), s32[]{:S(2)}) async-start(), calls=%async_computation | async-start | bytes 4456448 | tf_op jit(solution)/shard_map/all_gather | solution.py:540
  7.6 7.8 %collective-permute-start = (bf16[128,1024]{1,0:T(8,128)(2,1)S(1)}, bf16[128,1024]{1,0:T(8,128)(2,1)S(1)}, u32[]{:S(2)}, u32[]{:S(2)}) collective-permute-start(bf16[128,1024]{1,0:T(8,128)(2,1)S(1)} %constant_dynamic-slice_fusion), channel_id=1, source_target_pairs={{0,0},{64,16},{128,32},{192,48},{16,64},{80,80},{144,96},{208,112}... | collective-permute-start | bytes 786440 | tf_op jit(solution)/shard_map/ppermute | solution.py:539
  15.4 0.7 copy-start.2
  16.2 4.7 %copy-start.5 = (bf16[2048,2048]{1,0:T(8,128)(2,1)S(1)}, bf16[2048,2048]{1,0:T(8,128)(2,1)}, u32[]{:S(2)}) copy-start(bf16[2048,2048]{1,0:T(8,128)(2,1)} %param.6) | copy-start | bytes 25165828
  20.9 55.5 %copy-start.3 = (f32[2048]{0:T(1024)S(1)}, f32[2048]{0:T(1024)}, u32[]{:S(2)}) copy-start(f32[2048]{0:T(1024)} %param.8) | copy-start | bytes 24580
  20.9 55.5 %copy-start.4 = (f32[2048]{0:T(1024)S(1)}, f32[2048]{0:T(1024)}, u32[]{:S(2)}) copy-start(f32[2048]{0:T(1024)} %param.9) | copy-start | bytes 24580
  149.7 8.4 %copy-start.1 = (bf16[128,2048]{1,0:T(8,128)(2,1)S(1)}, bf16[128,2048]{1,0:T(8,128)(2,1)}, u32[]{:S(2)}) copy-start(bf16[128,2048]{1,0:T(8,128)(2,1)} %shard_map.56) | copy-start | bytes 1572868
  149.7 8.3 %collective-permute-start.1 = (bf16[2048,1024]{1,0:T(8,128)(2,1)}, bf16[2048,1024]{1,0:T(8,128)(2,1)S(1)}, u32[]{:S(2)}, u32[]{:S(2)}) collective-permute-start(bf16[2048,1024]{1,0:T(8,128)(2,1)} %all-gather.2.cloned.1.call-done), channel_id=1, source_target_pairs={{0,64},{64,0},{128,192},{192,128},{1,65},{65,1},{129,193},{193,129... | collective-permute-start | bytes 12582920 | tf_op jit(solution)/shard_map/ppermute | solution.py:543
Sparse Core Ops, SparseCore 0:
  16.3 93.9 all-gather.1

commit v27 on v25

--- a/solution.py
+++ b/solution.py
@@ -340,10 +340,6 @@
     mine, theirs = part_out[...], part_in[...]
     coll[me] = jnp.stack([jnp.where(half == 0, mine, theirs), jnp.where(half == 0, theirs, mine)])
 
-    for k in range(1, n):
-        step(coll.at[me], coll.at[me], k, device("pl", peer(k)), (send_c, recv_c)).start()
-    for k in range(1, n):
-        pending.append(step(coll.at[me], coll.at[me], k, device("pl", peer(k)), (send_c, recv_c)))
 
     def to_sibling(chunk_at):
         return pltpu.make_async_remote_copy(
@@ -353,6 +349,10 @@
 
     to_sibling(me).start()
     pending.append(to_sibling(me))
+    for k in range(1, n):
+        step(coll.at[me], coll.at[me], k, device("pl", peer(k)), (send_c, recv_c)).start()
+    for k in range(1, n):
+        pending.append(step(coll.at[me], coll.at[me], k, device("pl", peer(k)), (send_c, recv_c)))
     for k in range(1, n):
         step(coll.at[me], coll.at[sender(k)], k, device("pl", sender(k)), (send_c, recv_c)).wait_recv()
         to_sibling(sender(k)).start()

time: 168 us -> 168 us (level)
  no operation moved by 1% of the time
where the time goes in v27:
time: 168 us; the launch traced here: 167 us
  Pallas kernels  123 us (73%)
  matrix products  13.8 us (8%)
  between operations  13.5 us (8%)
  waiting for transfers between devices  7.29 us (4%)
  starting transfers between devices  4.84 us (3%)
  local copies, waits for them, and re-layouts  3.2 us (2%)
  other arithmetic  1.79 us (1%)
    pallas_call x1, Pallas kernels, gram_weighted(): pl.pallas_call(kernel, out_shape=jax.ShapeDtypeStruct((wshape[2], n_col *...  69.7 us
    pallas_call x1, Pallas kernels, modal_sum(): pl.pallas_call(kernel, out_shape=jax.ShapeDtypeStruct((2,) + block, jnp.b...  53.3 us
    dot_general x3, matrix products, outer_rows(): lax.dot_general(left_rows, right_rows, (((1,), (1,)), ((), ())), preferre...  7.07 us
    dot_general x1, matrix products, body(): mine = jnp.dot(own_modes, factor_cols, preferred_element_type=jnp.float32)  4.57 us
    ppermute x1, waiting for transfers between devices, body(): panel_piece = lax.ppermute(send_half, ('prow', 'pcol'), swap)  4.04 us
    ppermute x1, starting transfers between devices, body(): panel_piece = lax.ppermute(send_half, ('prow', 'pcol'), swap)  3.77 us
  transfers between devices with their start and end apart: 3, of which 2 were waited for; matrix products, arithmetic and copies ran while one was open for 9% of the time, Pallas kernels for 73%

profile of v27, /device:TPU:39, one launch (start us, length us, event | category | flops | bytes accessed | tf_op | source)
XLA Modules:
  0.0 167.4 jit_solution(7403165850075786977)
XLA Ops:
  6.5 0.0 copy-start
  6.5 0.0 all-gather.2.cloned.1.call-start
  6.5 1.1 constant_dynamic-slice_fusion
  7.6 3.8 %collective-permute-start = (bf16[128,1024]{1,0:T(8,128)(2,1)S(1)}, bf16[128,1024]{1,0:T(8,128)(2,1)S(1)}, u32[]{:S(2)}, u32[]{:S(2)}) collective-permute-start(bf16[128,1024]{1,0:T(8,128)(2,1)S(1)} %constant_dynamic-slice_fusion), channel_id=1, source_target_pairs={{0,0},{64,16},{128,32},{192,48},{16,64},{80,80},{144,96},{208,112}... | collective-permute-start | bytes 786440 | tf_op jit(solution)/shard_map/ppermute | solution.py:531
  11.4 4.0 %collective-permute-done = bf16[128,1024]{1,0:T(8,128)(2,1)S(1)} collective-permute-done((bf16[128,1024]{1,0:T(8,128)(2,1)S(1)}, bf16[128,1024]{1,0:T(8,128)(2,1)S(1)}, u32[]{:S(2)}, u32[]{:S(2)}) %collective-permute-start) | collective-permute-done | bytes 262176 | tf_op jit(solution)/shard_map/ppermute | solution.py:531
  15.4 0.0 copy-start.2
  15.4 0.7 copy-done.2
  16.1 0.0 all-gather.2.cloned.1.call-update
  16.2 0.0 copy-done
  16.2 0.0 copy-start.5
  16.2 4.6 %fusion.2.mine_ref = f32[1024,256]{1,0:T(8,128)} fusion(bf16[2048,256]{1,0:T(8,128)(2,1)S(1)} %copy-done, bf16[2048,2048]{1,0:T(8,128)(2,1)} %param.6, s32[]{:T(128)S(6)} %select_n.28), kind=kOutput, calls=%fused_computation.2 | convolution fusion | flops 1073741824 | bytes 6291460 | tf_op jit(solution)/shard_map/dot_general | solution.py:513
  20.8 0.1 copy-done.5
  20.9 0.0 copy-start.3
  20.9 0.0 copy-start.4
  20.9 2.1 %fusion.6.theirs_ref = bf16[1024,256]{1,0:T(8,128)(2,1)} fusion(bf16[2048,256]{1,0:T(8,128)(2,1)S(1)} %copy-done, bf16[2048,2048]{1,0:T(8,128)(2,1)S(1)} %copy-done.5, s32[]{:T(128)S(6)} %select_n.29), kind=kOutput, calls=%fused_computation.13 | convolution fusion | flops 1074003968 | bytes 5767172 | tf_op jit(solution)/shard_map/dot_general | solution.py:514
  23.0 53.3 %shard_map.55 = bf16[2,4,256,256]{3,2,1,0:T(8,128)(2,1)} custom-call(f32[1024,256]{1,0:T(8,128)} %fusion.2.mine_ref, bf16[1024,256]{1,0:T(8,128)(2,1)} %fusion.6.theirs_ref), custom_call_target="tpu_custom_call" | custom-call | tf_op jit(solution)/shard_map/pallas_call | solution.py:252
  76.3 0.0 copy-done.3
  76.4 0.0 copy-done.4
  76.4 1.8 %fusion.4 = (bf16[2048,256]{1,0:T(8,128)(2,1)S(1)}, bf16[2048,256]{1,0:T(8,128)(2,1)S(1)}) fusion(bf16[2,4,256,256]{3,2,1,0:T(8,128)(2,1)} %shard_map.55, f32[2048]{0:T(1024)S(1)} %get-tuple-element.11, f32[2048]{0:T(1024)S(1)} %get-tuple-element.12), kind=kLoop, calls=%fused_computation.11 | loop fusion | flops 2621440 | bytes 3162112 | tf_op jit(solution)/shard_map/convert_element_type | solution.py:519
  78.2 0.8 convolution_convert_fusion
  79.0 0.3 copy.6
  79.3 1.0 copy.7
  80.3 69.7 %shard_map.56 = bf16[128,2048]{1,0:T(8,128)(2,1)} custom-call(bf16[16,128,128]{2,1,0:T(8,128)(2,1)} %bitcast.10, bf16[128,2048]{1,0:T(8,128)(2,1)} %shapes_ref.1), custom_call_target="tpu_custom_call" | custom-call | tf_op jit(solution)/shard_map/pallas_call | solution.py:411
  150.0 0.0 copy-start.1
  150.0 0.0 all-gather.2.cloned.1.call-done
  150.0 1.1 collective-permute-start.1
  151.1 3.8 %fusion.9 = f32[128,2048]{1,0:T(8,128)S(1)} fusion(bf16[2048,1024]{1,0:T(8,128)(2,1)} %all-gather.2.cloned.1.call-done, bf16[128,2048]{1,0:T(8,128)(2,1)} %shard_map.56, s32[]{:T(128)S(6)} %select_n.28), kind=kOutput, calls=%fused_computation.14 | convolution fusion | flops 536870912 | bytes 5505028 | tf_op jit(solution)/shard_map/dot_general | solution.py:22
  154.9 3.2 %collective-permute-done.1 = bf16[2048,1024]{1,0:T(8,128)(2,1)S(1)} collective-permute-done((bf16[2048,1024]{1,0:T(8,128)(2,1)}, bf16[2048,1024]{1,0:T(8,128)(2,1)S(1)}, u32[]{:S(2)}, u32[]{:S(2)}) %collective-permute-start.1) | collective-permute-done | bytes 4194336 | tf_op jit(solution)/shard_map/ppermute | solution.py:535
  158.1 0.0 copy-done.1
  158.1 2.5 %convolution_add_fusion = f32[128,2048]{1,0:T(8,128)} fusion(f32[128,2048]{1,0:T(8,128)S(1)} %fusion.9, bf16[2048,1024]{1,0:T(8,128)(2,1)S(1)} %collective-permute-done.1, bf16[128,2048]{1,0:T(8,128)(2,1)S(1)} %copy-done.1, s32[]{:T(128)S(6)} %select_n.29), kind=kOutput, calls=%fused_computation.6 | convolution fusion | flops 537133056 | bytes 6553604 | tf_op jit(solution)/shard_map/dot_general | solution.py:22
  (1 shorter events, 0.0 us)
Async XLA Ops:
  6.5 9.6 %copy-start = (bf16[2048,256]{1,0:T(8,128)(2,1)S(1)}, bf16[2048,256]{1,0:T(8,128)(2,1)}, u32[]{:S(2)}) copy-start(bf16[2048,256]{1,0:T(8,128)(2,1)} %param.5) | copy-start | bytes 3145732
  6.5 143.5 %all-gather.2.cloned.1.call-start = ((), (), s32[]{:S(2)}) async-start(), calls=%async_computation | async-start | bytes 4456448 | tf_op jit(solution)/shard_map/all_gather | solution.py:532
  7.6 7.8 %collective-permute-start = (bf16[128,1024]{1,0:T(8,128)(2,1)S(1)}, bf16[128,1024]{1,0:T(8,128)(2,1)S(1)}, u32[]{:S(2)}, u32[]{:S(2)}) collective-permute-start(bf16[128,1024]{1,0:T(8,128)(2,1)S(1)} %constant_dynamic-slice_fusion), channel_id=1, source_target_pairs={{0,0},{64,16},{128,32},{192,48},{16,64},{80,80},{144,96},{208,112}... | collective-permute-start | bytes 786440 | tf_op jit(solution)/shard_map/ppermute | solution.py:531
  15.4 0.7 copy-start.2
  16.2 4.7 %copy-start.5 = (bf16[2048,2048]{1,0:T(8,128)(2,1)S(1)}, bf16[2048,2048]{1,0:T(8,128)(2,1)}, u32[]{:S(2)}) copy-start(bf16[2048,2048]{1,0:T(8,128)(2,1)} %param.6) | copy-start | bytes 25165828
  20.9 55.5 %copy-start.3 = (f32[2048]{0:T(1024)S(1)}, f32[2048]{0:T(1024)}, u32[]{:S(2)}) copy-start(f32[2048]{0:T(1024)} %param.8) | copy-start | bytes 24580
  20.9 55.5 %copy-start.4 = (f32[2048]{0:T(1024)S(1)}, f32[2048]{0:T(1024)}, u32[]{:S(2)}) copy-start(f32[2048]{0:T(1024)} %param.9) | copy-start | bytes 24580
  150.0 8.1 %copy-start.1 = (bf16[128,2048]{1,0:T(8,128)(2,1)S(1)}, bf16[128,2048]{1,0:T(8,128)(2,1)}, u32[]{:S(2)}) copy-start(bf16[128,2048]{1,0:T(8,128)(2,1)} %shard_map.56) | copy-start | bytes 1572868
  150.0 8.1 %collective-permute-start.1 = (bf16[2048,1024]{1,0:T(8,128)(2,1)}, bf16[2048,1024]{1,0:T(8,128)(2,1)S(1)}, u32[]{:S(2)}, u32[]{:S(2)}) collective-permute-start(bf16[2048,1024]{1,0:T(8,128)(2,1)} %all-gather.2.cloned.1.call-done), channel_id=1, source_target_pairs={{0,64},{64,0},{128,192},{192,128},{1,65},{65,1},{129,193},{193,129... | collective-permute-start | bytes 12582920 | tf_op jit(solution)/shard_map/ppermute | solution.py:535
Sparse Core Ops, SparseCore 0:
  16.3 93.9 all-gather.1

commit v28 on v25

--- a/solution.py
+++ b/solution.py
@@ -310,14 +310,14 @@
 
     pending = []
     barrier = pltpu.get_barrier_semaphore()
+    pl.semaphore_signal(barrier, inc=1, device_id=partner, device_id_type=MESH)
+    pl.semaphore_signal(barrier, inc=1, device_id=sibling, device_id_type=MESH)
     for k in range(1, n):
         pl.semaphore_signal(barrier, inc=1, device_id=device("pl", lax.rem(me + k, n)), device_id_type=MESH)
     for k in range(1, n_col):
         pl.semaphore_signal(
             barrier, inc=1, device_id=device("pcol", lax.rem(col + k, n_col)), device_id_type=MESH
         )
-    pl.semaphore_signal(barrier, inc=1, device_id=partner, device_id_type=MESH)
-    pl.semaphore_signal(barrier, inc=1, device_id=sibling, device_id_type=MESH)
     pl.semaphore_wait(barrier, n + n_col)
 
     peer = lambda k: lax.rem(me + k, n)

time: 168 us -> 168 us (level)
  no operation moved by 1% of the time
where the time goes in v28:
time: 168 us
  Pallas kernels  123 us (73%)
  matrix products  13.8 us (8%)
  between operations  13.5 us (8%)
  waiting for transfers between devices  7.28 us (4%)
  starting transfers between devices  5.01 us (3%)
  local copies, waits for them, and re-layouts  3.2 us (2%)
  other arithmetic  1.79 us (1%)
    pallas_call x1, Pallas kernels, gram_weighted(): pl.pallas_call(kernel, out_shape=jax.ShapeDtypeStruct((wshape[2], n_col *...  69.8 us
    pallas_call x1, Pallas kernels, modal_sum(): pl.pallas_call(kernel, out_shape=jax.ShapeDtypeStruct((2,) + block, jnp.b...  53.3 us
    dot_general x3, matrix products, outer_rows(): lax.dot_general(left_rows, right_rows, (((1,), (1,)), ((), ())), preferre...  7.08 us
    dot_general x1, matrix products, body(): mine = jnp.dot(own_modes, factor_cols, preferred_element_type=jnp.float32)  4.57 us
    ppermute x1, waiting for transfers between devices, body(): panel_piece = lax.ppermute(send_half, ('prow', 'pcol'), swap)  4.04 us
    ppermute x1, starting transfers between devices, body(): panel_piece = lax.ppermute(send_half, ('prow', 'pcol'), swap)  3.77 us
  transfers between devices with their start and end apart: 3, of which 2 were waited for; matrix products, arithmetic and copies ran while one was open for 9% of the time, Pallas kernels for 73%

profile of v28, /device:TPU:39, one launch (start us, length us, event | category | flops | bytes accessed | tf_op | source)
XLA Modules:
  0.0 167.7 jit_solution(1222001168075461965)
XLA Ops:
  6.5 0.0 copy-start
  6.5 0.0 all-gather.2.cloned.1.call-start
  6.5 1.1 constant_dynamic-slice_fusion
  7.6 3.8 %collective-permute-start = (bf16[128,1024]{1,0:T(8,128)(2,1)S(1)}, bf16[128,1024]{1,0:T(8,128)(2,1)S(1)}, u32[]{:S(2)}, u32[]{:S(2)}) collective-permute-start(bf16[128,1024]{1,0:T(8,128)(2,1)S(1)} %constant_dynamic-slice_fusion), channel_id=1, source_target_pairs={{0,0},{64,16},{128,32},{192,48},{16,64},{80,80},{144,96},{208,112}... | collective-permute-start | bytes 786440 | tf_op jit(solution)/shard_map/ppermute | solution.py:531
  11.4 4.0 %collective-permute-done = bf16[128,1024]{1,0:T(8,128)(2,1)S(1)} collective-permute-done((bf16[128,1024]{1,0:T(8,128)(2,1)S(1)}, bf16[128,1024]{1,0:T(8,128)(2,1)S(1)}, u32[]{:S(2)}, u32[]{:S(2)}) %collective-permute-start) | collective-permute-done | bytes 262176 | tf_op jit(solution)/shard_map/ppermute | solution.py:531
  15.4 0.0 copy-start.2
  15.4 0.7 copy-done.2
  16.1 0.0 all-gather.2.cloned.1.call-update
  16.2 0.0 copy-done
  16.2 0.0 copy-start.5
  16.2 4.6 %fusion.2.mine_ref = f32[1024,256]{1,0:T(8,128)} fusion(bf16[2048,256]{1,0:T(8,128)(2,1)S(1)} %copy-done, bf16[2048,2048]{1,0:T(8,128)(2,1)} %param.6, s32[]{:T(128)S(6)} %select_n.28), kind=kOutput, calls=%fused_computation.2 | convolution fusion | flops 1073741824 | bytes 6291460 | tf_op jit(solution)/shard_map/dot_general | solution.py:513
  20.8 0.1 copy-done.5
  20.9 0.0 copy-start.3
  20.9 0.0 copy-start.4
  20.9 2.1 %fusion.6.theirs_ref = bf16[1024,256]{1,0:T(8,128)(2,1)} fusion(bf16[2048,256]{1,0:T(8,128)(2,1)S(1)} %copy-done, bf16[2048,2048]{1,0:T(8,128)(2,1)S(1)} %copy-done.5, s32[]{:T(128)S(6)} %select_n.29), kind=kOutput, calls=%fused_computation.13 | convolution fusion | flops 1074003968 | bytes 5767172 | tf_op jit(solution)/shard_map/dot_general | solution.py:514
  23.0 53.3 %shard_map.55 = bf16[2,4,256,256]{3,2,1,0:T(8,128)(2,1)} custom-call(f32[1024,256]{1,0:T(8,128)} %fusion.2.mine_ref, bf16[1024,256]{1,0:T(8,128)(2,1)} %fusion.6.theirs_ref), custom_call_target="tpu_custom_call" | custom-call | tf_op jit(solution)/shard_map/pallas_call | solution.py:252
  76.3 0.0 copy-done.3
  76.4 0.0 copy-done.4
  76.4 1.8 %fusion.4 = (bf16[2048,256]{1,0:T(8,128)(2,1)S(1)}, bf16[2048,256]{1,0:T(8,128)(2,1)S(1)}) fusion(bf16[2,4,256,256]{3,2,1,0:T(8,128)(2,1)} %shard_map.55, f32[2048]{0:T(1024)S(1)} %get-tuple-element.11, f32[2048]{0:T(1024)S(1)} %get-tuple-element.12), kind=kLoop, calls=%fused_computation.11 | loop fusion | flops 2621440 | bytes 3162112 | tf_op jit(solution)/shard_map/convert_element_type | solution.py:519
  78.2 0.8 convolution_convert_fusion
  79.0 0.3 copy.6
  79.3 1.0 copy.7
  80.3 69.8 %shard_map.56 = bf16[128,2048]{1,0:T(8,128)(2,1)} custom-call(bf16[16,128,128]{2,1,0:T(8,128)(2,1)} %bitcast.10, bf16[128,2048]{1,0:T(8,128)(2,1)} %shapes_ref.1), custom_call_target="tpu_custom_call" | custom-call | tf_op jit(solution)/shard_map/pallas_call | solution.py:411
  150.0 0.0 copy-start.1
  150.0 0.0 all-gather.2.cloned.1.call-done
  150.1 1.2 collective-permute-start.1
  151.3 3.8 %fusion.9 = f32[128,2048]{1,0:T(8,128)S(1)} fusion(bf16[2048,1024]{1,0:T(8,128)(2,1)} %all-gather.2.cloned.1.call-done, bf16[128,2048]{1,0:T(8,128)(2,1)} %shard_map.56, s32[]{:T(128)S(6)} %select_n.28), kind=kOutput, calls=%fused_computation.14 | convolution fusion | flops 536870912 | bytes 5505028 | tf_op jit(solution)/shard_map/dot_general | solution.py:22
  155.1 3.2 %collective-permute-done.1 = bf16[2048,1024]{1,0:T(8,128)(2,1)S(1)} collective-permute-done((bf16[2048,1024]{1,0:T(8,128)(2,1)}, bf16[2048,1024]{1,0:T(8,128)(2,1)S(1)}, u32[]{:S(2)}, u32[]{:S(2)}) %collective-permute-start.1) | collective-permute-done | bytes 4194336 | tf_op jit(solution)/shard_map/ppermute | solution.py:535
  158.3 0.0 copy-done.1
  158.3 2.5 %convolution_add_fusion = f32[128,2048]{1,0:T(8,128)} fusion(f32[128,2048]{1,0:T(8,128)S(1)} %fusion.9, bf16[2048,1024]{1,0:T(8,128)(2,1)S(1)} %collective-permute-done.1, bf16[128,2048]{1,0:T(8,128)(2,1)S(1)} %copy-done.1, s32[]{:T(128)S(6)} %select_n.29), kind=kOutput, calls=%fused_computation.6 | convolution fusion | flops 537133056 | bytes 6553604 | tf_op jit(solution)/shard_map/dot_general | solution.py:22
  (1 shorter events, 0.0 us)
Async XLA Ops:
  6.5 9.6 %copy-start = (bf16[2048,256]{1,0:T(8,128)(2,1)S(1)}, bf16[2048,256]{1,0:T(8,128)(2,1)}, u32[]{:S(2)}) copy-start(bf16[2048,256]{1,0:T(8,128)(2,1)} %param.5) | copy-start | bytes 3145732
  6.5 143.5 %all-gather.2.cloned.1.call-start = ((), (), s32[]{:S(2)}) async-start(), calls=%async_computation | async-start | bytes 4456448 | tf_op jit(solution)/shard_map/all_gather | solution.py:532
  7.6 7.8 %collective-permute-start = (bf16[128,1024]{1,0:T(8,128)(2,1)S(1)}, bf16[128,1024]{1,0:T(8,128)(2,1)S(1)}, u32[]{:S(2)}, u32[]{:S(2)}) collective-permute-start(bf16[128,1024]{1,0:T(8,128)(2,1)S(1)} %constant_dynamic-slice_fusion), channel_id=1, source_target_pairs={{0,0},{64,16},{128,32},{192,48},{16,64},{80,80},{144,96},{208,112}... | collective-permute-start | bytes 786440 | tf_op jit(solution)/shard_map/ppermute | solution.py:531
  15.4 0.7 copy-start.2
  16.2 4.7 %copy-start.5 = (bf16[2048,2048]{1,0:T(8,128)(2,1)S(1)}, bf16[2048,2048]{1,0:T(8,128)(2,1)}, u32[]{:S(2)}) copy-start(bf16[2048,2048]{1,0:T(8,128)(2,1)} %param.6) | copy-start | bytes 25165828
  20.9 55.5 %copy-start.3 = (f32[2048]{0:T(1024)S(1)}, f32[2048]{0:T(1024)}, u32[]{:S(2)}) copy-start(f32[2048]{0:T(1024)} %param.8) | copy-start | bytes 24580
  20.9 55.5 %copy-start.4 = (f32[2048]{0:T(1024)S(1)}, f32[2048]{0:T(1024)}, u32[]{:S(2)}) copy-start(f32[2048]{0:T(1024)} %param.9) | copy-start | bytes 24580
  150.0 8.3 %copy-start.1 = (bf16[128,2048]{1,0:T(8,128)(2,1)S(1)}, bf16[128,2048]{1,0:T(8,128)(2,1)}, u32[]{:S(2)}) copy-start(bf16[128,2048]{1,0:T(8,128)(2,1)} %shard_map.56) | copy-start | bytes 1572868
  150.1 8.2 %collective-permute-start.1 = (bf16[2048,1024]{1,0:T(8,128)(2,1)}, bf16[2048,1024]{1,0:T(8,128)(2,1)S(1)}, u32[]{:S(2)}, u32[]{:S(2)}) collective-permute-start(bf16[2048,1024]{1,0:T(8,128)(2,1)} %all-gather.2.cloned.1.call-done), channel_id=1, source_target_pairs={{0,64},{64,0},{128,192},{192,128},{1,65},{65,1},{129,193},{193,129... | collective-permute-start | bytes 12582920 | tf_op jit(solution)/shard_map/ppermute | solution.py:535
Sparse Core Ops, SparseCore 0:
  16.3 93.8 all-gather.1
